TPU v7x, 256 devices: a whole 4x4x8 slice. The times are simulated.
256 devices in a mesh: seq: 16 (over x, z_lo), ch: 16 (over z_hi, y, core).
Axes of the slice: x: 4, y: 4, z: 8 (z_hi: 2, z_lo: 4; z = z_hi * 4 + z_lo), core: 2. Of those that a mesh axis runs over, the one named last changes fastest.
Arguments:
- signal: bfloat16 [8192, 2048], P('seq', 'ch'), may hold values from -6 to 6
- filter_raw: bfloat16 [8192, 2048], P('seq', 'ch'), may hold values from -6 to 6
- gate: bfloat16 [8192, 2048], P('seq', 'ch'), may hold values from -6 to 6
- d_out: bfloat16 [8192, 2048], P('seq', 'ch'), may hold values from -6 to 6
- w_first: bfloat16 [32, 64, 64], P('ch'), may hold values from -0.75 to 0.75
- w_second: bfloat16 [64, 32, 32], P('ch'), may hold values from -1 to 1
Outputs:
- grad_signal: bfloat16 [8192, 2048], P('seq', 'ch')
- grad_filter: bfloat16 [8192, 2048], P('seq', 'ch')
- grad_gate: bfloat16 [8192, 2048], P('seq', 'ch')
- grad_first: float32 [32, 64, 64], P('ch', 'seq')
- grad_second: float32 [64, 32, 32], P('ch', 'seq')
All inputs are finite; a program needn't handle non-finite values.
Results may differ from a plain program's by a relative error of at most 0.02.
Values may be sent and summed in bfloat16 or wider, within the bound.
No kernel may reach another device: no remote copies, remote signals or barrier semaphores. Data moves between devices by JAX's collectives and lax.ppermute only.
A program may use at most 64 MiB of HBM per device.

v0:
```python
import math

import jax
import jax.numpy as jnp
from jax import lax
from jax.sharding import PartitionSpec as P

HIGHEST = lax.Precision.HIGHEST


def counting(count):
    return jnp.arange(count, dtype=jnp.int32)


def phase_table(row_ids, col_ids, length, sign):
    angles = (
        2.0 * math.pi / length * (row_ids[:, None] * col_ids[None, :] % length).astype(jnp.float32)
    )
    return (jnp.cos(angles), sign * jnp.sin(angles))


def contract(form, table, real_part, imag_part):
    cosine, sine = table
    out_real = jnp.einsum(form, cosine, real_part, precision=HIGHEST) - jnp.einsum(
        form, sine, imag_part, precision=HIGHEST
    )
    out_imag = jnp.einsum(form, cosine, imag_part, precision=HIGHEST) + jnp.einsum(
        form, sine, real_part, precision=HIGHEST
    )
    return (out_real, out_imag)


def rotate(cosine, sine, real_part, imag_part):
    return (real_part * cosine - imag_part * sine, real_part * sine + imag_part * cosine)


def factors(length):
    return (length // 128, 128)


def local_forward(real_part, imag_part):
    fields, group, rows, width = real_part.shape
    outer, inner = factors(rows)
    real_part = real_part.reshape(fields, group, outer, inner, width)
    imag_part = imag_part.reshape(fields, group, outer, inner, width)
    real_part, imag_part = contract(
        "qa,fkabc->fkqbc",
        phase_table(counting(outer), counting(outer), outer, -1.0),
        real_part,
        imag_part,
    )
    cosine, sine = phase_table(counting(outer), counting(inner), rows, -1.0)
    real_part, imag_part = rotate(cosine[:, :, None], sine[:, :, None], real_part, imag_part)
    return contract(
        "rb,fkqbc->fkqrc",
        phase_table(counting(inner), counting(inner), inner, -1.0),
        real_part,
        imag_part,
    )


def local_inverse(real_part, imag_part):
    fields, group, outer, inner, width = real_part.shape
    rows = outer * inner
    real_part, imag_part = contract(
        "br,fkqrc->fkqbc",
        phase_table(counting(inner), counting(inner), inner, 1.0),
        real_part,
        imag_part,
    )
    cosine, sine = phase_table(counting(outer), counting(inner), rows, 1.0)
    real_part, imag_part = rotate(cosine[:, :, None], sine[:, :, None], real_part, imag_part)
    real_part, imag_part = contract(
        "aq,fkqbc->fkabc",
        phase_table(counting(outer), counting(outer), outer, 1.0),
        real_part,
        imag_part,
    )
    return (
        real_part.reshape(fields, group, rows, width),
        imag_part.reshape(fields, group, rows, width),
    )


def forward_transform(fields):
    devices = lax.axis_size("seq")
    count, rows, width = fields.shape
    piece = rows // devices
    span = 2 * devices
    whole = span * rows
    parts = lax.all_to_all(fields[:, None], "seq", split_axis=2, concat_axis=1, tiled=True)
    cosine, sine = phase_table(counting(span), counting(devices), span, -1.0)
    real_part = jnp.einsum("ka,fabc->fkbc", cosine, parts, precision=HIGHEST)
    imag_part = jnp.einsum("ka,fabc->fkbc", sine, parts, precision=HIGHEST)
    positions = lax.axis_index("seq") * piece + counting(piece)
    cosine, sine = phase_table(counting(span), positions, whole, -1.0)
    real_part, imag_part = rotate(cosine[:, :, None], sine[:, :, None], real_part, imag_part)
    spectrum = lax.all_to_all(
        jnp.stack([real_part, imag_part], axis=1), "seq", split_axis=2, concat_axis=3, tiled=True
    )
    return local_forward(spectrum[:, 0], spectrum[:, 1])


def inverse_transform(real_part, imag_part):
    devices = lax.axis_size("seq")
    real_part, imag_part = local_inverse(real_part, imag_part)
    group = real_part.shape[1]
    rows = real_part.shape[2]
    span = 2 * devices
    whole = span * rows
    classes = lax.axis_index("seq") * group + counting(group)
    cosine, sine = phase_table(classes, counting(rows), whole, 1.0)
    real_part, imag_part = rotate(cosine[:, :, None], sine[:, :, None], real_part, imag_part)
    gathered = lax.all_to_all(
        jnp.stack([real_part, imag_part], axis=1), "seq", split_axis=3, concat_axis=2, tiled=True
    )
    cosine, sine = phase_table(counting(devices), counting(span), span, 1.0)
    inverse_scale = 1.0 / whole
    out_real = (
        jnp.einsum("ak,fkbc->fabc", cosine, gathered[:, 0], precision=HIGHEST)
        - jnp.einsum("ak,fkbc->fabc", sine, gathered[:, 1], precision=HIGHEST)
    ) * inverse_scale
    slab = lax.all_to_all(out_real, "seq", split_axis=1, concat_axis=2, tiled=True)
    return slab[:, 0]


def adjoint_spectra(spectra_real, spectra_imag, incoming_real, incoming_imag):
    toward_signal_real = spectra_real[1] * incoming_real + spectra_imag[1] * incoming_imag
    toward_signal_imag = spectra_real[1] * incoming_imag - spectra_imag[1] * incoming_real
    toward_filter_real = spectra_real[0] * incoming_real + spectra_imag[0] * incoming_imag
    toward_filter_imag = spectra_real[0] * incoming_imag - spectra_imag[0] * incoming_real
    return (toward_signal_real, toward_signal_imag, toward_filter_real, toward_filter_imag)


def shards(signal, filter_raw, gate, d_out, w_first, w_second):
    rows, width = signal.shape
    scale = float(rows * lax.axis_size("seq")) ** (-0.5)
    signal_wide = signal.astype(jnp.float32)
    kernel = filter_raw.astype(jnp.float32) * scale
    spectra_real, spectra_imag = forward_transform(jnp.stack([signal_wide, kernel]))
    mixed_real = spectra_real[0] * spectra_real[1] - spectra_imag[0] * spectra_imag[1]
    mixed_imag = spectra_real[0] * spectra_imag[1] + spectra_imag[0] * spectra_real[1]
    conv = inverse_transform(mixed_real[None], mixed_imag[None])[0].astype(jnp.bfloat16)
    gate_wide = gate.astype(jnp.float32)
    product = (conv.astype(jnp.float32) * gate_wide).astype(jnp.bfloat16)
    blocks = w_first.shape[0]
    block = w_first.shape[1]
    product_blocks = product.reshape(rows, blocks, block)
    first_mix = jnp.einsum(
        "tij,ijk->tik", product_blocks, w_first, preferred_element_type=jnp.float32
    ).astype(jnp.bfloat16)
    received = lax.all_to_all(first_mix, "ch", split_axis=2, concat_axis=1, tiled=True)
    incoming = d_out.reshape(rows, w_second.shape[0], w_second.shape[1])
    second_back = jnp.einsum(
        "tko,kio->tki", incoming, w_second, preferred_element_type=jnp.float32
    ).astype(jnp.bfloat16)
    grad_second = jnp.einsum("tik,tko->kio", received, incoming, preferred_element_type=jnp.float32)
    returned = lax.all_to_all(second_back, "ch", split_axis=2, concat_axis=1, tiled=True)
    grad_product = jnp.einsum(
        "tki,ijk->tij", returned, w_first, preferred_element_type=jnp.float32
    ).reshape(rows, width)
    grad_first = jnp.einsum(
        "tij,tki->ijk", product_blocks, returned, preferred_element_type=jnp.float32
    )
    grad_gate = (grad_product * conv.astype(jnp.float32)).astype(jnp.bfloat16)
    grad_conv = grad_product * gate_wide
    incoming_real, incoming_imag = forward_transform(grad_conv[None])
    sig_real, sig_imag, fil_real, fil_imag = adjoint_spectra(
        spectra_real, spectra_imag, incoming_real[0], incoming_imag[0]
    )
    results = inverse_transform(jnp.stack([sig_real, fil_real]), jnp.stack([sig_imag, fil_imag]))
    grad_signal = results[0].astype(jnp.bfloat16)
    grad_filter = (results[1] * scale).astype(jnp.bfloat16)
    grad_first = lax.psum_scatter(
        grad_first.astype(jnp.bfloat16), "seq", scatter_dimension=1, tiled=True
    ).astype(jnp.float32)
    grad_second = lax.psum_scatter(grad_second, "seq", scatter_dimension=1, tiled=True)
    return (grad_signal, grad_filter, grad_gate, grad_first, grad_second)


def solution(mesh):
    in_specs = (
        P("seq", "ch"),
        P("seq", "ch"),
        P("seq", "ch"),
        P("seq", "ch"),
        P("ch", None, None),
        P("ch", None, None),
    )
    out_specs = (
        P("seq", "ch"),
        P("seq", "ch"),
        P("seq", "ch"),
        P("ch", "seq", None),
        P("ch", "seq", None),
    )
    return jax.shard_map(shards, mesh=mesh, in_specs=in_specs, out_specs=out_specs, check_vma=False)
```

profile of v0, /device:TPU:8, one launch (start us, length us, event | category | flops | bytes accessed | tf_op | source)
XLA Modules:
  0.0 462.7 jit_solution(11425884564633815950)
XLA Ops:
  0.7 1.1 copy.233
  2.8 20.1 %all_to_all.147 = bf16[512,4,32]{0,1,2:T(4,128)(2,1)S(1)} all-to-all(bf16[512,4,32]{0,1,2:T(4,128)(2,1)S(1)} %copy.234), channel_id=1, replica_groups=mesh['seq'=16,'ch'=16] {'ch'}, dimensions={2} | all-to-all | bytes 262144 | tf_op jit(solution)/shard_map/all_to_all | solution.py:158
  24.1 5.8 %all-to-all-start.3 = ((f32[1,1,512,128]{3,1,0,2:T(1,128)}), f32[1,1,512,128]{3,1,0,2:T(1,128)S(1)}, u32[]{:S(2)}, u32[]{:S(2)}) async-start(f32[1,1,512,128]{3,1,0,2:T(1,128)} %bitcast.38), calls=%async_computation.3 | async-start | bytes 524288 | tf_op jit(solution)/shard_map/all_to_all | solution.py:91
  29.9 1.3 maximum_bitcast_fusion
  31.2 10.9 %all-to-all-done.3 = f32[1,1,512,128]{3,1,0,2:T(1,128)S(1)} async-done(((f32[1,1,512,128]{3,1,0,2:T(1,128)}), f32[1,1,512,128]{3,1,0,2:T(1,128)S(1)}, u32[]{:S(2)}, u32[]{:S(2)}) %all-to-all-start.3) | async-done | bytes 262176 | tf_op jit(solution)/shard_map/all_to_all | solution.py:91
  42.1 3.6 all-to-all-start
  47.6 1.6 copy.240
  49.2 13.6 %all-to-all-done = f32[2,1,512,128]{3,0,1,2:T(2,128)S(1)} async-done(((f32[2,1,512,128]{3,0,1,2:T(2,128)}), f32[2,1,512,128]{3,0,1,2:T(2,128)S(1)}, u32[]{:S(2)}, u32[]{:S(2)}) %all-to-all-start) | async-done | bytes 524320 | tf_op jit(solution)/shard_map/all_to_all | solution.py:91
  62.7 3.7 all-to-all-start.4
  66.4 1.3 convolution_bitcast_fusion
  67.7 1.6 subtract_bitcast_fusion.1
  69.5 2.6 copy.222
  72.1 21.8 %all-to-all-done.4 = f32[1,2,32,32,128]{4,3,1,0,2:T(8,128)S(1)} async-done(((f32[1,2,32,32,128]{4,3,1,0,2:T(8,128)}), f32[1,2,32,32,128]{4,3,1,0,2:T(8,128)S(1)}, u32[]{:S(2)}, u32[]{:S(2)}) %all-to-all-start.4) | async-done | bytes 1048608 | tf_op jit(solution)/shard_map/all_to_all | solution.py:98
  93.9 4.2 all-to-all-start.1
  99.5 1.3 fusion.40
  100.8 1.3 fusion.8
  102.1 1.3 fusion.44
  103.5 2.7 add_bitcast_fusion.3
  106.2 1.2 copy.249
  107.4 1.2 copy.250
  109.5 1.6 fusion.15
  111.1 1.6 fusion.62
  112.7 35.0 %all-to-all-done.1 = f32[2,2,32,32,128]{4,3,0,1,2:T(8,128)S(1)} async-done(((f32[2,2,32,32,128]{4,3,0,1,2:T(8,128)}), f32[2,2,32,32,128]{4,3,0,1,2:T(8,128)S(1)}, u32[]{:S(2)}, u32[]{:S(2)}) %all-to-all-start.1) | async-done | bytes 2097184 | tf_op jit(solution)/shard_map/all_to_all | solution.py:98
  148.1 2.7 fusion.27
  150.8 2.5 fusion.23
  153.3 2.6 fusion.5
  156.0 4.9 %multiply_subtract_fusion = (f32[2,2,4,128,128]{4,2,3,1,0:T(4,128)}, f32[2,2,4,128,128]{4,2,3,1,0:T(4,128)S(1)}) fusion(f32[2,2,4,128,128]{4,2,3,1,0:T(4,128)S(1)} %fusion.5, f32[4,128]{0,1:T(8,128)S(1)} %copy.230, f32[4,128]{0,1:T(8,128)S(1)} %copy-done.11, f32[2,2,128,128,4]{3,4,2,1,0:T(4,128)S(1)} %fusion.23, f32[2,2,4,128,128]{4,3,2,1,0:T(8,128)S(1)} %bitcast.367), kind=kOutput, calls=%fused_computation.63 | convolution fusion | flops 14418160 | bytes 5246976 | tf_op jit(solution)/shard_map/qa,fkabc->fkqbc/dot_general | solution.py:27
  161.2 2.2 fusion.70
  163.4 1.5 copy.231
  165.0 1.2 fusion.72
  166.2 1.2 fusion.2
  167.5 1.2 fusion.3
  168.7 1.9 multiply_subtract_fusion.2
  173.1 1.9 subtract_bitcast_fusion.2
  175.0 1.3 copy.268
  176.3 1.9 fusion.158
  178.4 1.5 fusion.160
  180.0 2.1 fusion.6
  182.1 1.1 fusion.7
  183.6 1.8 copy.273
  185.4 4.5 all-to-all-start.7
  189.9 1.2 fusion.29
  191.2 1.2 fusion.30
  192.4 1.2 convolution_add_fusion.1
  193.7 1.4 subtract_bitcast_fusion
  195.9 1.9 fusion.166
  197.8 2.1 fusion
  200.0 1.9 fusion.168
  201.9 2.2 fusion.1
  204.3 13.0 %all-to-all-done.7 = f32[1,2,2,512,128]{4,2,1,0,3:T(2,128)} async-done(((f32[1,2,2,512,128]{4,2,1,0,3:T(2,128)}), f32[1,2,2,512,128]{4,2,1,0,3:T(2,128)}, u32[]{:S(2)}, u32[]{:S(2)}) %all-to-all-start.7) | async-done | bytes 1048608 | tf_op jit(solution)/shard_map/all_to_all | solution.py:114
  217.3 1.3 copy.274
  221.0 4.2 all-to-all-start.8
  225.7 3.0 copy.261
  228.7 4.9 %all-to-all-done.8 = bf16[1,16,32,128]{3,2,0,1:T(8,128)(2,1)} async-done(((bf16[1,16,32,128]{3,2,0,1:T(8,128)(2,1)}), bf16[1,16,32,128]{3,2,0,1:T(8,128)(2,1)}, u32[]{:S(2)}, u32[]{:S(2)}) %all-to-all-start.8) | async-done | bytes 131104 | tf_op jit(solution)/shard_map/all_to_all | solution.py:123
  233.6 3.7 all-to-all-start.5
  237.3 1.6 fusion.47
  240.1 45.9 %all-to-all-done.5 = f32[2,2,2,512,128]{4,2,0,1,3:T(2,128)S(1)} async-done(((f32[2,2,2,512,128]{4,2,0,1,3:T(2,128)}), f32[2,2,2,512,128]{4,2,0,1,3:T(2,128)S(1)}, u32[]{:S(2)}, u32[]{:S(2)}) %all-to-all-start.5) | async-done | bytes 2097184 | tf_op jit(solution)/shard_map/all_to_all | solution.py:114
  286.0 3.9 all-to-all-start.9
  290.3 1.6 copy.263
  293.4 1.0 copy.264
  294.4 4.3 all-to-all-done.9
  298.7 3.7 all-to-all-start.6
  304.5 80.4 %all-reduce = bf16[2,64,64]{2,1,0:T(8,128)(2,1)S(1)} all-reduce(bf16[2,64,64]{2,1,0:T(8,128)(2,1)S(1)} %convolution_convert_fusion.2), channel_id=2, replica_groups=mesh['seq'=16,'ch'=16] {'seq'}, use_global_device_ids=true, to_apply=%region_0.1.clone | all-reduce | flops 8192 | bytes 32768
  385.9 74.6 %all-reduce.1 = f32[4,32,32]{2,0,1:T(4,128)S(1)} all-reduce(f32[4,32,32]{2,0,1:T(4,128)S(1)} %copy.283), channel_id=3, replica_groups=mesh['seq'=16,'ch'=16] {'seq'}, use_global_device_ids=true, to_apply=%region_1.2.clone | all-reduce | flops 4096 | bytes 32768
  (100 shorter events, 20.9 us)
Async XLA Ops:
  0.6 22.4 %copy-start = (bf16[2,64,64]{2,1,0:T(8,128)(2,1)S(1)}, bf16[2,64,64]{2,1,0:T(8,128)(2,1)}, u32[]{:S(2)}) copy-start(bf16[2,64,64]{2,1,0:T(8,128)(2,1)} %param.10) | copy-start | bytes 49156
  0.6 22.7 %copy-start.12 = (bf16[512,128]{1,0:T(8,128)(2,1)S(1)}, bf16[512,128]{1,0:T(8,128)(2,1)}, u32[]{:S(2)}) copy-start(bf16[512,128]{1,0:T(8,128)(2,1)} %param.8) | copy-start | bytes 393220
  0.7 29.2 %copy-start.14 = (bf16[512,128]{1,0:T(8,128)(2,1)S(1)}, bf16[512,128]{1,0:T(8,128)(2,1)}, u32[]{:S(2)}) copy-start(bf16[512,128]{1,0:T(8,128)(2,1)} %param.6) | copy-start | bytes 393220
  0.7 29.2 %copy-start.15 = (bf16[512,128]{1,0:T(8,128)(2,1)S(1)}, bf16[512,128]{1,0:T(8,128)(2,1)}, u32[]{:S(2)}) copy-start(bf16[512,128]{1,0:T(8,128)(2,1)} %param.7) | copy-start | bytes 393220
  1.7 22.3 %copy-start.6 = (bf16[512,128]{0,1:T(8,128)(2,1)}, bf16[512,128]{0,1:T(8,128)(2,1)S(1)}, u32[]{:S(2)}) copy-start(bf16[512,128]{0,1:T(8,128)(2,1)S(1)} %copy.233) | copy-start | bytes 393220
  23.0 1.1 copy-start.8
  24.1 18.1 %all-to-all-start.3 = ((f32[1,1,512,128]{3,1,0,2:T(1,128)}), f32[1,1,512,128]{3,1,0,2:T(1,128)S(1)}, u32[]{:S(2)}, u32[]{:S(2)}) async-start(f32[1,1,512,128]{3,1,0,2:T(1,128)} %bitcast.38), calls=%async_computation.3 | async-start | bytes 524288 | tf_op jit(solution)/shard_map/all_to_all | solution.py:91
  42.1 20.6 %all-to-all-start = ((f32[2,1,512,128]{3,0,1,2:T(2,128)}), f32[2,1,512,128]{3,0,1,2:T(2,128)S(1)}, u32[]{:S(2)}, u32[]{:S(2)}) async-start(f32[2,1,512,128]{3,0,1,2:T(2,128)} %maximum_bitcast_fusion), calls=%async_computation | async-start | bytes 1048576 | tf_op jit(solution)/shard_map/all_to_all | solution.py:91
  62.7 31.1 %all-to-all-start.4 = ((f32[1,2,32,32,128]{4,3,1,0,2:T(8,128)}), f32[1,2,32,32,128]{4,3,1,0,2:T(8,128)S(1)}, u32[]{:S(2)}, u32[]{:S(2)}) async-start(f32[1,2,32,32,128]{4,3,1,0,2:T(8,128)} %copy.240), calls=%async_computation.4 | async-start | bytes 2097152 | tf_op jit(solution)/shard_map/all_to_all | solution.py:98
  93.9 53.9 %all-to-all-start.1 = ((f32[2,2,32,32,128]{4,3,0,1,2:T(8,128)}), f32[2,2,32,32,128]{4,3,0,1,2:T(8,128)S(1)}, u32[]{:S(2)}, u32[]{:S(2)}) async-start(f32[2,2,32,32,128]{4,3,0,1,2:T(8,128)} %copy.222), calls=%async_computation.1 | async-start | bytes 4194304 | tf_op jit(solution)/shard_map/all_to_all | solution.py:98
  99.4 4.0 copy-start.10
  153.3 2.7 copy-start.11
  164.9 1.2 copy-start.2
  167.4 1.3 copy-start.4
  167.5 1.3 copy-start.5
  175.0 3.2 copy-start.3
  185.4 5.7 %copy-start.1 = (f32[1,2,4,128,128]{3,4,2,1,0:T(8,128)S(1)}, f32[1,2,4,128,128]{3,4,2,1,0:T(8,128)}, u32[]{:S(2)}) copy-start(f32[1,2,4,128,128]{3,4,2,1,0:T(8,128)} %get-tuple-element.37) | copy-start | bytes 1572868
  185.4 31.9 %all-to-all-start.7 = ((f32[1,2,2,512,128]{4,2,1,0,3:T(2,128)}), f32[1,2,2,512,128]{4,2,1,0,3:T(2,128)}, u32[]{:S(2)}, u32[]{:S(2)}) async-start(f32[1,2,2,512,128]{4,2,1,0,3:T(2,128)} %copy.273), calls=%async_computation.7 | async-start | bytes 2097152 | tf_op jit(solution)/shard_map/all_to_all | solution.py:114
  221.0 12.6 %all-to-all-start.8 = ((bf16[1,16,32,128]{3,2,0,1:T(8,128)(2,1)}), bf16[1,16,32,128]{3,2,0,1:T(8,128)(2,1)}, u32[]{:S(2)}, u32[]{:S(2)}) async-start(bf16[1,16,32,128]{3,2,0,1:T(8,128)(2,1)} %copy.276), calls=%async_computation.8 | async-start | bytes 262144 | tf_op jit(solution)/shard_map/all_to_all | solution.py:123
  228.7 8.6 %copy-start.13 = (bf16[512,128]{1,0:T(8,128)(2,1)S(1)}, bf16[512,128]{1,0:T(8,128)(2,1)}, u32[]{:S(2)}) copy-start(bf16[512,128]{1,0:T(8,128)(2,1)} %param.8) | copy-start | bytes 393220
  233.6 52.4 %all-to-all-start.5 = ((f32[2,2,2,512,128]{4,2,0,1,3:T(2,128)}), f32[2,2,2,512,128]{4,2,0,1,3:T(2,128)S(1)}, u32[]{:S(2)}, u32[]{:S(2)}) async-start(f32[2,2,2,512,128]{4,2,0,1,3:T(2,128)} %copy.261), calls=%async_computation.5 | async-start | bytes 4194304 | tf_op jit(solution)/shard_map/all_to_all | solution.py:114
  286.0 12.7 %all-to-all-start.9 = ((bf16[512,2,64]{0,1,2:T(2,128)(2,1)}), bf16[512,2,64]{0,1,2:T(2,128)(2,1)S(1)}, u32[]{:S(2)}, u32[]{:S(2)}) async-start(bf16[512,2,64]{0,1,2:T(2,128)(2,1)} %copy.281), calls=%async_computation.9 | async-start | bytes 262144 | tf_op jit(solution)/shard_map/all_to_all | solution.py:152
  292.7 9.7 %copy-start.16 = (u32[256]{0:T(256)S(1)}, u32[256]{0:T(256)}, u32[]{:S(2)}) copy-start(u32[256]{0:T(256)} %constant.160) | copy-start | bytes 3076
  292.7 11.6 %copy-start.9 = (bf16[512,64,2]{0,1,2:T(8,128)(2,1)S(1)}, bf16[512,64,2]{0,1,2:T(8,128)(2,1)}, u32[]{:S(2)}) copy-start(bf16[512,64,2]{0,1,2:T(8,128)(2,1)} %copy-done.8) | copy-start | bytes 393220
  292.7 93.0 %copy-start.7 = (bf16[512,128]{0,1:T(8,128)(2,1)S(1)}, bf16[512,128]{0,1:T(8,128)(2,1)}, u32[]{:S(2)}) copy-start(bf16[512,128]{0,1:T(8,128)(2,1)} %copy-done.6) | copy-start | bytes 393220
  298.7 162.4 %all-to-all-start.6 = ((f32[2,16,32,128]{3,2,0,1:T(8,128)}), f32[2,16,32,128]{3,2,0,1:T(8,128)S(1)}, u32[]{:S(2)}, u32[]{:S(2)}) async-start(f32[2,16,32,128]{3,2,0,1:T(8,128)} %copy.264), calls=%async_computation.6 | async-start | bytes 1048576 | tf_op jit(solution)/shard_map/all_to_all | solution.py:123
where the time goes:
time: 470 us; the launch traced here: 463 us
  blocking collectives  175 us (37%)
  waiting for transfers between devices  149 us (32%)
  matrix products  63.8 us (14%)
  starting transfers between devices  37.1 us (8%)
  local copies, waits for them, and re-layouts  27.6 us (6%)
  other arithmetic  6.55 us (1%)
    unnamed x2, blocking collectives  155 us
    all_to_all x2, waiting for transfers between devices, inverse_transform(): lax.all_to_all(jnp.stack([real_part, imag_part], axis=1), 'seq', split_ax...  58.9 us
    all_to_all x2, waiting for transfers between devices, forward_transform(): lax.all_to_all(jnp.stack([real_part, imag_part], axis=1), 'seq', split_ax...  56.8 us
    all_to_all x2, waiting for transfers between devices, forward_transform(): lax.all_to_all(fields[:, None], 'seq', split_axis=2, concat_axis=1, tiled...  24.5 us
    all_to_all x1, blocking collectives, shards(): lax.all_to_all(second_back, 'ch', split_axis=2, concat_axis=1, tiled=True)  20.1 us
    dot_general x8, matrix products, contract(): jnp.einsum(form, sine, real_part, precision=HIGHEST)  15.6 us
    dot_general x8, matrix products, contract(): jnp.einsum(form, sine, imag_part, precision=HIGHEST)  14.7 us
    dot_general x8, matrix products, contract(): jnp.einsum(form, cosine, imag_part, precision=HIGHEST)  13.5 us
  transfers between devices with their start and end apart: 9, of which 8 were waited for; matrix products, arithmetic and copies ran while one was open for 11% of the time, Pallas kernels for 0%

commit v1 on v0

v1 whole, which is shorter than its diff:
```python
import math

import jax
import jax.numpy as jnp
import numpy as np
from jax import lax
from jax.experimental import pallas as pl
from jax.experimental.pallas import tpu as pltpu
from jax.sharding import PartitionSpec as P

F32 = jnp.float32
BF16 = jnp.bfloat16
HIGHEST = lax.Precision.HIGHEST
NN = (((1,), (0,)), ((), ()))
NT = (((1,), (1,)), ((), ()))
TN = (((0,), (0,)), ((), ()))


def dot(a, b, form=NN):
    return lax.dot_general(a, b, form, preferred_element_type=F32)


def exact_dot(a, b, form=NN):
    return lax.dot_general(a, b, form, preferred_element_type=F32, precision=HIGHEST)


def halves(table):
    high = table.astype(BF16)
    return high, (table - high.astype(np.float32)).astype(BF16)


def tables(devices, rows):
    lanes = 128
    length = 2 * devices * rows
    steps = devices * rows // lanes
    split = rows // lanes
    place = (np.arange(steps) % devices) * split + np.arange(steps) // devices
    turn = 2.0 * math.pi
    freq = np.arange(steps) + 0.5
    angle = turn * freq[:, None] * place[None, :] / (2 * steps)
    outer = np.concatenate([np.cos(angle), -np.sin(angle)], 0)
    scale = float(devices * rows) ** -0.5 * 2.0 / length
    back = scale * np.concatenate([np.cos(angle.T), -np.sin(angle.T)], 1)
    angle = turn * freq[:, None] * np.arange(lanes)[None, :] / length
    twiddle = np.concatenate([np.cos(angle), -np.sin(angle)], 1)
    angle = turn * (np.arange(lanes)[:, None] * np.arange(lanes)[None, :] % lanes) / lanes
    cosine, sine = np.cos(angle), np.sin(angle)
    inner = np.concatenate(
        [np.concatenate([cosine, -sine], 1), np.concatenate([sine, cosine], 1)], 0
    )
    outer_high, outer_low = halves(outer.astype(np.float32))
    back_high, back_low = halves(back.astype(np.float32))
    inner_high, inner_low = halves(inner.astype(np.float32))
    return (
        np.concatenate([outer_high, outer_low], 1),
        np.stack([back_high, back_low]),
        twiddle.astype(np.float32),
        np.stack([inner_high, inner_low]),
    )


def iotas(rows, cols):
    return (
        lax.broadcasted_iota(jnp.int32, (rows, cols), 0),
        lax.broadcasted_iota(jnp.int32, (rows, cols), 1),
    )


def ones_where(mask):
    return jnp.where(mask, 1.0, 0.0).astype(BF16)


def pair_order():
    row, col = iotas(256, 256)
    return ones_where((row // 16 == col % 128 // 8) & (row // 8 % 2 == col // 128) & (row % 8 == col % 8))


def unit():
    row, col = iotas(128, 128)
    return ones_where(row == col)


def first_blocks(w_first_ref):
    flat = w_first_ref[...].reshape(128, 64)
    row, col = iotas(64, 128)
    spread = dot(flat, ones_where(row == col // 8 * 4 + col % 4))
    row, col = iotas(128, 128)
    return jnp.where(row // 64 == col // 4 % 2, spread, 0.0).astype(BF16)


def entry_kernel(signal_ref, filter_ref, d_out_ref, w_second_ref, pair_ref, back_ref):
    flat = w_second_ref[...].reshape(128, 32)
    row, col = iotas(32, 128)
    spread = dot(flat, ones_where(row == col % 32))
    row, col = iotas(128, 128)
    spread = jnp.where(row // 32 == col // 32, spread, 0.0).astype(BF16)
    order = ones_where((row // 4 == col % 32) & (row % 4 == col // 32))
    weights = dot(order, spread).astype(BF16)
    back_ref[...] = dot(weights, d_out_ref[...], NT).astype(BF16)
    both = jnp.concatenate([signal_ref[...], filter_ref[...]], axis=1)
    pair_ref[...] = dot(pair_order(), both, NT).astype(BF16)


def gate_kernel(returned_ref, w_first_ref, gate_ref, incoming_ref):
    grad_product = dot(first_blocks(w_first_ref), returned_ref[...])
    gate = dot(unit(), gate_ref[...], NT)
    incoming_ref[...] = (grad_product * gate).astype(BF16)


def split(value):
    high = value.astype(BF16)
    return high, (value - high.astype(F32)).astype(BF16)


def by_channel(wide_ref, first, stride):
    columns = [wide_ref[pl.ds(first + c, 64, stride=stride), :] for c in range(8)]
    return jnp.concatenate(columns, axis=1).astype(BF16)


def by_slab(wide_ref, value, first, stride):
    for c in range(8):
        wide_ref[pl.ds(first + c, 64, stride=stride), :] = value[:, 128 * c : 128 * c + 128]


def unroll(wide_ref, value):
    rows = value.shape[0]
    for th in range(4):
        wide_ref[rows * th : rows * th + rows, :] = value[:, 128 * th : 128 * th + 128].astype(F32)


def enroll(wide_ref):
    rows = wide_ref.shape[0] // 4
    pieces = [wide_ref[rows * th : rows * th + rows, :].astype(BF16) for th in range(4)]
    return jnp.concatenate(pieces, axis=1)


def transform(values, outer_ref, twiddle_ref, inner_ref):
    stage = dot(outer_ref[...], jnp.concatenate([values, values], axis=0))
    cosine, sine = twiddle_ref[:, 0:128], twiddle_ref[:, 128:256]
    rows = []
    for c in range(8):
        real = stage[0:64, 128 * c : 128 * c + 128]
        imag = stage[64:128, 128 * c : 128 * c + 128]
        rows.append(
            jnp.concatenate([real * cosine - imag * sine, real * sine + imag * cosine], axis=1)
        )
    high, low = split(jnp.concatenate(rows, axis=0))
    return dot(high, inner_ref[0]) + dot(low, inner_ref[0]) + dot(high, inner_ref[1])


def restore(real, imag, back_ref, twiddle_ref, inner_ref):
    high, low = split(jnp.concatenate([real, imag], axis=1))
    stage = dot(high, inner_ref[0], NT) + dot(low, inner_ref[0], NT) + dot(high, inner_ref[1], NT)
    cosine, sine = twiddle_ref[:, 0:128], twiddle_ref[:, 128:256]
    columns = []
    for c in range(8):
        real = stage[64 * c : 64 * c + 64, 0:128]
        imag = stage[64 * c : 64 * c + 64, 128:256]
        columns.append(
            jnp.concatenate([real * cosine + imag * sine, imag * cosine - real * sine], axis=0)
        )
    high, low = split(jnp.concatenate(columns, axis=1))
    return dot(back_ref[0], high) + dot(back_ref[0], low) + dot(back_ref[1], high)


def conv_kernel(
    pair_ref, outer_ref, back_ref, twiddle_ref, inner_ref, conv_ref, spectra_ref, wide_ref, out_ref
):
    unroll(wide_ref, pair_ref[...])
    signal = transform(by_channel(wide_ref, 0, 16), outer_ref, twiddle_ref, inner_ref)
    kernel = transform(by_channel(wide_ref, 8, 16), outer_ref, twiddle_ref, inner_ref)
    spectra_ref[0] = signal
    spectra_ref[1] = kernel
    sr, si = signal[:, 0:128], signal[:, 128:256]
    kr, ki = kernel[:, 0:128], kernel[:, 128:256]
    result = restore(sr * kr - si * ki, sr * ki + si * kr, back_ref, twiddle_ref, inner_ref)
    by_slab(out_ref, result, 0, 8)
    conv_ref[...] = enroll(out_ref)


def adjoint_kernel(
    incoming_ref, spectra_ref, outer_ref, back_ref, twiddle_ref, inner_ref, pair_ref, wide_ref, out_ref
):
    unroll(wide_ref, incoming_ref[...])
    spectrum = transform(by_channel(wide_ref, 0, 8), outer_ref, twiddle_ref, inner_ref)
    gr, gi = spectrum[:, 0:128], spectrum[:, 128:256]
    for field in range(2):
        real, imag = spectra_ref[1 - field, :, 0:128], spectra_ref[1 - field, :, 128:256]
        result = restore(
            gr * real + gi * imag, gi * real - gr * imag, back_ref, twiddle_ref, inner_ref
        )
        by_slab(out_ref, result, 8 * field, 16)
    pair_ref[...] = enroll(out_ref)


def mix_kernel(conv_ref, gate_ref, w_first_ref, mix_ref):
    gate = dot(unit(), gate_ref[...], NT)
    product = (conv_ref[...].astype(F32) * gate).astype(BF16)
    mix_ref[...] = dot(first_blocks(w_first_ref), product, TN).astype(BF16)


def first_kernel(conv_ref, gate_ref, returned_ref, w_first_ref, grad_gate_ref, partial_ref):
    gate = dot(unit(), gate_ref[...], NT)
    conv = conv_ref[...].astype(F32)
    product = (conv * gate).astype(BF16)
    returned = returned_ref[...]
    grad_product = dot(first_blocks(w_first_ref), returned)
    grad_gate = (grad_product * conv).astype(BF16)
    grad_gate_ref[...] = dot(grad_gate, unit(), TN).astype(BF16)
    row, col = iotas(128, 128)
    grad = jnp.where(row // 64 == col // 4 % 2, dot(product, returned, NT), 0.0)
    order = jnp.where(
        (row // 8 == col % 64 // 4) & (row // 4 % 2 == col // 64) & (row % 4 == col % 4), 1.0, 0.0
    )
    row, col = iotas(128, 64)
    fold = jnp.where(row // 8 * 4 + row % 4 == col, 1.0, 0.0)
    partial_ref[...] = exact_dot(order, exact_dot(grad, fold))


def exit_kernel(pair_ref, signal_ref, filter_ref):
    both = dot(pair_ref[...], pair_order(), TN).astype(BF16)
    signal_ref[...] = both[:, 0:128]
    filter_ref[...] = both[:, 128:256]


def second_kernel(received_ref, d_out_ref, partial_ref, sums_ref):
    row, col = iotas(128, 128)
    grad = jnp.where(row % 4 == col // 32, dot(received_ref[...], d_out_ref[...]), 0.0)
    row, col = iotas(128, 64)
    fold = jnp.where(row % 32 == col, 1.0, 0.0)
    sums_ref[...] = jnp.concatenate([partial_ref[...], exact_dot(grad, fold)], axis=1)


def sum_kernel(sums_ref, first_ref, second_ref):
    total = sums_ref[0:8, :]
    for s in range(1, 16):
        total = total + sums_ref[8 * s : 8 * s + 8, :]
    for i in range(2):
        first_ref[i] = total[4 * i : 4 * i + 4, 0:64]
        for k in range(4):
            second_ref[k, i : i + 1, :] = total[4 * i + k : 4 * i + k + 1, 64:96]


def call(body, outs, scratch=(), flops=1 << 26, moved=1 << 19):
    return pl.pallas_call(
        body,
        out_shape=[jax.ShapeDtypeStruct(shape, kind) for shape, kind in outs],
        scratch_shapes=list(scratch),
        compiler_params=pltpu.CompilerParams(vmem_limit_bytes=32 << 20),
        cost_estimate=pl.CostEstimate(flops=flops, bytes_accessed=moved, transcendentals=0),
    )


def exchange(value, axis):
    rows, cols = value.shape
    pieces = value.reshape(16, rows // 16, cols)
    return lax.all_to_all(pieces, axis, split_axis=0, concat_axis=0, tiled=True).reshape(rows, cols)


def shards(signal, filter_raw, gate, d_out, w_first, w_second):
    rows, width = signal.shape
    outer, back, twiddle, inner = (jnp.asarray(t) for t in tables(lax.axis_size("seq"), rows))
    pair, second_back = call(
        entry_kernel, [((2 * width, rows), BF16), ((width, rows), BF16)]
    )(signal, filter_raw, d_out, w_second)
    returned = exchange(second_back, "ch")
    pair = exchange(pair, "seq")
    conv, spectra = call(
        conv_kernel,
        [((width, rows), BF16), ((2, 512, 256), F32)],
        [pltpu.VMEM((2 * width * 4, 128), F32), pltpu.VMEM((width * 4, 128), F32)],
        flops=1 << 30,
    )(pair, outer, back, twiddle, inner)
    conv = exchange(conv, "seq")
    incoming = call(gate_kernel, [((width, rows), BF16)])(returned, w_first, gate)[0]
    incoming = exchange(incoming, "seq")
    grads = call(
        adjoint_kernel,
        [((2 * width, rows), BF16)],
        [pltpu.VMEM((width * 4, 128), F32), pltpu.VMEM((2 * width * 4, 128), F32)],
        flops=1 << 30,
    )(incoming, spectra, outer, back, twiddle, inner)[0]
    grads = exchange(grads, "seq")
    mix = call(mix_kernel, [((width, rows), BF16)])(conv, gate, w_first)[0]
    received = exchange(mix, "ch")
    grad_gate, partial = call(first_kernel, [((rows, width), BF16), ((width, 64), F32)])(
        conv, gate, returned, w_first
    )
    grad_signal, grad_filter = call(exit_kernel, [((rows, width), BF16), ((rows, width), BF16)])(grads)
    sums = call(second_kernel, [((width, 128), F32)])(received, d_out, partial)[0]
    sums = exchange(sums, "seq")
    grad_first, grad_second = call(sum_kernel, [((2, 4, 64), F32), ((4, 2, 32), F32)])(sums)
    return (grad_signal, grad_filter, grad_gate, grad_first, grad_second)


def solution(mesh):
    in_specs = (
        P("seq", "ch"),
        P("seq", "ch"),
        P("seq", "ch"),
        P("seq", "ch"),
        P("ch", None, None),
        P("ch", None, None),
    )
    out_specs = (
        P("seq", "ch"),
        P("seq", "ch"),
        P("seq", "ch"),
        P("ch", "seq", None),
        P("ch", "seq", None),
    )
    return jax.shard_map(shards, mesh=mesh, in_specs=in_specs, out_specs=out_specs, check_vma=False)
```

time: 470 us -> 109 us (0.23); the launches traced: 463 us -> 108 us
  blocking collectives: 175 us -> 19.3 us
  waiting for transfers between devices: 149 us -> 43.8 us
  matrix products: 63.8 us -> 0 us
  local copies, waits for them, and re-layouts: 27.6 us -> 3.49 us
  Pallas kernels: 0 us -> 12.1 us
  starting transfers between devices: 37.1 us -> 28.7 us
  other arithmetic: 6.55 us -> 0 us
    unnamed x2 -> x0, blocking collectives: 155 us -> none
    all_to_all x9 -> x6, waiting for transfers between devices: 149 us -> 43.8 us  [exchange(): lax.all_to_all(pieces, axis, split_axis=0, concat_axis=0, tiled=True)]
    dot_general x45 -> x0, matrix products: 63.8 us -> none  [the longest x8 15.6 us: contract(): jnp.einsum(form, sine, real_part, precision=HIGHEST)]
    another operation x8 -> x0, local copies, waits for them, and re-layouts: 13 us -> none  [the longest x2 4.77 us: inverse_transform(): jnp.stack([real_part, imag_part], axis=1)]
    pallas_call x0 -> x9, Pallas kernels: none -> 12.1 us  [the longest x1 2.8 us: shards(): call(adjoint_kernel, [((2 * width, rows), BF16)], [pltpu.VMEM((width * 4,...]
    all_to_all x9 -> x6, starting transfers between devices: 37.1 us -> 28.7 us  [exchange(): lax.all_to_all(pieces, axis, split_axis=0, concat_axis=0, tiled=True)]
    all_to_all x12 -> x0, local copies, waits for them, and re-layouts: 4.73 us -> none  [the longest x4 4.13 us: inverse_transform(): lax.all_to_all(jnp.stack([real_part, imag_part], axis=1), 'seq', split_ax...]
  transfers between devices with their start and end apart: 9 -> 6, of which waited for: 8 -> 6; matrix products, arithmetic and copies ran while one was open for 11% -> 0% of each run, Pallas kernels for 0% -> 10%
where the time goes in v1:
time: 109 us; the launch traced here: 108 us
  waiting for transfers between devices  43.8 us (40%)
  starting transfers between devices  28.7 us (26%)
  blocking collectives  19.3 us (18%)
  Pallas kernels  12.1 us (11%)
  local copies, waits for them, and re-layouts  3.49 us (3%)
    all_to_all x6, waiting for transfers between devices, exchange(): lax.all_to_all(pieces, axis, split_axis=0, concat_axis=0, tiled=True)  43.8 us
    all_to_all x6, starting transfers between devices, exchange(): lax.all_to_all(pieces, axis, split_axis=0, concat_axis=0, tiled=True)  28.7 us
    all_to_all x1, blocking collectives, exchange(): lax.all_to_all(pieces, axis, split_axis=0, concat_axis=0, tiled=True)  19.3 us
    unnamed x22, local copies, waits for them, and re-layouts  3.49 us
    pallas_call x1, Pallas kernels, shards(): call(adjoint_kernel, [((2 * width, rows), BF16)], [pltpu.VMEM((width * 4,...  2.8 us
    pallas_call x1, Pallas kernels, shards(): call(conv_kernel, [((width, rows), BF16), ((2, 512, 256), F32)], [pltpu.V...  2.2 us
  transfers between devices with their start and end apart: 6, of which 6 were waited for; matrix products, arithmetic and copies ran while one was open for 0% of the time, Pallas kernels for 10%

profile of v1, /device:TPU:8, one launch (start us, length us, event | category | flops | bytes accessed | tf_op | source)
XLA Modules:
  0.0 108.1 jit_solution(5680586595614754736)
XLA Ops:
  0.6 0.0 copy-start.1
  0.6 0.9 copy-done.1
  1.5 0.0 copy-start.4
  1.5 0.9 copy-done.4
  2.4 0.0 copy-start.5
  2.4 0.9 copy-done.5
  3.3 0.0 copy-start.6
  3.4 0.8 copy-done.6
  4.1 1.1 %shard_map.137 = (bf16[256,512]{1,0:T(8,128)(2,1)S(1)}, bf16[128,512]{1,0:T(8,128)(2,1)}) custom-call(bf16[512,128]{1,0:T(8,128)(2,1)S(1)} %copy-done.4, bf16[512,128]{1,0:T(8,128)(2,1)S(1)} %copy-done.5, bf16[512,128]{1,0:T(8,128)(2,1)S(1)} %copy-done.1, bf16[4,32,32]{2,1,0:T(8,128)(2,1)S(1)} %copy-done.6), custom_call_target="tpu_custom_call" | custom-call | flops 67108864 | bytes 524288 | tf_op jit(solution)/shard_map/pallas_call | solution.py:263
  5.2 0.0 copy-start.8
  5.2 0.0 copy-start.9
  5.2 0.0 copy-start.10
  5.2 19.3 %all_to_all.35 = bf16[16,16,512]{2,1,0:T(8,128)(2,1)S(1)} all-to-all(bf16[16,16,512]{2,1,0:T(8,128)(2,1)S(1)} %bitcast.21), channel_id=1, replica_groups=mesh['seq'=16,'ch'=16] {'seq'}, dimensions={0} | all-to-all | bytes 524288 | tf_op jit(solution)/shard_map/all_to_all | solution.py:257
  24.5 0.0 copy-start.7
  24.5 9.0 %all-to-all-start = ((bf16[16,8,512]{2,1,0:T(8,128)(2,1)}), bf16[16,8,512]{2,1,0:T(8,128)(2,1)S(1)}, u32[]{:S(2)}, u32[]{:S(2)}) async-start(bf16[16,8,512]{2,1,0:T(8,128)(2,1)} %bitcast), calls=%async_computation | async-start | bytes 262144 | tf_op jit(solution)/shard_map/all_to_all | solution.py:257
  33.5 0.0 copy-done.8
  33.5 0.0 copy-done.9
  33.5 0.0 copy-done.10
  33.5 0.0 copy-done.7
  33.5 2.2 %shard_map.139 = (bf16[128,512]{1,0:T(8,128)(2,1)}, f32[2,512,256]{2,1,0:T(8,128)S(1)}) custom-call(bf16[256,512]{1,0:T(8,128)(2,1)S(1)} %bitcast.20, bf16[128,128]{1,0:T(8,128)(2,1)S(1)} %copy-done.9, bf16[2,64,128]{2,1,0:T(8,128)(2,1)S(1)} %copy-done.10, f32[64,256]{1,0:T(8,128)S(1)} %copy-done.8, bf16[2,256,256]{2,1,0:T(8,128)(2,1)S(1)} %copy-done.7), custom_call_target="tpu_custom_call" | custom-call | flops 1073741824 | bytes 524288 | tf_op jit(solution)/shard_map/pallas_call | solution.py:268
  35.7 6.6 %all-to-all-done = bf16[16,8,512]{2,1,0:T(8,128)(2,1)S(1)} async-done(((bf16[16,8,512]{2,1,0:T(8,128)(2,1)}), bf16[16,8,512]{2,1,0:T(8,128)(2,1)S(1)}, u32[]{:S(2)}, u32[]{:S(2)}) %all-to-all-start) | async-done | bytes 131104 | tf_op jit(solution)/shard_map/all_to_all | solution.py:257
  42.3 0.0 copy-start
  42.3 0.0 copy-start.3
  42.3 3.6 %all-to-all-start.4 = ((bf16[16,8,512]{2,1,0:T(8,128)(2,1)}), bf16[16,8,512]{2,1,0:T(8,128)(2,1)S(1)}, u32[]{:S(2)}, u32[]{:S(2)}) async-start(bf16[16,8,512]{2,1,0:T(8,128)(2,1)} %bitcast.8), calls=%async_computation.4 | async-start | bytes 262144 | tf_op jit(solution)/shard_map/all_to_all | solution.py:257
  45.9 0.0 copy-done
  45.9 0.0 copy-done.3
  45.9 1.0 shard_map.138
  46.9 7.8 %all-to-all-done.4 = bf16[16,8,512]{2,1,0:T(8,128)(2,1)S(1)} async-done(((bf16[16,8,512]{2,1,0:T(8,128)(2,1)}), bf16[16,8,512]{2,1,0:T(8,128)(2,1)S(1)}, u32[]{:S(2)}, u32[]{:S(2)}) %all-to-all-start.4) | async-done | bytes 131104 | tf_op jit(solution)/shard_map/all_to_all | solution.py:257
  54.7 3.5 %all-to-all-start.1 = ((bf16[16,8,512]{2,1,0:T(8,128)(2,1)}), bf16[16,8,512]{2,1,0:T(8,128)(2,1)S(1)}, u32[]{:S(2)}, u32[]{:S(2)}) async-start(bf16[16,8,512]{2,1,0:T(8,128)(2,1)} %bitcast.2), calls=%async_computation.1 | async-start | bytes 262144 | tf_op jit(solution)/shard_map/all_to_all | solution.py:257
  58.2 1.1 shard_map.143
  59.3 7.3 %all-to-all-done.1 = bf16[16,8,512]{2,1,0:T(8,128)(2,1)S(1)} async-done(((bf16[16,8,512]{2,1,0:T(8,128)(2,1)}), bf16[16,8,512]{2,1,0:T(8,128)(2,1)S(1)}, u32[]{:S(2)}, u32[]{:S(2)}) %all-to-all-start.1) | async-done | bytes 131104 | tf_op jit(solution)/shard_map/all_to_all | solution.py:257
  66.6 5.2 %all-to-all-start.5 = ((bf16[16,8,512]{2,1,0:T(8,128)(2,1)}), bf16[16,8,512]{2,1,0:T(8,128)(2,1)S(1)}, u32[]{:S(2)}, u32[]{:S(2)}) async-start(bf16[16,8,512]{2,1,0:T(8,128)(2,1)} %bitcast.10), calls=%async_computation.5 | async-start | bytes 262144 | tf_op jit(solution)/shard_map/all_to_all | solution.py:257
  71.8 2.8 %shard_map.140 = bf16[256,512]{1,0:T(8,128)(2,1)} custom-call(bf16[128,512]{1,0:T(8,128)(2,1)S(1)} %bitcast.22, f32[2,512,256]{2,1,0:T(8,128)S(1)} %get-tuple-element.17.spectra_ref, bf16[128,128]{1,0:T(8,128)(2,1)S(1)} %copy-done.9, bf16[2,64,128]{2,1,0:T(8,128)(2,1)S(1)} %copy-done.10, f32[64,256]{1,0:T(8,128)S(1)} %copy-done.8, ...), custom_call_target="tpu_custom_call" | custom-call | flops 1073741824 | bytes 524288 | tf_op jit(solution)/shard_map/pallas_call | solution.py:277
  74.6 6.0 %all-to-all-done.5 = bf16[16,8,512]{2,1,0:T(8,128)(2,1)S(1)} async-done(((bf16[16,8,512]{2,1,0:T(8,128)(2,1)}), bf16[16,8,512]{2,1,0:T(8,128)(2,1)S(1)}, u32[]{:S(2)}, u32[]{:S(2)}) %all-to-all-start.5) | async-done | bytes 131104 | tf_op jit(solution)/shard_map/all_to_all | solution.py:257
  80.7 3.8 %all-to-all-start.3 = ((bf16[16,16,512]{2,1,0:T(8,128)(2,1)}), bf16[16,16,512]{2,1,0:T(8,128)(2,1)S(1)}, u32[]{:S(2)}, u32[]{:S(2)}) async-start(bf16[16,16,512]{2,1,0:T(8,128)(2,1)} %bitcast.6), calls=%async_computation.3 | async-start | bytes 524288 | tf_op jit(solution)/shard_map/all_to_all | solution.py:257
  84.5 0.0 copy-start.2
  84.5 1.2 %shard_map.142 = (bf16[512,128]{1,0:T(8,128)(2,1)}, f32[128,64]{1,0:T(8,128)S(1)}) custom-call(bf16[128,512]{1,0:T(8,128)(2,1)S(1)} %bitcast.17, bf16[512,128]{1,0:T(8,128)(2,1)S(1)} %copy-done, bf16[128,512]{1,0:T(8,128)(2,1)S(1)} %bitcast.15, bf16[2,64,64]{2,1,0:T(8,128)(2,1)S(1)} %copy-done.3), custom_call_target="tpu_custom_call" | custom-call | flops 67108864 | bytes 524288 | tf_op jit(solution)/shard_map/pallas_call | solution.py:286
  85.8 0.0 copy-done.2
  85.8 1.1 shard_map.144
  86.8 9.0 %all-to-all-done.3 = bf16[16,16,512]{2,1,0:T(8,128)(2,1)S(1)} async-done(((bf16[16,16,512]{2,1,0:T(8,128)(2,1)}), bf16[16,16,512]{2,1,0:T(8,128)(2,1)S(1)}, u32[]{:S(2)}, u32[]{:S(2)}) %all-to-all-start.3) | async-done | bytes 262176 | tf_op jit(solution)/shard_map/all_to_all | solution.py:257
  95.9 3.5 %all-to-all-start.6 = ((f32[16,8,128]{2,1,0:T(8,128)}), f32[16,8,128]{2,1,0:T(8,128)S(1)}, u32[]{:S(2)}, u32[]{:S(2)}) async-start(f32[16,8,128]{2,1,0:T(8,128)} %bitcast.12), calls=%async_computation.6 | async-start | bytes 131072 | tf_op jit(solution)/shard_map/all_to_all | solution.py:257
  99.4 1.0 shard_map.141
  100.3 7.1 %all-to-all-done.6 = f32[16,8,128]{2,1,0:T(8,128)S(1)} async-done(((f32[16,8,128]{2,1,0:T(8,128)}), f32[16,8,128]{2,1,0:T(8,128)S(1)}, u32[]{:S(2)}, u32[]{:S(2)}) %all-to-all-start.6) | async-done | bytes 65568 | tf_op jit(solution)/shard_map/all_to_all | solution.py:257
  107.4 0.7 shard_map.145
Async XLA Ops:
  0.6 0.9 copy-start.1
  1.5 0.9 copy-start.4
  2.4 0.9 copy-start.5
  3.3 0.8 copy-start.6
  5.2 28.3 %copy-start.8 = (f32[64,256]{1,0:T(8,128)S(1)}, f32[64,256]{1,0:T(8,128)}, u32[]{:S(2)}) copy-start(f32[64,256]{1,0:T(8,128)} %constant.10.clone.twiddle_ref) | copy-start | bytes 196612
  5.2 28.3 %copy-start.9 = (bf16[128,128]{1,0:T(8,128)(2,1)S(1)}, bf16[128,128]{1,0:T(8,128)(2,1)}, u32[]{:S(2)}) copy-start(bf16[128,128]{1,0:T(8,128)(2,1)} %constant.8.clone.outer_ref) | copy-start | bytes 98308
  5.2 28.3 %copy-start.10 = (bf16[2,64,128]{2,1,0:T(8,128)(2,1)S(1)}, bf16[2,64,128]{2,1,0:T(8,128)(2,1)}, u32[]{:S(2)}) copy-start(bf16[2,64,128]{2,1,0:T(8,128)(2,1)} %constant.9.clone.back_ref) | copy-start | bytes 98308
  24.5 9.0 %copy-start.7 = (bf16[2,256,256]{2,1,0:T(8,128)(2,1)S(1)}, bf16[2,256,256]{2,1,0:T(8,128)(2,1)}, u32[]{:S(2)}) copy-start(bf16[2,256,256]{2,1,0:T(8,128)(2,1)} %constant.11.clone.inner_ref) | copy-start | bytes 786436
  24.5 17.8 %all-to-all-start = ((bf16[16,8,512]{2,1,0:T(8,128)(2,1)}), bf16[16,8,512]{2,1,0:T(8,128)(2,1)S(1)}, u32[]{:S(2)}, u32[]{:S(2)}) async-start(bf16[16,8,512]{2,1,0:T(8,128)(2,1)} %bitcast), calls=%async_computation | async-start | bytes 262144 | tf_op jit(solution)/shard_map/all_to_all | solution.py:257
  42.3 3.7 %copy-start = (bf16[512,128]{1,0:T(8,128)(2,1)S(1)}, bf16[512,128]{1,0:T(8,128)(2,1)}, u32[]{:S(2)}) copy-start(bf16[512,128]{1,0:T(8,128)(2,1)} %gate_ref.5) | copy-start | bytes 393220
  42.3 3.7 %copy-start.3 = (bf16[2,64,64]{2,1,0:T(8,128)(2,1)S(1)}, bf16[2,64,64]{2,1,0:T(8,128)(2,1)}, u32[]{:S(2)}) copy-start(bf16[2,64,64]{2,1,0:T(8,128)(2,1)} %w_first_ref.5) | copy-start | bytes 49156
  42.3 12.5 %all-to-all-start.4 = ((bf16[16,8,512]{2,1,0:T(8,128)(2,1)}), bf16[16,8,512]{2,1,0:T(8,128)(2,1)S(1)}, u32[]{:S(2)}, u32[]{:S(2)}) async-start(bf16[16,8,512]{2,1,0:T(8,128)(2,1)} %bitcast.8), calls=%async_computation.4 | async-start | bytes 262144 | tf_op jit(solution)/shard_map/all_to_all | solution.py:257
  54.7 11.9 %all-to-all-start.1 = ((bf16[16,8,512]{2,1,0:T(8,128)(2,1)}), bf16[16,8,512]{2,1,0:T(8,128)(2,1)S(1)}, u32[]{:S(2)}, u32[]{:S(2)}) async-start(bf16[16,8,512]{2,1,0:T(8,128)(2,1)} %bitcast.2), calls=%async_computation.1 | async-start | bytes 262144 | tf_op jit(solution)/shard_map/all_to_all | solution.py:257
  66.6 14.1 %all-to-all-start.5 = ((bf16[16,8,512]{2,1,0:T(8,128)(2,1)}), bf16[16,8,512]{2,1,0:T(8,128)(2,1)S(1)}, u32[]{:S(2)}, u32[]{:S(2)}) async-start(bf16[16,8,512]{2,1,0:T(8,128)(2,1)} %bitcast.10), calls=%async_computation.5 | async-start | bytes 262144 | tf_op jit(solution)/shard_map/all_to_all | solution.py:257
  80.7 15.2 %all-to-all-start.3 = ((bf16[16,16,512]{2,1,0:T(8,128)(2,1)}), bf16[16,16,512]{2,1,0:T(8,128)(2,1)S(1)}, u32[]{:S(2)}, u32[]{:S(2)}) async-start(bf16[16,16,512]{2,1,0:T(8,128)(2,1)} %bitcast.6), calls=%async_computation.3 | async-start | bytes 524288 | tf_op jit(solution)/shard_map/all_to_all | solution.py:257
  84.5 1.3 %copy-start.2 = (bf16[512,128]{1,0:T(8,128)(2,1)S(1)}, bf16[512,128]{1,0:T(8,128)(2,1)}, u32[]{:S(2)}) copy-start(bf16[512,128]{1,0:T(8,128)(2,1)} %d_out_ref.3) | copy-start | bytes 393220
  95.9 11.6 %all-to-all-start.6 = ((f32[16,8,128]{2,1,0:T(8,128)}), f32[16,8,128]{2,1,0:T(8,128)S(1)}, u32[]{:S(2)}, u32[]{:S(2)}) async-start(f32[16,8,128]{2,1,0:T(8,128)} %bitcast.12), calls=%async_computation.6 | async-start | bytes 131072 | tf_op jit(solution)/shard_map/all_to_all | solution.py:257

commit v2 on v1

--- a/solution.py
+++ b/solution.py
@@ -10,7 +10,6 @@
 
 F32 = jnp.float32
 BF16 = jnp.bfloat16
-HIGHEST = lax.Precision.HIGHEST
 NN = (((1,), (0,)), ((), ()))
 NT = (((1,), (1,)), ((), ()))
 TN = (((0,), (0,)), ((), ()))
@@ -18,10 +17,6 @@
 
 def dot(a, b, form=NN):
     return lax.dot_general(a, b, form, preferred_element_type=F32)
-
-
-def exact_dot(a, b, form=NN):
-    return lax.dot_general(a, b, form, preferred_element_type=F32, precision=HIGHEST)
 
 
 def halves(table):
@@ -80,15 +75,21 @@
     return ones_where(row == col)
 
 
-def first_blocks(w_first_ref):
-    flat = w_first_ref[...].reshape(128, 64)
-    row, col = iotas(64, 128)
-    spread = dot(flat, ones_where(row == col // 8 * 4 + col % 4))
-    row, col = iotas(128, 128)
-    return jnp.where(row // 64 == col // 4 % 2, spread, 0.0).astype(BF16)
-
-
-def entry_kernel(signal_ref, filter_ref, d_out_ref, w_second_ref, pair_ref, back_ref):
+def pair_kernel(signal_hbm, filter_hbm, pair_ref, both_ref, sems):
+    copies = [
+        pltpu.make_async_copy(source, both_ref.at[field], sems.at[field])
+        for field, source in enumerate((signal_hbm, filter_hbm))
+    ]
+    for copy in copies:
+        copy.start()
+    order = pair_order()
+    for copy in copies:
+        copy.wait()
+    both = jnp.concatenate([both_ref[0], both_ref[1]], axis=1)
+    pair_ref[...] = dot(order, both, NT).astype(BF16)
+
+
+def back_kernel(d_out_ref, w_second_ref, back_ref):
     flat = w_second_ref[...].reshape(128, 32)
     row, col = iotas(32, 128)
     spread = dot(flat, ones_where(row == col % 32))
@@ -97,14 +98,25 @@
     order = ones_where((row // 4 == col % 32) & (row % 4 == col // 32))
     weights = dot(order, spread).astype(BF16)
     back_ref[...] = dot(weights, d_out_ref[...], NT).astype(BF16)
-    both = jnp.concatenate([signal_ref[...], filter_ref[...]], axis=1)
-    pair_ref[...] = dot(pair_order(), both, NT).astype(BF16)
-
-
-def gate_kernel(returned_ref, w_first_ref, gate_ref, incoming_ref):
-    grad_product = dot(first_blocks(w_first_ref), returned_ref[...])
-    gate = dot(unit(), gate_ref[...], NT)
-    incoming_ref[...] = (grad_product * gate).astype(BF16)
+
+
+def prepare_kernel(gate_ref, w_first_ref, gate_out_ref, blocks_ref):
+    flat = w_first_ref[...].reshape(128, 64)
+    row, col = iotas(64, 128)
+    spread = dot(flat, ones_where(row == col // 8 * 4 + col % 4))
+    row, col = iotas(128, 128)
+    blocks_ref[...] = jnp.where(row // 64 == col // 4 % 2, spread, 0.0).astype(BF16)
+    gate_out_ref[...] = dot(unit(), gate_ref[...], NT)
+
+
+def gate_kernel(returned_ref, blocks_ref, gate_ref, conv_ref, pair_ref):
+    incoming = dot(blocks_ref[...], returned_ref[...]) * gate_ref[...]
+    rows = []
+    for p in range(16):
+        pieces = [conv_ref[128 * th + 8 * p : 128 * th + 8 * p + 8, :] for th in range(4)]
+        rows.append(jnp.concatenate(pieces, axis=1))
+        rows.append(incoming[8 * p : 8 * p + 8, :])
+    pair_ref[...] = jnp.concatenate(rows, axis=0).astype(BF16)
 
 
 def split(value):
@@ -163,9 +175,7 @@
     return dot(back_ref[0], high) + dot(back_ref[0], low) + dot(back_ref[1], high)
 
 
-def conv_kernel(
-    pair_ref, outer_ref, back_ref, twiddle_ref, inner_ref, conv_ref, spectra_ref, wide_ref, out_ref
-):
+def conv_kernel(pair_ref, outer_ref, back_ref, twiddle_ref, inner_ref, conv_ref, spectra_ref, wide_ref):
     unroll(wide_ref, pair_ref[...])
     signal = transform(by_channel(wide_ref, 0, 16), outer_ref, twiddle_ref, inner_ref)
     kernel = transform(by_channel(wide_ref, 8, 16), outer_ref, twiddle_ref, inner_ref)
@@ -174,15 +184,14 @@
     sr, si = signal[:, 0:128], signal[:, 128:256]
     kr, ki = kernel[:, 0:128], kernel[:, 128:256]
     result = restore(sr * kr - si * ki, sr * ki + si * kr, back_ref, twiddle_ref, inner_ref)
-    by_slab(out_ref, result, 0, 8)
-    conv_ref[...] = enroll(out_ref)
+    by_slab(conv_ref, result, 0, 8)
 
 
 def adjoint_kernel(
-    incoming_ref, spectra_ref, outer_ref, back_ref, twiddle_ref, inner_ref, pair_ref, wide_ref, out_ref
+    pair_ref, spectra_ref, outer_ref, back_ref, twiddle_ref, inner_ref, grads_ref, wide_ref, out_ref
 ):
-    unroll(wide_ref, incoming_ref[...])
-    spectrum = transform(by_channel(wide_ref, 0, 8), outer_ref, twiddle_ref, inner_ref)
+    unroll(wide_ref, pair_ref[...])
+    spectrum = transform(by_channel(wide_ref, 8, 16), outer_ref, twiddle_ref, inner_ref)
     gr, gi = spectrum[:, 0:128], spectrum[:, 128:256]
     for field in range(2):
         real, imag = spectra_ref[1 - field, :, 0:128], spectra_ref[1 - field, :, 128:256]
@@ -190,64 +199,79 @@
             gr * real + gi * imag, gi * real - gr * imag, back_ref, twiddle_ref, inner_ref
         )
         by_slab(out_ref, result, 8 * field, 16)
-    pair_ref[...] = enroll(out_ref)
-
-
-def mix_kernel(conv_ref, gate_ref, w_first_ref, mix_ref):
-    gate = dot(unit(), gate_ref[...], NT)
-    product = (conv_ref[...].astype(F32) * gate).astype(BF16)
-    mix_ref[...] = dot(first_blocks(w_first_ref), product, TN).astype(BF16)
-
-
-def first_kernel(conv_ref, gate_ref, returned_ref, w_first_ref, grad_gate_ref, partial_ref):
-    gate = dot(unit(), gate_ref[...], NT)
-    conv = conv_ref[...].astype(F32)
-    product = (conv * gate).astype(BF16)
+    grads_ref[...] = enroll(out_ref)
+
+
+def conv_rows(pair_ref):
+    wide = pair_ref[...].astype(F32)
+    return jnp.concatenate([wide[16 * p : 16 * p + 8, :] for p in range(16)], axis=0)
+
+
+def mix_kernel(pair_ref, gate_ref, blocks_ref, mix_ref):
+    product = (conv_rows(pair_ref) * gate_ref[...]).astype(BF16)
+    mix_ref[...] = dot(blocks_ref[...], product, TN).astype(BF16)
+
+
+def first_kernel(pair_ref, gate_ref, returned_ref, blocks_ref, grad_gate_ref, partial_ref):
+    conv = conv_rows(pair_ref)
+    product = (conv * gate_ref[...]).astype(BF16)
     returned = returned_ref[...]
-    grad_product = dot(first_blocks(w_first_ref), returned)
-    grad_gate = (grad_product * conv).astype(BF16)
+    grad_gate = (dot(blocks_ref[...], returned) * conv).astype(BF16)
     grad_gate_ref[...] = dot(grad_gate, unit(), TN).astype(BF16)
     row, col = iotas(128, 128)
     grad = jnp.where(row // 64 == col // 4 % 2, dot(product, returned, NT), 0.0)
-    order = jnp.where(
-        (row // 8 == col % 64 // 4) & (row // 4 % 2 == col // 64) & (row % 4 == col % 4), 1.0, 0.0
+    order = ones_where(
+        (row // 8 == col % 64 // 4) & (row // 4 % 2 == col // 64) & (row % 4 == col % 4)
     )
     row, col = iotas(128, 64)
-    fold = jnp.where(row // 8 * 4 + row % 4 == col, 1.0, 0.0)
-    partial_ref[...] = exact_dot(order, exact_dot(grad, fold))
-
-
-def exit_kernel(pair_ref, signal_ref, filter_ref):
-    both = dot(pair_ref[...], pair_order(), TN).astype(BF16)
+    fold = ones_where(row // 8 * 4 + row % 4 == col)
+    for part, piece in enumerate(split(grad)):
+        partial_ref[part] = dot(order, dot(piece, fold).astype(BF16))
+
+
+def second_kernel(received_ref, d_out_ref, partial_ref, grads_ref, sums_ref):
+    row, col = iotas(128, 128)
+    grad = jnp.where(row % 4 == col // 32, dot(received_ref[...], d_out_ref[...]), 0.0)
+    row, col = iotas(128, 64)
+    fold = ones_where(row % 32 == col)
+    high, low = [
+        jnp.concatenate([partial_ref[part], dot(piece, fold)], axis=1)
+        for part, piece in enumerate(split(grad))
+    ]
+    rows = []
+    for p in range(16):
+        rows.append(high[8 * p : 8 * p + 8, :])
+        rows.append(low[8 * p : 8 * p + 8, :])
+    sums_ref[:, 0:512] = grads_ref[...]
+    sums_ref[:, 512:640] = jnp.concatenate(rows, axis=0).astype(BF16)
+
+
+def exit_kernel(sums_ref, signal_ref, filter_ref, first_ref, second_ref):
+    both = dot(sums_ref[:, 0:512], pair_order(), TN).astype(BF16)
     signal_ref[...] = both[:, 0:128]
     filter_ref[...] = both[:, 128:256]
-
-
-def second_kernel(received_ref, d_out_ref, partial_ref, sums_ref):
-    row, col = iotas(128, 128)
-    grad = jnp.where(row % 4 == col // 32, dot(received_ref[...], d_out_ref[...]), 0.0)
-    row, col = iotas(128, 64)
-    fold = jnp.where(row % 32 == col, 1.0, 0.0)
-    sums_ref[...] = jnp.concatenate([partial_ref[...], exact_dot(grad, fold)], axis=1)
-
-
-def sum_kernel(sums_ref, first_ref, second_ref):
-    total = sums_ref[0:8, :]
-    for s in range(1, 16):
-        total = total + sums_ref[8 * s : 8 * s + 8, :]
+    wide = sums_ref[:, 512:640].astype(F32)
+    total = wide[0:16, :]
+    for p in range(1, 16):
+        total = total + wide[16 * p : 16 * p + 16, :]
+    total = total[0:8, :] + total[8:16, :]
     for i in range(2):
         first_ref[i] = total[4 * i : 4 * i + 4, 0:64]
         for k in range(4):
             second_ref[k, i : i + 1, :] = total[4 * i + k : 4 * i + k + 1, 64:96]
 
 
-def call(body, outs, scratch=(), flops=1 << 26, moved=1 << 19):
+def call(body, outs, scratch=(), flops=1 << 26, moved=1 << 19, held=None):
+    extra = {}
+    if held is not None:
+        extra["in_specs"] = [pl.BlockSpec(memory_space=held[0])] * held[1]
     return pl.pallas_call(
         body,
         out_shape=[jax.ShapeDtypeStruct(shape, kind) for shape, kind in outs],
         scratch_shapes=list(scratch),
         compiler_params=pltpu.CompilerParams(vmem_limit_bytes=32 << 20),
         cost_estimate=pl.CostEstimate(flops=flops, bytes_accessed=moved, transcendentals=0),
+        **extra,
     )
 
 
@@ -260,36 +284,42 @@
 def shards(signal, filter_raw, gate, d_out, w_first, w_second):
     rows, width = signal.shape
     outer, back, twiddle, inner = (jnp.asarray(t) for t in tables(lax.axis_size("seq"), rows))
-    pair, second_back = call(
-        entry_kernel, [((2 * width, rows), BF16), ((width, rows), BF16)]
-    )(signal, filter_raw, d_out, w_second)
+    single, double = ((width, rows), BF16), ((2 * width, rows), BF16)
+    slab = ((rows, width), BF16)
+    pair = call(
+        pair_kernel,
+        [double],
+        [pltpu.VMEM((2, rows, width), BF16), pltpu.SemaphoreType.DMA((2,))],
+        held=(pltpu.HBM, 2),
+    )(signal, filter_raw)[0]
+    pair = exchange(pair, "seq")
+    second_back = call(back_kernel, [single])(d_out, w_second)[0]
+    gate, blocks = call(prepare_kernel, [((width, rows), F32), ((128, 128), BF16)])(gate, w_first)
     returned = exchange(second_back, "ch")
-    pair = exchange(pair, "seq")
     conv, spectra = call(
         conv_kernel,
-        [((width, rows), BF16), ((2, 512, 256), F32)],
-        [pltpu.VMEM((2 * width * 4, 128), F32), pltpu.VMEM((width * 4, 128), F32)],
+        [((4 * width, 128), F32), ((2, 512, 256), F32)],
+        [pltpu.VMEM((2 * width * 4, 128), F32)],
         flops=1 << 30,
     )(pair, outer, back, twiddle, inner)
-    conv = exchange(conv, "seq")
-    incoming = call(gate_kernel, [((width, rows), BF16)])(returned, w_first, gate)[0]
-    incoming = exchange(incoming, "seq")
+    pair = call(gate_kernel, [double])(returned, blocks, gate, conv)[0]
+    pair = exchange(pair, "seq")
+    mix = call(mix_kernel, [single])(pair, gate, blocks)[0]
+    received = exchange(mix, "ch")
     grads = call(
         adjoint_kernel,
-        [((2 * width, rows), BF16)],
-        [pltpu.VMEM((width * 4, 128), F32), pltpu.VMEM((2 * width * 4, 128), F32)],
+        [double],
+        [pltpu.VMEM((2 * width * 4, 128), F32), pltpu.VMEM((2 * width * 4, 128), F32)],
         flops=1 << 30,
-    )(incoming, spectra, outer, back, twiddle, inner)[0]
-    grads = exchange(grads, "seq")
-    mix = call(mix_kernel, [((width, rows), BF16)])(conv, gate, w_first)[0]
-    received = exchange(mix, "ch")
-    grad_gate, partial = call(first_kernel, [((rows, width), BF16), ((width, 64), F32)])(
-        conv, gate, returned, w_first
-    )
-    grad_signal, grad_filter = call(exit_kernel, [((rows, width), BF16), ((rows, width), BF16)])(grads)
-    sums = call(second_kernel, [((width, 128), F32)])(received, d_out, partial)[0]
+    )(pair, spectra, outer, back, twiddle, inner)[0]
+    grad_gate, partial = call(first_kernel, [slab, ((2, width, 64), F32)])(
+        pair, gate, returned, blocks
+    )
+    sums = call(second_kernel, [((2 * width, rows + 128), BF16)])(received, d_out, partial, grads)[0]
     sums = exchange(sums, "seq")
-    grad_first, grad_second = call(sum_kernel, [((2, 4, 64), F32), ((4, 2, 32), F32)])(sums)
+    grad_signal, grad_filter, grad_first, grad_second = call(
+        exit_kernel, [slab, slab, ((2, 4, 64), F32), ((4, 2, 32), F32)]
+    )(sums)
     return (grad_signal, grad_filter, grad_gate, grad_first, grad_second)
 
 

time: 109 us -> 89.7 us (0.82)
  waiting for transfers between devices: 43.8 us -> 21.8 us
  blocking collectives: 19.3 us -> 31.4 us
  starting transfers between devices: 28.7 us -> 22.4 us
  Pallas kernels: 12.1 us -> 9.68 us
    all_to_all x6 -> x3, waiting for transfers between devices: 43.8 us -> 21.8 us  [exchange(): lax.all_to_all(pieces, axis, split_axis=0, concat_axis=0, tiled=True)]
    all_to_all x1 -> x2, blocking collectives: 19.3 us -> 31.4 us  [exchange(): lax.all_to_all(pieces, axis, split_axis=0, concat_axis=0, tiled=True)]
    all_to_all x6 -> x3, starting transfers between devices: 28.7 us -> 22.4 us  [exchange(): lax.all_to_all(pieces, axis, split_axis=0, concat_axis=0, tiled=True)]
    pallas_call x9 -> x10, Pallas kernels: 12.1 us -> 9.68 us  [the longest x1 2.11 us: shards(): call(adjoint_kernel, [double], [pltpu.VMEM((2 * width * 4, 128), F32), pl...]
    unnamed x22 -> x20, local copies, waits for them, and re-layouts: 3.49 us -> 2.44 us
  transfers between devices with their start and end apart: 6 -> 3, of which waited for: 6 -> 3; matrix products, arithmetic and copies ran while one was open for 0% -> 0% of each run, Pallas kernels for 10% -> 7%
where the time goes in v2:
time: 89.7 us; the launch traced here: 88.6 us
  blocking collectives  31.4 us (35%)
  starting transfers between devices  22.4 us (25%)
  waiting for transfers between devices  21.8 us (24%)
  Pallas kernels  9.68 us (11%)
  local copies, waits for them, and re-layouts  2.44 us (3%)
    all_to_all x2, blocking collectives, exchange(): lax.all_to_all(pieces, axis, split_axis=0, concat_axis=0, tiled=True)  31.4 us
    all_to_all x3, starting transfers between devices, exchange(): lax.all_to_all(pieces, axis, split_axis=0, concat_axis=0, tiled=True)  22.4 us
    all_to_all x3, waiting for transfers between devices, exchange(): lax.all_to_all(pieces, axis, split_axis=0, concat_axis=0, tiled=True)  21.8 us
    unnamed x20, local copies, waits for them, and re-layouts  2.44 us
    pallas_call x1, Pallas kernels, shards(): call(adjoint_kernel, [double], [pltpu.VMEM((2 * width * 4, 128), F32), pl...  2.11 us
  transfers between devices with their start and end apart: 3, of which 3 were waited for; matrix products, arithmetic and copies ran while one was open for 0% of the time, Pallas kernels for 7%

profile of v2, /device:TPU:8, one launch (start us, length us, event | category | flops | bytes accessed | tf_op | source)
XLA Modules:
  0.0 88.6 jit_solution(116262522364045170)
XLA Ops:
  0.6 0.0 copy-start.1
  0.6 0.9 %copy-done.1 = bf16[512,128]{1,0:T(8,128)(2,1)S(1)} copy-done((bf16[512,128]{1,0:T(8,128)(2,1)S(1)}, bf16[512,128]{1,0:T(8,128)(2,1)}, u32[]{:S(2)}) %copy-start.1) | copy-done | bytes 131096
  1.5 0.0 copy-start.2
  1.5 0.9 %copy-done.2 = bf16[512,128]{1,0:T(8,128)(2,1)S(1)} copy-done((bf16[512,128]{1,0:T(8,128)(2,1)S(1)}, bf16[512,128]{1,0:T(8,128)(2,1)}, u32[]{:S(2)}) %copy-start.2) | copy-done | bytes 131096
  2.4 1.3 %shard_map.139 = bf16[256,512]{1,0:T(8,128)(2,1)} custom-call(bf16[512,128]{1,0:T(8,128)(2,1)S(1)} %copy-done.1, bf16[512,128]{1,0:T(8,128)(2,1)S(1)} %copy-done.2), custom_call_target="tpu_custom_call" | custom-call | flops 67108864 | bytes 524288 | tf_op jit(solution)/shard_map/pallas_call | solution.py:289
  3.8 0.0 copy-start
  3.8 0.0 copy-start.3
  3.8 8.6 %all-to-all-start.1 = ((bf16[16,16,512]{2,1,0:T(8,128)(2,1)}), bf16[16,16,512]{2,1,0:T(8,128)(2,1)S(1)}, u32[]{:S(2)}, u32[]{:S(2)}) async-start(bf16[16,16,512]{2,1,0:T(8,128)(2,1)} %bitcast.2), calls=%async_computation.1 | async-start | bytes 524288 | tf_op jit(solution)/shard_map/all_to_all | solution.py:281
  12.4 0.0 copy-done
  12.4 0.0 copy-done.3
  12.5 0.0 copy-start.6
  12.5 1.1 %shard_map.137 = bf16[128,512]{1,0:T(8,128)(2,1)} custom-call(bf16[512,128]{1,0:T(8,128)(2,1)S(1)} %copy-done, bf16[4,32,32]{2,1,0:T(8,128)(2,1)S(1)} %copy-done.3), custom_call_target="tpu_custom_call" | custom-call | flops 67108864 | bytes 524288 | tf_op jit(solution)/shard_map/pallas_call | solution.py:296
  13.5 9.8 %all-to-all-done.1 = bf16[16,16,512]{2,1,0:T(8,128)(2,1)S(1)} async-done(((bf16[16,16,512]{2,1,0:T(8,128)(2,1)}), bf16[16,16,512]{2,1,0:T(8,128)(2,1)S(1)}, u32[]{:S(2)}, u32[]{:S(2)}) %all-to-all-start.1) | async-done | bytes 262176 | tf_op jit(solution)/shard_map/all_to_all | solution.py:281
  23.3 0.0 copy-start.4
  23.3 0.0 copy-start.5
  23.3 9.0 %all-to-all-start = ((bf16[16,8,512]{2,1,0:T(8,128)(2,1)}), bf16[16,8,512]{2,1,0:T(8,128)(2,1)S(1)}, u32[]{:S(2)}, u32[]{:S(2)}) async-start(bf16[16,8,512]{2,1,0:T(8,128)(2,1)} %bitcast), calls=%async_computation | async-start | bytes 262144 | tf_op jit(solution)/shard_map/all_to_all | solution.py:281
  32.3 0.0 copy-done.4
  32.3 0.0 copy-done.5
  32.3 0.0 copy-start.7
  32.3 0.0 copy-start.8
  32.4 0.0 copy-start.9
  32.4 0.2 shard_map.138
  32.6 0.0 copy-done.6
  32.6 0.6 copy-done.7
  33.2 0.0 copy-done.8
  33.2 0.0 copy-done.9
  33.2 1.5 %shard_map.140 = (f32[512,128]{1,0:T(8,128)S(1)}, f32[2,512,256]{2,1,0:T(8,128)S(1)}) custom-call(bf16[256,512]{1,0:T(8,128)(2,1)S(1)} %bitcast.19, bf16[128,128]{1,0:T(8,128)(2,1)S(1)} %copy-done.9, bf16[2,64,128]{2,1,0:T(8,128)(2,1)S(1)} %copy-done.8, f32[64,256]{1,0:T(8,128)S(1)} %copy-done.7, bf16[2,256,256]{2,1,0:T(8,128)(2,1)S(1)} %copy-done.6), custom_call_target="tpu_custom_call" | custom-call | flops 1073741824 | bytes 524288 | tf_op jit(solution)/shard_map/pallas_call | solution.py:299
  34.7 6.4 %all-to-all-done = bf16[16,8,512]{2,1,0:T(8,128)(2,1)S(1)} async-done(((bf16[16,8,512]{2,1,0:T(8,128)(2,1)}), bf16[16,8,512]{2,1,0:T(8,128)(2,1)S(1)}, u32[]{:S(2)}, u32[]{:S(2)}) %all-to-all-start) | async-done | bytes 131104 | tf_op jit(solution)/shard_map/all_to_all | solution.py:281
  41.1 0.2 shard_map.141
  41.3 15.0 %all_to_all.25 = bf16[16,16,512]{2,1,0:T(8,128)(2,1)S(1)} all-to-all(bf16[16,16,512]{2,1,0:T(8,128)(2,1)S(1)} %bitcast.17), channel_id=1, replica_groups=mesh['seq'=16,'ch'=16] {'seq'}, dimensions={0} | all-to-all | bytes 524288 | tf_op jit(solution)/shard_map/all_to_all | solution.py:281
  56.3 0.9 shard_map.142
  57.2 4.8 %all-to-all-start.3 = ((bf16[16,8,512]{2,1,0:T(8,128)(2,1)}), bf16[16,8,512]{2,1,0:T(8,128)(2,1)S(1)}, u32[]{:S(2)}, u32[]{:S(2)}) async-start(bf16[16,8,512]{2,1,0:T(8,128)(2,1)} %bitcast.6), calls=%async_computation.3 | async-start | bytes 262144 | tf_op jit(solution)/shard_map/all_to_all | solution.py:281
  62.0 1.1 %shard_map.143 = (bf16[512,128]{1,0:T(8,128)(2,1)}, f32[2,128,64]{2,1,0:T(8,128)S(1)}) custom-call(bf16[256,512]{1,0:T(8,128)(2,1)S(1)} %bitcast.11, f32[128,512]{1,0:T(8,128)S(1)} %get-tuple-element.16.gate_ref, bf16[128,512]{1,0:T(8,128)(2,1)S(1)} %bitcast.16, bf16[128,128]{1,0:T(8,128)(2,1)S(1)} %get-tuple-element.15.blocks_ref), custom_call_target="tpu_custom_call" | custom-call | flops 67108864 | bytes 524288 | tf_op jit(solution)/shard_map/pallas_call | solution.py:315
  63.0 2.1 %shard_map.144.grads_ref = bf16[256,512]{1,0:T(8,128)(2,1)S(1)} custom-call(bf16[256,512]{1,0:T(8,128)(2,1)S(1)} %bitcast.12, f32[2,512,256]{2,1,0:T(8,128)S(1)} %get-tuple-element.19.spectra_ref, bf16[128,128]{1,0:T(8,128)(2,1)S(1)} %copy-done.9, bf16[2,64,128]{2,1,0:T(8,128)(2,1)S(1)} %copy-done.8, f32[64,256]{1,0:T(8,128)S(1)} %copy-done.7, ...), custom_call_target="tpu_custom_call" | custom-call | flops 1073741824 | bytes 524288 | tf_op jit(solution)/shard_map/pallas_call | solution.py:309
  65.2 5.7 %all-to-all-done.3 = bf16[16,8,512]{2,1,0:T(8,128)(2,1)S(1)} async-done(((bf16[16,8,512]{2,1,0:T(8,128)(2,1)}), bf16[16,8,512]{2,1,0:T(8,128)(2,1)S(1)}, u32[]{:S(2)}, u32[]{:S(2)}) %all-to-all-start.3) | async-done | bytes 131104 | tf_op jit(solution)/shard_map/all_to_all | solution.py:281
  70.8 0.4 shard_map.145
  71.2 16.4 %all_to_all.26 = bf16[16,16,640]{2,1,0:T(8,128)(2,1)S(1)} all-to-all(bf16[16,16,640]{2,1,0:T(8,128)(2,1)S(1)} %bitcast.14), channel_id=1, replica_groups=mesh['seq'=16,'ch'=16] {'seq'}, dimensions={0} | all-to-all | bytes 655360 | tf_op jit(solution)/shard_map/all_to_all | solution.py:281
  87.6 1.0 %shard_map.146 = (bf16[512,128]{1,0:T(8,128)(2,1)}, bf16[512,128]{1,0:T(8,128)(2,1)}, f32[2,4,64]{2,1,0:T(4,128)}, f32[4,2,32]{2,1,0:T(2,128)}) custom-call(bf16[256,640]{1,0:T(8,128)(2,1)S(1)} %bitcast.13), custom_call_target="tpu_custom_call" | custom-call | flops 67108864 | bytes 524288 | tf_op jit(solution)/shard_map/pallas_call | solution.py:320
Async XLA Ops:
  0.6 0.9 %copy-start.1 = (bf16[512,128]{1,0:T(8,128)(2,1)S(1)}, bf16[512,128]{1,0:T(8,128)(2,1)}, u32[]{:S(2)}) copy-start(bf16[512,128]{1,0:T(8,128)(2,1)} %signal_hbm.1) | copy-start | bytes 393220
  1.5 0.9 %copy-start.2 = (bf16[512,128]{1,0:T(8,128)(2,1)S(1)}, bf16[512,128]{1,0:T(8,128)(2,1)}, u32[]{:S(2)}) copy-start(bf16[512,128]{1,0:T(8,128)(2,1)} %filter_hbm.1) | copy-start | bytes 393220
  3.8 8.6 %copy-start = (bf16[512,128]{1,0:T(8,128)(2,1)S(1)}, bf16[512,128]{1,0:T(8,128)(2,1)}, u32[]{:S(2)}) copy-start(bf16[512,128]{1,0:T(8,128)(2,1)} %d_out_ref.3) | copy-start | bytes 393220
  3.8 8.6 %copy-start.3 = (bf16[4,32,32]{2,1,0:T(8,128)(2,1)S(1)}, bf16[4,32,32]{2,1,0:T(8,128)(2,1)}, u32[]{:S(2)}) copy-start(bf16[4,32,32]{2,1,0:T(8,128)(2,1)} %w_second_ref.1) | copy-start | bytes 24580
  3.8 19.5 %all-to-all-start.1 = ((bf16[16,16,512]{2,1,0:T(8,128)(2,1)}), bf16[16,16,512]{2,1,0:T(8,128)(2,1)S(1)}, u32[]{:S(2)}, u32[]{:S(2)}) async-start(bf16[16,16,512]{2,1,0:T(8,128)(2,1)} %bitcast.2), calls=%async_computation.1 | async-start | bytes 524288 | tf_op jit(solution)/shard_map/all_to_all | solution.py:281
  12.5 20.1 %copy-start.6 = (bf16[2,256,256]{2,1,0:T(8,128)(2,1)S(1)}, bf16[2,256,256]{2,1,0:T(8,128)(2,1)}, u32[]{:S(2)}) copy-start(bf16[2,256,256]{2,1,0:T(8,128)(2,1)} %constant.11.clone.inner_ref) | copy-start | bytes 786436
  23.3 9.0 %copy-start.4 = (bf16[512,128]{1,0:T(8,128)(2,1)S(1)}, bf16[512,128]{1,0:T(8,128)(2,1)}, u32[]{:S(2)}) copy-start(bf16[512,128]{1,0:T(8,128)(2,1)} %gate_ref.1) | copy-start | bytes 393220
  23.3 9.0 %copy-start.5 = (bf16[2,64,64]{2,1,0:T(8,128)(2,1)S(1)}, bf16[2,64,64]{2,1,0:T(8,128)(2,1)}, u32[]{:S(2)}) copy-start(bf16[2,64,64]{2,1,0:T(8,128)(2,1)} %w_first_ref.1) | copy-start | bytes 49156
  23.3 17.8 %all-to-all-start = ((bf16[16,8,512]{2,1,0:T(8,128)(2,1)}), bf16[16,8,512]{2,1,0:T(8,128)(2,1)S(1)}, u32[]{:S(2)}, u32[]{:S(2)}) async-start(bf16[16,8,512]{2,1,0:T(8,128)(2,1)} %bitcast), calls=%async_computation | async-start | bytes 262144 | tf_op jit(solution)/shard_map/all_to_all | solution.py:281
  32.3 0.8 copy-start.7
  32.3 0.8 copy-start.8
  32.4 0.8 copy-start.9
  57.2 13.7 %all-to-all-start.3 = ((bf16[16,8,512]{2,1,0:T(8,128)(2,1)}), bf16[16,8,512]{2,1,0:T(8,128)(2,1)S(1)}, u32[]{:S(2)}, u32[]{:S(2)}) async-start(bf16[16,8,512]{2,1,0:T(8,128)(2,1)} %bitcast.6), calls=%async_computation.3 | async-start | bytes 262144 | tf_op jit(solution)/shard_map/all_to_all | solution.py:281

commit v3 on v2

--- a/solution.py
+++ b/solution.py
@@ -89,28 +89,59 @@
     pair_ref[...] = dot(order, both, NT).astype(BF16)
 
 
-def back_kernel(d_out_ref, w_second_ref, back_ref):
+def place():
+    index = lax.axis_index("ch")
+    return index // 8, index // 2 % 4, index % 2
+
+
+def partner(slot_y, slot_zc, step):
+    z, y, core = place()
+    z = (z + slot_zc // 2) % 2
+    core = (core + slot_zc) % 2
+    y = (y + 4 + step * slot_y) % 4
+    return z * 8 + y * 2 + core
+
+
+def back_kernel(d_out_ref, w_second_ref, near_ref, core_ref, far_ref, cross_ref):
     flat = w_second_ref[...].reshape(128, 32)
     row, col = iotas(32, 128)
     spread = dot(flat, ones_where(row == col % 32))
     row, col = iotas(128, 128)
     spread = jnp.where(row // 32 == col // 32, spread, 0.0).astype(BF16)
-    order = ones_where((row // 4 == col % 32) & (row % 4 == col // 32))
+    block = 2 * partner(row // 8 % 4, row // 32, 1) + row // 4 % 2
+    order = ones_where((block == col % 32) & (row % 4 == col // 32))
     weights = dot(order, spread).astype(BF16)
-    back_ref[...] = dot(weights, d_out_ref[...], NT).astype(BF16)
-
-
-def prepare_kernel(gate_ref, w_first_ref, gate_out_ref, blocks_ref):
+    result = dot(weights, d_out_ref[...], NT).astype(BF16)
+    for zc, ref in enumerate((near_ref, core_ref, far_ref, cross_ref)):
+        ref[...] = result[32 * zc : 32 * zc + 32, :]
+
+
+def repack_kernel(*refs):
+    values = [ref[...].astype(F32) for ref in refs[:4]]
+    for y, ref in enumerate(refs[4:]):
+        ref[...] = jnp.concatenate([v[8 * y : 8 * y + 8, :] for v in values], axis=0).astype(BF16)
+
+
+def source(col):
+    return partner(col // 32, col // 8 % 4, -1)
+
+
+def prepare_kernel(gate_ref, w_first_ref, gate_out_ref, blocks_ref, own_ref):
     flat = w_first_ref[...].reshape(128, 64)
     row, col = iotas(64, 128)
-    spread = dot(flat, ones_where(row == col // 8 * 4 + col % 4))
-    row, col = iotas(128, 128)
-    blocks_ref[...] = jnp.where(row // 64 == col // 4 % 2, spread, 0.0).astype(BF16)
+    keep_row, keep_col = iotas(128, 128)
+    keep = keep_row // 64 == keep_col // 4 % 2
+    for ref, group in ((blocks_ref, col // 8), (own_ref, source(col))):
+        spread = dot(flat, ones_where(row == group * 4 + col % 4))
+        ref[...] = jnp.where(keep, spread, 0.0).astype(BF16)
     gate_out_ref[...] = dot(unit(), gate_ref[...], NT)
 
 
-def gate_kernel(returned_ref, blocks_ref, gate_ref, conv_ref, pair_ref):
-    incoming = dot(blocks_ref[...], returned_ref[...]) * gate_ref[...]
+def gate_kernel(near_ref, first_ref, second_ref, third_ref, own_ref, gate_ref, conv_ref, pair_ref, returned_ref):
+    pieces = [ref[...] for ref in (near_ref, first_ref, second_ref, third_ref)]
+    returned = jnp.concatenate(pieces, axis=0)
+    returned_ref[...] = returned
+    incoming = dot(own_ref[...], returned) * gate_ref[...]
     rows = []
     for p in range(16):
         pieces = [conv_ref[128 * th + 8 * p : 128 * th + 8 * p + 8, :] for th in range(4)]
@@ -212,11 +243,11 @@
     mix_ref[...] = dot(blocks_ref[...], product, TN).astype(BF16)
 
 
-def first_kernel(pair_ref, gate_ref, returned_ref, blocks_ref, grad_gate_ref, partial_ref):
+def first_kernel(pair_ref, gate_ref, returned_ref, own_ref, grad_gate_ref, partial_ref):
     conv = conv_rows(pair_ref)
     product = (conv * gate_ref[...]).astype(BF16)
     returned = returned_ref[...]
-    grad_gate = (dot(blocks_ref[...], returned) * conv).astype(BF16)
+    grad_gate = (dot(own_ref[...], returned) * conv).astype(BF16)
     grad_gate_ref[...] = dot(grad_gate, unit(), TN).astype(BF16)
     row, col = iotas(128, 128)
     grad = jnp.where(row // 64 == col // 4 % 2, dot(product, returned, NT), 0.0)
@@ -224,7 +255,7 @@
         (row // 8 == col % 64 // 4) & (row // 4 % 2 == col // 64) & (row % 4 == col % 4)
     )
     row, col = iotas(128, 64)
-    fold = ones_where(row // 8 * 4 + row % 4 == col)
+    fold = ones_where(source(row) * 4 + row % 4 == col)
     for part, piece in enumerate(split(grad)):
         partial_ref[part] = dot(order, dot(piece, fold).astype(BF16))
 
@@ -261,7 +292,7 @@
             second_ref[k, i : i + 1, :] = total[4 * i + k : 4 * i + k + 1, 64:96]
 
 
-def call(body, outs, scratch=(), flops=1 << 26, moved=1 << 19, held=None):
+def call(body, outs, scratch=(), flops=1 << 26, moved=1 << 19, held=None, limit=32 << 20):
     extra = {}
     if held is not None:
         extra["in_specs"] = [pl.BlockSpec(memory_space=held[0])] * held[1]
@@ -269,7 +300,7 @@
         body,
         out_shape=[jax.ShapeDtypeStruct(shape, kind) for shape, kind in outs],
         scratch_shapes=list(scratch),
-        compiler_params=pltpu.CompilerParams(vmem_limit_bytes=32 << 20),
+        compiler_params=pltpu.CompilerParams(vmem_limit_bytes=limit),
         cost_estimate=pl.CostEstimate(flops=flops, bytes_accessed=moved, transcendentals=0),
         **extra,
     )
@@ -279,6 +310,14 @@
     rows, cols = value.shape
     pieces = value.reshape(16, rows // 16, cols)
     return lax.all_to_all(pieces, axis, split_axis=0, concat_axis=0, tiled=True).reshape(rows, cols)
+
+
+def shift(value, y, zc):
+    pairs = []
+    for index in range(16):
+        z, there, core = (index // 8 + zc // 2) % 2, (index // 2 + y) % 4, (index + zc) % 2
+        pairs.append((index, z * 8 + there * 2 + core))
+    return lax.ppermute(value, "ch", pairs)
 
 
 def shards(signal, filter_raw, gate, d_out, w_first, w_second):
@@ -290,19 +329,24 @@
         pair_kernel,
         [double],
         [pltpu.VMEM((2, rows, width), BF16), pltpu.SemaphoreType.DMA((2,))],
-        held=(pltpu.HBM, 2),
+        held=(pl.ANY, 2),
+        limit=60 << 20,
     )(signal, filter_raw)[0]
     pair = exchange(pair, "seq")
-    second_back = call(back_kernel, [single])(d_out, w_second)[0]
-    gate, blocks = call(prepare_kernel, [((width, rows), F32), ((128, 128), BF16)])(gate, w_first)
-    returned = exchange(second_back, "ch")
+    quarter = ((width // 4, rows), BF16)
+    near, *others = call(back_kernel, [quarter] * 4)(d_out, w_second)
+    others = [shift(value, 0, zc) for zc, value in zip((1, 2, 3), others)]
+    near, *others = call(repack_kernel, [quarter] * 4)(near, *others)
+    others = [shift(value, y, 0) for y, value in zip((1, 2, 3), others)]
+    square = ((128, 128), BF16)
+    gate, blocks, own = call(prepare_kernel, [((width, rows), F32), square, square])(gate, w_first)
     conv, spectra = call(
         conv_kernel,
         [((4 * width, 128), F32), ((2, 512, 256), F32)],
         [pltpu.VMEM((2 * width * 4, 128), F32)],
         flops=1 << 30,
     )(pair, outer, back, twiddle, inner)
-    pair = call(gate_kernel, [double])(returned, blocks, gate, conv)[0]
+    pair, returned = call(gate_kernel, [double, single])(near, *others, own, gate, conv)
     pair = exchange(pair, "seq")
     mix = call(mix_kernel, [single])(pair, gate, blocks)[0]
     received = exchange(mix, "ch")
@@ -313,7 +357,7 @@
         flops=1 << 30,
     )(pair, spectra, outer, back, twiddle, inner)[0]
     grad_gate, partial = call(first_kernel, [slab, ((2, width, 64), F32)])(
-        pair, gate, returned, blocks
+        pair, gate, returned, own
     )
     sums = call(second_kernel, [((2 * width, rows + 128), BF16)])(received, d_out, partial, grads)[0]
     sums = exchange(sums, "seq")

time: 89.7 us -> 82.7 us (0.922)
  waiting for transfers between devices: 21.8 us -> 12.6 us
  starting transfers between devices: 22.4 us -> 25.7 us
  local copies, waits for them, and re-layouts: 2.44 us -> 0.04 us
  blocking collectives: 31.4 us -> 32.9 us
    all_to_all x3 -> x2, waiting for transfers between devices: 21.8 us -> 5.63 us  [exchange(): lax.all_to_all(pieces, axis, split_axis=0, concat_axis=0, tiled=True)]
    ppermute x0 -> x6, starting transfers between devices: none -> 10.9 us  [shift(): return lax.ppermute(value, 'ch', pairs)]
    all_to_all x3 -> x2, starting transfers between devices: 22.4 us -> 14.8 us  [exchange(): lax.all_to_all(pieces, axis, split_axis=0, concat_axis=0, tiled=True)]
    ppermute x0 -> x6, waiting for transfers between devices: none -> 6.98 us  [shift(): return lax.ppermute(value, 'ch', pairs)]
    unnamed x20 -> x16, local copies, waits for them, and re-layouts: 2.44 us -> 0.04 us
    all_to_all x2, blocking collectives: 31.4 us -> 32.9 us  [exchange(): lax.all_to_all(pieces, axis, split_axis=0, concat_axis=0, tiled=True)]
    pallas_call x4 -> x5, Pallas kernels: 2.5 us -> 1.89 us  [the longest x1 1.05 us: shards(): call(first_kernel, [slab, ((2, width, 64), F32)])(pair, gate, returned, own)]
  transfers between devices with their start and end apart: 3 -> 8, of which waited for: 3 -> 4; matrix products, arithmetic and copies ran while one was open for 0% -> 0% of each run, Pallas kernels for 7% -> 7%
where the time goes in v3:
time: 82.7 us; the launch traced here: 81.7 us
  blocking collectives  32.9 us (40%)
  starting transfers between devices  25.7 us (31%)
  waiting for transfers between devices  12.6 us (15%)
  Pallas kernels  9.68 us (12%)
    all_to_all x2, blocking collectives, exchange(): lax.all_to_all(pieces, axis, split_axis=0, concat_axis=0, tiled=True)  32.9 us
    all_to_all x2, starting transfers between devices, exchange(): lax.all_to_all(pieces, axis, split_axis=0, concat_axis=0, tiled=True)  14.8 us
    ppermute x6, starting transfers between devices, shift(): return lax.ppermute(value, 'ch', pairs)  10.9 us
    ppermute x6, waiting for transfers between devices, shift(): return lax.ppermute(value, 'ch', pairs)  6.98 us
    all_to_all x2, waiting for transfers between devices, exchange(): lax.all_to_all(pieces, axis, split_axis=0, concat_axis=0, tiled=True)  5.63 us
    pallas_call x1, Pallas kernels, shards(): call(adjoint_kernel, [double], [pltpu.VMEM((2 * width * 4, 128), F32), pl...  2.11 us
    pallas_call x1, Pallas kernels, shards(): call(pair_kernel, [double], [pltpu.VMEM((2, rows, width), BF16), pltpu.Se...  1.96 us
  transfers between devices with their start and end apart: 8, of which 4 were waited for; matrix products, arithmetic and copies ran while one was open for 0% of the time, Pallas kernels for 7%

profile of v3, /device:TPU:8, one launch (start us, length us, event | category | flops | bytes accessed | tf_op | source)
XLA Modules:
  0.0 81.7 jit_solution(12922823215567582041)
XLA Ops:
  0.6 2.0 %shard_map.140 = bf16[256,512]{1,0:T(8,128)(2,1)} custom-call(bf16[512,128]{1,0:T(8,128)(2,1)} %signal_hbm.1, bf16[512,128]{1,0:T(8,128)(2,1)} %filter_hbm.1), custom_call_target="tpu_custom_call" | custom-call | flops 67108864 | bytes 524288 | tf_op jit(solution)/shard_map/pallas_call | solution.py:328
  2.6 0.0 copy-start
  2.6 0.0 copy-start.2
  2.6 8.6 %all-to-all-start = ((bf16[16,16,512]{2,1,0:T(8,128)(2,1)}), bf16[16,16,512]{2,1,0:T(8,128)(2,1)S(1)}, u32[]{:S(2)}, u32[]{:S(2)}) async-start(bf16[16,16,512]{2,1,0:T(8,128)(2,1)} %bitcast.16), calls=%async_computation | async-start | bytes 524288 | tf_op jit(solution)/shard_map/all_to_all | solution.py:312
  11.2 0.0 copy-done
  11.3 0.0 copy-done.2
  11.3 0.0 copy-start.1
  11.3 0.0 copy-start.3
  11.3 0.4 shard_map.137
  11.7 0.0 copy-start.4
  11.7 0.1 collective-permute-start
  11.8 4.6 %collective-permute-start.1 = (bf16[32,512]{1,0:T(8,128)(2,1)S(1)}, bf16[32,512]{1,0:T(8,128)(2,1)S(1)}, u32[]{:S(2)}, u32[]{:S(2)}) collective-permute-start(bf16[32,512]{1,0:T(8,128)(2,1)S(1)} %get-tuple-element.28), channel_id=1, source_target_pairs={{0,8},{1,9},{2,10},{3,11},{4,12},{5,13},{6,14},{7,15},{8,0},{9,1},... | collective-permute-start | bytes 98312 | tf_op jit(solution)/shard_map/ppermute | solution.py:320
  16.4 1.2 %collective-permute-start.2 = (bf16[32,512]{1,0:T(8,128)(2,1)S(1)}, bf16[32,512]{1,0:T(8,128)(2,1)S(1)}, u32[]{:S(2)}, u32[]{:S(2)}) collective-permute-start(bf16[32,512]{1,0:T(8,128)(2,1)S(1)} %get-tuple-element.29), channel_id=1, source_target_pairs={{0,9},{1,8},{2,11},{3,10},{4,13},{5,12},{6,15},{7,14},{8,1},{9,0},... | collective-permute-start | bytes 98312 | tf_op jit(solution)/shard_map/ppermute | solution.py:320
  17.6 0.0 copy-done.1
  17.6 0.0 copy-done.3
  17.6 0.2 shard_map.139
  17.8 0.0 collective-permute-done.refs_1_
  17.9 3.3 %collective-permute-done.1.refs_2_ = bf16[32,512]{1,0:T(8,128)(2,1)S(1)} collective-permute-done((bf16[32,512]{1,0:T(8,128)(2,1)S(1)}, bf16[32,512]{1,0:T(8,128)(2,1)S(1)}, u32[]{:S(2)}, u32[]{:S(2)}) %collective-permute-start.1) | collective-permute-done | bytes 32800 | tf_op jit(solution)/shard_map/ppermute | solution.py:320
  21.2 3.2 %collective-permute-done.2.refs_3_ = bf16[32,512]{1,0:T(8,128)(2,1)S(1)} collective-permute-done((bf16[32,512]{1,0:T(8,128)(2,1)S(1)}, bf16[32,512]{1,0:T(8,128)(2,1)S(1)}, u32[]{:S(2)}, u32[]{:S(2)}) %collective-permute-start.2) | collective-permute-done | bytes 32800 | tf_op jit(solution)/shard_map/ppermute | solution.py:320
  24.3 0.0 copy-start.5
  24.3 0.0 copy-start.6
  24.3 0.0 copy-start.7
  24.4 1.7 %collective-permute-start.3 = (bf16[32,512]{1,0:T(8,128)(2,1)S(1)}, bf16[32,512]{1,0:T(8,128)(2,1)S(1)}, u32[]{:S(2)}, u32[]{:S(2)}) collective-permute-start(bf16[32,512]{1,0:T(8,128)(2,1)S(1)} %get-tuple-element.31), channel_id=1, source_target_pairs={{0,2},{1,3},{2,4},{3,5},{4,6},{5,7},{6,0},{7,1},{8,10},{9,11},{10,... | collective-permute-start | bytes 98312 | tf_op jit(solution)/shard_map/ppermute | solution.py:320
  26.0 0.9 %collective-permute-start.4 = (bf16[32,512]{1,0:T(8,128)(2,1)S(1)}, bf16[32,512]{1,0:T(8,128)(2,1)S(1)}, u32[]{:S(2)}, u32[]{:S(2)}) collective-permute-start(bf16[32,512]{1,0:T(8,128)(2,1)S(1)} %get-tuple-element.32), channel_id=1, source_target_pairs={{0,4},{1,5},{2,6},{3,7},{4,0},{5,1},{6,2},{7,3},{8,12},{9,13},{10,... | collective-permute-start | bytes 98312 | tf_op jit(solution)/shard_map/ppermute | solution.py:320
  26.9 2.4 %collective-permute-start.5 = (bf16[32,512]{1,0:T(8,128)(2,1)S(1)}, bf16[32,512]{1,0:T(8,128)(2,1)S(1)}, u32[]{:S(2)}, u32[]{:S(2)}) collective-permute-start(bf16[32,512]{1,0:T(8,128)(2,1)S(1)} %get-tuple-element.33), channel_id=1, source_target_pairs={{0,6},{1,7},{2,0},{3,1},{4,2},{5,3},{6,4},{7,5},{8,14},{9,15},{10,... | collective-permute-start | bytes 98312 | tf_op jit(solution)/shard_map/ppermute | solution.py:320
  29.4 0.0 all-to-all-done
  29.4 0.0 copy-done.4
  29.4 0.0 copy-done.5
  29.4 0.0 copy-done.6
  29.4 0.0 copy-done.7
  29.4 1.5 %shard_map.141 = (f32[512,128]{1,0:T(8,128)S(1)}, f32[2,512,256]{2,1,0:T(8,128)S(1)}) custom-call(bf16[256,512]{1,0:T(8,128)(2,1)S(1)} %bitcast.14, bf16[128,128]{1,0:T(8,128)(2,1)S(1)} %copy-done.7, bf16[2,64,128]{2,1,0:T(8,128)(2,1)S(1)} %copy-done.6, f32[64,256]{1,0:T(8,128)S(1)} %copy-done.5, bf16[2,256,256]{2,1,0:T(8,128)(2,1)S(1)} %copy-done.4), custom_call_target="tpu_custom_call" | custom-call | flops 1073741824 | bytes 524288 | tf_op jit(solution)/shard_map/pallas_call | solution.py:343
  30.9 0.0 collective-permute-done.3.first_ref
  30.9 0.5 collective-permute-done.4.second_ref
  31.4 0.0 collective-permute-done.5.third_ref
  31.4 0.2 shard_map.142
  31.6 16.6 %all_to_all.20 = bf16[16,16,512]{2,1,0:T(8,128)(2,1)S(1)} all-to-all(bf16[16,16,512]{2,1,0:T(8,128)(2,1)S(1)} %bitcast.15), channel_id=1, replica_groups=mesh['seq'=16,'ch'=16] {'seq'}, dimensions={0} | all-to-all | bytes 524288 | tf_op jit(solution)/shard_map/all_to_all | solution.py:312
  48.2 0.9 %shard_map.143 = bf16[128,512]{1,0:T(8,128)(2,1)} custom-call(bf16[256,512]{1,0:T(8,128)(2,1)S(1)} %bitcast.8, f32[128,512]{1,0:T(8,128)S(1)} %get-tuple-element.35.gate_ref, bf16[128,128]{1,0:T(8,128)(2,1)S(1)} %get-tuple-element.38.blocks_ref), custom_call_target="tpu_custom_call" | custom-call | flops 67108864 | bytes 524288 | tf_op jit(solution)/shard_map/pallas_call | solution.py:351
  49.1 6.2 %all-to-all-start.2 = ((bf16[16,8,512]{2,1,0:T(8,128)(2,1)}), bf16[16,8,512]{2,1,0:T(8,128)(2,1)S(1)}, u32[]{:S(2)}, u32[]{:S(2)}) async-start(bf16[16,8,512]{2,1,0:T(8,128)(2,1)} %bitcast.4), calls=%async_computation.2 | async-start | bytes 262144 | tf_op jit(solution)/shard_map/all_to_all | solution.py:312
  55.3 1.1 %shard_map.144 = (bf16[512,128]{1,0:T(8,128)(2,1)}, f32[2,128,64]{2,1,0:T(8,128)S(1)}) custom-call(bf16[256,512]{1,0:T(8,128)(2,1)S(1)} %bitcast.9, f32[128,512]{1,0:T(8,128)S(1)} %get-tuple-element.35.gate_ref, bf16[128,512]{1,0:T(8,128)(2,1)S(1)} %get-tuple-element.39.returned_ref, bf16[128,128]{1,0:T(8,128)(2,1)S(1)} %get-tuple-element.34.own_ref), custom_call_target="tpu_custom_call" | custom-call | flops 67108864 | bytes 524288 | tf_op jit(solution)/shard_map/pallas_call | solution.py:359
  56.3 2.1 %shard_map.145.grads_ref = bf16[256,512]{1,0:T(8,128)(2,1)S(1)} custom-call(bf16[256,512]{1,0:T(8,128)(2,1)S(1)} %bitcast.10, f32[2,512,256]{2,1,0:T(8,128)S(1)} %get-tuple-element.41.spectra_ref, bf16[128,128]{1,0:T(8,128)(2,1)S(1)} %copy-done.7, bf16[2,64,128]{2,1,0:T(8,128)(2,1)S(1)} %copy-done.6, f32[64,256]{1,0:T(8,128)S(1)} %copy-done.5, ...), custom_call_target="tpu_custom_call" | custom-call | flops 1073741824 | bytes 524288 | tf_op jit(solution)/shard_map/pallas_call | solution.py:353
  58.4 5.6 %all-to-all-done.2 = bf16[16,8,512]{2,1,0:T(8,128)(2,1)S(1)} async-done(((bf16[16,8,512]{2,1,0:T(8,128)(2,1)}), bf16[16,8,512]{2,1,0:T(8,128)(2,1)S(1)}, u32[]{:S(2)}, u32[]{:S(2)}) %all-to-all-start.2) | async-done | bytes 131104 | tf_op jit(solution)/shard_map/all_to_all | solution.py:312
  64.0 0.4 shard_map.146
  64.4 16.4 %all_to_all.21 = bf16[16,16,640]{2,1,0:T(8,128)(2,1)S(1)} all-to-all(bf16[16,16,640]{2,1,0:T(8,128)(2,1)S(1)} %bitcast.12), channel_id=1, replica_groups=mesh['seq'=16,'ch'=16] {'seq'}, dimensions={0} | all-to-all | bytes 655360 | tf_op jit(solution)/shard_map/all_to_all | solution.py:312
  80.8 1.0 %shard_map.147 = (bf16[512,128]{1,0:T(8,128)(2,1)}, bf16[512,128]{1,0:T(8,128)(2,1)}, f32[2,4,64]{2,1,0:T(4,128)}, f32[4,2,32]{2,1,0:T(2,128)}) custom-call(bf16[256,640]{1,0:T(8,128)(2,1)S(1)} %bitcast.11), custom_call_target="tpu_custom_call" | custom-call | flops 67108864 | bytes 524288 | tf_op jit(solution)/shard_map/pallas_call | solution.py:364
  (1 shorter events, 0.0 us)
Async XLA Ops:
  2.6 8.6 %copy-start = (bf16[512,128]{1,0:T(8,128)(2,1)S(1)}, bf16[512,128]{1,0:T(8,128)(2,1)}, u32[]{:S(2)}) copy-start(bf16[512,128]{1,0:T(8,128)(2,1)} %d_out_ref.3) | copy-start | bytes 393220
  2.6 8.6 %copy-start.2 = (bf16[4,32,32]{2,1,0:T(8,128)(2,1)S(1)}, bf16[4,32,32]{2,1,0:T(8,128)(2,1)}, u32[]{:S(2)}) copy-start(bf16[4,32,32]{2,1,0:T(8,128)(2,1)} %w_second_ref.1) | copy-start | bytes 24580
  2.6 26.7 %all-to-all-start = ((bf16[16,16,512]{2,1,0:T(8,128)(2,1)}), bf16[16,16,512]{2,1,0:T(8,128)(2,1)S(1)}, u32[]{:S(2)}, u32[]{:S(2)}) async-start(bf16[16,16,512]{2,1,0:T(8,128)(2,1)} %bitcast.16), calls=%async_computation | async-start | bytes 524288 | tf_op jit(solution)/shard_map/all_to_all | solution.py:312
  11.3 6.3 %copy-start.1 = (bf16[512,128]{1,0:T(8,128)(2,1)S(1)}, bf16[512,128]{1,0:T(8,128)(2,1)}, u32[]{:S(2)}) copy-start(bf16[512,128]{1,0:T(8,128)(2,1)} %gate_ref.1) | copy-start | bytes 393220
  11.3 6.3 %copy-start.3 = (bf16[2,64,64]{2,1,0:T(8,128)(2,1)S(1)}, bf16[2,64,64]{2,1,0:T(8,128)(2,1)}, u32[]{:S(2)}) copy-start(bf16[2,64,64]{2,1,0:T(8,128)(2,1)} %w_first_ref.1) | copy-start | bytes 49156
  11.7 17.6 %copy-start.4 = (bf16[2,256,256]{2,1,0:T(8,128)(2,1)S(1)}, bf16[2,256,256]{2,1,0:T(8,128)(2,1)}, u32[]{:S(2)}) copy-start(bf16[2,256,256]{2,1,0:T(8,128)(2,1)} %constant.11.clone.inner_ref) | copy-start | bytes 786436
  11.7 6.1 %collective-permute-start = (bf16[32,512]{1,0:T(8,128)(2,1)S(1)}, bf16[32,512]{1,0:T(8,128)(2,1)S(1)}, u32[]{:S(2)}, u32[]{:S(2)}) collective-permute-start(bf16[32,512]{1,0:T(8,128)(2,1)S(1)} %get-tuple-element.27), channel_id=1, source_target_pairs={{0,1},{1,0},{2,3},{3,2},{4,5},{5,4},{6,7},{7,6},{8,9},{9,8},{10,11... | collective-permute-start | bytes 98312 | tf_op jit(solution)/shard_map/ppermute | solution.py:320
  11.8 9.3 %collective-permute-start.1 = (bf16[32,512]{1,0:T(8,128)(2,1)S(1)}, bf16[32,512]{1,0:T(8,128)(2,1)S(1)}, u32[]{:S(2)}, u32[]{:S(2)}) collective-permute-start(bf16[32,512]{1,0:T(8,128)(2,1)S(1)} %get-tuple-element.28), channel_id=1, source_target_pairs={{0,8},{1,9},{2,10},{3,11},{4,12},{5,13},{6,14},{7,15},{8,0},{9,1},... | collective-permute-start | bytes 98312 | tf_op jit(solution)/shard_map/ppermute | solution.py:320
  16.4 7.9 %collective-permute-start.2 = (bf16[32,512]{1,0:T(8,128)(2,1)S(1)}, bf16[32,512]{1,0:T(8,128)(2,1)S(1)}, u32[]{:S(2)}, u32[]{:S(2)}) collective-permute-start(bf16[32,512]{1,0:T(8,128)(2,1)S(1)} %get-tuple-element.29), channel_id=1, source_target_pairs={{0,9},{1,8},{2,11},{3,10},{4,13},{5,12},{6,15},{7,14},{8,1},{9,0},... | collective-permute-start | bytes 98312 | tf_op jit(solution)/shard_map/ppermute | solution.py:320
  24.3 5.0 %copy-start.5 = (f32[64,256]{1,0:T(8,128)S(1)}, f32[64,256]{1,0:T(8,128)}, u32[]{:S(2)}) copy-start(f32[64,256]{1,0:T(8,128)} %constant.10.clone.twiddle_ref) | copy-start | bytes 196612
  24.3 5.0 %copy-start.6 = (bf16[2,64,128]{2,1,0:T(8,128)(2,1)S(1)}, bf16[2,64,128]{2,1,0:T(8,128)(2,1)}, u32[]{:S(2)}) copy-start(bf16[2,64,128]{2,1,0:T(8,128)(2,1)} %constant.9.clone.back_ref) | copy-start | bytes 98308
  24.3 5.0 %copy-start.7 = (bf16[128,128]{1,0:T(8,128)(2,1)S(1)}, bf16[128,128]{1,0:T(8,128)(2,1)}, u32[]{:S(2)}) copy-start(bf16[128,128]{1,0:T(8,128)(2,1)} %constant.8.clone.outer_ref) | copy-start | bytes 98308
  24.4 6.6 %collective-permute-start.3 = (bf16[32,512]{1,0:T(8,128)(2,1)S(1)}, bf16[32,512]{1,0:T(8,128)(2,1)S(1)}, u32[]{:S(2)}, u32[]{:S(2)}) collective-permute-start(bf16[32,512]{1,0:T(8,128)(2,1)S(1)} %get-tuple-element.31), channel_id=1, source_target_pairs={{0,2},{1,3},{2,4},{3,5},{4,6},{5,7},{6,0},{7,1},{8,10},{9,11},{10,... | collective-permute-start | bytes 98312 | tf_op jit(solution)/shard_map/ppermute | solution.py:320
  26.0 5.4 %collective-permute-start.4 = (bf16[32,512]{1,0:T(8,128)(2,1)S(1)}, bf16[32,512]{1,0:T(8,128)(2,1)S(1)}, u32[]{:S(2)}, u32[]{:S(2)}) collective-permute-start(bf16[32,512]{1,0:T(8,128)(2,1)S(1)} %get-tuple-element.32), channel_id=1, source_target_pairs={{0,4},{1,5},{2,6},{3,7},{4,0},{5,1},{6,2},{7,3},{8,12},{9,13},{10,... | collective-permute-start | bytes 98312 | tf_op jit(solution)/shard_map/ppermute | solution.py:320
  26.9 4.5 %collective-permute-start.5 = (bf16[32,512]{1,0:T(8,128)(2,1)S(1)}, bf16[32,512]{1,0:T(8,128)(2,1)S(1)}, u32[]{:S(2)}, u32[]{:S(2)}) collective-permute-start(bf16[32,512]{1,0:T(8,128)(2,1)S(1)} %get-tuple-element.33), channel_id=1, source_target_pairs={{0,6},{1,7},{2,0},{3,1},{4,2},{5,3},{6,4},{7,5},{8,14},{9,15},{10,... | collective-permute-start | bytes 98312 | tf_op jit(solution)/shard_map/ppermute | solution.py:320
  49.1 15.0 %all-to-all-start.2 = ((bf16[16,8,512]{2,1,0:T(8,128)(2,1)}), bf16[16,8,512]{2,1,0:T(8,128)(2,1)S(1)}, u32[]{:S(2)}, u32[]{:S(2)}) async-start(bf16[16,8,512]{2,1,0:T(8,128)(2,1)} %bitcast.4), calls=%async_computation.2 | async-start | bytes 262144 | tf_op jit(solution)/shard_map/all_to_all | solution.py:312

commit v4 on v3

--- a/solution.py
+++ b/solution.py
@@ -75,18 +75,9 @@
     return ones_where(row == col)
 
 
-def pair_kernel(signal_hbm, filter_hbm, pair_ref, both_ref, sems):
-    copies = [
-        pltpu.make_async_copy(source, both_ref.at[field], sems.at[field])
-        for field, source in enumerate((signal_hbm, filter_hbm))
-    ]
-    for copy in copies:
-        copy.start()
-    order = pair_order()
-    for copy in copies:
-        copy.wait()
-    both = jnp.concatenate([both_ref[0], both_ref[1]], axis=1)
-    pair_ref[...] = dot(order, both, NT).astype(BF16)
+def pair_kernel(signal_ref, filter_ref, pair_ref):
+    both = jnp.concatenate([signal_ref[...], filter_ref[...]], axis=1)
+    pair_ref[...] = dot(pair_order(), both, NT).astype(BF16)
 
 
 def place():
@@ -102,7 +93,15 @@
     return z * 8 + y * 2 + core
 
 
-def back_kernel(d_out_ref, w_second_ref, near_ref, core_ref, far_ref, cross_ref):
+def back_kernel(d_out_hbm, w_second_hbm, *refs):
+    outs, (d_out_ref, w_second_ref, sems) = refs[:4], refs[4:]
+    copies = [
+        pltpu.make_async_copy(w_second_hbm, w_second_ref, sems.at[0]),
+        pltpu.make_async_copy(d_out_hbm, d_out_ref, sems.at[1]),
+    ]
+    for copy in copies:
+        copy.start()
+    copies[0].wait()
     flat = w_second_ref[...].reshape(128, 32)
     row, col = iotas(32, 128)
     spread = dot(flat, ones_where(row == col % 32))
@@ -111,8 +110,9 @@
     block = 2 * partner(row // 8 % 4, row // 32, 1) + row // 4 % 2
     order = ones_where((block == col % 32) & (row % 4 == col // 32))
     weights = dot(order, spread).astype(BF16)
+    copies[1].wait()
     result = dot(weights, d_out_ref[...], NT).astype(BF16)
-    for zc, ref in enumerate((near_ref, core_ref, far_ref, cross_ref)):
+    for zc, ref in enumerate(outs):
         ref[...] = result[32 * zc : 32 * zc + 32, :]
 
 
@@ -137,17 +137,21 @@
     gate_out_ref[...] = dot(unit(), gate_ref[...], NT)
 
 
-def gate_kernel(near_ref, first_ref, second_ref, third_ref, own_ref, gate_ref, conv_ref, pair_ref, returned_ref):
-    pieces = [ref[...] for ref in (near_ref, first_ref, second_ref, third_ref)]
-    returned = jnp.concatenate(pieces, axis=0)
+def slab(slot_x, slot_z, step):
+    index = lax.axis_index("seq")
+    return (index // 4 + 4 + step * slot_x) % 4 * 4 + (index % 4 + 4 + step * slot_z) % 4
+
+
+def gate_kernel(*refs):
+    pieces, (own_ref, gate_ref), outs, returned_ref = refs[:4], refs[4:6], refs[6:10], refs[10]
+    returned = jnp.concatenate([ref[...] for ref in pieces], axis=0)
     returned_ref[...] = returned
-    incoming = dot(own_ref[...], returned) * gate_ref[...]
-    rows = []
-    for p in range(16):
-        pieces = [conv_ref[128 * th + 8 * p : 128 * th + 8 * p + 8, :] for th in range(4)]
-        rows.append(jnp.concatenate(pieces, axis=1))
-        rows.append(incoming[8 * p : 8 * p + 8, :])
-    pair_ref[...] = jnp.concatenate(rows, axis=0).astype(BF16)
+    incoming = (dot(own_ref[...], returned) * gate_ref[...]).astype(BF16)
+    row, col = iotas(128, 128)
+    order = ones_where(slab(row // 32, row // 8 % 4, 1) * 8 + row % 8 == col)
+    result = dot(order, incoming).astype(BF16)
+    for x, ref in enumerate(outs):
+        ref[...] = result[32 * x : 32 * x + 32, :]
 
 
 def split(value):
@@ -177,8 +181,8 @@
     return jnp.concatenate(pieces, axis=1)
 
 
-def transform(values, outer_ref, twiddle_ref, inner_ref):
-    stage = dot(outer_ref[...], jnp.concatenate([values, values], axis=0))
+def transform(values, outer, twiddle_ref, inner_ref):
+    stage = dot(outer, jnp.concatenate([values, values], axis=0))
     cosine, sine = twiddle_ref[:, 0:128], twiddle_ref[:, 128:256]
     rows = []
     for c in range(8):
@@ -206,23 +210,29 @@
     return dot(back_ref[0], high) + dot(back_ref[0], low) + dot(back_ref[1], high)
 
 
-def conv_kernel(pair_ref, outer_ref, back_ref, twiddle_ref, inner_ref, conv_ref, spectra_ref, wide_ref):
+def conv_kernel(
+    pair_ref, outer_ref, back_ref, twiddle_ref, inner_ref, conv_ref, spectra_ref, wide_ref, out_ref
+):
     unroll(wide_ref, pair_ref[...])
-    signal = transform(by_channel(wide_ref, 0, 16), outer_ref, twiddle_ref, inner_ref)
-    kernel = transform(by_channel(wide_ref, 8, 16), outer_ref, twiddle_ref, inner_ref)
+    signal = transform(by_channel(wide_ref, 0, 16), outer_ref[...], twiddle_ref, inner_ref)
+    kernel = transform(by_channel(wide_ref, 8, 16), outer_ref[...], twiddle_ref, inner_ref)
     spectra_ref[0] = signal
     spectra_ref[1] = kernel
     sr, si = signal[:, 0:128], signal[:, 128:256]
     kr, ki = kernel[:, 0:128], kernel[:, 128:256]
     result = restore(sr * kr - si * ki, sr * ki + si * kr, back_ref, twiddle_ref, inner_ref)
-    by_slab(conv_ref, result, 0, 8)
-
-
-def adjoint_kernel(
-    pair_ref, spectra_ref, outer_ref, back_ref, twiddle_ref, inner_ref, grads_ref, wide_ref, out_ref
-):
-    unroll(wide_ref, pair_ref[...])
-    spectrum = transform(by_channel(wide_ref, 8, 16), outer_ref, twiddle_ref, inner_ref)
+    by_slab(out_ref, result, 0, 8)
+    conv_ref[...] = enroll(out_ref)
+
+
+def adjoint_kernel(*refs):
+    pieces, (spectra_ref, outer_ref, back_ref, twiddle_ref, inner_ref) = refs[:4], refs[4:9]
+    grads_ref, wide_ref, out_ref = refs[9:]
+    unroll(wide_ref, jnp.concatenate([ref[...] for ref in pieces], axis=0))
+    row, col = iotas(128, 128)
+    order = ones_where(row == col // 16 * 16 + slab(col % 4, col // 4 % 4, -1))
+    outer = dot(outer_ref[...], order).astype(BF16)
+    spectrum = transform(by_channel(wide_ref, 0, 8), outer, twiddle_ref, inner_ref)
     gr, gi = spectrum[:, 0:128], spectrum[:, 128:256]
     for field in range(2):
         real, imag = spectra_ref[1 - field, :, 0:128], spectra_ref[1 - field, :, 128:256]
@@ -233,18 +243,13 @@
     grads_ref[...] = enroll(out_ref)
 
 
-def conv_rows(pair_ref):
-    wide = pair_ref[...].astype(F32)
-    return jnp.concatenate([wide[16 * p : 16 * p + 8, :] for p in range(16)], axis=0)
-
-
-def mix_kernel(pair_ref, gate_ref, blocks_ref, mix_ref):
-    product = (conv_rows(pair_ref) * gate_ref[...]).astype(BF16)
+def mix_kernel(conv_ref, gate_ref, blocks_ref, mix_ref):
+    product = (conv_ref[...].astype(F32) * gate_ref[...]).astype(BF16)
     mix_ref[...] = dot(blocks_ref[...], product, TN).astype(BF16)
 
 
-def first_kernel(pair_ref, gate_ref, returned_ref, own_ref, grad_gate_ref, partial_ref):
-    conv = conv_rows(pair_ref)
+def first_kernel(conv_ref, gate_ref, returned_ref, own_ref, grad_gate_ref, partial_ref):
+    conv = conv_ref[...].astype(F32)
     product = (conv * gate_ref[...]).astype(BF16)
     returned = returned_ref[...]
     grad_gate = (dot(own_ref[...], returned) * conv).astype(BF16)
@@ -320,49 +325,66 @@
     return lax.ppermute(value, "ch", pairs)
 
 
+def slide(value, x, z):
+    pairs = [(index, (index // 4 + x) % 4 * 4 + (index + z) % 4) for index in range(16)]
+    return lax.ppermute(value, "seq", pairs)
+
+
+def after(value, *done):
+    return lax.optimization_barrier((value, *done))[0]
+
+
 def shards(signal, filter_raw, gate, d_out, w_first, w_second):
     rows, width = signal.shape
     outer, back, twiddle, inner = (jnp.asarray(t) for t in tables(lax.axis_size("seq"), rows))
     single, double = ((width, rows), BF16), ((2 * width, rows), BF16)
-    slab = ((rows, width), BF16)
-    pair = call(
-        pair_kernel,
-        [double],
-        [pltpu.VMEM((2, rows, width), BF16), pltpu.SemaphoreType.DMA((2,))],
+    slabs = ((rows, width), BF16)
+    quarter, square = ((width // 4, rows), BF16), ((128, 128), BF16)
+    near, *others = call(
+        back_kernel,
+        [quarter] * 4,
+        [
+            pltpu.VMEM(d_out.shape, BF16),
+            pltpu.VMEM(w_second.shape, BF16),
+            pltpu.SemaphoreType.DMA((2,)),
+        ],
         held=(pl.ANY, 2),
         limit=60 << 20,
-    )(signal, filter_raw)[0]
+    )(d_out, w_second)
+    others = [shift(value, 0, zc) for zc, value in zip((1, 2, 3), others)]
+    pair = call(pair_kernel, [double])(signal, filter_raw)[0]
     pair = exchange(pair, "seq")
-    quarter = ((width // 4, rows), BF16)
-    near, *others = call(back_kernel, [quarter] * 4)(d_out, w_second)
-    others = [shift(value, 0, zc) for zc, value in zip((1, 2, 3), others)]
-    near, *others = call(repack_kernel, [quarter] * 4)(near, *others)
+    near, *others = call(repack_kernel, [quarter] * 4, flops=1 << 35)(near, *others)
+    pair = after(pair, near, *others)
     others = [shift(value, y, 0) for y, value in zip((1, 2, 3), others)]
-    square = ((128, 128), BF16)
     gate, blocks, own = call(prepare_kernel, [((width, rows), F32), square, square])(gate, w_first)
     conv, spectra = call(
         conv_kernel,
-        [((4 * width, 128), F32), ((2, 512, 256), F32)],
-        [pltpu.VMEM((2 * width * 4, 128), F32)],
+        [single, ((2, 512, 256), F32)],
+        [pltpu.VMEM((2 * width * 4, 128), F32), pltpu.VMEM((width * 4, 128), F32)],
         flops=1 << 30,
     )(pair, outer, back, twiddle, inner)
-    pair, returned = call(gate_kernel, [double, single])(near, *others, own, gate, conv)
-    pair = exchange(pair, "seq")
-    mix = call(mix_kernel, [single])(pair, gate, blocks)[0]
-    received = exchange(mix, "ch")
+    conv = exchange(after(conv, *others), "seq")
+    near, *others, returned = call(gate_kernel, [quarter] * 4 + [single])(near, *others, own, gate)
+    conv = after(conv, near, *others)
+    others = [slide(value, x, 0) for x, value in zip((1, 2, 3), others)]
+    mix = call(mix_kernel, [single])(conv, gate, blocks)[0]
+    near, *others = call(repack_kernel, [quarter] * 4)(near, *others)
+    received = exchange(after(mix, near, *others), "ch")
+    others = [slide(value, 0, z) for z, value in zip((1, 2, 3), others)]
     grads = call(
         adjoint_kernel,
         [double],
-        [pltpu.VMEM((2 * width * 4, 128), F32), pltpu.VMEM((2 * width * 4, 128), F32)],
+        [pltpu.VMEM((width * 4, 128), F32), pltpu.VMEM((2 * width * 4, 128), F32)],
         flops=1 << 30,
-    )(pair, spectra, outer, back, twiddle, inner)[0]
-    grad_gate, partial = call(first_kernel, [slab, ((2, width, 64), F32)])(
-        pair, gate, returned, own
+    )(near, *others, spectra, outer, back, twiddle, inner)[0]
+    grad_gate, partial = call(first_kernel, [slabs, ((2, width, 64), F32)])(
+        conv, gate, returned, own
     )
     sums = call(second_kernel, [((2 * width, rows + 128), BF16)])(received, d_out, partial, grads)[0]
     sums = exchange(sums, "seq")
     grad_signal, grad_filter, grad_first, grad_second = call(
-        exit_kernel, [slab, slab, ((2, 4, 64), F32), ((4, 2, 32), F32)]
+        exit_kernel, [slabs, slabs, ((2, 4, 64), F32), ((4, 2, 32), F32)]
     )(sums)
     return (grad_signal, grad_filter, grad_gate, grad_first, grad_second)
 

time: 82.7 us -> 86.6 us (1.047)
  starting transfers between devices: 25.7 us -> 43.4 us
  blocking collectives: 32.9 us -> 16.9 us
  Pallas kernels: 9.68 us -> 11.1 us
  local copies, waits for them, and re-layouts: 0.04 us -> 0.96 us
    all_to_all x2 -> x1, blocking collectives: 32.9 us -> 16.9 us  [exchange(): lax.all_to_all(pieces, axis, split_axis=0, concat_axis=0, tiled=True)]
    ppermute x0 -> x6, starting transfers between devices: none -> 11.4 us  [slide(): return lax.ppermute(value, 'seq', pairs)]
    ppermute x6, waiting for transfers between devices: 6.98 us -> 0.02 us  [shift(): return lax.ppermute(value, 'ch', pairs)]
    ppermute x0 -> x6, waiting for transfers between devices: none -> 6.67 us  [slide(): return lax.ppermute(value, 'seq', pairs)]
    all_to_all x2 -> x3, starting transfers between devices: 14.8 us -> 19.6 us  [exchange(): lax.all_to_all(pieces, axis, split_axis=0, concat_axis=0, tiled=True)]
    ppermute x6, starting transfers between devices: 10.9 us -> 12.4 us  [shift(): return lax.ppermute(value, 'ch', pairs)]
    pallas_call x8 -> x9, Pallas kernels: 9.08 us -> 10.5 us  [the longest x1 2.2 us: shards(): call(conv_kernel, [single, ((2, 512, 256), F32)], [pltpu.VMEM((2 * width...]
    unnamed x16 -> x20, local copies, waits for them, and re-layouts: 0.04 us -> 0.96 us
  transfers between devices with their start and end apart: 8 -> 15, of which waited for: 4 -> 5; matrix products, arithmetic and copies ran while one was open for 0% -> 0% of each run, Pallas kernels for 7% -> 8%
where the time goes in v4:
time: 86.6 us; the launch traced here: 86.2 us
  starting transfers between devices  43.4 us (50%)
  blocking collectives  16.9 us (20%)
  waiting for transfers between devices  13 us (15%)
  Pallas kernels  11.1 us (13%)
  local copies, waits for them, and re-layouts  0.96 us (1%)
    all_to_all x3, starting transfers between devices, exchange(): lax.all_to_all(pieces, axis, split_axis=0, concat_axis=0, tiled=True)  19.6 us
    all_to_all x1, blocking collectives, exchange(): lax.all_to_all(pieces, axis, split_axis=0, concat_axis=0, tiled=True)  16.9 us
    ppermute x6, starting transfers between devices, shift(): return lax.ppermute(value, 'ch', pairs)  12.4 us
    ppermute x6, starting transfers between devices, slide(): return lax.ppermute(value, 'seq', pairs)  11.4 us
    ppermute x6, waiting for transfers between devices, slide(): return lax.ppermute(value, 'seq', pairs)  6.67 us
    all_to_all x3, waiting for transfers between devices, exchange(): lax.all_to_all(pieces, axis, split_axis=0, concat_axis=0, tiled=True)  6.28 us
    pallas_call x1, Pallas kernels, shards(): call(conv_kernel, [single, ((2, 512, 256), F32)], [pltpu.VMEM((2 * width...  2.2 us
    pallas_call x1, Pallas kernels, shards(): call(adjoint_kernel, [double], [pltpu.VMEM((width * 4, 128), F32), pltpu....  2.17 us
  transfers between devices with their start and end apart: 15, of which 5 were waited for; matrix products, arithmetic and copies ran while one was open for 0% of the time, Pallas kernels for 8%

profile of v4, /device:TPU:8, one launch (start us, length us, event | category | flops | bytes accessed | tf_op | source)
XLA Modules:
  0.0 86.2 jit_solution(8210827334785213582)
XLA Ops:
  0.6 0.0 copy-start.1
  0.6 1.9 %shard_map.138 = (bf16[32,512]{1,0:T(8,128)(2,1)}, bf16[32,512]{1,0:T(8,128)(2,1)}, bf16[32,512]{1,0:T(8,128)(2,1)}, bf16[32,512]{1,0:T(8,128)(2,1)}) custom-call(bf16[512,128]{1,0:T(8,128)(2,1)} %d_out_ref.1, bf16[4,32,32]{2,1,0:T(8,128)(2,1)} %w_second_hbm.1), custom_call_target="tpu_custom_call" | custom-call | flops 67108864 | bytes 524288 | tf_op jit(solution)/shard_map/pallas_call | solution.py:343
  2.6 0.1 collective-permute-start
  2.7 7.3 %collective-permute-start.1 = (bf16[32,512]{1,0:T(8,128)(2,1)}, bf16[32,512]{1,0:T(8,128)(2,1)S(1)}, u32[]{:S(2)}, u32[]{:S(2)}) collective-permute-start(bf16[32,512]{1,0:T(8,128)(2,1)} %get-tuple-element.39), channel_id=1, source_target_pairs={{0,8},{1,9},{2,10},{3,11},{4,12},{5,13},{6,14},{7,15},{8,0},{9,1},... | collective-permute-start | bytes 98312 | tf_op jit(solution)/shard_map/ppermute | solution.py:325
  10.0 0.1 collective-permute-start.2
  10.0 0.0 copy-done.1
  10.0 0.0 copy-start.2
  10.0 0.9 %copy-done.2 = bf16[512,128]{1,0:T(8,128)(2,1)S(1)} copy-done((bf16[512,128]{1,0:T(8,128)(2,1)S(1)}, bf16[512,128]{1,0:T(8,128)(2,1)}, u32[]{:S(2)}) %copy-start.2) | copy-done | bytes 131096
  10.9 1.0 %shard_map.137 = bf16[256,512]{1,0:T(8,128)(2,1)} custom-call(bf16[512,128]{1,0:T(8,128)(2,1)S(1)} %copy-done.1, bf16[512,128]{1,0:T(8,128)(2,1)S(1)} %copy-done.2), custom_call_target="tpu_custom_call" | custom-call | flops 67108864 | bytes 524288 | tf_op jit(solution)/shard_map/pallas_call | solution.py:355
  11.9 0.0 copy-start.9
  11.9 7.1 %all-to-all-start = ((bf16[16,16,512]{2,1,0:T(8,128)(2,1)}), bf16[16,16,512]{2,1,0:T(8,128)(2,1)S(1)}, u32[]{:S(2)}, u32[]{:S(2)}) async-start(bf16[16,16,512]{2,1,0:T(8,128)(2,1)} %bitcast), calls=%async_computation | async-start | bytes 524288 | tf_op jit(solution)/shard_map/all_to_all | solution.py:317
  19.0 0.0 collective-permute-done.refs_1_
  19.0 0.0 collective-permute-done.1.refs_2_
  19.0 0.0 collective-permute-done.2.refs_3_
  19.0 0.0 copy-done.9
  19.0 0.0 copy-start.5
  19.0 0.0 copy-start.6
  19.0 0.0 copy-start.7
  19.0 0.0 copy-start.8
  19.1 1.7 %collective-permute-start.3 = (bf16[32,512]{1,0:T(8,128)(2,1)S(1)}, bf16[32,512]{1,0:T(8,128)(2,1)S(1)}, u32[]{:S(2)}, u32[]{:S(2)}) collective-permute-start(bf16[32,512]{1,0:T(8,128)(2,1)S(1)} %get-tuple-element.42), channel_id=1, source_target_pairs={{0,2},{1,3},{2,4},{3,5},{4,6},{5,7},{6,0},{7,1},{8,10},{9,11},{10,... | collective-permute-start | bytes 98312 | tf_op jit(solution)/shard_map/ppermute | solution.py:325
  20.7 0.9 %collective-permute-start.4 = (bf16[32,512]{1,0:T(8,128)(2,1)S(1)}, bf16[32,512]{1,0:T(8,128)(2,1)S(1)}, u32[]{:S(2)}, u32[]{:S(2)}) collective-permute-start(bf16[32,512]{1,0:T(8,128)(2,1)S(1)} %get-tuple-element.43), channel_id=1, source_target_pairs={{0,4},{1,5},{2,6},{3,7},{4,0},{5,1},{6,2},{7,3},{8,12},{9,13},{10,... | collective-permute-start | bytes 98312 | tf_op jit(solution)/shard_map/ppermute | solution.py:325
  21.7 2.4 %collective-permute-start.5 = (bf16[32,512]{1,0:T(8,128)(2,1)S(1)}, bf16[32,512]{1,0:T(8,128)(2,1)S(1)}, u32[]{:S(2)}, u32[]{:S(2)}) collective-permute-start(bf16[32,512]{1,0:T(8,128)(2,1)S(1)} %get-tuple-element.44), channel_id=1, source_target_pairs={{0,6},{1,7},{2,0},{3,1},{4,2},{5,3},{6,4},{7,5},{8,14},{9,15},{10,... | collective-permute-start | bytes 98312 | tf_op jit(solution)/shard_map/ppermute | solution.py:325
  24.1 6.3 %all-to-all-done = bf16[16,16,512]{2,1,0:T(8,128)(2,1)S(1)} async-done(((bf16[16,16,512]{2,1,0:T(8,128)(2,1)}), bf16[16,16,512]{2,1,0:T(8,128)(2,1)S(1)}, u32[]{:S(2)}, u32[]{:S(2)}) %all-to-all-start) | async-done | bytes 262176 | tf_op jit(solution)/shard_map/all_to_all | solution.py:317
  30.4 0.0 copy-done.5
  30.4 0.0 copy-done.6
  30.4 0.0 copy-done.7
  30.4 0.0 copy-done.8
  30.4 2.2 %shard_map.140 = (bf16[128,512]{1,0:T(8,128)(2,1)}, f32[2,512,256]{2,1,0:T(8,128)S(1)}) custom-call(bf16[256,512]{1,0:T(8,128)(2,1)S(1)} %bitcast.13, bf16[128,128]{1,0:T(8,128)(2,1)S(1)} %copy-done.7, bf16[2,64,128]{2,1,0:T(8,128)(2,1)S(1)} %copy-done.8, f32[64,256]{1,0:T(8,128)S(1)} %copy-done.6, bf16[2,256,256]{2,1,0:T(8,128)(2,1)S(1)} %copy-done.5), custom_call_target="tpu_custom_call" | custom-call | flops 1073741824 | bytes 524288 | tf_op jit(solution)/shard_map/pallas_call | solution.py:361
  32.6 0.0 collective-permute-done.3.refs_1_
  32.6 0.0 collective-permute-done.4.refs_2_
  32.6 0.0 collective-permute-done.5.refs_3_
  32.6 0.0 copy-start.3
  32.6 0.0 copy-start.4
  32.6 3.7 %all-to-all-start.1 = ((bf16[16,8,512]{2,1,0:T(8,128)(2,1)}), bf16[16,8,512]{2,1,0:T(8,128)(2,1)S(1)}, u32[]{:S(2)}, u32[]{:S(2)}) async-start(bf16[16,8,512]{2,1,0:T(8,128)(2,1)} %bitcast.2), calls=%async_computation.1 | async-start | bytes 262144 | tf_op jit(solution)/shard_map/all_to_all | solution.py:317
  36.3 0.0 copy-done.3
  36.3 0.0 copy-done.4
  36.3 0.2 shard_map.141
  36.5 0.3 shard_map.142
  36.9 1.9 %collective-permute-start.6 = (bf16[32,512]{1,0:T(8,128)(2,1)S(1)}, bf16[32,512]{1,0:T(8,128)(2,1)S(1)}, u32[]{:S(2)}, u32[]{:S(2)}) collective-permute-start(bf16[32,512]{1,0:T(8,128)(2,1)S(1)} %get-tuple-element.51), channel_id=1, source_target_pairs={{0,64},{16,80},{32,96},{48,112},{64,128},{80,144},{96,160},{112,17... | collective-permute-start | bytes 98312 | tf_op jit(solution)/shard_map/ppermute | solution.py:330
  38.8 2.7 %collective-permute-start.7 = (bf16[32,512]{1,0:T(8,128)(2,1)S(1)}, bf16[32,512]{1,0:T(8,128)(2,1)S(1)}, u32[]{:S(2)}, u32[]{:S(2)}) collective-permute-start(bf16[32,512]{1,0:T(8,128)(2,1)S(1)} %get-tuple-element.52), channel_id=1, source_target_pairs={{0,128},{16,144},{32,160},{48,176},{64,192},{80,208},{96,224},{112... | collective-permute-start | bytes 98312 | tf_op jit(solution)/shard_map/ppermute | solution.py:330
  41.5 1.4 %collective-permute-start.8 = (bf16[32,512]{1,0:T(8,128)(2,1)S(1)}, bf16[32,512]{1,0:T(8,128)(2,1)S(1)}, u32[]{:S(2)}, u32[]{:S(2)}) collective-permute-start(bf16[32,512]{1,0:T(8,128)(2,1)S(1)} %get-tuple-element.53), channel_id=1, source_target_pairs={{0,192},{16,208},{32,224},{48,240},{64,0},{80,16},{96,32},{112,48}... | collective-permute-start | bytes 98312 | tf_op jit(solution)/shard_map/ppermute | solution.py:330
  42.9 0.0 collective-permute-done.6.refs_1_
  42.9 1.4 %collective-permute-done.7.refs_2_ = bf16[32,512]{1,0:T(8,128)(2,1)S(1)} collective-permute-done((bf16[32,512]{1,0:T(8,128)(2,1)S(1)}, bf16[32,512]{1,0:T(8,128)(2,1)S(1)}, u32[]{:S(2)}, u32[]{:S(2)}) %collective-permute-start.7) | collective-permute-done | bytes 32800 | tf_op jit(solution)/shard_map/ppermute | solution.py:330
  44.3 1.1 %collective-permute-done.8.refs_3_ = bf16[32,512]{1,0:T(8,128)(2,1)S(1)} collective-permute-done((bf16[32,512]{1,0:T(8,128)(2,1)S(1)}, bf16[32,512]{1,0:T(8,128)(2,1)S(1)}, u32[]{:S(2)}, u32[]{:S(2)}) %collective-permute-start.8) | collective-permute-done | bytes 32800 | tf_op jit(solution)/shard_map/ppermute | solution.py:330
  45.4 0.0 all-to-all-done.1
  45.4 0.9 %shard_map.143 = bf16[128,512]{1,0:T(8,128)(2,1)} custom-call(bf16[128,512]{1,0:T(8,128)(2,1)S(1)} %bitcast.10, f32[128,512]{1,0:T(8,128)S(1)} %get-tuple-element.49.refs_5_.gate_ref, bf16[128,128]{1,0:T(8,128)(2,1)S(1)} %get-tuple-element.55.blocks_ref), custom_call_target="tpu_custom_call" | custom-call | flops 67108864 | bytes 524288 | tf_op jit(solution)/shard_map/pallas_call | solution.py:371
  46.3 8.9 %all-to-all-start.2 = ((bf16[16,8,512]{2,1,0:T(8,128)(2,1)}), bf16[16,8,512]{2,1,0:T(8,128)(2,1)S(1)}, u32[]{:S(2)}, u32[]{:S(2)}) async-start(bf16[16,8,512]{2,1,0:T(8,128)(2,1)} %bitcast.4), calls=%async_computation.2 | async-start | bytes 262144 | tf_op jit(solution)/shard_map/all_to_all | solution.py:317
  55.2 1.5 %collective-permute-start.9 = (bf16[32,512]{1,0:T(8,128)(2,1)S(1)}, bf16[32,512]{1,0:T(8,128)(2,1)S(1)}, u32[]{:S(2)}, u32[]{:S(2)}) collective-permute-start(bf16[32,512]{1,0:T(8,128)(2,1)S(1)} %get-tuple-element.57), channel_id=1, source_target_pairs={{0,16},{16,32},{32,48},{48,0},{64,80},{80,96},{96,112},{112,64},{1... | collective-permute-start | bytes 98312 | tf_op jit(solution)/shard_map/ppermute | solution.py:330
  56.6 2.4 %collective-permute-start.10 = (bf16[32,512]{1,0:T(8,128)(2,1)S(1)}, bf16[32,512]{1,0:T(8,128)(2,1)S(1)}, u32[]{:S(2)}, u32[]{:S(2)}) collective-permute-start(bf16[32,512]{1,0:T(8,128)(2,1)S(1)} %get-tuple-element.58), channel_id=1, source_target_pairs={{0,32},{16,48},{32,0},{48,16},{64,96},{80,112},{96,64},{112,80},{1... | collective-permute-start | bytes 98312 | tf_op jit(solution)/shard_map/ppermute | solution.py:330
  59.0 1.5 %collective-permute-start.11 = (bf16[32,512]{1,0:T(8,128)(2,1)S(1)}, bf16[32,512]{1,0:T(8,128)(2,1)S(1)}, u32[]{:S(2)}, u32[]{:S(2)}) collective-permute-start(bf16[32,512]{1,0:T(8,128)(2,1)S(1)} %get-tuple-element.59), channel_id=1, source_target_pairs={{0,48},{16,0},{32,16},{48,32},{64,112},{80,64},{96,80},{112,96},{1... | collective-permute-start | bytes 98312 | tf_op jit(solution)/shard_map/ppermute | solution.py:330
  60.5 1.8 %collective-permute-done.9.refs_1_ = bf16[32,512]{1,0:T(8,128)(2,1)S(1)} collective-permute-done((bf16[32,512]{1,0:T(8,128)(2,1)S(1)}, bf16[32,512]{1,0:T(8,128)(2,1)S(1)}, u32[]{:S(2)}, u32[]{:S(2)}) %collective-permute-start.9) | collective-permute-done | bytes 32800 | tf_op jit(solution)/shard_map/ppermute | solution.py:330
  62.3 2.4 %collective-permute-done.10.refs_2_ = bf16[32,512]{1,0:T(8,128)(2,1)S(1)} collective-permute-done((bf16[32,512]{1,0:T(8,128)(2,1)S(1)}, bf16[32,512]{1,0:T(8,128)(2,1)S(1)}, u32[]{:S(2)}, u32[]{:S(2)}) %collective-permute-start.10) | collective-permute-done | bytes 32800 | tf_op jit(solution)/shard_map/ppermute | solution.py:330
  64.7 0.0 collective-permute-done.11.refs_3_
  64.7 2.2 %shard_map.146.grads_ref = bf16[256,512]{1,0:T(8,128)(2,1)S(1)} custom-call(bf16[32,512]{1,0:T(8,128)(2,1)S(1)} %get-tuple-element.56.refs_0_, bf16[32,512]{1,0:T(8,128)(2,1)S(1)} %collective-permute-done.9.refs_1_, bf16[32,512]{1,0:T(8,128)(2,1)S(1)} %collective-permute-done.10.refs_2_, bf16[32,512]{1,0:T(8,128)(2,1)S(1)} %collective-permute-done.11.refs_3_, ...), custom_call_target="tpu_custom_call" | custom-call | flops 1073741824 | bytes 524288 | tf_op jit(solution)/shard_map/pallas_call | solution.py:375
  66.8 0.0 copy-start
  66.8 1.1 %shard_map.145 = (bf16[512,128]{1,0:T(8,128)(2,1)}, f32[2,128,64]{2,1,0:T(8,128)S(1)}) custom-call(bf16[128,512]{1,0:T(8,128)(2,1)S(1)} %bitcast.11, f32[128,512]{1,0:T(8,128)S(1)} %get-tuple-element.49.refs_5_.gate_ref, bf16[128,512]{1,0:T(8,128)(2,1)S(1)} %get-tuple-element.61.returned_ref, bf16[128,128]{1,0:T(8,128)(2,1)S(1)} %get-tuple-element.48.refs_4_.own_ref), custom_call_target="tpu_custom_call" | custom-call | flops 67108864 | bytes 524288 | tf_op jit(solution)/shard_map/pallas_call | solution.py:381
  67.9 0.0 all-to-all-done.2
  67.9 0.0 copy-done
  67.9 0.4 shard_map.147
  68.3 16.9 %all_to_all.20 = bf16[16,16,640]{2,1,0:T(8,128)(2,1)S(1)} all-to-all(bf16[16,16,640]{2,1,0:T(8,128)(2,1)S(1)} %bitcast.9), channel_id=1, replica_groups=mesh['seq'=16,'ch'=16] {'seq'}, dimensions={0} | all-to-all | bytes 655360 | tf_op jit(solution)/shard_map/all_to_all | solution.py:317
  85.2 1.0 %shard_map.148 = (bf16[512,128]{1,0:T(8,128)(2,1)}, bf16[512,128]{1,0:T(8,128)(2,1)}, f32[2,4,64]{2,1,0:T(4,128)}, f32[4,2,32]{2,1,0:T(2,128)}) custom-call(bf16[256,640]{1,0:T(8,128)(2,1)S(1)} %bitcast.8), custom_call_target="tpu_custom_call" | custom-call | flops 67108864 | bytes 524288 | tf_op jit(solution)/shard_map/pallas_call | solution.py:386
  (2 shorter events, 0.0 us)
Async XLA Ops:
  0.6 9.4 %copy-start.1 = (bf16[512,128]{1,0:T(8,128)(2,1)S(1)}, bf16[512,128]{1,0:T(8,128)(2,1)}, u32[]{:S(2)}) copy-start(bf16[512,128]{1,0:T(8,128)(2,1)} %signal_ref.1) | copy-start | bytes 393220
  2.6 16.4 %collective-permute-start = (bf16[32,512]{1,0:T(8,128)(2,1)}, bf16[32,512]{1,0:T(8,128)(2,1)S(1)}, u32[]{:S(2)}, u32[]{:S(2)}) collective-permute-start(bf16[32,512]{1,0:T(8,128)(2,1)} %get-tuple-element.38), channel_id=1, source_target_pairs={{0,1},{1,0},{2,3},{3,2},{4,5},{5,4},{6,7},{7,6},{8,9},{9,8},{10,11... | collective-permute-start | bytes 98312 | tf_op jit(solution)/shard_map/ppermute | solution.py:325
  2.7 16.3 %collective-permute-start.1 = (bf16[32,512]{1,0:T(8,128)(2,1)}, bf16[32,512]{1,0:T(8,128)(2,1)S(1)}, u32[]{:S(2)}, u32[]{:S(2)}) collective-permute-start(bf16[32,512]{1,0:T(8,128)(2,1)} %get-tuple-element.39), channel_id=1, source_target_pairs={{0,8},{1,9},{2,10},{3,11},{4,12},{5,13},{6,14},{7,15},{8,0},{9,1},... | collective-permute-start | bytes 98312 | tf_op jit(solution)/shard_map/ppermute | solution.py:325
  10.0 9.0 %collective-permute-start.2 = (bf16[32,512]{1,0:T(8,128)(2,1)}, bf16[32,512]{1,0:T(8,128)(2,1)S(1)}, u32[]{:S(2)}, u32[]{:S(2)}) collective-permute-start(bf16[32,512]{1,0:T(8,128)(2,1)} %get-tuple-element.40), channel_id=1, source_target_pairs={{0,9},{1,8},{2,11},{3,10},{4,13},{5,12},{6,15},{7,14},{8,1},{9,0},... | collective-permute-start | bytes 98312 | tf_op jit(solution)/shard_map/ppermute | solution.py:325
  10.0 0.9 %copy-start.2 = (bf16[512,128]{1,0:T(8,128)(2,1)S(1)}, bf16[512,128]{1,0:T(8,128)(2,1)}, u32[]{:S(2)}) copy-start(bf16[512,128]{1,0:T(8,128)(2,1)} %filter_ref.1) | copy-start | bytes 393220
  11.9 7.1 %copy-start.9 = (bf16[32,512]{1,0:T(8,128)(2,1)S(1)}, bf16[32,512]{1,0:T(8,128)(2,1)}, u32[]{:S(2)}) copy-start(bf16[32,512]{1,0:T(8,128)(2,1)} %get-tuple-element.37.refs_0_) | copy-start | bytes 98308
  11.9 18.5 %all-to-all-start = ((bf16[16,16,512]{2,1,0:T(8,128)(2,1)}), bf16[16,16,512]{2,1,0:T(8,128)(2,1)S(1)}, u32[]{:S(2)}, u32[]{:S(2)}) async-start(bf16[16,16,512]{2,1,0:T(8,128)(2,1)} %bitcast), calls=%async_computation | async-start | bytes 524288 | tf_op jit(solution)/shard_map/all_to_all | solution.py:317
  19.0 11.4 %copy-start.5 = (bf16[2,256,256]{2,1,0:T(8,128)(2,1)S(1)}, bf16[2,256,256]{2,1,0:T(8,128)(2,1)}, u32[]{:S(2)}) copy-start(bf16[2,256,256]{2,1,0:T(8,128)(2,1)} %constant.11.clone.inner_ref.refs_8_) | copy-start | bytes 786436
  19.0 11.3 %copy-start.6 = (f32[64,256]{1,0:T(8,128)S(1)}, f32[64,256]{1,0:T(8,128)}, u32[]{:S(2)}) copy-start(f32[64,256]{1,0:T(8,128)} %constant.10.clone.twiddle_ref.refs_7_) | copy-start | bytes 196612
  19.0 11.3 %copy-start.7 = (bf16[128,128]{1,0:T(8,128)(2,1)S(1)}, bf16[128,128]{1,0:T(8,128)(2,1)}, u32[]{:S(2)}) copy-start(bf16[128,128]{1,0:T(8,128)(2,1)} %constant.8.clone.outer_ref.refs_5_) | copy-start | bytes 98308
  19.0 11.3 %copy-start.8 = (bf16[2,64,128]{2,1,0:T(8,128)(2,1)S(1)}, bf16[2,64,128]{2,1,0:T(8,128)(2,1)}, u32[]{:S(2)}) copy-start(bf16[2,64,128]{2,1,0:T(8,128)(2,1)} %constant.9.clone.back_ref.refs_6_) | copy-start | bytes 98308
  19.1 13.5 %collective-permute-start.3 = (bf16[32,512]{1,0:T(8,128)(2,1)S(1)}, bf16[32,512]{1,0:T(8,128)(2,1)S(1)}, u32[]{:S(2)}, u32[]{:S(2)}) collective-permute-start(bf16[32,512]{1,0:T(8,128)(2,1)S(1)} %get-tuple-element.42), channel_id=1, source_target_pairs={{0,2},{1,3},{2,4},{3,5},{4,6},{5,7},{6,0},{7,1},{8,10},{9,11},{10,... | collective-permute-start | bytes 98312 | tf_op jit(solution)/shard_map/ppermute | solution.py:325
  20.7 11.9 %collective-permute-start.4 = (bf16[32,512]{1,0:T(8,128)(2,1)S(1)}, bf16[32,512]{1,0:T(8,128)(2,1)S(1)}, u32[]{:S(2)}, u32[]{:S(2)}) collective-permute-start(bf16[32,512]{1,0:T(8,128)(2,1)S(1)} %get-tuple-element.43), channel_id=1, source_target_pairs={{0,4},{1,5},{2,6},{3,7},{4,0},{5,1},{6,2},{7,3},{8,12},{9,13},{10,... | collective-permute-start | bytes 98312 | tf_op jit(solution)/shard_map/ppermute | solution.py:325
  21.7 10.9 %collective-permute-start.5 = (bf16[32,512]{1,0:T(8,128)(2,1)S(1)}, bf16[32,512]{1,0:T(8,128)(2,1)S(1)}, u32[]{:S(2)}, u32[]{:S(2)}) collective-permute-start(bf16[32,512]{1,0:T(8,128)(2,1)S(1)} %get-tuple-element.44), channel_id=1, source_target_pairs={{0,6},{1,7},{2,0},{3,1},{4,2},{5,3},{6,4},{7,5},{8,14},{9,15},{10,... | collective-permute-start | bytes 98312 | tf_op jit(solution)/shard_map/ppermute | solution.py:325
  32.6 3.7 %copy-start.3 = (bf16[512,128]{1,0:T(8,128)(2,1)S(1)}, bf16[512,128]{1,0:T(8,128)(2,1)}, u32[]{:S(2)}) copy-start(bf16[512,128]{1,0:T(8,128)(2,1)} %gate_ref.1) | copy-start | bytes 393220
  32.6 3.7 %copy-start.4 = (bf16[2,64,64]{2,1,0:T(8,128)(2,1)S(1)}, bf16[2,64,64]{2,1,0:T(8,128)(2,1)}, u32[]{:S(2)}) copy-start(bf16[2,64,64]{2,1,0:T(8,128)(2,1)} %w_first_ref.1) | copy-start | bytes 49156
  32.6 12.8 %all-to-all-start.1 = ((bf16[16,8,512]{2,1,0:T(8,128)(2,1)}), bf16[16,8,512]{2,1,0:T(8,128)(2,1)S(1)}, u32[]{:S(2)}, u32[]{:S(2)}) async-start(bf16[16,8,512]{2,1,0:T(8,128)(2,1)} %bitcast.2), calls=%async_computation.1 | async-start | bytes 262144 | tf_op jit(solution)/shard_map/all_to_all | solution.py:317
  36.9 6.1 %collective-permute-start.6 = (bf16[32,512]{1,0:T(8,128)(2,1)S(1)}, bf16[32,512]{1,0:T(8,128)(2,1)S(1)}, u32[]{:S(2)}, u32[]{:S(2)}) collective-permute-start(bf16[32,512]{1,0:T(8,128)(2,1)S(1)} %get-tuple-element.51), channel_id=1, source_target_pairs={{0,64},{16,80},{32,96},{48,112},{64,128},{80,144},{96,160},{112,17... | collective-permute-start | bytes 98312 | tf_op jit(solution)/shard_map/ppermute | solution.py:330
  38.8 5.6 %collective-permute-start.7 = (bf16[32,512]{1,0:T(8,128)(2,1)S(1)}, bf16[32,512]{1,0:T(8,128)(2,1)S(1)}, u32[]{:S(2)}, u32[]{:S(2)}) collective-permute-start(bf16[32,512]{1,0:T(8,128)(2,1)S(1)} %get-tuple-element.52), channel_id=1, source_target_pairs={{0,128},{16,144},{32,160},{48,176},{64,192},{80,208},{96,224},{112... | collective-permute-start | bytes 98312 | tf_op jit(solution)/shard_map/ppermute | solution.py:330
  41.5 3.9 %collective-permute-start.8 = (bf16[32,512]{1,0:T(8,128)(2,1)S(1)}, bf16[32,512]{1,0:T(8,128)(2,1)S(1)}, u32[]{:S(2)}, u32[]{:S(2)}) collective-permute-start(bf16[32,512]{1,0:T(8,128)(2,1)S(1)} %get-tuple-element.53), channel_id=1, source_target_pairs={{0,192},{16,208},{32,224},{48,240},{64,0},{80,16},{96,32},{112,48}... | collective-permute-start | bytes 98312 | tf_op jit(solution)/shard_map/ppermute | solution.py:330
  46.3 21.6 %all-to-all-start.2 = ((bf16[16,8,512]{2,1,0:T(8,128)(2,1)}), bf16[16,8,512]{2,1,0:T(8,128)(2,1)S(1)}, u32[]{:S(2)}, u32[]{:S(2)}) async-start(bf16[16,8,512]{2,1,0:T(8,128)(2,1)} %bitcast.4), calls=%async_computation.2 | async-start | bytes 262144 | tf_op jit(solution)/shard_map/all_to_all | solution.py:317
  55.2 7.1 %collective-permute-start.9 = (bf16[32,512]{1,0:T(8,128)(2,1)S(1)}, bf16[32,512]{1,0:T(8,128)(2,1)S(1)}, u32[]{:S(2)}, u32[]{:S(2)}) collective-permute-start(bf16[32,512]{1,0:T(8,128)(2,1)S(1)} %get-tuple-element.57), channel_id=1, source_target_pairs={{0,16},{16,32},{32,48},{48,0},{64,80},{80,96},{96,112},{112,64},{1... | collective-permute-start | bytes 98312 | tf_op jit(solution)/shard_map/ppermute | solution.py:330
  56.6 8.0 %collective-permute-start.10 = (bf16[32,512]{1,0:T(8,128)(2,1)S(1)}, bf16[32,512]{1,0:T(8,128)(2,1)S(1)}, u32[]{:S(2)}, u32[]{:S(2)}) collective-permute-start(bf16[32,512]{1,0:T(8,128)(2,1)S(1)} %get-tuple-element.58), channel_id=1, source_target_pairs={{0,32},{16,48},{32,0},{48,16},{64,96},{80,112},{96,64},{112,80},{1... | collective-permute-start | bytes 98312 | tf_op jit(solution)/shard_map/ppermute | solution.py:330
  59.0 5.6 %collective-permute-start.11 = (bf16[32,512]{1,0:T(8,128)(2,1)S(1)}, bf16[32,512]{1,0:T(8,128)(2,1)S(1)}, u32[]{:S(2)}, u32[]{:S(2)}) collective-permute-start(bf16[32,512]{1,0:T(8,128)(2,1)S(1)} %get-tuple-element.59), channel_id=1, source_target_pairs={{0,48},{16,0},{32,16},{48,32},{64,112},{80,64},{96,80},{112,96},{1... | collective-permute-start | bytes 98312 | tf_op jit(solution)/shard_map/ppermute | solution.py:330
  66.8 1.1 %copy-start = (bf16[512,128]{1,0:T(8,128)(2,1)S(1)}, bf16[512,128]{1,0:T(8,128)(2,1)}, u32[]{:S(2)}) copy-start(bf16[512,128]{1,0:T(8,128)(2,1)} %d_out_ref.1) | copy-start | bytes 393220

commit v5 on v3

--- a/solution.py
+++ b/solution.py
@@ -75,18 +75,9 @@
     return ones_where(row == col)
 
 
-def pair_kernel(signal_hbm, filter_hbm, pair_ref, both_ref, sems):
-    copies = [
-        pltpu.make_async_copy(source, both_ref.at[field], sems.at[field])
-        for field, source in enumerate((signal_hbm, filter_hbm))
-    ]
-    for copy in copies:
-        copy.start()
-    order = pair_order()
-    for copy in copies:
-        copy.wait()
-    both = jnp.concatenate([both_ref[0], both_ref[1]], axis=1)
-    pair_ref[...] = dot(order, both, NT).astype(BF16)
+def pair_kernel(signal_ref, filter_ref, pair_ref):
+    both = jnp.concatenate([signal_ref[...], filter_ref[...]], axis=1)
+    pair_ref[...] = dot(pair_order(), both, NT).astype(BF16)
 
 
 def place():
@@ -102,7 +93,15 @@
     return z * 8 + y * 2 + core
 
 
-def back_kernel(d_out_ref, w_second_ref, near_ref, core_ref, far_ref, cross_ref):
+def back_kernel(d_out_hbm, w_second_hbm, *refs):
+    outs, (d_out_ref, w_second_ref, sems) = refs[:3], refs[3:]
+    copies = [
+        pltpu.make_async_copy(w_second_hbm, w_second_ref, sems.at[0]),
+        pltpu.make_async_copy(d_out_hbm, d_out_ref, sems.at[1]),
+    ]
+    for copy in copies:
+        copy.start()
+    copies[0].wait()
     flat = w_second_ref[...].reshape(128, 32)
     row, col = iotas(32, 128)
     spread = dot(flat, ones_where(row == col % 32))
@@ -111,14 +110,21 @@
     block = 2 * partner(row // 8 % 4, row // 32, 1) + row // 4 % 2
     order = ones_where((block == col % 32) & (row % 4 == col // 32))
     weights = dot(order, spread).astype(BF16)
+    copies[1].wait()
     result = dot(weights, d_out_ref[...], NT).astype(BF16)
-    for zc, ref in enumerate((near_ref, core_ref, far_ref, cross_ref)):
-        ref[...] = result[32 * zc : 32 * zc + 32, :]
-
-
-def repack_kernel(*refs):
-    values = [ref[...].astype(F32) for ref in refs[:4]]
-    for y, ref in enumerate(refs[4:]):
+    for ref, start in zip(outs, (0, 32, 64)):
+        ref[...] = result[start : start + ref.shape[0], :]
+
+
+def core_kernel(core_ref, far_ref, message_ref):
+    message_ref[0:32, :] = core_ref[...]
+    message_ref[32:64, :] = far_ref[32:64, :]
+
+
+def repack_kernel(near_ref, core_ref, far_ref, *outs):
+    near, core, far = (ref[...].astype(F32) for ref in (near_ref, core_ref, far_ref))
+    values = (near, core[0:32, :], far[0:32, :], core[32:64, :])
+    for y, ref in enumerate(outs):
         ref[...] = jnp.concatenate([v[8 * y : 8 * y + 8, :] for v in values], axis=0).astype(BF16)
 
 
@@ -325,18 +331,24 @@
     outer, back, twiddle, inner = (jnp.asarray(t) for t in tables(lax.axis_size("seq"), rows))
     single, double = ((width, rows), BF16), ((2 * width, rows), BF16)
     slab = ((rows, width), BF16)
-    pair = call(
-        pair_kernel,
-        [double],
-        [pltpu.VMEM((2, rows, width), BF16), pltpu.SemaphoreType.DMA((2,))],
+    quarter, half = ((width // 4, rows), BF16), ((width // 2, rows), BF16)
+    near, core, far = call(
+        back_kernel,
+        [quarter, quarter, half],
+        [
+            pltpu.VMEM(d_out.shape, BF16),
+            pltpu.VMEM(w_second.shape, BF16),
+            pltpu.SemaphoreType.DMA((2,)),
+        ],
         held=(pl.ANY, 2),
         limit=60 << 20,
-    )(signal, filter_raw)[0]
+    )(d_out, w_second)
+    far = shift(far, 0, 2)
+    pair = call(pair_kernel, [double])(signal, filter_raw)[0]
     pair = exchange(pair, "seq")
-    quarter = ((width // 4, rows), BF16)
-    near, *others = call(back_kernel, [quarter] * 4)(d_out, w_second)
-    others = [shift(value, 0, zc) for zc, value in zip((1, 2, 3), others)]
-    near, *others = call(repack_kernel, [quarter] * 4)(near, *others)
+    core = shift(call(core_kernel, [half], flops=1 << 35)(core, far)[0], 0, 1)
+    near, *others = call(repack_kernel, [quarter] * 4)(near, core, far)
+    pair = lax.optimization_barrier((pair, near))[0]
     others = [shift(value, y, 0) for y, value in zip((1, 2, 3), others)]
     square = ((128, 128), BF16)
     gate, blocks, own = call(prepare_kernel, [((width, rows), F32), square, square])(gate, w_first)

time: 82.7 us -> 78.1 us (0.944)
  blocking collectives: 32.9 us -> 29.9 us
  waiting for transfers between devices: 12.6 us -> 10 us
  local copies, waits for them, and re-layouts: 0.04 us -> 1.69 us
  starting transfers between devices: 25.7 us -> 24.4 us
    ppermute x6 -> x5, waiting for transfers between devices: 6.98 us -> 0.28 us  [shift(): return lax.ppermute(value, 'ch', pairs)]
    all_to_all x2, waiting for transfers between devices: 5.63 us -> 9.75 us  [exchange(): lax.all_to_all(pieces, axis, split_axis=0, concat_axis=0, tiled=True)]
    all_to_all x2, blocking collectives: 32.9 us -> 29.9 us  [exchange(): lax.all_to_all(pieces, axis, split_axis=0, concat_axis=0, tiled=True)]
    all_to_all x2, starting transfers between devices: 14.8 us -> 12.1 us  [exchange(): lax.all_to_all(pieces, axis, split_axis=0, concat_axis=0, tiled=True)]
    unnamed x16 -> x22, local copies, waits for them, and re-layouts: 0.04 us -> 1.69 us
    ppermute x6 -> x5, starting transfers between devices: 10.9 us -> 12.4 us  [shift(): return lax.ppermute(value, 'ch', pairs)]
    pallas_call x3 -> x4, Pallas kernels: 2.4 us -> 2.94 us  [the longest x1 1.95 us: shards(): call(back_kernel, [quarter, quarter, half], [pltpu.VMEM(d_out.shape, BF16...]
  transfers between devices with their start and end apart: 8 -> 7, of which waited for: 4 -> 3; matrix products, arithmetic and copies ran while one was open for 0% -> 0% of each run, Pallas kernels for 7% -> 8%
where the time goes in v5:
time: 78.1 us; the launch traced here: 77.1 us
  blocking collectives  29.9 us (38%)
  starting transfers between devices  24.4 us (31%)
  Pallas kernels  10.2 us (13%)
  waiting for transfers between devices  10 us (13%)
  local copies, waits for them, and re-layouts  1.69 us (2%)
  between operations  0.81 us (1%)
    all_to_all x2, blocking collectives, exchange(): lax.all_to_all(pieces, axis, split_axis=0, concat_axis=0, tiled=True)  29.9 us
    ppermute x5, starting transfers between devices, shift(): return lax.ppermute(value, 'ch', pairs)  12.4 us
    all_to_all x2, starting transfers between devices, exchange(): lax.all_to_all(pieces, axis, split_axis=0, concat_axis=0, tiled=True)  12.1 us
    all_to_all x2, waiting for transfers between devices, exchange(): lax.all_to_all(pieces, axis, split_axis=0, concat_axis=0, tiled=True)  9.75 us
    pallas_call x1, Pallas kernels, shards(): call(adjoint_kernel, [double], [pltpu.VMEM((2 * width * 4, 128), F32), pl...  2.11 us
    pallas_call x1, Pallas kernels, shards(): call(back_kernel, [quarter, quarter, half], [pltpu.VMEM(d_out.shape, BF16...  1.95 us
    unnamed x22, local copies, waits for them, and re-layouts  1.69 us
  transfers between devices with their start and end apart: 7, of which 3 were waited for; matrix products, arithmetic and copies ran while one was open for 0% of the time, Pallas kernels for 8%

profile of v5, /device:TPU:8, one launch (start us, length us, event | category | flops | bytes accessed | tf_op | source)
XLA Modules:
  0.0 77.1 jit_solution(5933771826592433933)
XLA Ops:
  0.6 0.0 copy-start.1
  0.6 1.9 %shard_map.137 = (bf16[32,512]{1,0:T(8,128)(2,1)}, bf16[32,512]{1,0:T(8,128)(2,1)}, bf16[64,512]{1,0:T(8,128)(2,1)}) custom-call(bf16[512,128]{1,0:T(8,128)(2,1)} %d_out_ref.1, bf16[4,32,32]{2,1,0:T(8,128)(2,1)} %w_second_hbm.1), custom_call_target="tpu_custom_call" | custom-call | flops 67108864 | bytes 524288 | tf_op jit(solution)/shard_map/pallas_call | solution.py:335
  2.6 7.3 %collective-permute-start = (bf16[64,512]{1,0:T(8,128)(2,1)}, bf16[64,512]{1,0:T(8,128)(2,1)S(1)}, u32[]{:S(2)}, u32[]{:S(2)}) collective-permute-start(bf16[64,512]{1,0:T(8,128)(2,1)} %get-tuple-element.28), channel_id=1, source_target_pairs={{0,8},{1,9},{2,10},{3,11},{4,12},{5,13},{6,14},{7,15},{8,0},{9,1},... | collective-permute-start | bytes 196616 | tf_op jit(solution)/shard_map/ppermute | solution.py:326
  9.9 0.0 copy-done.1
  9.9 0.0 copy-start.2
  9.9 0.9 %copy-done.2 = bf16[512,128]{1,0:T(8,128)(2,1)S(1)} copy-done((bf16[512,128]{1,0:T(8,128)(2,1)S(1)}, bf16[512,128]{1,0:T(8,128)(2,1)}, u32[]{:S(2)}) %copy-start.2) | copy-done | bytes 131096
  10.8 1.0 %shard_map.141 = bf16[256,512]{1,0:T(8,128)(2,1)} custom-call(bf16[512,128]{1,0:T(8,128)(2,1)S(1)} %copy-done.1, bf16[512,128]{1,0:T(8,128)(2,1)S(1)} %copy-done.2), custom_call_target="tpu_custom_call" | custom-call | flops 67108864 | bytes 524288 | tf_op jit(solution)/shard_map/pallas_call | solution.py:347
  11.8 0.0 copy-start.10
  11.8 5.9 %all-to-all-start = ((bf16[16,16,512]{2,1,0:T(8,128)(2,1)}), bf16[16,16,512]{2,1,0:T(8,128)(2,1)S(1)}, u32[]{:S(2)}, u32[]{:S(2)}) async-start(bf16[16,16,512]{2,1,0:T(8,128)(2,1)} %bitcast), calls=%async_computation | async-start | bytes 524288 | tf_op jit(solution)/shard_map/all_to_all | solution.py:318
  17.7 0.0 collective-permute-done.far_ref
  17.7 0.0 copy-done.10
  17.7 0.0 copy-start.3
  17.7 0.0 copy-start.4
  17.7 0.0 copy-start.9
  17.7 0.0 copy-start.5
  17.7 0.1 collective-permute-start.1
  17.8 0.7 copy-done.3
  18.6 0.0 copy-done.4
  18.6 0.2 shard_map.140
  18.8 0.3 collective-permute-done.1.core_ref
  19.1 0.0 copy-done.9
  19.1 0.0 copy-start.6
  19.1 0.0 copy-start.7
  19.1 0.0 copy-start.8
  19.1 1.7 %collective-permute-start.2 = (bf16[32,512]{1,0:T(8,128)(2,1)S(1)}, bf16[32,512]{1,0:T(8,128)(2,1)S(1)}, u32[]{:S(2)}, u32[]{:S(2)}) collective-permute-start(bf16[32,512]{1,0:T(8,128)(2,1)S(1)} %get-tuple-element.30), channel_id=1, source_target_pairs={{0,2},{1,3},{2,4},{3,5},{4,6},{5,7},{6,0},{7,1},{8,10},{9,11},{10,... | collective-permute-start | bytes 98312 | tf_op jit(solution)/shard_map/ppermute | solution.py:326
  20.8 0.9 %collective-permute-start.3 = (bf16[32,512]{1,0:T(8,128)(2,1)S(1)}, bf16[32,512]{1,0:T(8,128)(2,1)S(1)}, u32[]{:S(2)}, u32[]{:S(2)}) collective-permute-start(bf16[32,512]{1,0:T(8,128)(2,1)S(1)} %get-tuple-element.31), channel_id=1, source_target_pairs={{0,4},{1,5},{2,6},{3,7},{4,0},{5,1},{6,2},{7,3},{8,12},{9,13},{10,... | collective-permute-start | bytes 98312 | tf_op jit(solution)/shard_map/ppermute | solution.py:326
  21.7 2.4 %collective-permute-start.4 = (bf16[32,512]{1,0:T(8,128)(2,1)S(1)}, bf16[32,512]{1,0:T(8,128)(2,1)S(1)}, u32[]{:S(2)}, u32[]{:S(2)}) collective-permute-start(bf16[32,512]{1,0:T(8,128)(2,1)S(1)} %get-tuple-element.32), channel_id=1, source_target_pairs={{0,6},{1,7},{2,0},{3,1},{4,2},{5,3},{6,4},{7,5},{8,14},{9,15},{10,... | collective-permute-start | bytes 98312 | tf_op jit(solution)/shard_map/ppermute | solution.py:326
  24.1 4.1 %all-to-all-done = bf16[16,16,512]{2,1,0:T(8,128)(2,1)S(1)} async-done(((bf16[16,16,512]{2,1,0:T(8,128)(2,1)}), bf16[16,16,512]{2,1,0:T(8,128)(2,1)S(1)}, u32[]{:S(2)}, u32[]{:S(2)}) %all-to-all-start) | async-done | bytes 262176 | tf_op jit(solution)/shard_map/all_to_all | solution.py:318
  28.3 0.0 copy-done.5
  28.3 0.0 copy-done.6
  28.3 0.0 copy-done.7
  28.3 0.0 copy-done.8
  28.3 1.5 %shard_map.142 = (f32[512,128]{1,0:T(8,128)S(1)}, f32[2,512,256]{2,1,0:T(8,128)S(1)}) custom-call(bf16[256,512]{1,0:T(8,128)(2,1)S(1)} %bitcast.14, bf16[128,128]{1,0:T(8,128)(2,1)S(1)} %copy-done.8, bf16[2,64,128]{2,1,0:T(8,128)(2,1)S(1)} %copy-done.7, f32[64,256]{1,0:T(8,128)S(1)} %copy-done.6, bf16[2,256,256]{2,1,0:T(8,128)(2,1)S(1)} %copy-done.5), custom_call_target="tpu_custom_call" | custom-call | flops 1073741824 | bytes 524288 | tf_op jit(solution)/shard_map/pallas_call | solution.py:355
  29.8 0.0 collective-permute-done.2.first_ref
  29.8 0.0 collective-permute-done.3.second_ref
  29.8 0.0 collective-permute-done.4.third_ref
  29.9 0.2 shard_map.143
  30.0 13.5 %all_to_all.20 = bf16[16,16,512]{2,1,0:T(8,128)(2,1)S(1)} all-to-all(bf16[16,16,512]{2,1,0:T(8,128)(2,1)S(1)} %bitcast.15), channel_id=1, replica_groups=mesh['seq'=16,'ch'=16] {'seq'}, dimensions={0} | all-to-all | bytes 524288 | tf_op jit(solution)/shard_map/all_to_all | solution.py:318
  43.6 0.9 %shard_map.144 = bf16[128,512]{1,0:T(8,128)(2,1)} custom-call(bf16[256,512]{1,0:T(8,128)(2,1)S(1)} %bitcast.8, f32[128,512]{1,0:T(8,128)S(1)} %get-tuple-element.34.gate_ref, bf16[128,128]{1,0:T(8,128)(2,1)S(1)} %get-tuple-element.38.blocks_ref), custom_call_target="tpu_custom_call" | custom-call | flops 67108864 | bytes 524288 | tf_op jit(solution)/shard_map/pallas_call | solution.py:363
  44.4 6.2 %all-to-all-start.2 = ((bf16[16,8,512]{2,1,0:T(8,128)(2,1)}), bf16[16,8,512]{2,1,0:T(8,128)(2,1)S(1)}, u32[]{:S(2)}, u32[]{:S(2)}) async-start(bf16[16,8,512]{2,1,0:T(8,128)(2,1)} %bitcast.4), calls=%async_computation.2 | async-start | bytes 262144 | tf_op jit(solution)/shard_map/all_to_all | solution.py:318
  50.6 1.1 %shard_map.145 = (bf16[512,128]{1,0:T(8,128)(2,1)}, f32[2,128,64]{2,1,0:T(8,128)S(1)}) custom-call(bf16[256,512]{1,0:T(8,128)(2,1)S(1)} %bitcast.9, f32[128,512]{1,0:T(8,128)S(1)} %get-tuple-element.34.gate_ref, bf16[128,512]{1,0:T(8,128)(2,1)S(1)} %get-tuple-element.39.returned_ref, bf16[128,128]{1,0:T(8,128)(2,1)S(1)} %get-tuple-element.33.own_ref), custom_call_target="tpu_custom_call" | custom-call | flops 67108864 | bytes 524288 | tf_op jit(solution)/shard_map/pallas_call | solution.py:371
  51.7 0.0 copy-start
  51.7 2.1 %shard_map.146.grads_ref = bf16[256,512]{1,0:T(8,128)(2,1)S(1)} custom-call(bf16[256,512]{1,0:T(8,128)(2,1)S(1)} %bitcast.10, f32[2,512,256]{2,1,0:T(8,128)S(1)} %get-tuple-element.41.spectra_ref, bf16[128,128]{1,0:T(8,128)(2,1)S(1)} %copy-done.8, bf16[2,64,128]{2,1,0:T(8,128)(2,1)S(1)} %copy-done.7, f32[64,256]{1,0:T(8,128)S(1)} %copy-done.6, ...), custom_call_target="tpu_custom_call" | custom-call | flops 1073741824 | bytes 524288 | tf_op jit(solution)/shard_map/pallas_call | solution.py:365
  53.8 5.6 %all-to-all-done.2 = bf16[16,8,512]{2,1,0:T(8,128)(2,1)S(1)} async-done(((bf16[16,8,512]{2,1,0:T(8,128)(2,1)}), bf16[16,8,512]{2,1,0:T(8,128)(2,1)S(1)}, u32[]{:S(2)}, u32[]{:S(2)}) %all-to-all-start.2) | async-done | bytes 131104 | tf_op jit(solution)/shard_map/all_to_all | solution.py:318
  59.4 0.0 copy-done
  59.4 0.4 shard_map.147
  59.8 16.3 %all_to_all.21 = bf16[16,16,640]{2,1,0:T(8,128)(2,1)S(1)} all-to-all(bf16[16,16,640]{2,1,0:T(8,128)(2,1)S(1)} %bitcast.12), channel_id=1, replica_groups=mesh['seq'=16,'ch'=16] {'seq'}, dimensions={0} | all-to-all | bytes 655360 | tf_op jit(solution)/shard_map/all_to_all | solution.py:318
  76.1 1.0 %shard_map.148 = (bf16[512,128]{1,0:T(8,128)(2,1)}, bf16[512,128]{1,0:T(8,128)(2,1)}, f32[2,4,64]{2,1,0:T(4,128)}, f32[4,2,32]{2,1,0:T(2,128)}) custom-call(bf16[256,640]{1,0:T(8,128)(2,1)S(1)} %bitcast.11), custom_call_target="tpu_custom_call" | custom-call | flops 67108864 | bytes 524288 | tf_op jit(solution)/shard_map/pallas_call | solution.py:376
  (2 shorter events, 0.0 us)
Async XLA Ops:
  0.6 9.2 %copy-start.1 = (bf16[512,128]{1,0:T(8,128)(2,1)S(1)}, bf16[512,128]{1,0:T(8,128)(2,1)}, u32[]{:S(2)}) copy-start(bf16[512,128]{1,0:T(8,128)(2,1)} %signal_ref.1) | copy-start | bytes 393220
  2.6 15.1 %collective-permute-start = (bf16[64,512]{1,0:T(8,128)(2,1)}, bf16[64,512]{1,0:T(8,128)(2,1)S(1)}, u32[]{:S(2)}, u32[]{:S(2)}) collective-permute-start(bf16[64,512]{1,0:T(8,128)(2,1)} %get-tuple-element.28), channel_id=1, source_target_pairs={{0,8},{1,9},{2,10},{3,11},{4,12},{5,13},{6,14},{7,15},{8,0},{9,1},... | collective-permute-start | bytes 196616 | tf_op jit(solution)/shard_map/ppermute | solution.py:326
  9.9 0.9 %copy-start.2 = (bf16[512,128]{1,0:T(8,128)(2,1)S(1)}, bf16[512,128]{1,0:T(8,128)(2,1)}, u32[]{:S(2)}) copy-start(bf16[512,128]{1,0:T(8,128)(2,1)} %filter_ref.1) | copy-start | bytes 393220
  11.8 5.9 %copy-start.10 = (bf16[32,512]{1,0:T(8,128)(2,1)S(1)}, bf16[32,512]{1,0:T(8,128)(2,1)}, u32[]{:S(2)}) copy-start(bf16[32,512]{1,0:T(8,128)(2,1)} %get-tuple-element.27.core_ref) | copy-start | bytes 98308
  11.8 16.5 %all-to-all-start = ((bf16[16,16,512]{2,1,0:T(8,128)(2,1)}), bf16[16,16,512]{2,1,0:T(8,128)(2,1)S(1)}, u32[]{:S(2)}, u32[]{:S(2)}) async-start(bf16[16,16,512]{2,1,0:T(8,128)(2,1)} %bitcast), calls=%async_computation | async-start | bytes 524288 | tf_op jit(solution)/shard_map/all_to_all | solution.py:318
  17.7 0.9 %copy-start.3 = (bf16[512,128]{1,0:T(8,128)(2,1)S(1)}, bf16[512,128]{1,0:T(8,128)(2,1)}, u32[]{:S(2)}) copy-start(bf16[512,128]{1,0:T(8,128)(2,1)} %gate_ref.1) | copy-start | bytes 393220
  17.7 0.9 %copy-start.4 = (bf16[2,64,64]{2,1,0:T(8,128)(2,1)S(1)}, bf16[2,64,64]{2,1,0:T(8,128)(2,1)}, u32[]{:S(2)}) copy-start(bf16[2,64,64]{2,1,0:T(8,128)(2,1)} %w_first_ref.1) | copy-start | bytes 49156
  17.7 1.4 %copy-start.9 = (bf16[32,512]{1,0:T(8,128)(2,1)S(1)}, bf16[32,512]{1,0:T(8,128)(2,1)}, u32[]{:S(2)}) copy-start(bf16[32,512]{1,0:T(8,128)(2,1)} %get-tuple-element.26.near_ref) | copy-start | bytes 98308
  17.7 10.5 %copy-start.5 = (bf16[2,256,256]{2,1,0:T(8,128)(2,1)S(1)}, bf16[2,256,256]{2,1,0:T(8,128)(2,1)}, u32[]{:S(2)}) copy-start(bf16[2,256,256]{2,1,0:T(8,128)(2,1)} %constant.11.clone.inner_ref) | copy-start | bytes 786436
  17.7 1.3 %collective-permute-start.1 = (bf16[64,512]{1,0:T(8,128)(2,1)S(1)}, bf16[64,512]{1,0:T(8,128)(2,1)S(1)}, u32[]{:S(2)}, u32[]{:S(2)}) collective-permute-start(bf16[64,512]{1,0:T(8,128)(2,1)S(1)} %shard_map.138), channel_id=1, source_target_pairs={{0,1},{1,0},{2,3},{3,2},{4,5},{5,4},{6,7},{7,6},{8,9},{9,8},{10,11... | collective-permute-start | bytes 196616 | tf_op jit(solution)/shard_map/ppermute | solution.py:326
  19.1 9.2 %copy-start.6 = (f32[64,256]{1,0:T(8,128)S(1)}, f32[64,256]{1,0:T(8,128)}, u32[]{:S(2)}) copy-start(f32[64,256]{1,0:T(8,128)} %constant.10.clone.twiddle_ref) | copy-start | bytes 196612
  19.1 9.2 %copy-start.7 = (bf16[2,64,128]{2,1,0:T(8,128)(2,1)S(1)}, bf16[2,64,128]{2,1,0:T(8,128)(2,1)}, u32[]{:S(2)}) copy-start(bf16[2,64,128]{2,1,0:T(8,128)(2,1)} %constant.9.clone.back_ref) | copy-start | bytes 98308
  19.1 9.2 %copy-start.8 = (bf16[128,128]{1,0:T(8,128)(2,1)S(1)}, bf16[128,128]{1,0:T(8,128)(2,1)}, u32[]{:S(2)}) copy-start(bf16[128,128]{1,0:T(8,128)(2,1)} %constant.8.clone.outer_ref) | copy-start | bytes 98308
  19.1 10.7 %collective-permute-start.2 = (bf16[32,512]{1,0:T(8,128)(2,1)S(1)}, bf16[32,512]{1,0:T(8,128)(2,1)S(1)}, u32[]{:S(2)}, u32[]{:S(2)}) collective-permute-start(bf16[32,512]{1,0:T(8,128)(2,1)S(1)} %get-tuple-element.30), channel_id=1, source_target_pairs={{0,2},{1,3},{2,4},{3,5},{4,6},{5,7},{6,0},{7,1},{8,10},{9,11},{10,... | collective-permute-start | bytes 98312 | tf_op jit(solution)/shard_map/ppermute | solution.py:326
  20.8 9.1 %collective-permute-start.3 = (bf16[32,512]{1,0:T(8,128)(2,1)S(1)}, bf16[32,512]{1,0:T(8,128)(2,1)S(1)}, u32[]{:S(2)}, u32[]{:S(2)}) collective-permute-start(bf16[32,512]{1,0:T(8,128)(2,1)S(1)} %get-tuple-element.31), channel_id=1, source_target_pairs={{0,4},{1,5},{2,6},{3,7},{4,0},{5,1},{6,2},{7,3},{8,12},{9,13},{10,... | collective-permute-start | bytes 98312 | tf_op jit(solution)/shard_map/ppermute | solution.py:326
  21.7 8.1 %collective-permute-start.4 = (bf16[32,512]{1,0:T(8,128)(2,1)S(1)}, bf16[32,512]{1,0:T(8,128)(2,1)S(1)}, u32[]{:S(2)}, u32[]{:S(2)}) collective-permute-start(bf16[32,512]{1,0:T(8,128)(2,1)S(1)} %get-tuple-element.32), channel_id=1, source_target_pairs={{0,6},{1,7},{2,0},{3,1},{4,2},{5,3},{6,4},{7,5},{8,14},{9,15},{10,... | collective-permute-start | bytes 98312 | tf_op jit(solution)/shard_map/ppermute | solution.py:326
  44.4 15.0 %all-to-all-start.2 = ((bf16[16,8,512]{2,1,0:T(8,128)(2,1)}), bf16[16,8,512]{2,1,0:T(8,128)(2,1)S(1)}, u32[]{:S(2)}, u32[]{:S(2)}) async-start(bf16[16,8,512]{2,1,0:T(8,128)(2,1)} %bitcast.4), calls=%async_computation.2 | async-start | bytes 262144 | tf_op jit(solution)/shard_map/all_to_all | solution.py:318
  51.7 7.7 %copy-start = (bf16[512,128]{1,0:T(8,128)(2,1)S(1)}, bf16[512,128]{1,0:T(8,128)(2,1)}, u32[]{:S(2)}) copy-start(bf16[512,128]{1,0:T(8,128)(2,1)} %d_out_ref.1) | copy-start | bytes 393220

commit v6 on v5

--- a/solution.py
+++ b/solution.py
@@ -75,11 +75,6 @@
     return ones_where(row == col)
 
 
-def pair_kernel(signal_ref, filter_ref, pair_ref):
-    both = jnp.concatenate([signal_ref[...], filter_ref[...]], axis=1)
-    pair_ref[...] = dot(pair_order(), both, NT).astype(BF16)
-
-
 def place():
     index = lax.axis_index("ch")
     return index // 8, index // 2 % 4, index % 2
@@ -93,27 +88,56 @@
     return z * 8 + y * 2 + core
 
 
-def back_kernel(d_out_hbm, w_second_hbm, *refs):
-    outs, (d_out_ref, w_second_ref, sems) = refs[:3], refs[3:]
+def entry_kernel(
+    d_out_hbm,
+    w_second_hbm,
+    signal_hbm,
+    filter_hbm,
+    near_ref,
+    core_ref,
+    far_ref,
+    pair_hbm,
+    d_out_ref,
+    w_second_ref,
+    both_ref,
+    pair_ref,
+    sems,
+):
     copies = [
-        pltpu.make_async_copy(w_second_hbm, w_second_ref, sems.at[0]),
-        pltpu.make_async_copy(d_out_hbm, d_out_ref, sems.at[1]),
+        pltpu.make_async_copy(source, target, sems.at[index])
+        for index, (source, target) in enumerate(
+            (
+                (signal_hbm, both_ref.at[0]),
+                (filter_hbm, both_ref.at[1]),
+                (w_second_hbm, w_second_ref),
+                (d_out_hbm, d_out_ref),
+            )
+        )
     ]
     for copy in copies:
         copy.start()
-    copies[0].wait()
-    flat = w_second_ref[...].reshape(128, 32)
+    pairs = pair_order()
     row, col = iotas(32, 128)
-    spread = dot(flat, ones_where(row == col % 32))
+    copies_of = ones_where(row == col % 32)
     row, col = iotas(128, 128)
-    spread = jnp.where(row // 32 == col // 32, spread, 0.0).astype(BF16)
+    keep = row // 32 == col // 32
     block = 2 * partner(row // 8 % 4, row // 32, 1) + row // 4 % 2
     order = ones_where((block == col % 32) & (row % 4 == col // 32))
+    copies[0].wait()
+    copies[1].wait()
+    both = jnp.concatenate([both_ref[0], both_ref[1]], axis=1)
+    pair_ref[...] = dot(pairs, both, NT).astype(BF16)
+    leave = pltpu.make_async_copy(pair_ref, pair_hbm, sems.at[4])
+    leave.start()
+    copies[2].wait()
+    flat = w_second_ref[...].reshape(128, 32)
+    spread = jnp.where(keep, dot(flat, copies_of), 0.0).astype(BF16)
     weights = dot(order, spread).astype(BF16)
-    copies[1].wait()
+    copies[3].wait()
     result = dot(weights, d_out_ref[...], NT).astype(BF16)
-    for ref, start in zip(outs, (0, 32, 64)):
+    for ref, start in zip((near_ref, core_ref, far_ref), (0, 32, 64)):
         ref[...] = result[start : start + ref.shape[0], :]
+    leave.wait()
 
 
 def core_kernel(core_ref, far_ref, message_ref):
@@ -235,8 +259,8 @@
         result = restore(
             gr * real + gi * imag, gi * real - gr * imag, back_ref, twiddle_ref, inner_ref
         )
-        by_slab(out_ref, result, 8 * field, 16)
-    grads_ref[...] = enroll(out_ref)
+        by_slab(out_ref, result, 0, 8)
+        grads_ref[:, 512 * field : 512 * field + 512] = enroll(out_ref)
 
 
 def conv_rows(pair_ref):
@@ -262,51 +286,53 @@
     )
     row, col = iotas(128, 64)
     fold = ones_where(source(row) * 4 + row % 4 == col)
-    for part, piece in enumerate(split(grad)):
-        partial_ref[part] = dot(order, dot(piece, fold).astype(BF16))
+    partial_ref[...] = dot(order, dot(grad.astype(BF16), fold).astype(BF16))
 
 
 def second_kernel(received_ref, d_out_ref, partial_ref, grads_ref, sums_ref):
     row, col = iotas(128, 128)
     grad = jnp.where(row % 4 == col // 32, dot(received_ref[...], d_out_ref[...]), 0.0)
-    row, col = iotas(128, 64)
+    row, col = iotas(128, 32)
     fold = ones_where(row % 32 == col)
-    high, low = [
-        jnp.concatenate([partial_ref[part], dot(piece, fold)], axis=1)
-        for part, piece in enumerate(split(grad))
-    ]
-    rows = []
-    for p in range(16):
-        rows.append(high[8 * p : 8 * p + 8, :])
-        rows.append(low[8 * p : 8 * p + 8, :])
-    sums_ref[:, 0:512] = grads_ref[...]
-    sums_ref[:, 512:640] = jnp.concatenate(rows, axis=0).astype(BF16)
-
-
-def exit_kernel(sums_ref, signal_ref, filter_ref, first_ref, second_ref):
-    both = dot(sums_ref[:, 0:512], pair_order(), TN).astype(BF16)
-    signal_ref[...] = both[:, 0:128]
-    filter_ref[...] = both[:, 128:256]
-    wide = sums_ref[:, 512:640].astype(F32)
-    total = wide[0:16, :]
+    pieces = [partial_ref[...]] + [dot(piece, fold) for piece in split(grad)]
+    sums_ref[:, 0:1024] = grads_ref[...]
+    sums_ref[:, 1024:1152] = jnp.concatenate(pieces, axis=1).astype(BF16)
+
+
+def exit_kernel(sums_ref, signal_hbm, filter_hbm, first_ref, second_ref, both_ref, sems):
+    square = unit()
+    copies = []
+    for field, target in enumerate((signal_hbm, filter_hbm)):
+        values = sums_ref[:, 512 * field : 512 * field + 512]
+        both_ref[field] = dot(values, square, TN).astype(BF16)
+        copies.append(pltpu.make_async_copy(both_ref.at[field], target, sems.at[field]))
+        copies[-1].start()
+    wide = sums_ref[:, 1024:1152].astype(F32)
+    total = wide[0:8, :]
     for p in range(1, 16):
-        total = total + wide[16 * p : 16 * p + 16, :]
-    total = total[0:8, :] + total[8:16, :]
+        total = total + wide[8 * p : 8 * p + 8, :]
+    second = total[:, 64:96] + total[:, 96:128]
     for i in range(2):
         first_ref[i] = total[4 * i : 4 * i + 4, 0:64]
         for k in range(4):
-            second_ref[k, i : i + 1, :] = total[4 * i + k : 4 * i + k + 1, 64:96]
-
-
-def call(body, outs, scratch=(), flops=1 << 26, moved=1 << 19, held=None, limit=32 << 20):
+            second_ref[k, i : i + 1, :] = second[4 * i + k : 4 * i + k + 1, :]
+    for copy in copies:
+        copy.wait()
+
+
+def call(body, outs, scratch=(), flops=1 << 26, moved=1 << 19, spaces=None):
     extra = {}
-    if held is not None:
-        extra["in_specs"] = [pl.BlockSpec(memory_space=held[0])] * held[1]
+    if spaces is not None:
+        extra["in_specs"], extra["out_specs"] = [
+            [pl.BlockSpec(memory_space=space) for space in side] for side in spaces
+        ]
     return pl.pallas_call(
         body,
-        out_shape=[jax.ShapeDtypeStruct(shape, kind) for shape, kind in outs],
+        out_shape=[
+            pltpu.VMEM(*out[:2]) if len(out) > 2 else jax.ShapeDtypeStruct(*out) for out in outs
+        ],
         scratch_shapes=list(scratch),
-        compiler_params=pltpu.CompilerParams(vmem_limit_bytes=limit),
+        compiler_params=pltpu.CompilerParams(vmem_limit_bytes=32 << 20),
         cost_estimate=pl.CostEstimate(flops=flops, bytes_accessed=moved, transcendentals=0),
         **extra,
     )
@@ -332,19 +358,20 @@
     single, double = ((width, rows), BF16), ((2 * width, rows), BF16)
     slab = ((rows, width), BF16)
     quarter, half = ((width // 4, rows), BF16), ((width // 2, rows), BF16)
-    near, core, far = call(
-        back_kernel,
-        [quarter, quarter, half],
+    held = [pltpu.with_memory_space_constraint(v, pltpu.HBM) for v in (d_out, w_second, signal, filter_raw)]
+    near, core, far, pair = call(
+        entry_kernel,
+        [quarter + (True,), quarter + (True,), half + (True,), double],
         [
             pltpu.VMEM(d_out.shape, BF16),
             pltpu.VMEM(w_second.shape, BF16),
-            pltpu.SemaphoreType.DMA((2,)),
+            pltpu.VMEM((2, rows, width), BF16),
+            pltpu.VMEM((2 * width, rows), BF16),
+            pltpu.SemaphoreType.DMA((5,)),
         ],
-        held=(pl.ANY, 2),
-        limit=60 << 20,
-    )(d_out, w_second)
+        spaces=([pl.ANY] * 4, [pltpu.VMEM] * 3 + [pl.ANY]),
+    )(*held)
     far = shift(far, 0, 2)
-    pair = call(pair_kernel, [double])(signal, filter_raw)[0]
     pair = exchange(pair, "seq")
     core = shift(call(core_kernel, [half], flops=1 << 35)(core, far)[0], 0, 1)
     near, *others = call(repack_kernel, [quarter] * 4)(near, core, far)
@@ -364,17 +391,20 @@
     received = exchange(mix, "ch")
     grads = call(
         adjoint_kernel,
-        [double],
-        [pltpu.VMEM((2 * width * 4, 128), F32), pltpu.VMEM((2 * width * 4, 128), F32)],
+        [((width, 2 * rows), BF16)],
+        [pltpu.VMEM((2 * width * 4, 128), F32), pltpu.VMEM((width * 4, 128), F32)],
         flops=1 << 30,
     )(pair, spectra, outer, back, twiddle, inner)[0]
-    grad_gate, partial = call(first_kernel, [slab, ((2, width, 64), F32)])(
+    grad_gate, partial = call(first_kernel, [slab, ((width, 64), F32)])(
         pair, gate, returned, own
     )
-    sums = call(second_kernel, [((2 * width, rows + 128), BF16)])(received, d_out, partial, grads)[0]
+    sums = call(second_kernel, [((width, 2 * rows + 128), BF16)])(received, d_out, partial, grads)[0]
     sums = exchange(sums, "seq")
     grad_signal, grad_filter, grad_first, grad_second = call(
-        exit_kernel, [slab, slab, ((2, 4, 64), F32), ((4, 2, 32), F32)]
+        exit_kernel,
+        [slab, slab, ((2, 4, 64), F32), ((4, 2, 32), F32)],
+        [pltpu.VMEM((2, rows, width), BF16), pltpu.SemaphoreType.DMA((2,))],
+        spaces=([pltpu.VMEM], [pl.ANY] * 2 + [pltpu.VMEM] * 2),
     )(sums)
     return (grad_signal, grad_filter, grad_gate, grad_first, grad_second)
 

time: 78.1 us -> 75.9 us (0.972)
  local copies, waits for them, and re-layouts: 1.69 us -> 0.79 us
    unnamed x22 -> x14, local copies, waits for them, and re-layouts: 1.69 us -> 0.79 us
    pallas_call x6 -> x5, Pallas kernels: 7.42 us -> 6.99 us  [the longest x1 2.03 us: shards(): call(adjoint_kernel, [((width, 2 * rows), BF16)], [pltpu.VMEM((2 * width...]
  transfers between devices with their start and end apart: 7 -> 7, of which waited for: 3 -> 3; matrix products, arithmetic and copies ran while one was open for 0% -> 0% of each run, Pallas kernels for 8% -> 6%
where the time goes in v6:
time: 75.9 us; the launch traced here: 75 us
  blocking collectives  29.2 us (38%)
  starting transfers between devices  24.3 us (32%)
  waiting for transfers between devices  10.1 us (13%)
  Pallas kernels  9.8 us (13%)
  local copies, waits for them, and re-layouts  0.79 us (1%)
  between operations  0.78 us (1%)
    all_to_all x2, blocking collectives, exchange(): lax.all_to_all(pieces, axis, split_axis=0, concat_axis=0, tiled=True)  29.2 us
    ppermute x5, starting transfers between devices, shift(): return lax.ppermute(value, 'ch', pairs)  12.4 us
    all_to_all x2, starting transfers between devices, exchange(): lax.all_to_all(pieces, axis, split_axis=0, concat_axis=0, tiled=True)  11.9 us
    all_to_all x2, waiting for transfers between devices, exchange(): lax.all_to_all(pieces, axis, split_axis=0, concat_axis=0, tiled=True)  9.87 us
    pallas_call x1, Pallas kernels, shards(): call(adjoint_kernel, [((width, 2 * rows), BF16)], [pltpu.VMEM((2 * width...  2.03 us
    pallas_call x1, Pallas kernels, shards(): call(entry_kernel, [quarter + (True,), quarter + (True,), half + (True,),...  1.98 us
    pallas_call x1, Pallas kernels, shards(): call(exit_kernel, [slab, slab, ((2, 4, 64), F32), ((4, 2, 32), F32)], [pl...  1.57 us
    pallas_call x1, Pallas kernels, shards(): call(conv_kernel, [((4 * width, 128), F32), ((2, 512, 256), F32)], [pltpu...  1.52 us
  transfers between devices with their start and end apart: 7, of which 3 were waited for; matrix products, arithmetic and copies ran while one was open for 0% of the time, Pallas kernels for 6%

profile of v6, /device:TPU:8, one launch (start us, length us, event | category | flops | bytes accessed | tf_op | source)
XLA Modules:
  0.0 75.0 jit_solution(6640348563152066441)
XLA Ops:
  0.6 2.0 %shard_map.137 = (bf16[32,512]{1,0:T(8,128)(2,1)S(1)}, bf16[32,512]{1,0:T(8,128)(2,1)S(1)}, bf16[64,512]{1,0:T(8,128)(2,1)S(1)}, bf16[256,512]{1,0:T(8,128)(2,1)}) custom-call(bf16[512,128]{1,0:T(8,128)(2,1)} %d_out_ref.1, bf16[4,32,32]{2,1,0:T(8,128)(2,1)} %w_second_hbm.1, bf16[512,128]{1,0:T(8,128)(2,1)} %signal_hbm.1, bf16[512,128]{1,0:T(8,128)(2,1)} %filter_hbm.1), custom_call_target="tpu_custom_call" | custom-call | flops 67108864 | bytes 524288 | tf_op jit(solution)/shard_map/pallas_call | solution.py:362
  2.6 7.3 %collective-permute-start = (bf16[64,512]{1,0:T(8,128)(2,1)S(1)}, bf16[64,512]{1,0:T(8,128)(2,1)S(1)}, u32[]{:S(2)}, u32[]{:S(2)}) collective-permute-start(bf16[64,512]{1,0:T(8,128)(2,1)S(1)} %get-tuple-element.29), channel_id=1, source_target_pairs={{0,8},{1,9},{2,10},{3,11},{4,12},{5,13},{6,14},{7,15},{8,0},{9,1},... | collective-permute-start | bytes 196616 | tf_op jit(solution)/shard_map/ppermute | solution.py:352
  9.9 5.8 %all-to-all-start = ((bf16[16,16,512]{2,1,0:T(8,128)(2,1)}), bf16[16,16,512]{2,1,0:T(8,128)(2,1)S(1)}, u32[]{:S(2)}, u32[]{:S(2)}) async-start(bf16[16,16,512]{2,1,0:T(8,128)(2,1)} %bitcast), calls=%async_computation | async-start | bytes 524288 | tf_op jit(solution)/shard_map/all_to_all | solution.py:344
  15.7 0.0 collective-permute-done.far_ref
  15.7 0.0 copy-start.1
  15.7 0.0 copy-start.2
  15.7 0.0 copy-start.3
  15.7 0.1 collective-permute-start.1
  15.8 0.8 %copy-done.1 = bf16[512,128]{1,0:T(8,128)(2,1)S(1)} copy-done((bf16[512,128]{1,0:T(8,128)(2,1)S(1)}, bf16[512,128]{1,0:T(8,128)(2,1)}, u32[]{:S(2)}) %copy-start.1) | copy-done | bytes 131096
  16.6 0.0 copy-done.2
  16.6 0.2 shard_map.140
  16.8 0.3 collective-permute-done.1.core_ref
  17.1 0.0 copy-start.4
  17.1 0.0 copy-start.5
  17.1 0.0 copy-start.6
  17.1 1.7 %collective-permute-start.2 = (bf16[32,512]{1,0:T(8,128)(2,1)S(1)}, bf16[32,512]{1,0:T(8,128)(2,1)S(1)}, u32[]{:S(2)}, u32[]{:S(2)}) collective-permute-start(bf16[32,512]{1,0:T(8,128)(2,1)S(1)} %get-tuple-element.31), channel_id=1, source_target_pairs={{0,2},{1,3},{2,4},{3,5},{4,6},{5,7},{6,0},{7,1},{8,10},{9,11},{10,... | collective-permute-start | bytes 98312 | tf_op jit(solution)/shard_map/ppermute | solution.py:352
  18.7 0.9 %collective-permute-start.3 = (bf16[32,512]{1,0:T(8,128)(2,1)S(1)}, bf16[32,512]{1,0:T(8,128)(2,1)S(1)}, u32[]{:S(2)}, u32[]{:S(2)}) collective-permute-start(bf16[32,512]{1,0:T(8,128)(2,1)S(1)} %get-tuple-element.32), channel_id=1, source_target_pairs={{0,4},{1,5},{2,6},{3,7},{4,0},{5,1},{6,2},{7,3},{8,12},{9,13},{10,... | collective-permute-start | bytes 98312 | tf_op jit(solution)/shard_map/ppermute | solution.py:352
  19.7 2.4 %collective-permute-start.4 = (bf16[32,512]{1,0:T(8,128)(2,1)S(1)}, bf16[32,512]{1,0:T(8,128)(2,1)S(1)}, u32[]{:S(2)}, u32[]{:S(2)}) collective-permute-start(bf16[32,512]{1,0:T(8,128)(2,1)S(1)} %get-tuple-element.33), channel_id=1, source_target_pairs={{0,6},{1,7},{2,0},{3,1},{4,2},{5,3},{6,4},{7,5},{8,14},{9,15},{10,... | collective-permute-start | bytes 98312 | tf_op jit(solution)/shard_map/ppermute | solution.py:352
  22.1 4.2 %all-to-all-done = bf16[16,16,512]{2,1,0:T(8,128)(2,1)S(1)} async-done(((bf16[16,16,512]{2,1,0:T(8,128)(2,1)}), bf16[16,16,512]{2,1,0:T(8,128)(2,1)S(1)}, u32[]{:S(2)}, u32[]{:S(2)}) %all-to-all-start) | async-done | bytes 262176 | tf_op jit(solution)/shard_map/all_to_all | solution.py:344
  26.3 0.0 copy-done.3
  26.3 0.0 copy-done.4
  26.3 0.0 copy-done.5
  26.3 0.0 copy-done.6
  26.3 1.5 %shard_map.141 = (f32[512,128]{1,0:T(8,128)S(1)}, f32[2,512,256]{2,1,0:T(8,128)S(1)}) custom-call(bf16[256,512]{1,0:T(8,128)(2,1)S(1)} %bitcast.14, bf16[128,128]{1,0:T(8,128)(2,1)S(1)} %copy-done.6, bf16[2,64,128]{2,1,0:T(8,128)(2,1)S(1)} %copy-done.5, f32[64,256]{1,0:T(8,128)S(1)} %copy-done.4, bf16[2,256,256]{2,1,0:T(8,128)(2,1)S(1)} %copy-done.3), custom_call_target="tpu_custom_call" | custom-call | flops 1073741824 | bytes 524288 | tf_op jit(solution)/shard_map/pallas_call | solution.py:382
  27.8 0.0 collective-permute-done.2.first_ref
  27.8 0.0 collective-permute-done.3.second_ref
  27.8 0.0 collective-permute-done.4.third_ref
  27.9 0.2 shard_map.142
  28.0 13.5 %all_to_all.20 = bf16[16,16,512]{2,1,0:T(8,128)(2,1)S(1)} all-to-all(bf16[16,16,512]{2,1,0:T(8,128)(2,1)S(1)} %bitcast.15), channel_id=1, replica_groups=mesh['seq'=16,'ch'=16] {'seq'}, dimensions={0} | all-to-all | bytes 524288 | tf_op jit(solution)/shard_map/all_to_all | solution.py:344
  41.6 0.9 %shard_map.143 = bf16[128,512]{1,0:T(8,128)(2,1)} custom-call(bf16[256,512]{1,0:T(8,128)(2,1)S(1)} %bitcast.8, f32[128,512]{1,0:T(8,128)S(1)} %get-tuple-element.35.gate_ref, bf16[128,128]{1,0:T(8,128)(2,1)S(1)} %get-tuple-element.40.blocks_ref), custom_call_target="tpu_custom_call" | custom-call | flops 67108864 | bytes 524288 | tf_op jit(solution)/shard_map/pallas_call | solution.py:390
  42.4 6.2 %all-to-all-start.2 = ((bf16[16,8,512]{2,1,0:T(8,128)(2,1)}), bf16[16,8,512]{2,1,0:T(8,128)(2,1)S(1)}, u32[]{:S(2)}, u32[]{:S(2)}) async-start(bf16[16,8,512]{2,1,0:T(8,128)(2,1)} %bitcast.4), calls=%async_computation.2 | async-start | bytes 262144 | tf_op jit(solution)/shard_map/all_to_all | solution.py:344
  48.6 1.1 %shard_map.144 = (bf16[512,128]{1,0:T(8,128)(2,1)}, f32[128,64]{1,0:T(8,128)S(1)}) custom-call(bf16[256,512]{1,0:T(8,128)(2,1)S(1)} %bitcast.9, f32[128,512]{1,0:T(8,128)S(1)} %get-tuple-element.35.gate_ref, bf16[128,512]{1,0:T(8,128)(2,1)S(1)} %get-tuple-element.41.returned_ref, bf16[128,128]{1,0:T(8,128)(2,1)S(1)} %get-tuple-element.34.own_ref), custom_call_target="tpu_custom_call" | custom-call | flops 67108864 | bytes 524288 | tf_op jit(solution)/shard_map/pallas_call | solution.py:398
  49.6 0.0 copy-start
  49.6 2.0 %shard_map.145.grads_ref = bf16[128,1024]{1,0:T(8,128)(2,1)S(1)} custom-call(bf16[256,512]{1,0:T(8,128)(2,1)S(1)} %bitcast.10, f32[2,512,256]{2,1,0:T(8,128)S(1)} %get-tuple-element.43.spectra_ref, bf16[128,128]{1,0:T(8,128)(2,1)S(1)} %copy-done.6, bf16[2,64,128]{2,1,0:T(8,128)(2,1)S(1)} %copy-done.5, f32[64,256]{1,0:T(8,128)S(1)} %copy-done.4, ...), custom_call_target="tpu_custom_call" | custom-call | flops 1073741824 | bytes 524288 | tf_op jit(solution)/shard_map/pallas_call | solution.py:392
  51.7 5.7 %all-to-all-done.2 = bf16[16,8,512]{2,1,0:T(8,128)(2,1)S(1)} async-done(((bf16[16,8,512]{2,1,0:T(8,128)(2,1)}), bf16[16,8,512]{2,1,0:T(8,128)(2,1)S(1)}, u32[]{:S(2)}, u32[]{:S(2)}) %all-to-all-start.2) | async-done | bytes 131104 | tf_op jit(solution)/shard_map/all_to_all | solution.py:344
  57.4 0.0 copy-done
  57.4 0.4 shard_map.146
  57.7 15.6 %all_to_all.21 = bf16[16,8,1152]{2,1,0:T(8,128)(2,1)S(1)} all-to-all(bf16[16,8,1152]{2,1,0:T(8,128)(2,1)S(1)} %bitcast.11), channel_id=1, replica_groups=mesh['seq'=16,'ch'=16] {'seq'}, dimensions={0} | all-to-all | bytes 589824 | tf_op jit(solution)/shard_map/all_to_all | solution.py:344
  73.4 1.6 %shard_map.147 = (bf16[512,128]{1,0:T(8,128)(2,1)}, bf16[512,128]{1,0:T(8,128)(2,1)}, f32[2,4,64]{2,1,0:T(4,128)}, f32[4,2,32]{2,1,0:T(2,128)}) custom-call(bf16[128,1152]{1,0:T(8,128)(2,1)S(1)} %bitcast.12), custom_call_target="tpu_custom_call" | custom-call | flops 67108864 | bytes 524288 | tf_op jit(solution)/shard_map/pallas_call | solution.py:403
  (2 shorter events, 0.0 us)
Async XLA Ops:
  2.6 13.1 %collective-permute-start = (bf16[64,512]{1,0:T(8,128)(2,1)S(1)}, bf16[64,512]{1,0:T(8,128)(2,1)S(1)}, u32[]{:S(2)}, u32[]{:S(2)}) collective-permute-start(bf16[64,512]{1,0:T(8,128)(2,1)S(1)} %get-tuple-element.29), channel_id=1, source_target_pairs={{0,8},{1,9},{2,10},{3,11},{4,12},{5,13},{6,14},{7,15},{8,0},{9,1},... | collective-permute-start | bytes 196616 | tf_op jit(solution)/shard_map/ppermute | solution.py:352
  9.9 16.4 %all-to-all-start = ((bf16[16,16,512]{2,1,0:T(8,128)(2,1)}), bf16[16,16,512]{2,1,0:T(8,128)(2,1)S(1)}, u32[]{:S(2)}, u32[]{:S(2)}) async-start(bf16[16,16,512]{2,1,0:T(8,128)(2,1)} %bitcast), calls=%async_computation | async-start | bytes 524288 | tf_op jit(solution)/shard_map/all_to_all | solution.py:344
  15.7 0.9 %copy-start.1 = (bf16[512,128]{1,0:T(8,128)(2,1)S(1)}, bf16[512,128]{1,0:T(8,128)(2,1)}, u32[]{:S(2)}) copy-start(bf16[512,128]{1,0:T(8,128)(2,1)} %gate_ref.1) | copy-start | bytes 393220
  15.7 0.9 %copy-start.2 = (bf16[2,64,64]{2,1,0:T(8,128)(2,1)S(1)}, bf16[2,64,64]{2,1,0:T(8,128)(2,1)}, u32[]{:S(2)}) copy-start(bf16[2,64,64]{2,1,0:T(8,128)(2,1)} %w_first_ref.1) | copy-start | bytes 49156
  15.7 10.6 %copy-start.3 = (bf16[2,256,256]{2,1,0:T(8,128)(2,1)S(1)}, bf16[2,256,256]{2,1,0:T(8,128)(2,1)}, u32[]{:S(2)}) copy-start(bf16[2,256,256]{2,1,0:T(8,128)(2,1)} %constant.11.clone.inner_ref) | copy-start | bytes 786436
  15.7 1.3 %collective-permute-start.1 = (bf16[64,512]{1,0:T(8,128)(2,1)S(1)}, bf16[64,512]{1,0:T(8,128)(2,1)S(1)}, u32[]{:S(2)}, u32[]{:S(2)}) collective-permute-start(bf16[64,512]{1,0:T(8,128)(2,1)S(1)} %shard_map.138), channel_id=1, source_target_pairs={{0,1},{1,0},{2,3},{3,2},{4,5},{5,4},{6,7},{7,6},{8,9},{9,8},{10,11... | collective-permute-start | bytes 196616 | tf_op jit(solution)/shard_map/ppermute | solution.py:352
  17.1 9.2 %copy-start.4 = (f32[64,256]{1,0:T(8,128)S(1)}, f32[64,256]{1,0:T(8,128)}, u32[]{:S(2)}) copy-start(f32[64,256]{1,0:T(8,128)} %constant.10.clone.twiddle_ref) | copy-start | bytes 196612
  17.1 9.2 %copy-start.5 = (bf16[2,64,128]{2,1,0:T(8,128)(2,1)S(1)}, bf16[2,64,128]{2,1,0:T(8,128)(2,1)}, u32[]{:S(2)}) copy-start(bf16[2,64,128]{2,1,0:T(8,128)(2,1)} %constant.9.clone.back_ref) | copy-start | bytes 98308
  17.1 9.2 %copy-start.6 = (bf16[128,128]{1,0:T(8,128)(2,1)S(1)}, bf16[128,128]{1,0:T(8,128)(2,1)}, u32[]{:S(2)}) copy-start(bf16[128,128]{1,0:T(8,128)(2,1)} %constant.8.clone.outer_ref) | copy-start | bytes 98308
  17.1 10.7 %collective-permute-start.2 = (bf16[32,512]{1,0:T(8,128)(2,1)S(1)}, bf16[32,512]{1,0:T(8,128)(2,1)S(1)}, u32[]{:S(2)}, u32[]{:S(2)}) collective-permute-start(bf16[32,512]{1,0:T(8,128)(2,1)S(1)} %get-tuple-element.31), channel_id=1, source_target_pairs={{0,2},{1,3},{2,4},{3,5},{4,6},{5,7},{6,0},{7,1},{8,10},{9,11},{10,... | collective-permute-start | bytes 98312 | tf_op jit(solution)/shard_map/ppermute | solution.py:352
  18.7 9.1 %collective-permute-start.3 = (bf16[32,512]{1,0:T(8,128)(2,1)S(1)}, bf16[32,512]{1,0:T(8,128)(2,1)S(1)}, u32[]{:S(2)}, u32[]{:S(2)}) collective-permute-start(bf16[32,512]{1,0:T(8,128)(2,1)S(1)} %get-tuple-element.32), channel_id=1, source_target_pairs={{0,4},{1,5},{2,6},{3,7},{4,0},{5,1},{6,2},{7,3},{8,12},{9,13},{10,... | collective-permute-start | bytes 98312 | tf_op jit(solution)/shard_map/ppermute | solution.py:352
  19.7 8.2 %collective-permute-start.4 = (bf16[32,512]{1,0:T(8,128)(2,1)S(1)}, bf16[32,512]{1,0:T(8,128)(2,1)S(1)}, u32[]{:S(2)}, u32[]{:S(2)}) collective-permute-start(bf16[32,512]{1,0:T(8,128)(2,1)S(1)} %get-tuple-element.33), channel_id=1, source_target_pairs={{0,6},{1,7},{2,0},{3,1},{4,2},{5,3},{6,4},{7,5},{8,14},{9,15},{10,... | collective-permute-start | bytes 98312 | tf_op jit(solution)/shard_map/ppermute | solution.py:352
  42.4 15.0 %all-to-all-start.2 = ((bf16[16,8,512]{2,1,0:T(8,128)(2,1)}), bf16[16,8,512]{2,1,0:T(8,128)(2,1)S(1)}, u32[]{:S(2)}, u32[]{:S(2)}) async-start(bf16[16,8,512]{2,1,0:T(8,128)(2,1)} %bitcast.4), calls=%async_computation.2 | async-start | bytes 262144 | tf_op jit(solution)/shard_map/all_to_all | solution.py:344
  49.6 7.7 %copy-start = (bf16[512,128]{1,0:T(8,128)(2,1)S(1)}, bf16[512,128]{1,0:T(8,128)(2,1)}, u32[]{:S(2)}) copy-start(bf16[512,128]{1,0:T(8,128)(2,1)} %d_out_ref.1) | copy-start | bytes 393220

commit v7 on v6

--- a/solution.py
+++ b/solution.py
@@ -299,14 +299,20 @@
     sums_ref[:, 1024:1152] = jnp.concatenate(pieces, axis=1).astype(BF16)
 
 
-def exit_kernel(sums_ref, signal_hbm, filter_hbm, first_ref, second_ref, both_ref, sems):
+def exit_kernel(
+    sums_ref, signal_hbm, filter_hbm, first_hbm, second_hbm, both_ref, first_ref, second_ref, sems
+):
+    copies = []
+
+    def leave(source, target):
+        copies.append(pltpu.make_async_copy(source, target, sems.at[len(copies)]))
+        copies[-1].start()
+
     square = unit()
-    copies = []
     for field, target in enumerate((signal_hbm, filter_hbm)):
         values = sums_ref[:, 512 * field : 512 * field + 512]
         both_ref[field] = dot(values, square, TN).astype(BF16)
-        copies.append(pltpu.make_async_copy(both_ref.at[field], target, sems.at[field]))
-        copies[-1].start()
+        leave(both_ref.at[field], target)
     wide = sums_ref[:, 1024:1152].astype(F32)
     total = wide[0:8, :]
     for p in range(1, 16):
@@ -316,6 +322,8 @@
         first_ref[i] = total[4 * i : 4 * i + 4, 0:64]
         for k in range(4):
             second_ref[k, i : i + 1, :] = second[4 * i + k : 4 * i + k + 1, :]
+    leave(first_ref, first_hbm)
+    leave(second_ref, second_hbm)
     for copy in copies:
         copy.wait()
 
@@ -403,8 +411,13 @@
     grad_signal, grad_filter, grad_first, grad_second = call(
         exit_kernel,
         [slab, slab, ((2, 4, 64), F32), ((4, 2, 32), F32)],
-        [pltpu.VMEM((2, rows, width), BF16), pltpu.SemaphoreType.DMA((2,))],
-        spaces=([pltpu.VMEM], [pl.ANY] * 2 + [pltpu.VMEM] * 2),
+        [
+            pltpu.VMEM((2, rows, width), BF16),
+            pltpu.VMEM((2, 4, 64), F32),
+            pltpu.VMEM((4, 2, 32), F32),
+            pltpu.SemaphoreType.DMA((4,)),
+        ],
+        spaces=([pltpu.VMEM], [pl.ANY] * 4),
     )(sums)
     return (grad_signal, grad_filter, grad_gate, grad_first, grad_second)
 

time: 75.9 us -> 75.4 us (level)
  transfers between devices with their start and end apart: 7 -> 7, of which waited for: 3 -> 3; matrix products, arithmetic and copies ran while one was open for 0% -> 0% of each run, Pallas kernels for 6% -> 7%
where the time goes in v7:
time: 75.4 us; the launch traced here: 74.4 us
  blocking collectives  29.2 us (39%)
  starting transfers between devices  24.3 us (32%)
  waiting for transfers between devices  10.1 us (13%)
  Pallas kernels  9.22 us (12%)
  local copies, waits for them, and re-layouts  0.79 us (1%)
  between operations  0.78 us (1%)
    all_to_all x2, blocking collectives, exchange(): lax.all_to_all(pieces, axis, split_axis=0, concat_axis=0, tiled=True)  29.2 us
    ppermute x5, starting transfers between devices, shift(): return lax.ppermute(value, 'ch', pairs)  12.4 us
    all_to_all x2, starting transfers between devices, exchange(): lax.all_to_all(pieces, axis, split_axis=0, concat_axis=0, tiled=True)  11.9 us
    all_to_all x2, waiting for transfers between devices, exchange(): lax.all_to_all(pieces, axis, split_axis=0, concat_axis=0, tiled=True)  9.87 us
    pallas_call x1, Pallas kernels, shards(): call(adjoint_kernel, [((width, 2 * rows), BF16)], [pltpu.VMEM((2 * width...  2.03 us
    pallas_call x1, Pallas kernels, shards(): call(entry_kernel, [quarter + (True,), quarter + (True,), half + (True,),...  1.98 us
    pallas_call x1, Pallas kernels, shards(): call(conv_kernel, [((4 * width, 128), F32), ((2, 512, 256), F32)], [pltpu...  1.52 us
  transfers between devices with their start and end apart: 7, of which 3 were waited for; matrix products, arithmetic and copies ran while one was open for 0% of the time, Pallas kernels for 7%

profile of v7, /device:TPU:8, one launch (start us, length us, event | category | flops | bytes accessed | tf_op | source)
XLA Modules:
  0.0 74.4 jit_solution(12745967509338511617)
XLA Ops:
  0.6 2.0 %shard_map.137 = (bf16[32,512]{1,0:T(8,128)(2,1)S(1)}, bf16[32,512]{1,0:T(8,128)(2,1)S(1)}, bf16[64,512]{1,0:T(8,128)(2,1)S(1)}, bf16[256,512]{1,0:T(8,128)(2,1)}) custom-call(bf16[512,128]{1,0:T(8,128)(2,1)} %d_out_ref.1, bf16[4,32,32]{2,1,0:T(8,128)(2,1)} %w_second_hbm.1, bf16[512,128]{1,0:T(8,128)(2,1)} %signal_hbm.1, bf16[512,128]{1,0:T(8,128)(2,1)} %filter_hbm.1), custom_call_target="tpu_custom_call" | custom-call | flops 67108864 | bytes 524288 | tf_op jit(solution)/shard_map/pallas_call | solution.py:370
  2.6 7.3 %collective-permute-start = (bf16[64,512]{1,0:T(8,128)(2,1)S(1)}, bf16[64,512]{1,0:T(8,128)(2,1)S(1)}, u32[]{:S(2)}, u32[]{:S(2)}) collective-permute-start(bf16[64,512]{1,0:T(8,128)(2,1)S(1)} %get-tuple-element.29), channel_id=1, source_target_pairs={{0,8},{1,9},{2,10},{3,11},{4,12},{5,13},{6,14},{7,15},{8,0},{9,1},... | collective-permute-start | bytes 196616 | tf_op jit(solution)/shard_map/ppermute | solution.py:360
  9.9 5.8 %all-to-all-start = ((bf16[16,16,512]{2,1,0:T(8,128)(2,1)}), bf16[16,16,512]{2,1,0:T(8,128)(2,1)S(1)}, u32[]{:S(2)}, u32[]{:S(2)}) async-start(bf16[16,16,512]{2,1,0:T(8,128)(2,1)} %bitcast), calls=%async_computation | async-start | bytes 524288 | tf_op jit(solution)/shard_map/all_to_all | solution.py:352
  15.7 0.0 collective-permute-done.far_ref
  15.7 0.0 copy-start.1
  15.7 0.0 copy-start.2
  15.7 0.0 copy-start.3
  15.7 0.1 collective-permute-start.1
  15.8 0.8 %copy-done.1 = bf16[512,128]{1,0:T(8,128)(2,1)S(1)} copy-done((bf16[512,128]{1,0:T(8,128)(2,1)S(1)}, bf16[512,128]{1,0:T(8,128)(2,1)}, u32[]{:S(2)}) %copy-start.1) | copy-done | bytes 131096
  16.6 0.0 copy-done.2
  16.6 0.2 shard_map.140
  16.8 0.3 collective-permute-done.1.core_ref
  17.1 0.0 copy-start.4
  17.1 0.0 copy-start.5
  17.1 0.0 copy-start.6
  17.1 1.7 %collective-permute-start.2 = (bf16[32,512]{1,0:T(8,128)(2,1)S(1)}, bf16[32,512]{1,0:T(8,128)(2,1)S(1)}, u32[]{:S(2)}, u32[]{:S(2)}) collective-permute-start(bf16[32,512]{1,0:T(8,128)(2,1)S(1)} %get-tuple-element.31), channel_id=1, source_target_pairs={{0,2},{1,3},{2,4},{3,5},{4,6},{5,7},{6,0},{7,1},{8,10},{9,11},{10,... | collective-permute-start | bytes 98312 | tf_op jit(solution)/shard_map/ppermute | solution.py:360
  18.7 0.9 %collective-permute-start.3 = (bf16[32,512]{1,0:T(8,128)(2,1)S(1)}, bf16[32,512]{1,0:T(8,128)(2,1)S(1)}, u32[]{:S(2)}, u32[]{:S(2)}) collective-permute-start(bf16[32,512]{1,0:T(8,128)(2,1)S(1)} %get-tuple-element.32), channel_id=1, source_target_pairs={{0,4},{1,5},{2,6},{3,7},{4,0},{5,1},{6,2},{7,3},{8,12},{9,13},{10,... | collective-permute-start | bytes 98312 | tf_op jit(solution)/shard_map/ppermute | solution.py:360
  19.7 2.4 %collective-permute-start.4 = (bf16[32,512]{1,0:T(8,128)(2,1)S(1)}, bf16[32,512]{1,0:T(8,128)(2,1)S(1)}, u32[]{:S(2)}, u32[]{:S(2)}) collective-permute-start(bf16[32,512]{1,0:T(8,128)(2,1)S(1)} %get-tuple-element.33), channel_id=1, source_target_pairs={{0,6},{1,7},{2,0},{3,1},{4,2},{5,3},{6,4},{7,5},{8,14},{9,15},{10,... | collective-permute-start | bytes 98312 | tf_op jit(solution)/shard_map/ppermute | solution.py:360
  22.1 4.2 %all-to-all-done = bf16[16,16,512]{2,1,0:T(8,128)(2,1)S(1)} async-done(((bf16[16,16,512]{2,1,0:T(8,128)(2,1)}), bf16[16,16,512]{2,1,0:T(8,128)(2,1)S(1)}, u32[]{:S(2)}, u32[]{:S(2)}) %all-to-all-start) | async-done | bytes 262176 | tf_op jit(solution)/shard_map/all_to_all | solution.py:352
  26.3 0.0 copy-done.3
  26.3 0.0 copy-done.4
  26.3 0.0 copy-done.5
  26.3 0.0 copy-done.6
  26.3 1.5 %shard_map.141 = (f32[512,128]{1,0:T(8,128)S(1)}, f32[2,512,256]{2,1,0:T(8,128)S(1)}) custom-call(bf16[256,512]{1,0:T(8,128)(2,1)S(1)} %bitcast.14, bf16[128,128]{1,0:T(8,128)(2,1)S(1)} %copy-done.6, bf16[2,64,128]{2,1,0:T(8,128)(2,1)S(1)} %copy-done.5, f32[64,256]{1,0:T(8,128)S(1)} %copy-done.4, bf16[2,256,256]{2,1,0:T(8,128)(2,1)S(1)} %copy-done.3), custom_call_target="tpu_custom_call" | custom-call | flops 1073741824 | bytes 524288 | tf_op jit(solution)/shard_map/pallas_call | solution.py:390
  27.8 0.0 collective-permute-done.2.first_ref
  27.8 0.0 collective-permute-done.3.second_ref
  27.8 0.0 collective-permute-done.4.third_ref
  27.9 0.2 shard_map.142
  28.0 13.5 %all_to_all.20 = bf16[16,16,512]{2,1,0:T(8,128)(2,1)S(1)} all-to-all(bf16[16,16,512]{2,1,0:T(8,128)(2,1)S(1)} %bitcast.15), channel_id=1, replica_groups=mesh['seq'=16,'ch'=16] {'seq'}, dimensions={0} | all-to-all | bytes 524288 | tf_op jit(solution)/shard_map/all_to_all | solution.py:352
  41.6 0.9 %shard_map.143 = bf16[128,512]{1,0:T(8,128)(2,1)} custom-call(bf16[256,512]{1,0:T(8,128)(2,1)S(1)} %bitcast.8, f32[128,512]{1,0:T(8,128)S(1)} %get-tuple-element.35.gate_ref, bf16[128,128]{1,0:T(8,128)(2,1)S(1)} %get-tuple-element.40.blocks_ref), custom_call_target="tpu_custom_call" | custom-call | flops 67108864 | bytes 524288 | tf_op jit(solution)/shard_map/pallas_call | solution.py:398
  42.4 6.2 %all-to-all-start.2 = ((bf16[16,8,512]{2,1,0:T(8,128)(2,1)}), bf16[16,8,512]{2,1,0:T(8,128)(2,1)S(1)}, u32[]{:S(2)}, u32[]{:S(2)}) async-start(bf16[16,8,512]{2,1,0:T(8,128)(2,1)} %bitcast.4), calls=%async_computation.2 | async-start | bytes 262144 | tf_op jit(solution)/shard_map/all_to_all | solution.py:352
  48.6 1.1 %shard_map.144 = (bf16[512,128]{1,0:T(8,128)(2,1)}, f32[128,64]{1,0:T(8,128)S(1)}) custom-call(bf16[256,512]{1,0:T(8,128)(2,1)S(1)} %bitcast.9, f32[128,512]{1,0:T(8,128)S(1)} %get-tuple-element.35.gate_ref, bf16[128,512]{1,0:T(8,128)(2,1)S(1)} %get-tuple-element.41.returned_ref, bf16[128,128]{1,0:T(8,128)(2,1)S(1)} %get-tuple-element.34.own_ref), custom_call_target="tpu_custom_call" | custom-call | flops 67108864 | bytes 524288 | tf_op jit(solution)/shard_map/pallas_call | solution.py:406
  49.6 0.0 copy-start
  49.6 2.0 %shard_map.145.grads_ref = bf16[128,1024]{1,0:T(8,128)(2,1)S(1)} custom-call(bf16[256,512]{1,0:T(8,128)(2,1)S(1)} %bitcast.10, f32[2,512,256]{2,1,0:T(8,128)S(1)} %get-tuple-element.43.spectra_ref, bf16[128,128]{1,0:T(8,128)(2,1)S(1)} %copy-done.6, bf16[2,64,128]{2,1,0:T(8,128)(2,1)S(1)} %copy-done.5, f32[64,256]{1,0:T(8,128)S(1)} %copy-done.4, ...), custom_call_target="tpu_custom_call" | custom-call | flops 1073741824 | bytes 524288 | tf_op jit(solution)/shard_map/pallas_call | solution.py:400
  51.7 5.7 %all-to-all-done.2 = bf16[16,8,512]{2,1,0:T(8,128)(2,1)S(1)} async-done(((bf16[16,8,512]{2,1,0:T(8,128)(2,1)}), bf16[16,8,512]{2,1,0:T(8,128)(2,1)S(1)}, u32[]{:S(2)}, u32[]{:S(2)}) %all-to-all-start.2) | async-done | bytes 131104 | tf_op jit(solution)/shard_map/all_to_all | solution.py:352
  57.4 0.0 copy-done
  57.4 0.4 shard_map.146
  57.7 15.6 %all_to_all.21 = bf16[16,8,1152]{2,1,0:T(8,128)(2,1)S(1)} all-to-all(bf16[16,8,1152]{2,1,0:T(8,128)(2,1)S(1)} %bitcast.11), channel_id=1, replica_groups=mesh['seq'=16,'ch'=16] {'seq'}, dimensions={0} | all-to-all | bytes 589824 | tf_op jit(solution)/shard_map/all_to_all | solution.py:352
  73.4 1.0 %shard_map.147 = (bf16[512,128]{1,0:T(8,128)(2,1)}, bf16[512,128]{1,0:T(8,128)(2,1)}, f32[2,4,64]{2,1,0:T(4,128)}, f32[4,2,32]{2,1,0:T(2,128)}) custom-call(bf16[128,1152]{1,0:T(8,128)(2,1)S(1)} %bitcast.12), custom_call_target="tpu_custom_call" | custom-call | flops 67108864 | bytes 524288 | tf_op jit(solution)/shard_map/pallas_call | solution.py:411
  (2 shorter events, 0.0 us)
Async XLA Ops:
  2.6 13.1 %collective-permute-start = (bf16[64,512]{1,0:T(8,128)(2,1)S(1)}, bf16[64,512]{1,0:T(8,128)(2,1)S(1)}, u32[]{:S(2)}, u32[]{:S(2)}) collective-permute-start(bf16[64,512]{1,0:T(8,128)(2,1)S(1)} %get-tuple-element.29), channel_id=1, source_target_pairs={{0,8},{1,9},{2,10},{3,11},{4,12},{5,13},{6,14},{7,15},{8,0},{9,1},... | collective-permute-start | bytes 196616 | tf_op jit(solution)/shard_map/ppermute | solution.py:360
  9.9 16.4 %all-to-all-start = ((bf16[16,16,512]{2,1,0:T(8,128)(2,1)}), bf16[16,16,512]{2,1,0:T(8,128)(2,1)S(1)}, u32[]{:S(2)}, u32[]{:S(2)}) async-start(bf16[16,16,512]{2,1,0:T(8,128)(2,1)} %bitcast), calls=%async_computation | async-start | bytes 524288 | tf_op jit(solution)/shard_map/all_to_all | solution.py:352
  15.7 0.9 %copy-start.1 = (bf16[512,128]{1,0:T(8,128)(2,1)S(1)}, bf16[512,128]{1,0:T(8,128)(2,1)}, u32[]{:S(2)}) copy-start(bf16[512,128]{1,0:T(8,128)(2,1)} %gate_ref.1) | copy-start | bytes 393220
  15.7 0.9 %copy-start.2 = (bf16[2,64,64]{2,1,0:T(8,128)(2,1)S(1)}, bf16[2,64,64]{2,1,0:T(8,128)(2,1)}, u32[]{:S(2)}) copy-start(bf16[2,64,64]{2,1,0:T(8,128)(2,1)} %w_first_ref.1) | copy-start | bytes 49156
  15.7 10.6 %copy-start.3 = (bf16[2,256,256]{2,1,0:T(8,128)(2,1)S(1)}, bf16[2,256,256]{2,1,0:T(8,128)(2,1)}, u32[]{:S(2)}) copy-start(bf16[2,256,256]{2,1,0:T(8,128)(2,1)} %constant.11.clone.inner_ref) | copy-start | bytes 786436
  15.7 1.3 %collective-permute-start.1 = (bf16[64,512]{1,0:T(8,128)(2,1)S(1)}, bf16[64,512]{1,0:T(8,128)(2,1)S(1)}, u32[]{:S(2)}, u32[]{:S(2)}) collective-permute-start(bf16[64,512]{1,0:T(8,128)(2,1)S(1)} %shard_map.138), channel_id=1, source_target_pairs={{0,1},{1,0},{2,3},{3,2},{4,5},{5,4},{6,7},{7,6},{8,9},{9,8},{10,11... | collective-permute-start | bytes 196616 | tf_op jit(solution)/shard_map/ppermute | solution.py:360
  17.1 9.2 %copy-start.4 = (f32[64,256]{1,0:T(8,128)S(1)}, f32[64,256]{1,0:T(8,128)}, u32[]{:S(2)}) copy-start(f32[64,256]{1,0:T(8,128)} %constant.10.clone.twiddle_ref) | copy-start | bytes 196612
  17.1 9.2 %copy-start.5 = (bf16[2,64,128]{2,1,0:T(8,128)(2,1)S(1)}, bf16[2,64,128]{2,1,0:T(8,128)(2,1)}, u32[]{:S(2)}) copy-start(bf16[2,64,128]{2,1,0:T(8,128)(2,1)} %constant.9.clone.back_ref) | copy-start | bytes 98308
  17.1 9.2 %copy-start.6 = (bf16[128,128]{1,0:T(8,128)(2,1)S(1)}, bf16[128,128]{1,0:T(8,128)(2,1)}, u32[]{:S(2)}) copy-start(bf16[128,128]{1,0:T(8,128)(2,1)} %constant.8.clone.outer_ref) | copy-start | bytes 98308
  17.1 10.7 %collective-permute-start.2 = (bf16[32,512]{1,0:T(8,128)(2,1)S(1)}, bf16[32,512]{1,0:T(8,128)(2,1)S(1)}, u32[]{:S(2)}, u32[]{:S(2)}) collective-permute-start(bf16[32,512]{1,0:T(8,128)(2,1)S(1)} %get-tuple-element.31), channel_id=1, source_target_pairs={{0,2},{1,3},{2,4},{3,5},{4,6},{5,7},{6,0},{7,1},{8,10},{9,11},{10,... | collective-permute-start | bytes 98312 | tf_op jit(solution)/shard_map/ppermute | solution.py:360
  18.7 9.1 %collective-permute-start.3 = (bf16[32,512]{1,0:T(8,128)(2,1)S(1)}, bf16[32,512]{1,0:T(8,128)(2,1)S(1)}, u32[]{:S(2)}, u32[]{:S(2)}) collective-permute-start(bf16[32,512]{1,0:T(8,128)(2,1)S(1)} %get-tuple-element.32), channel_id=1, source_target_pairs={{0,4},{1,5},{2,6},{3,7},{4,0},{5,1},{6,2},{7,3},{8,12},{9,13},{10,... | collective-permute-start | bytes 98312 | tf_op jit(solution)/shard_map/ppermute | solution.py:360
  19.7 8.2 %collective-permute-start.4 = (bf16[32,512]{1,0:T(8,128)(2,1)S(1)}, bf16[32,512]{1,0:T(8,128)(2,1)S(1)}, u32[]{:S(2)}, u32[]{:S(2)}) collective-permute-start(bf16[32,512]{1,0:T(8,128)(2,1)S(1)} %get-tuple-element.33), channel_id=1, source_target_pairs={{0,6},{1,7},{2,0},{3,1},{4,2},{5,3},{6,4},{7,5},{8,14},{9,15},{10,... | collective-permute-start | bytes 98312 | tf_op jit(solution)/shard_map/ppermute | solution.py:360
  42.4 15.0 %all-to-all-start.2 = ((bf16[16,8,512]{2,1,0:T(8,128)(2,1)}), bf16[16,8,512]{2,1,0:T(8,128)(2,1)S(1)}, u32[]{:S(2)}, u32[]{:S(2)}) async-start(bf16[16,8,512]{2,1,0:T(8,128)(2,1)} %bitcast.4), calls=%async_computation.2 | async-start | bytes 262144 | tf_op jit(solution)/shard_map/all_to_all | solution.py:352
  49.6 7.7 %copy-start = (bf16[512,128]{1,0:T(8,128)(2,1)S(1)}, bf16[512,128]{1,0:T(8,128)(2,1)}, u32[]{:S(2)}) copy-start(bf16[512,128]{1,0:T(8,128)(2,1)} %d_out_ref.1) | copy-start | bytes 393220

commit v8 on v6

--- a/solution.py
+++ b/solution.py
@@ -121,7 +121,7 @@
     copies_of = ones_where(row == col % 32)
     row, col = iotas(128, 128)
     keep = row // 32 == col // 32
-    block = 2 * partner(row // 8 % 4, row // 32, 1) + row // 4 % 2
+    block = 2 * target(row) + row // 4 % 2
     order = ones_where((block == col % 32) & (row % 4 == col // 32))
     copies[0].wait()
     copies[1].wait()
@@ -152,6 +152,10 @@
         ref[...] = jnp.concatenate([v[8 * y : 8 * y + 8, :] for v in values], axis=0).astype(BF16)
 
 
+def target(col):
+    return partner(col // 8 % 4, col // 32, 1)
+
+
 def source(col):
     return partner(col // 32, col // 8 % 4, -1)
 
@@ -161,7 +165,7 @@
     row, col = iotas(64, 128)
     keep_row, keep_col = iotas(128, 128)
     keep = keep_row // 64 == keep_col // 4 % 2
-    for ref, group in ((blocks_ref, col // 8), (own_ref, source(col))):
+    for ref, group in ((blocks_ref, target(col)), (own_ref, source(col))):
         spread = dot(flat, ones_where(row == group * 4 + col % 4))
         ref[...] = jnp.where(keep, spread, 0.0).astype(BF16)
     gate_out_ref[...] = dot(unit(), gate_ref[...], NT)
@@ -268,9 +272,11 @@
     return jnp.concatenate([wide[16 * p : 16 * p + 8, :] for p in range(16)], axis=0)
 
 
-def mix_kernel(pair_ref, gate_ref, blocks_ref, mix_ref):
+def mix_kernel(pair_ref, gate_ref, blocks_ref, near_ref, core_ref, far_ref):
     product = (conv_rows(pair_ref) * gate_ref[...]).astype(BF16)
-    mix_ref[...] = dot(blocks_ref[...], product, TN).astype(BF16)
+    result = dot(blocks_ref[...], product, TN).astype(BF16)
+    for ref, start in zip((near_ref, core_ref, far_ref), (0, 32, 64)):
+        ref[...] = result[start : start + ref.shape[0], :]
 
 
 def first_kernel(pair_ref, gate_ref, returned_ref, own_ref, grad_gate_ref, partial_ref):
@@ -289,25 +295,37 @@
     partial_ref[...] = dot(order, dot(grad.astype(BF16), fold).astype(BF16))
 
 
-def second_kernel(received_ref, d_out_ref, partial_ref, grads_ref, sums_ref):
+def second_kernel(*refs):
+    pieces, (d_out_ref, partial_ref, sums_ref) = refs[:4], refs[4:]
+    received = jnp.concatenate([ref[...] for ref in pieces], axis=0)
     row, col = iotas(128, 128)
-    grad = jnp.where(row % 4 == col // 32, dot(received_ref[...], d_out_ref[...]), 0.0)
+    grad = jnp.where(row % 4 == col // 32, dot(received, d_out_ref[...]), 0.0)
+    order = ones_where((source(col) == row // 8) & (row % 8 == col % 8))
     row, col = iotas(128, 32)
     fold = ones_where(row % 32 == col)
-    pieces = [partial_ref[...]] + [dot(piece, fold) for piece in split(grad)]
-    sums_ref[:, 0:1024] = grads_ref[...]
-    sums_ref[:, 1024:1152] = jnp.concatenate(pieces, axis=1).astype(BF16)
-
-
-def exit_kernel(sums_ref, signal_hbm, filter_hbm, first_ref, second_ref, both_ref, sems):
+    parts = [dot(order, dot(piece, fold).astype(BF16)) for piece in split(grad)]
+    sums_ref[...] = jnp.concatenate([partial_ref[...]] + parts, axis=1).astype(BF16)
+
+
+def leave_all(pairs, sems):
+    copies = []
+    for index, (source, target) in enumerate(pairs):
+        copies.append(pltpu.make_async_copy(source, target, sems.at[index]))
+        copies[-1].start()
+    for copy in copies:
+        copy.wait()
+
+
+def exit_kernel(grads_ref, signal_hbm, filter_hbm, both_ref, sems):
     square = unit()
-    copies = []
-    for field, target in enumerate((signal_hbm, filter_hbm)):
-        values = sums_ref[:, 512 * field : 512 * field + 512]
+    for field in range(2):
+        values = grads_ref[:, 512 * field : 512 * field + 512]
         both_ref[field] = dot(values, square, TN).astype(BF16)
-        copies.append(pltpu.make_async_copy(both_ref.at[field], target, sems.at[field]))
-        copies[-1].start()
-    wide = sums_ref[:, 1024:1152].astype(F32)
+    leave_all(((both_ref.at[0], signal_hbm), (both_ref.at[1], filter_hbm)), sems)
+
+
+def sum_kernel(sums_ref, first_ref, second_ref):
+    wide = sums_ref[...].astype(F32)
     total = wide[0:8, :]
     for p in range(1, 16):
         total = total + wide[8 * p : 8 * p + 8, :]
@@ -316,8 +334,6 @@
         first_ref[i] = total[4 * i : 4 * i + 4, 0:64]
         for k in range(4):
             second_ref[k, i : i + 1, :] = second[4 * i + k : 4 * i + k + 1, :]
-    for copy in copies:
-        copy.wait()
 
 
 def call(body, outs, scratch=(), flops=1 << 26, moved=1 << 19, spaces=None):
@@ -350,6 +366,14 @@
         z, there, core = (index // 8 + zc // 2) % 2, (index // 2 + y) % 4, (index + zc) % 2
         pairs.append((index, z * 8 + there * 2 + core))
     return lax.ppermute(value, "ch", pairs)
+
+
+def cross(near, core, far):
+    rows, width = near.shape
+    half, quarter = ((2 * rows, width), BF16), ((rows, width), BF16)
+    core = shift(call(core_kernel, [half], flops=1 << 35)(core, far)[0], 0, 1)
+    near, *others = call(repack_kernel, [quarter] * 4)(near, core, far)
+    return near, lambda: [shift(value, y, 0) for y, value in zip((1, 2, 3), others)]
 
 
 def shards(signal, filter_raw, gate, d_out, w_first, w_second):
@@ -373,10 +397,9 @@
     )(*held)
     far = shift(far, 0, 2)
     pair = exchange(pair, "seq")
-    core = shift(call(core_kernel, [half], flops=1 << 35)(core, far)[0], 0, 1)
-    near, *others = call(repack_kernel, [quarter] * 4)(near, core, far)
+    near, turns = cross(near, core, far)
     pair = lax.optimization_barrier((pair, near))[0]
-    others = [shift(value, y, 0) for y, value in zip((1, 2, 3), others)]
+    others = turns()
     square = ((128, 128), BF16)
     gate, blocks, own = call(prepare_kernel, [((width, rows), F32), square, square])(gate, w_first)
     conv, spectra = call(
@@ -387,25 +410,31 @@
     )(pair, outer, back, twiddle, inner)
     pair, returned = call(gate_kernel, [double, single])(near, *others, own, gate, conv)
     pair = exchange(pair, "seq")
-    mix = call(mix_kernel, [single])(pair, gate, blocks)[0]
-    received = exchange(mix, "ch")
+    near, core, far = call(mix_kernel, [quarter + (True,), quarter + (True,), half + (True,)])(
+        pair, gate, blocks
+    )
+    far = shift(far, 0, 2)
     grads = call(
         adjoint_kernel,
         [((width, 2 * rows), BF16)],
         [pltpu.VMEM((2 * width * 4, 128), F32), pltpu.VMEM((width * 4, 128), F32)],
         flops=1 << 30,
     )(pair, spectra, outer, back, twiddle, inner)[0]
+    grads = exchange(grads, "seq")
     grad_gate, partial = call(first_kernel, [slab, ((width, 64), F32)])(
         pair, gate, returned, own
     )
-    sums = call(second_kernel, [((width, 2 * rows + 128), BF16)])(received, d_out, partial, grads)[0]
+    near, turns = cross(near, core, far)
+    sums = call(second_kernel, [((width, 128), BF16)])(near, *turns(), d_out, partial)[0]
+    sums, grads = lax.optimization_barrier((sums, grads))
     sums = exchange(sums, "seq")
-    grad_signal, grad_filter, grad_first, grad_second = call(
+    grad_signal, grad_filter = call(
         exit_kernel,
-        [slab, slab, ((2, 4, 64), F32), ((4, 2, 32), F32)],
+        [slab, slab],
         [pltpu.VMEM((2, rows, width), BF16), pltpu.SemaphoreType.DMA((2,))],
-        spaces=([pltpu.VMEM], [pl.ANY] * 2 + [pltpu.VMEM] * 2),
-    )(sums)
+        spaces=([pltpu.VMEM], [pl.ANY] * 2),
+    )(grads)
+    grad_first, grad_second = call(sum_kernel, [((2, 4, 64), F32), ((4, 2, 32), F32)])(sums)
     return (grad_signal, grad_filter, grad_gate, grad_first, grad_second)
 
 

time: 75.9 us -> 76.8 us (1.012)
  blocking collectives: 29.2 us -> 13.5 us
  starting transfers between devices: 24.3 us -> 35.8 us
  waiting for transfers between devices: 10.1 us -> 14.4 us
  Pallas kernels: 9.8 us -> 10.8 us
    all_to_all x2 -> x1, blocking collectives: 29.2 us -> 13.5 us  [exchange(): lax.all_to_all(pieces, axis, split_axis=0, concat_axis=0, tiled=True)]
    ppermute x5 -> x10, starting transfers between devices: 12.4 us -> 19.4 us  [shift(): return lax.ppermute(value, 'ch', pairs)]
    all_to_all x2 -> x3, starting transfers between devices: 11.9 us -> 16.4 us  [exchange(): lax.all_to_all(pieces, axis, split_axis=0, concat_axis=0, tiled=True)]
    ppermute x5 -> x10, waiting for transfers between devices: 0.27 us -> 3.16 us  [shift(): return lax.ppermute(value, 'ch', pairs)]
    all_to_all x2 -> x3, waiting for transfers between devices: 9.87 us -> 11.2 us  [exchange(): lax.all_to_all(pieces, axis, split_axis=0, concat_axis=0, tiled=True)]
    pallas_call x5 -> x8, Pallas kernels: 2.81 us -> 3.09 us  [the longest x1 1.13 us: shards(): call(second_kernel, [((width, 128), BF16)])(near, *turns(), d_out, partial)]
  transfers between devices with their start and end apart: 7 -> 13, of which waited for: 3 -> 7; matrix products, arithmetic and copies ran while one was open for 0% -> 0% of each run, Pallas kernels for 6% -> 10%
where the time goes in v8:
time: 76.8 us; the launch traced here: 76.1 us
  starting transfers between devices  35.8 us (47%)
  waiting for transfers between devices  14.4 us (19%)
  blocking collectives  13.5 us (18%)
  Pallas kernels  10.8 us (14%)
  between operations  0.81 us (1%)
  local copies, waits for them, and re-layouts  0.79 us (1%)
    ppermute x10, starting transfers between devices, shift(): return lax.ppermute(value, 'ch', pairs)  19.4 us
    all_to_all x3, starting transfers between devices, exchange(): lax.all_to_all(pieces, axis, split_axis=0, concat_axis=0, tiled=True)  16.4 us
    all_to_all x1, blocking collectives, exchange(): lax.all_to_all(pieces, axis, split_axis=0, concat_axis=0, tiled=True)  13.5 us
    all_to_all x3, waiting for transfers between devices, exchange(): lax.all_to_all(pieces, axis, split_axis=0, concat_axis=0, tiled=True)  11.2 us
    ppermute x10, waiting for transfers between devices, shift(): return lax.ppermute(value, 'ch', pairs)  3.16 us
    pallas_call x1, Pallas kernels, shards(): call(adjoint_kernel, [((width, 2 * rows), BF16)], [pltpu.VMEM((2 * width...  2.73 us
    pallas_call x1, Pallas kernels, shards(): call(entry_kernel, [quarter + (True,), quarter + (True,), half + (True,),...  1.97 us
  transfers between devices with their start and end apart: 13, of which 7 were waited for; matrix products, arithmetic and copies ran while one was open for 0% of the time, Pallas kernels for 10%

profile of v8, /device:TPU:8, one launch (start us, length us, event | category | flops | bytes accessed | tf_op | source)
XLA Modules:
  0.0 76.1 jit_solution(7172700771724594362)
XLA Ops:
  0.6 2.0 %shard_map.137 = (bf16[32,512]{1,0:T(8,128)(2,1)S(1)}, bf16[32,512]{1,0:T(8,128)(2,1)S(1)}, bf16[64,512]{1,0:T(8,128)(2,1)S(1)}, bf16[256,512]{1,0:T(8,128)(2,1)}) custom-call(bf16[512,128]{1,0:T(8,128)(2,1)} %refs_4_.1, bf16[4,32,32]{2,1,0:T(8,128)(2,1)} %w_second_hbm.1, bf16[512,128]{1,0:T(8,128)(2,1)} %signal_hbm.1, bf16[512,128]{1,0:T(8,128)(2,1)} %filter_hbm.1), custom_call_target="tpu_custom_call" | custom-call | flops 67108864 | bytes 524288 | tf_op jit(solution)/shard_map/pallas_call | solution.py:386
  2.6 7.3 %collective-permute-start = (bf16[64,512]{1,0:T(8,128)(2,1)S(1)}, bf16[64,512]{1,0:T(8,128)(2,1)S(1)}, u32[]{:S(2)}, u32[]{:S(2)}) collective-permute-start(bf16[64,512]{1,0:T(8,128)(2,1)S(1)} %get-tuple-element.38), channel_id=1, source_target_pairs={{0,8},{1,9},{2,10},{3,11},{4,12},{5,13},{6,14},{7,15},{8,0},{9,1},... | collective-permute-start | bytes 196616 | tf_op jit(solution)/shard_map/ppermute | solution.py:368
  9.9 5.8 %all-to-all-start = ((bf16[16,16,512]{2,1,0:T(8,128)(2,1)}), bf16[16,16,512]{2,1,0:T(8,128)(2,1)S(1)}, u32[]{:S(2)}, u32[]{:S(2)}) async-start(bf16[16,16,512]{2,1,0:T(8,128)(2,1)} %bitcast), calls=%async_computation | async-start | bytes 524288 | tf_op jit(solution)/shard_map/all_to_all | solution.py:360
  15.7 0.0 collective-permute-done.far_ref
  15.7 0.0 copy-start.1
  15.7 0.0 copy-start.2
  15.7 0.0 copy-start.3
  15.7 0.1 collective-permute-start.1
  15.8 0.8 copy-done.1
  16.6 0.0 copy-done.2
  16.6 0.2 shard_map.140
  16.8 0.2 collective-permute-done.1.core_ref
  17.1 0.0 copy-start.4
  17.1 0.0 copy-start.5
  17.1 0.0 copy-start.6
  17.1 1.7 %collective-permute-start.2 = (bf16[32,512]{1,0:T(8,128)(2,1)S(1)}, bf16[32,512]{1,0:T(8,128)(2,1)S(1)}, u32[]{:S(2)}, u32[]{:S(2)}) collective-permute-start(bf16[32,512]{1,0:T(8,128)(2,1)S(1)} %get-tuple-element.40), channel_id=1, source_target_pairs={{0,2},{1,3},{2,4},{3,5},{4,6},{5,7},{6,0},{7,1},{8,10},{9,11},{10,... | collective-permute-start | bytes 98312 | tf_op jit(solution)/shard_map/ppermute | solution.py:368
  18.7 0.9 %collective-permute-start.3 = (bf16[32,512]{1,0:T(8,128)(2,1)S(1)}, bf16[32,512]{1,0:T(8,128)(2,1)S(1)}, u32[]{:S(2)}, u32[]{:S(2)}) collective-permute-start(bf16[32,512]{1,0:T(8,128)(2,1)S(1)} %get-tuple-element.41), channel_id=1, source_target_pairs={{0,4},{1,5},{2,6},{3,7},{4,0},{5,1},{6,2},{7,3},{8,12},{9,13},{10,... | collective-permute-start | bytes 98312 | tf_op jit(solution)/shard_map/ppermute | solution.py:368
  19.7 2.4 %collective-permute-start.4 = (bf16[32,512]{1,0:T(8,128)(2,1)S(1)}, bf16[32,512]{1,0:T(8,128)(2,1)S(1)}, u32[]{:S(2)}, u32[]{:S(2)}) collective-permute-start(bf16[32,512]{1,0:T(8,128)(2,1)S(1)} %get-tuple-element.42), channel_id=1, source_target_pairs={{0,6},{1,7},{2,0},{3,1},{4,2},{5,3},{6,4},{7,5},{8,14},{9,15},{10,... | collective-permute-start | bytes 98312 | tf_op jit(solution)/shard_map/ppermute | solution.py:368
  22.1 4.2 %all-to-all-done = bf16[16,16,512]{2,1,0:T(8,128)(2,1)S(1)} async-done(((bf16[16,16,512]{2,1,0:T(8,128)(2,1)}), bf16[16,16,512]{2,1,0:T(8,128)(2,1)S(1)}, u32[]{:S(2)}, u32[]{:S(2)}) %all-to-all-start) | async-done | bytes 262176 | tf_op jit(solution)/shard_map/all_to_all | solution.py:360
  26.3 0.0 copy-done.3
  26.3 0.0 copy-done.4
  26.3 0.0 copy-done.5
  26.3 0.0 copy-done.6
  26.3 1.5 %shard_map.141 = (f32[512,128]{1,0:T(8,128)S(1)}, f32[2,512,256]{2,1,0:T(8,128)S(1)}) custom-call(bf16[256,512]{1,0:T(8,128)(2,1)S(1)} %bitcast.12, bf16[128,128]{1,0:T(8,128)(2,1)S(1)} %copy-done.6, bf16[2,64,128]{2,1,0:T(8,128)(2,1)S(1)} %copy-done.5, f32[64,256]{1,0:T(8,128)S(1)} %copy-done.4, bf16[2,256,256]{2,1,0:T(8,128)(2,1)S(1)} %copy-done.3), custom_call_target="tpu_custom_call" | custom-call | flops 1073741824 | bytes 524288 | tf_op jit(solution)/shard_map/pallas_call | solution.py:405
  27.8 0.0 collective-permute-done.2.first_ref
  27.8 0.0 collective-permute-done.3.second_ref
  27.8 0.0 collective-permute-done.4.third_ref
  27.9 0.2 shard_map.142
  28.0 13.5 %all_to_all.20 = bf16[16,16,512]{2,1,0:T(8,128)(2,1)S(1)} all-to-all(bf16[16,16,512]{2,1,0:T(8,128)(2,1)S(1)} %bitcast.13), channel_id=1, replica_groups=mesh['seq'=16,'ch'=16] {'seq'}, dimensions={0} | all-to-all | bytes 524288 | tf_op jit(solution)/shard_map/all_to_all | solution.py:360
  41.5 0.2 shard_map.143
  41.8 1.5 %collective-permute-start.5 = (bf16[64,512]{1,0:T(8,128)(2,1)S(1)}, bf16[64,512]{1,0:T(8,128)(2,1)S(1)}, u32[]{:S(2)}, u32[]{:S(2)}) collective-permute-start(bf16[64,512]{1,0:T(8,128)(2,1)S(1)} %get-tuple-element.52), channel_id=1, source_target_pairs={{0,8},{1,9},{2,10},{3,11},{4,12},{5,13},{6,14},{7,15},{8,0},{9,1},... | collective-permute-start | bytes 196616 | tf_op jit(solution)/shard_map/ppermute | solution.py:368
  43.3 2.7 %shard_map.148 = bf16[128,1024]{1,0:T(8,128)(2,1)} custom-call(bf16[256,512]{1,0:T(8,128)(2,1)S(1)} %bitcast.9, f32[2,512,256]{2,1,0:T(8,128)S(1)} %get-tuple-element.59.spectra_ref, bf16[128,128]{1,0:T(8,128)(2,1)S(1)} %copy-done.6, bf16[2,64,128]{2,1,0:T(8,128)(2,1)S(1)} %copy-done.5, f32[64,256]{1,0:T(8,128)S(1)} %copy-done.4, ...), custom_call_target="tpu_custom_call" | custom-call | flops 1073741824 | bytes 524288 | tf_op jit(solution)/shard_map/pallas_call | solution.py:417
  46.0 3.5 %all-to-all-start.2 = ((bf16[16,8,1024]{2,1,0:T(8,128)(2,1)}), bf16[16,8,1024]{2,1,0:T(8,128)(2,1)S(1)}, u32[]{:S(2)}, u32[]{:S(2)}) async-start(bf16[16,8,1024]{2,1,0:T(8,128)(2,1)} %bitcast.4), calls=%async_computation.2 | async-start | bytes 524288 | tf_op jit(solution)/shard_map/all_to_all | solution.py:360
  49.6 0.5 collective-permute-done.5.far_ref
  50.0 0.0 collective-permute-start.6
  50.0 1.2 %collective-permute-done.6.core_ref = bf16[64,512]{1,0:T(8,128)(2,1)S(1)} collective-permute-done((bf16[64,512]{1,0:T(8,128)(2,1)S(1)}, bf16[64,512]{1,0:T(8,128)(2,1)S(1)}, u32[]{:S(2)}, u32[]{:S(2)}) %collective-permute-start.6) | collective-permute-done | bytes 65568 | tf_op jit(solution)/shard_map/ppermute | solution.py:368
  51.3 1.5 %collective-permute-start.7 = (bf16[32,512]{1,0:T(8,128)(2,1)S(1)}, bf16[32,512]{1,0:T(8,128)(2,1)S(1)}, u32[]{:S(2)}, u32[]{:S(2)}) collective-permute-start(bf16[32,512]{1,0:T(8,128)(2,1)S(1)} %get-tuple-element.54), channel_id=1, source_target_pairs={{0,2},{1,3},{2,4},{3,5},{4,6},{5,7},{6,0},{7,1},{8,10},{9,11},{10,... | collective-permute-start | bytes 98312 | tf_op jit(solution)/shard_map/ppermute | solution.py:368
  52.8 2.4 %collective-permute-start.8 = (bf16[32,512]{1,0:T(8,128)(2,1)S(1)}, bf16[32,512]{1,0:T(8,128)(2,1)S(1)}, u32[]{:S(2)}, u32[]{:S(2)}) collective-permute-start(bf16[32,512]{1,0:T(8,128)(2,1)S(1)} %get-tuple-element.55), channel_id=1, source_target_pairs={{0,4},{1,5},{2,6},{3,7},{4,0},{5,1},{6,2},{7,3},{8,12},{9,13},{10,... | collective-permute-start | bytes 98312 | tf_op jit(solution)/shard_map/ppermute | solution.py:368
  55.2 1.7 %collective-permute-start.9 = (bf16[32,512]{1,0:T(8,128)(2,1)S(1)}, bf16[32,512]{1,0:T(8,128)(2,1)S(1)}, u32[]{:S(2)}, u32[]{:S(2)}) collective-permute-start(bf16[32,512]{1,0:T(8,128)(2,1)S(1)} %get-tuple-element.56), channel_id=1, source_target_pairs={{0,6},{1,7},{2,0},{3,1},{4,2},{5,3},{6,4},{7,5},{8,14},{9,15},{10,... | collective-permute-start | bytes 98312 | tf_op jit(solution)/shard_map/ppermute | solution.py:368
  56.8 0.0 copy-start
  56.8 1.1 %shard_map.146 = (bf16[512,128]{1,0:T(8,128)(2,1)}, f32[128,64]{1,0:T(8,128)S(1)}) custom-call(bf16[256,512]{1,0:T(8,128)(2,1)S(1)} %bitcast.10, f32[128,512]{1,0:T(8,128)S(1)} %get-tuple-element.44.gate_ref, bf16[128,512]{1,0:T(8,128)(2,1)S(1)} %get-tuple-element.57.returned_ref, bf16[128,128]{1,0:T(8,128)(2,1)S(1)} %get-tuple-element.43.own_ref), custom_call_target="tpu_custom_call" | custom-call | flops 67108864 | bytes 524288 | tf_op jit(solution)/shard_map/pallas_call | solution.py:424
  57.9 0.0 collective-permute-done.7.refs_1_
  57.9 0.4 collective-permute-done.8.refs_2_
  58.2 0.8 %collective-permute-done.9.refs_3_ = bf16[32,512]{1,0:T(8,128)(2,1)S(1)} collective-permute-done((bf16[32,512]{1,0:T(8,128)(2,1)S(1)}, bf16[32,512]{1,0:T(8,128)(2,1)S(1)}, u32[]{:S(2)}, u32[]{:S(2)}) %collective-permute-start.9) | collective-permute-done | bytes 32800 | tf_op jit(solution)/shard_map/ppermute | solution.py:368
  59.1 0.0 copy-done
  59.1 1.1 %shard_map.147 = bf16[128,128]{1,0:T(8,128)(2,1)} custom-call(bf16[32,512]{1,0:T(8,128)(2,1)S(1)} %get-tuple-element.53.refs_0_, bf16[32,512]{1,0:T(8,128)(2,1)S(1)} %collective-permute-done.7.refs_1_, bf16[32,512]{1,0:T(8,128)(2,1)S(1)} %collective-permute-done.8.refs_2_, bf16[32,512]{1,0:T(8,128)(2,1)S(1)} %collective-permute-done.9.refs_3_, ...), custom_call_target="tpu_custom_call" | custom-call | flops 67108864 | bytes 524288 | tf_op jit(solution)/shard_map/pallas_call | solution.py:428
  60.2 0.0 all-to-all-done.2
  60.2 7.1 %all-to-all-start.3 = ((bf16[16,8,128]{2,1,0:T(8,128)(2,1)}), bf16[16,8,128]{2,1,0:T(8,128)(2,1)S(1)}, u32[]{:S(2)}, u32[]{:S(2)}) async-start(bf16[16,8,128]{2,1,0:T(8,128)(2,1)} %bitcast.6), calls=%async_computation.3 | async-start | bytes 65536 | tf_op jit(solution)/shard_map/all_to_all | solution.py:360
  67.3 1.0 %shard_map.149 = (bf16[512,128]{1,0:T(8,128)(2,1)}, bf16[512,128]{1,0:T(8,128)(2,1)}) custom-call(bf16[128,1024]{1,0:T(8,128)(2,1)S(1)} %bitcast.11), custom_call_target="tpu_custom_call" | custom-call | flops 67108864 | bytes 524288 | tf_op jit(solution)/shard_map/pallas_call | solution.py:431
  68.3 7.0 %all-to-all-done.3 = bf16[16,8,128]{2,1,0:T(8,128)(2,1)S(1)} async-done(((bf16[16,8,128]{2,1,0:T(8,128)(2,1)}), bf16[16,8,128]{2,1,0:T(8,128)(2,1)S(1)}, u32[]{:S(2)}, u32[]{:S(2)}) %all-to-all-start.3) | async-done | bytes 32800 | tf_op jit(solution)/shard_map/all_to_all | solution.py:360
  75.3 0.8 shard_map.150
  (4 shorter events, 0.0 us)
Async XLA Ops:
  2.6 13.1 %collective-permute-start = (bf16[64,512]{1,0:T(8,128)(2,1)S(1)}, bf16[64,512]{1,0:T(8,128)(2,1)S(1)}, u32[]{:S(2)}, u32[]{:S(2)}) collective-permute-start(bf16[64,512]{1,0:T(8,128)(2,1)S(1)} %get-tuple-element.38), channel_id=1, source_target_pairs={{0,8},{1,9},{2,10},{3,11},{4,12},{5,13},{6,14},{7,15},{8,0},{9,1},... | collective-permute-start | bytes 196616 | tf_op jit(solution)/shard_map/ppermute | solution.py:368
  9.9 16.4 %all-to-all-start = ((bf16[16,16,512]{2,1,0:T(8,128)(2,1)}), bf16[16,16,512]{2,1,0:T(8,128)(2,1)S(1)}, u32[]{:S(2)}, u32[]{:S(2)}) async-start(bf16[16,16,512]{2,1,0:T(8,128)(2,1)} %bitcast), calls=%async_computation | async-start | bytes 524288 | tf_op jit(solution)/shard_map/all_to_all | solution.py:360
  15.7 0.9 %copy-start.1 = (bf16[512,128]{1,0:T(8,128)(2,1)S(1)}, bf16[512,128]{1,0:T(8,128)(2,1)}, u32[]{:S(2)}) copy-start(bf16[512,128]{1,0:T(8,128)(2,1)} %gate_ref.1) | copy-start | bytes 393220
  15.7 0.9 %copy-start.2 = (bf16[2,64,64]{2,1,0:T(8,128)(2,1)S(1)}, bf16[2,64,64]{2,1,0:T(8,128)(2,1)}, u32[]{:S(2)}) copy-start(bf16[2,64,64]{2,1,0:T(8,128)(2,1)} %w_first_ref.1) | copy-start | bytes 49156
  15.7 10.6 %copy-start.3 = (bf16[2,256,256]{2,1,0:T(8,128)(2,1)S(1)}, bf16[2,256,256]{2,1,0:T(8,128)(2,1)}, u32[]{:S(2)}) copy-start(bf16[2,256,256]{2,1,0:T(8,128)(2,1)} %constant.11.clone.inner_ref) | copy-start | bytes 786436
  15.7 1.3 %collective-permute-start.1 = (bf16[64,512]{1,0:T(8,128)(2,1)S(1)}, bf16[64,512]{1,0:T(8,128)(2,1)S(1)}, u32[]{:S(2)}, u32[]{:S(2)}) collective-permute-start(bf16[64,512]{1,0:T(8,128)(2,1)S(1)} %shard_map.138), channel_id=1, source_target_pairs={{0,1},{1,0},{2,3},{3,2},{4,5},{5,4},{6,7},{7,6},{8,9},{9,8},{10,11... | collective-permute-start | bytes 196616 | tf_op jit(solution)/shard_map/ppermute | solution.py:368
  17.1 9.2 %copy-start.4 = (f32[64,256]{1,0:T(8,128)S(1)}, f32[64,256]{1,0:T(8,128)}, u32[]{:S(2)}) copy-start(f32[64,256]{1,0:T(8,128)} %constant.10.clone.twiddle_ref) | copy-start | bytes 196612
  17.1 9.2 %copy-start.5 = (bf16[2,64,128]{2,1,0:T(8,128)(2,1)S(1)}, bf16[2,64,128]{2,1,0:T(8,128)(2,1)}, u32[]{:S(2)}) copy-start(bf16[2,64,128]{2,1,0:T(8,128)(2,1)} %constant.9.clone.back_ref) | copy-start | bytes 98308
  17.1 9.2 %copy-start.6 = (bf16[128,128]{1,0:T(8,128)(2,1)S(1)}, bf16[128,128]{1,0:T(8,128)(2,1)}, u32[]{:S(2)}) copy-start(bf16[128,128]{1,0:T(8,128)(2,1)} %constant.8.clone.outer_ref) | copy-start | bytes 98308
  17.1 10.7 %collective-permute-start.2 = (bf16[32,512]{1,0:T(8,128)(2,1)S(1)}, bf16[32,512]{1,0:T(8,128)(2,1)S(1)}, u32[]{:S(2)}, u32[]{:S(2)}) collective-permute-start(bf16[32,512]{1,0:T(8,128)(2,1)S(1)} %get-tuple-element.40), channel_id=1, source_target_pairs={{0,2},{1,3},{2,4},{3,5},{4,6},{5,7},{6,0},{7,1},{8,10},{9,11},{10,... | collective-permute-start | bytes 98312 | tf_op jit(solution)/shard_map/ppermute | solution.py:368
  18.7 9.1 %collective-permute-start.3 = (bf16[32,512]{1,0:T(8,128)(2,1)S(1)}, bf16[32,512]{1,0:T(8,128)(2,1)S(1)}, u32[]{:S(2)}, u32[]{:S(2)}) collective-permute-start(bf16[32,512]{1,0:T(8,128)(2,1)S(1)} %get-tuple-element.41), channel_id=1, source_target_pairs={{0,4},{1,5},{2,6},{3,7},{4,0},{5,1},{6,2},{7,3},{8,12},{9,13},{10,... | collective-permute-start | bytes 98312 | tf_op jit(solution)/shard_map/ppermute | solution.py:368
  19.7 8.2 %collective-permute-start.4 = (bf16[32,512]{1,0:T(8,128)(2,1)S(1)}, bf16[32,512]{1,0:T(8,128)(2,1)S(1)}, u32[]{:S(2)}, u32[]{:S(2)}) collective-permute-start(bf16[32,512]{1,0:T(8,128)(2,1)S(1)} %get-tuple-element.42), channel_id=1, source_target_pairs={{0,6},{1,7},{2,0},{3,1},{4,2},{5,3},{6,4},{7,5},{8,14},{9,15},{10,... | collective-permute-start | bytes 98312 | tf_op jit(solution)/shard_map/ppermute | solution.py:368
  41.8 8.3 %collective-permute-start.5 = (bf16[64,512]{1,0:T(8,128)(2,1)S(1)}, bf16[64,512]{1,0:T(8,128)(2,1)S(1)}, u32[]{:S(2)}, u32[]{:S(2)}) collective-permute-start(bf16[64,512]{1,0:T(8,128)(2,1)S(1)} %get-tuple-element.52), channel_id=1, source_target_pairs={{0,8},{1,9},{2,10},{3,11},{4,12},{5,13},{6,14},{7,15},{8,0},{9,1},... | collective-permute-start | bytes 196616 | tf_op jit(solution)/shard_map/ppermute | solution.py:368
  46.0 14.2 %all-to-all-start.2 = ((bf16[16,8,1024]{2,1,0:T(8,128)(2,1)}), bf16[16,8,1024]{2,1,0:T(8,128)(2,1)S(1)}, u32[]{:S(2)}, u32[]{:S(2)}) async-start(bf16[16,8,1024]{2,1,0:T(8,128)(2,1)} %bitcast.4), calls=%async_computation.2 | async-start | bytes 524288 | tf_op jit(solution)/shard_map/all_to_all | solution.py:360
  50.0 1.3 %collective-permute-start.6 = (bf16[64,512]{1,0:T(8,128)(2,1)S(1)}, bf16[64,512]{1,0:T(8,128)(2,1)S(1)}, u32[]{:S(2)}, u32[]{:S(2)}) collective-permute-start(bf16[64,512]{1,0:T(8,128)(2,1)S(1)} %shard_map.144), channel_id=1, source_target_pairs={{0,1},{1,0},{2,3},{3,2},{4,5},{5,4},{6,7},{7,6},{8,9},{9,8},{10,11... | collective-permute-start | bytes 196616 | tf_op jit(solution)/shard_map/ppermute | solution.py:368
  51.3 6.6 %collective-permute-start.7 = (bf16[32,512]{1,0:T(8,128)(2,1)S(1)}, bf16[32,512]{1,0:T(8,128)(2,1)S(1)}, u32[]{:S(2)}, u32[]{:S(2)}) collective-permute-start(bf16[32,512]{1,0:T(8,128)(2,1)S(1)} %get-tuple-element.54), channel_id=1, source_target_pairs={{0,2},{1,3},{2,4},{3,5},{4,6},{5,7},{6,0},{7,1},{8,10},{9,11},{10,... | collective-permute-start | bytes 98312 | tf_op jit(solution)/shard_map/ppermute | solution.py:368
  52.8 5.4 %collective-permute-start.8 = (bf16[32,512]{1,0:T(8,128)(2,1)S(1)}, bf16[32,512]{1,0:T(8,128)(2,1)S(1)}, u32[]{:S(2)}, u32[]{:S(2)}) collective-permute-start(bf16[32,512]{1,0:T(8,128)(2,1)S(1)} %get-tuple-element.55), channel_id=1, source_target_pairs={{0,4},{1,5},{2,6},{3,7},{4,0},{5,1},{6,2},{7,3},{8,12},{9,13},{10,... | collective-permute-start | bytes 98312 | tf_op jit(solution)/shard_map/ppermute | solution.py:368
  55.2 3.9 %collective-permute-start.9 = (bf16[32,512]{1,0:T(8,128)(2,1)S(1)}, bf16[32,512]{1,0:T(8,128)(2,1)S(1)}, u32[]{:S(2)}, u32[]{:S(2)}) collective-permute-start(bf16[32,512]{1,0:T(8,128)(2,1)S(1)} %get-tuple-element.56), channel_id=1, source_target_pairs={{0,6},{1,7},{2,0},{3,1},{4,2},{5,3},{6,4},{7,5},{8,14},{9,15},{10,... | collective-permute-start | bytes 98312 | tf_op jit(solution)/shard_map/ppermute | solution.py:368
  56.8 2.3 %copy-start = (bf16[512,128]{1,0:T(8,128)(2,1)S(1)}, bf16[512,128]{1,0:T(8,128)(2,1)}, u32[]{:S(2)}) copy-start(bf16[512,128]{1,0:T(8,128)(2,1)} %refs_4_.1) | copy-start | bytes 393220
  60.2 15.1 %all-to-all-start.3 = ((bf16[16,8,128]{2,1,0:T(8,128)(2,1)}), bf16[16,8,128]{2,1,0:T(8,128)(2,1)S(1)}, u32[]{:S(2)}, u32[]{:S(2)}) async-start(bf16[16,8,128]{2,1,0:T(8,128)(2,1)} %bitcast.6), calls=%async_computation.3 | async-start | bytes 65536 | tf_op jit(solution)/shard_map/all_to_all | solution.py:360

commit v9 on v7

--- a/solution.py
+++ b/solution.py
@@ -395,8 +395,6 @@
     )(pair, outer, back, twiddle, inner)
     pair, returned = call(gate_kernel, [double, single])(near, *others, own, gate, conv)
     pair = exchange(pair, "seq")
-    mix = call(mix_kernel, [single])(pair, gate, blocks)[0]
-    received = exchange(mix, "ch")
     grads = call(
         adjoint_kernel,
         [((width, 2 * rows), BF16)],
@@ -406,6 +404,9 @@
     grad_gate, partial = call(first_kernel, [slab, ((width, 64), F32)])(
         pair, gate, returned, own
     )
+    pair, grads, partial = lax.optimization_barrier((pair, grads, partial))
+    mix = call(mix_kernel, [single])(pair, gate, blocks)[0]
+    received = exchange(mix, "ch")
     sums = call(second_kernel, [((width, 2 * rows + 128), BF16)])(received, d_out, partial, grads)[0]
     sums = exchange(sums, "seq")
     grad_signal, grad_filter, grad_first, grad_second = call(

time: 75.4 us -> 77.7 us (1.031)
  blocking collectives: 29.2 us -> 44 us
  starting transfers between devices: 24.3 us -> 18.1 us
  waiting for transfers between devices: 10.1 us -> 4.44 us
    all_to_all x2 -> x3, blocking collectives: 29.2 us -> 44 us  [exchange(): lax.all_to_all(pieces, axis, split_axis=0, concat_axis=0, tiled=True)]
    all_to_all x2 -> x1, starting transfers between devices: 11.9 us -> 5.77 us  [exchange(): lax.all_to_all(pieces, axis, split_axis=0, concat_axis=0, tiled=True)]
    all_to_all x2 -> x1, waiting for transfers between devices: 9.87 us -> 4.18 us  [exchange(): lax.all_to_all(pieces, axis, split_axis=0, concat_axis=0, tiled=True)]
  transfers between devices with their start and end apart: 7 -> 6, of which waited for: 3 -> 2; matrix products, arithmetic and copies ran while one was open for 0% -> 0% of each run, Pallas kernels for 7% -> 2%
where the time goes in v9:
time: 77.7 us; the launch traced here: 76.8 us
  blocking collectives  44 us (57%)
  starting transfers between devices  18.1 us (23%)
  Pallas kernels  8.58 us (11%)
  waiting for transfers between devices  4.44 us (6%)
  local copies, waits for them, and re-layouts  0.79 us (1%)
  between operations  0.79 us (1%)
    all_to_all x3, blocking collectives, exchange(): lax.all_to_all(pieces, axis, split_axis=0, concat_axis=0, tiled=True)  44 us
    ppermute x5, starting transfers between devices, shift(): return lax.ppermute(value, 'ch', pairs)  12.4 us
    all_to_all x1, starting transfers between devices, exchange(): lax.all_to_all(pieces, axis, split_axis=0, concat_axis=0, tiled=True)  5.77 us
    all_to_all x1, waiting for transfers between devices, exchange(): lax.all_to_all(pieces, axis, split_axis=0, concat_axis=0, tiled=True)  4.18 us
    pallas_call x1, Pallas kernels, shards(): call(adjoint_kernel, [((width, 2 * rows), BF16)], [pltpu.VMEM((2 * width...  2.03 us
    pallas_call x1, Pallas kernels, shards(): call(entry_kernel, [quarter + (True,), quarter + (True,), half + (True,),...  1.98 us
  transfers between devices with their start and end apart: 6, of which 2 were waited for; matrix products, arithmetic and copies ran while one was open for 0% of the time, Pallas kernels for 2%

profile of v9, /device:TPU:8, one launch (start us, length us, event | category | flops | bytes accessed | tf_op | source)
XLA Modules:
  0.0 76.8 jit_solution(12552357967875296665)
XLA Ops:
  0.6 2.0 %shard_map.137 = (bf16[32,512]{1,0:T(8,128)(2,1)S(1)}, bf16[32,512]{1,0:T(8,128)(2,1)S(1)}, bf16[64,512]{1,0:T(8,128)(2,1)S(1)}, bf16[256,512]{1,0:T(8,128)(2,1)}) custom-call(bf16[512,128]{1,0:T(8,128)(2,1)} %d_out_ref.1, bf16[4,32,32]{2,1,0:T(8,128)(2,1)} %w_second_hbm.1, bf16[512,128]{1,0:T(8,128)(2,1)} %signal_hbm.1, bf16[512,128]{1,0:T(8,128)(2,1)} %filter_hbm.1), custom_call_target="tpu_custom_call" | custom-call | flops 67108864 | bytes 524288 | tf_op jit(solution)/shard_map/pallas_call | solution.py:370
  2.6 7.3 %collective-permute-start = (bf16[64,512]{1,0:T(8,128)(2,1)S(1)}, bf16[64,512]{1,0:T(8,128)(2,1)S(1)}, u32[]{:S(2)}, u32[]{:S(2)}) collective-permute-start(bf16[64,512]{1,0:T(8,128)(2,1)S(1)} %get-tuple-element.32), channel_id=1, source_target_pairs={{0,8},{1,9},{2,10},{3,11},{4,12},{5,13},{6,14},{7,15},{8,0},{9,1},... | collective-permute-start | bytes 196616 | tf_op jit(solution)/shard_map/ppermute | solution.py:360
  9.9 5.8 %all-to-all-start = ((bf16[16,16,512]{2,1,0:T(8,128)(2,1)}), bf16[16,16,512]{2,1,0:T(8,128)(2,1)S(1)}, u32[]{:S(2)}, u32[]{:S(2)}) async-start(bf16[16,16,512]{2,1,0:T(8,128)(2,1)} %bitcast), calls=%async_computation | async-start | bytes 524288 | tf_op jit(solution)/shard_map/all_to_all | solution.py:352
  15.7 0.0 collective-permute-done.far_ref
  15.7 0.0 copy-start.1
  15.7 0.0 copy-start.2
  15.7 0.0 copy-start.3
  15.7 0.1 collective-permute-start.1
  15.8 0.8 copy-done.1
  16.6 0.0 copy-done.2
  16.6 0.2 shard_map.140
  16.8 0.3 collective-permute-done.1.core_ref
  17.1 0.0 copy-start.4
  17.1 0.0 copy-start.5
  17.1 0.0 copy-start.6
  17.1 1.7 %collective-permute-start.2 = (bf16[32,512]{1,0:T(8,128)(2,1)S(1)}, bf16[32,512]{1,0:T(8,128)(2,1)S(1)}, u32[]{:S(2)}, u32[]{:S(2)}) collective-permute-start(bf16[32,512]{1,0:T(8,128)(2,1)S(1)} %get-tuple-element.34), channel_id=1, source_target_pairs={{0,2},{1,3},{2,4},{3,5},{4,6},{5,7},{6,0},{7,1},{8,10},{9,11},{10,... | collective-permute-start | bytes 98312 | tf_op jit(solution)/shard_map/ppermute | solution.py:360
  18.7 0.9 %collective-permute-start.3 = (bf16[32,512]{1,0:T(8,128)(2,1)S(1)}, bf16[32,512]{1,0:T(8,128)(2,1)S(1)}, u32[]{:S(2)}, u32[]{:S(2)}) collective-permute-start(bf16[32,512]{1,0:T(8,128)(2,1)S(1)} %get-tuple-element.35), channel_id=1, source_target_pairs={{0,4},{1,5},{2,6},{3,7},{4,0},{5,1},{6,2},{7,3},{8,12},{9,13},{10,... | collective-permute-start | bytes 98312 | tf_op jit(solution)/shard_map/ppermute | solution.py:360
  19.7 2.4 %collective-permute-start.4 = (bf16[32,512]{1,0:T(8,128)(2,1)S(1)}, bf16[32,512]{1,0:T(8,128)(2,1)S(1)}, u32[]{:S(2)}, u32[]{:S(2)}) collective-permute-start(bf16[32,512]{1,0:T(8,128)(2,1)S(1)} %get-tuple-element.36), channel_id=1, source_target_pairs={{0,6},{1,7},{2,0},{3,1},{4,2},{5,3},{6,4},{7,5},{8,14},{9,15},{10,... | collective-permute-start | bytes 98312 | tf_op jit(solution)/shard_map/ppermute | solution.py:360
  22.1 4.2 %all-to-all-done = bf16[16,16,512]{2,1,0:T(8,128)(2,1)S(1)} async-done(((bf16[16,16,512]{2,1,0:T(8,128)(2,1)}), bf16[16,16,512]{2,1,0:T(8,128)(2,1)S(1)}, u32[]{:S(2)}, u32[]{:S(2)}) %all-to-all-start) | async-done | bytes 262176 | tf_op jit(solution)/shard_map/all_to_all | solution.py:352
  26.3 0.0 copy-done.3
  26.3 0.0 copy-done.4
  26.3 0.0 copy-done.5
  26.3 0.0 copy-done.6
  26.3 1.5 %shard_map.141 = (f32[512,128]{1,0:T(8,128)S(1)}, f32[2,512,256]{2,1,0:T(8,128)S(1)}) custom-call(bf16[256,512]{1,0:T(8,128)(2,1)S(1)} %bitcast.15, bf16[128,128]{1,0:T(8,128)(2,1)S(1)} %copy-done.6, bf16[2,64,128]{2,1,0:T(8,128)(2,1)S(1)} %copy-done.5, f32[64,256]{1,0:T(8,128)S(1)} %copy-done.4, bf16[2,256,256]{2,1,0:T(8,128)(2,1)S(1)} %copy-done.3), custom_call_target="tpu_custom_call" | custom-call | flops 1073741824 | bytes 524288 | tf_op jit(solution)/shard_map/pallas_call | solution.py:390
  27.8 0.0 collective-permute-done.2.first_ref
  27.8 0.0 collective-permute-done.3.second_ref
  27.8 0.0 collective-permute-done.4.third_ref
  27.9 0.2 shard_map.142
  28.0 13.5 %all_to_all.20 = bf16[16,16,512]{2,1,0:T(8,128)(2,1)S(1)} all-to-all(bf16[16,16,512]{2,1,0:T(8,128)(2,1)S(1)} %bitcast.16), channel_id=1, replica_groups=mesh['seq'=16,'ch'=16] {'seq'}, dimensions={0} | all-to-all | bytes 524288 | tf_op jit(solution)/shard_map/all_to_all | solution.py:352
  41.6 2.0 %shard_map.143.grads_ref = bf16[128,1024]{1,0:T(8,128)(2,1)S(1)} custom-call(bf16[256,512]{1,0:T(8,128)(2,1)S(1)} %bitcast.8, f32[2,512,256]{2,1,0:T(8,128)S(1)} %get-tuple-element.43.spectra_ref, bf16[128,128]{1,0:T(8,128)(2,1)S(1)} %copy-done.6, bf16[2,64,128]{2,1,0:T(8,128)(2,1)S(1)} %copy-done.5, f32[64,256]{1,0:T(8,128)S(1)} %copy-done.4, ...), custom_call_target="tpu_custom_call" | custom-call | flops 1073741824 | bytes 524288 | tf_op jit(solution)/shard_map/pallas_call | solution.py:398
  43.6 1.1 %shard_map.144 = (bf16[512,128]{1,0:T(8,128)(2,1)}, f32[128,64]{1,0:T(8,128)S(1)}) custom-call(bf16[256,512]{1,0:T(8,128)(2,1)S(1)} %bitcast.9, f32[128,512]{1,0:T(8,128)S(1)} %get-tuple-element.38.gate_ref, bf16[128,512]{1,0:T(8,128)(2,1)S(1)} %get-tuple-element.44.returned_ref, bf16[128,128]{1,0:T(8,128)(2,1)S(1)} %get-tuple-element.37.own_ref), custom_call_target="tpu_custom_call" | custom-call | flops 67108864 | bytes 524288 | tf_op jit(solution)/shard_map/pallas_call | solution.py:404
  44.7 0.2 shard_map.145
  44.9 0.0 copy-start
  44.9 14.9 %all_to_all.21 = bf16[16,8,512]{2,1,0:T(8,128)(2,1)S(1)} all-to-all(bf16[16,8,512]{2,1,0:T(8,128)(2,1)S(1)} %bitcast.14), channel_id=1, replica_groups=mesh['seq'=16,'ch'=16] {'ch'}, dimensions={0} | all-to-all | bytes 262144 | tf_op jit(solution)/shard_map/all_to_all | solution.py:352
  59.7 0.0 copy-done
  59.8 0.4 shard_map.146
  60.1 15.6 %all_to_all.22 = bf16[16,8,1152]{2,1,0:T(8,128)(2,1)S(1)} all-to-all(bf16[16,8,1152]{2,1,0:T(8,128)(2,1)S(1)} %bitcast.11), channel_id=1, replica_groups=mesh['seq'=16,'ch'=16] {'seq'}, dimensions={0} | all-to-all | bytes 589824 | tf_op jit(solution)/shard_map/all_to_all | solution.py:352
  75.8 1.0 %shard_map.147 = (bf16[512,128]{1,0:T(8,128)(2,1)}, bf16[512,128]{1,0:T(8,128)(2,1)}, f32[2,4,64]{2,1,0:T(4,128)}, f32[4,2,32]{2,1,0:T(2,128)}) custom-call(bf16[128,1152]{1,0:T(8,128)(2,1)S(1)} %bitcast.12), custom_call_target="tpu_custom_call" | custom-call | flops 67108864 | bytes 524288 | tf_op jit(solution)/shard_map/pallas_call | solution.py:412
  (2 shorter events, 0.0 us)
Async XLA Ops:
  2.6 13.1 %collective-permute-start = (bf16[64,512]{1,0:T(8,128)(2,1)S(1)}, bf16[64,512]{1,0:T(8,128)(2,1)S(1)}, u32[]{:S(2)}, u32[]{:S(2)}) collective-permute-start(bf16[64,512]{1,0:T(8,128)(2,1)S(1)} %get-tuple-element.32), channel_id=1, source_target_pairs={{0,8},{1,9},{2,10},{3,11},{4,12},{5,13},{6,14},{7,15},{8,0},{9,1},... | collective-permute-start | bytes 196616 | tf_op jit(solution)/shard_map/ppermute | solution.py:360
  9.9 16.4 %all-to-all-start = ((bf16[16,16,512]{2,1,0:T(8,128)(2,1)}), bf16[16,16,512]{2,1,0:T(8,128)(2,1)S(1)}, u32[]{:S(2)}, u32[]{:S(2)}) async-start(bf16[16,16,512]{2,1,0:T(8,128)(2,1)} %bitcast), calls=%async_computation | async-start | bytes 524288 | tf_op jit(solution)/shard_map/all_to_all | solution.py:352
  15.7 0.9 %copy-start.1 = (bf16[512,128]{1,0:T(8,128)(2,1)S(1)}, bf16[512,128]{1,0:T(8,128)(2,1)}, u32[]{:S(2)}) copy-start(bf16[512,128]{1,0:T(8,128)(2,1)} %gate_ref.1) | copy-start | bytes 393220
  15.7 0.9 %copy-start.2 = (bf16[2,64,64]{2,1,0:T(8,128)(2,1)S(1)}, bf16[2,64,64]{2,1,0:T(8,128)(2,1)}, u32[]{:S(2)}) copy-start(bf16[2,64,64]{2,1,0:T(8,128)(2,1)} %w_first_ref.1) | copy-start | bytes 49156
  15.7 10.6 %copy-start.3 = (bf16[2,256,256]{2,1,0:T(8,128)(2,1)S(1)}, bf16[2,256,256]{2,1,0:T(8,128)(2,1)}, u32[]{:S(2)}) copy-start(bf16[2,256,256]{2,1,0:T(8,128)(2,1)} %constant.11.clone.inner_ref) | copy-start | bytes 786436
  15.7 1.3 %collective-permute-start.1 = (bf16[64,512]{1,0:T(8,128)(2,1)S(1)}, bf16[64,512]{1,0:T(8,128)(2,1)S(1)}, u32[]{:S(2)}, u32[]{:S(2)}) collective-permute-start(bf16[64,512]{1,0:T(8,128)(2,1)S(1)} %shard_map.138), channel_id=1, source_target_pairs={{0,1},{1,0},{2,3},{3,2},{4,5},{5,4},{6,7},{7,6},{8,9},{9,8},{10,11... | collective-permute-start | bytes 196616 | tf_op jit(solution)/shard_map/ppermute | solution.py:360
  17.1 9.2 %copy-start.4 = (f32[64,256]{1,0:T(8,128)S(1)}, f32[64,256]{1,0:T(8,128)}, u32[]{:S(2)}) copy-start(f32[64,256]{1,0:T(8,128)} %constant.10.clone.twiddle_ref) | copy-start | bytes 196612
  17.1 9.2 %copy-start.5 = (bf16[2,64,128]{2,1,0:T(8,128)(2,1)S(1)}, bf16[2,64,128]{2,1,0:T(8,128)(2,1)}, u32[]{:S(2)}) copy-start(bf16[2,64,128]{2,1,0:T(8,128)(2,1)} %constant.9.clone.back_ref) | copy-start | bytes 98308
  17.1 9.2 %copy-start.6 = (bf16[128,128]{1,0:T(8,128)(2,1)S(1)}, bf16[128,128]{1,0:T(8,128)(2,1)}, u32[]{:S(2)}) copy-start(bf16[128,128]{1,0:T(8,128)(2,1)} %constant.8.clone.outer_ref) | copy-start | bytes 98308
  17.1 10.7 %collective-permute-start.2 = (bf16[32,512]{1,0:T(8,128)(2,1)S(1)}, bf16[32,512]{1,0:T(8,128)(2,1)S(1)}, u32[]{:S(2)}, u32[]{:S(2)}) collective-permute-start(bf16[32,512]{1,0:T(8,128)(2,1)S(1)} %get-tuple-element.34), channel_id=1, source_target_pairs={{0,2},{1,3},{2,4},{3,5},{4,6},{5,7},{6,0},{7,1},{8,10},{9,11},{10,... | collective-permute-start | bytes 98312 | tf_op jit(solution)/shard_map/ppermute | solution.py:360
  18.7 9.1 %collective-permute-start.3 = (bf16[32,512]{1,0:T(8,128)(2,1)S(1)}, bf16[32,512]{1,0:T(8,128)(2,1)S(1)}, u32[]{:S(2)}, u32[]{:S(2)}) collective-permute-start(bf16[32,512]{1,0:T(8,128)(2,1)S(1)} %get-tuple-element.35), channel_id=1, source_target_pairs={{0,4},{1,5},{2,6},{3,7},{4,0},{5,1},{6,2},{7,3},{8,12},{9,13},{10,... | collective-permute-start | bytes 98312 | tf_op jit(solution)/shard_map/ppermute | solution.py:360
  19.7 8.2 %collective-permute-start.4 = (bf16[32,512]{1,0:T(8,128)(2,1)S(1)}, bf16[32,512]{1,0:T(8,128)(2,1)S(1)}, u32[]{:S(2)}, u32[]{:S(2)}) collective-permute-start(bf16[32,512]{1,0:T(8,128)(2,1)S(1)} %get-tuple-element.36), channel_id=1, source_target_pairs={{0,6},{1,7},{2,0},{3,1},{4,2},{5,3},{6,4},{7,5},{8,14},{9,15},{10,... | collective-permute-start | bytes 98312 | tf_op jit(solution)/shard_map/ppermute | solution.py:360
  44.9 14.9 %copy-start = (bf16[512,128]{1,0:T(8,128)(2,1)S(1)}, bf16[512,128]{1,0:T(8,128)(2,1)}, u32[]{:S(2)}) copy-start(bf16[512,128]{1,0:T(8,128)(2,1)} %d_out_ref.1) | copy-start | bytes 393220

commit v10 on v7

--- a/solution.py
+++ b/solution.py
@@ -48,7 +48,7 @@
     inner_high, inner_low = halves(inner.astype(np.float32))
     return (
         np.concatenate([outer_high, outer_low], 1),
-        np.stack([back_high, back_low]),
+        np.concatenate([back_high, back_low], 0),
         twiddle.astype(np.float32),
         np.stack([inner_high, inner_low]),
     )
@@ -96,6 +96,7 @@
     near_ref,
     core_ref,
     far_ref,
+    cross_ref,
     pair_hbm,
     d_out_ref,
     w_second_ref,
@@ -135,20 +136,14 @@
     weights = dot(order, spread).astype(BF16)
     copies[3].wait()
     result = dot(weights, d_out_ref[...], NT).astype(BF16)
-    for ref, start in zip((near_ref, core_ref, far_ref), (0, 32, 64)):
-        ref[...] = result[start : start + ref.shape[0], :]
+    for zc, ref in enumerate((near_ref, core_ref, far_ref, cross_ref)):
+        ref[...] = result[32 * zc : 32 * zc + 32, :]
     leave.wait()
 
 
-def core_kernel(core_ref, far_ref, message_ref):
-    message_ref[0:32, :] = core_ref[...]
-    message_ref[32:64, :] = far_ref[32:64, :]
-
-
-def repack_kernel(near_ref, core_ref, far_ref, *outs):
-    near, core, far = (ref[...].astype(F32) for ref in (near_ref, core_ref, far_ref))
-    values = (near, core[0:32, :], far[0:32, :], core[32:64, :])
-    for y, ref in enumerate(outs):
+def repack_kernel(*refs):
+    values = [ref[...].astype(F32) for ref in refs[:4]]
+    for y, ref in enumerate(refs[4:]):
         ref[...] = jnp.concatenate([v[8 * y : 8 * y + 8, :] for v in values], axis=0).astype(BF16)
 
 
@@ -233,7 +228,8 @@
             jnp.concatenate([real * cosine + imag * sine, imag * cosine - real * sine], axis=0)
         )
     high, low = split(jnp.concatenate(columns, axis=1))
-    return dot(back_ref[0], high) + dot(back_ref[0], low) + dot(back_ref[1], high)
+    both = dot(back_ref[...], high)
+    return both[0:64, :] + both[64:128, :] + dot(back_ref[0:64, :], low)
 
 
 def conv_kernel(pair_ref, outer_ref, back_ref, twiddle_ref, inner_ref, conv_ref, spectra_ref, wide_ref):
@@ -365,11 +361,11 @@
     outer, back, twiddle, inner = (jnp.asarray(t) for t in tables(lax.axis_size("seq"), rows))
     single, double = ((width, rows), BF16), ((2 * width, rows), BF16)
     slab = ((rows, width), BF16)
-    quarter, half = ((width // 4, rows), BF16), ((width // 2, rows), BF16)
+    quarter = ((width // 4, rows), BF16)
     held = [pltpu.with_memory_space_constraint(v, pltpu.HBM) for v in (d_out, w_second, signal, filter_raw)]
-    near, core, far, pair = call(
+    near, *others, pair = call(
         entry_kernel,
-        [quarter + (True,), quarter + (True,), half + (True,), double],
+        [quarter + (True,)] * 4 + [double],
         [
             pltpu.VMEM(d_out.shape, BF16),
             pltpu.VMEM(w_second.shape, BF16),
@@ -377,12 +373,11 @@
             pltpu.VMEM((2 * width, rows), BF16),
             pltpu.SemaphoreType.DMA((5,)),
         ],
-        spaces=([pl.ANY] * 4, [pltpu.VMEM] * 3 + [pl.ANY]),
+        spaces=([pl.ANY] * 4, [pltpu.VMEM] * 4 + [pl.ANY]),
     )(*held)
-    far = shift(far, 0, 2)
+    others = [shift(value, 0, zc) for zc, value in zip((1, 2, 3), others)]
     pair = exchange(pair, "seq")
-    core = shift(call(core_kernel, [half], flops=1 << 35)(core, far)[0], 0, 1)
-    near, *others = call(repack_kernel, [quarter] * 4)(near, core, far)
+    near, *others = call(repack_kernel, [quarter] * 4, flops=1 << 35)(near, *others)
     pair = lax.optimization_barrier((pair, near))[0]
     others = [shift(value, y, 0) for y, value in zip((1, 2, 3), others)]
     square = ((128, 128), BF16)

time: 75.4 us -> 80.7 us (1.070)
  starting transfers between devices: 24.3 us -> 28.6 us
  waiting for transfers between devices: 10.1 us -> 11.9 us
    all_to_all x2, starting transfers between devices: 11.9 us -> 16.2 us  [exchange(): lax.all_to_all(pieces, axis, split_axis=0, concat_axis=0, tiled=True)]
    all_to_all x2, waiting for transfers between devices: 9.87 us -> 11.8 us  [exchange(): lax.all_to_all(pieces, axis, split_axis=0, concat_axis=0, tiled=True)]
    ppermute x5 -> x6, starting transfers between devices: 12.4 us -> 12.4 us  [shift(): return lax.ppermute(value, 'ch', pairs)]
    pallas_call x3 -> x2, Pallas kernels: 1.99 us -> 1.99 us  [the longest x1 1.98 us: shards(): call(entry_kernel, [quarter + (True,)] * 4 + [double], [pltpu.VMEM(d_out....]
  transfers between devices with their start and end apart: 7 -> 8, of which waited for: 3 -> 2; matrix products, arithmetic and copies ran while one was open for 0% -> 0% of each run, Pallas kernels for 7% -> 6%
where the time goes in v10:
time: 80.7 us; the launch traced here: 79.7 us
  blocking collectives  29.3 us (36%)
  starting transfers between devices  28.6 us (35%)
  waiting for transfers between devices  11.9 us (15%)
  Pallas kernels  9.04 us (11%)
    all_to_all x2, blocking collectives, exchange(): lax.all_to_all(pieces, axis, split_axis=0, concat_axis=0, tiled=True)  29.3 us
    all_to_all x2, starting transfers between devices, exchange(): lax.all_to_all(pieces, axis, split_axis=0, concat_axis=0, tiled=True)  16.2 us
    ppermute x6, starting transfers between devices, shift(): return lax.ppermute(value, 'ch', pairs)  12.4 us
    all_to_all x2, waiting for transfers between devices, exchange(): lax.all_to_all(pieces, axis, split_axis=0, concat_axis=0, tiled=True)  11.8 us
    pallas_call x1, Pallas kernels, shards(): call(entry_kernel, [quarter + (True,)] * 4 + [double], [pltpu.VMEM(d_out....  1.98 us
    pallas_call x1, Pallas kernels, shards(): call(adjoint_kernel, [((width, 2 * rows), BF16)], [pltpu.VMEM((2 * width...  1.92 us
  transfers between devices with their start and end apart: 8, of which 2 were waited for; matrix products, arithmetic and copies ran while one was open for 0% of the time, Pallas kernels for 6%

profile of v10, /device:TPU:8, one launch (start us, length us, event | category | flops | bytes accessed | tf_op | source)
XLA Modules:
  0.0 79.7 jit_solution(6400915365855805724)
XLA Ops:
  0.6 2.0 %shard_map.137 = (bf16[32,512]{1,0:T(8,128)(2,1)S(1)}, bf16[32,512]{1,0:T(8,128)(2,1)S(1)}, bf16[32,512]{1,0:T(8,128)(2,1)S(1)}, bf16[32,512]{1,0:T(8,128)(2,1)S(1)}, bf16[256,512]{1,0:T(8,128)(2,1)}) custom-call(bf16[512,128]{1,0:T(8,128)(2,1)} %d_out_ref.1, bf16[4,32,32]{2,1,0:T(8,128)(2,1)} %w_second_hbm.1, bf16[512,128]{1,0:T(8,128)(2,1)} %signal_hbm.1, ...), custom_call_target="tpu_custom_call" | custom-call | flops 67108864 | bytes 524288 | tf_op jit(solution)/shard_map/pallas_call | solution.py:366
  2.6 0.1 collective-permute-start
  2.7 7.3 %collective-permute-start.1 = (bf16[32,512]{1,0:T(8,128)(2,1)S(1)}, bf16[32,512]{1,0:T(8,128)(2,1)S(1)}, u32[]{:S(2)}, u32[]{:S(2)}) collective-permute-start(bf16[32,512]{1,0:T(8,128)(2,1)S(1)} %get-tuple-element.30), channel_id=1, source_target_pairs={{0,8},{1,9},{2,10},{3,11},{4,12},{5,13},{6,14},{7,15},{8,0},{9,1},... | collective-permute-start | bytes 98312 | tf_op jit(solution)/shard_map/ppermute | solution.py:356
  10.0 0.1 collective-permute-start.2
  10.0 0.0 copy-start.1
  10.0 0.0 copy-start.2
  10.0 7.1 %all-to-all-start = ((bf16[16,16,512]{2,1,0:T(8,128)(2,1)}), bf16[16,16,512]{2,1,0:T(8,128)(2,1)S(1)}, u32[]{:S(2)}, u32[]{:S(2)}) async-start(bf16[16,16,512]{2,1,0:T(8,128)(2,1)} %bitcast), calls=%async_computation | async-start | bytes 524288 | tf_op jit(solution)/shard_map/all_to_all | solution.py:348
  17.1 0.0 copy-done.1
  17.1 0.0 copy-done.2
  17.1 0.2 shard_map.139
  17.4 0.0 collective-permute-done.refs_1_
  17.4 0.0 collective-permute-done.1.refs_2_
  17.4 0.0 collective-permute-done.2.refs_3_
  17.4 0.0 copy-start.3
  17.4 0.0 copy-start.4
  17.4 0.0 copy-start.5
  17.4 0.0 copy-start.6
  17.5 1.7 %collective-permute-start.3 = (bf16[32,512]{1,0:T(8,128)(2,1)S(1)}, bf16[32,512]{1,0:T(8,128)(2,1)S(1)}, u32[]{:S(2)}, u32[]{:S(2)}) collective-permute-start(bf16[32,512]{1,0:T(8,128)(2,1)S(1)} %get-tuple-element.33), channel_id=1, source_target_pairs={{0,2},{1,3},{2,4},{3,5},{4,6},{5,7},{6,0},{7,1},{8,10},{9,11},{10,... | collective-permute-start | bytes 98312 | tf_op jit(solution)/shard_map/ppermute | solution.py:356
  19.1 0.9 %collective-permute-start.4 = (bf16[32,512]{1,0:T(8,128)(2,1)S(1)}, bf16[32,512]{1,0:T(8,128)(2,1)S(1)}, u32[]{:S(2)}, u32[]{:S(2)}) collective-permute-start(bf16[32,512]{1,0:T(8,128)(2,1)S(1)} %get-tuple-element.34), channel_id=1, source_target_pairs={{0,4},{1,5},{2,6},{3,7},{4,0},{5,1},{6,2},{7,3},{8,12},{9,13},{10,... | collective-permute-start | bytes 98312 | tf_op jit(solution)/shard_map/ppermute | solution.py:356
  20.1 2.4 %collective-permute-start.5 = (bf16[32,512]{1,0:T(8,128)(2,1)S(1)}, bf16[32,512]{1,0:T(8,128)(2,1)S(1)}, u32[]{:S(2)}, u32[]{:S(2)}) collective-permute-start(bf16[32,512]{1,0:T(8,128)(2,1)S(1)} %get-tuple-element.35), channel_id=1, source_target_pairs={{0,6},{1,7},{2,0},{3,1},{4,2},{5,3},{6,4},{7,5},{8,14},{9,15},{10,... | collective-permute-start | bytes 98312 | tf_op jit(solution)/shard_map/ppermute | solution.py:356
  22.5 6.0 %all-to-all-done = bf16[16,16,512]{2,1,0:T(8,128)(2,1)S(1)} async-done(((bf16[16,16,512]{2,1,0:T(8,128)(2,1)}), bf16[16,16,512]{2,1,0:T(8,128)(2,1)S(1)}, u32[]{:S(2)}, u32[]{:S(2)}) %all-to-all-start) | async-done | bytes 262176 | tf_op jit(solution)/shard_map/all_to_all | solution.py:348
  28.5 0.0 copy-done.3
  28.5 0.0 copy-done.4
  28.5 0.0 copy-done.5
  28.5 0.0 copy-done.6
  28.5 1.5 %shard_map.140 = (f32[512,128]{1,0:T(8,128)S(1)}, f32[2,512,256]{2,1,0:T(8,128)S(1)}) custom-call(bf16[256,512]{1,0:T(8,128)(2,1)S(1)} %bitcast.14, bf16[128,128]{1,0:T(8,128)(2,1)S(1)} %copy-done.6, bf16[128,128]{1,0:T(8,128)(2,1)S(1)} %copy-done.5, f32[64,256]{1,0:T(8,128)S(1)} %copy-done.4, bf16[2,256,256]{2,1,0:T(8,128)(2,1)S(1)} %copy-done.3), custom_call_target="tpu_custom_call" | custom-call | flops 1073741824 | bytes 524288 | tf_op jit(solution)/shard_map/pallas_call | solution.py:385
  30.0 0.0 collective-permute-done.3.first_ref
  30.0 0.0 collective-permute-done.4.second_ref
  30.0 0.0 collective-permute-done.5.third_ref
  30.0 0.2 shard_map.141
  30.2 13.6 %all_to_all.20 = bf16[16,16,512]{2,1,0:T(8,128)(2,1)S(1)} all-to-all(bf16[16,16,512]{2,1,0:T(8,128)(2,1)S(1)} %bitcast.15), channel_id=1, replica_groups=mesh['seq'=16,'ch'=16] {'seq'}, dimensions={0} | all-to-all | bytes 524288 | tf_op jit(solution)/shard_map/all_to_all | solution.py:348
  43.8 0.9 %shard_map.142 = bf16[128,512]{1,0:T(8,128)(2,1)} custom-call(bf16[256,512]{1,0:T(8,128)(2,1)S(1)} %bitcast.8, f32[128,512]{1,0:T(8,128)S(1)} %get-tuple-element.37.gate_ref, bf16[128,128]{1,0:T(8,128)(2,1)S(1)} %get-tuple-element.42.blocks_ref), custom_call_target="tpu_custom_call" | custom-call | flops 67108864 | bytes 524288 | tf_op jit(solution)/shard_map/pallas_call | solution.py:393
  44.7 9.2 %all-to-all-start.2 = ((bf16[16,8,512]{2,1,0:T(8,128)(2,1)}), bf16[16,8,512]{2,1,0:T(8,128)(2,1)S(1)}, u32[]{:S(2)}, u32[]{:S(2)}) async-start(bf16[16,8,512]{2,1,0:T(8,128)(2,1)} %bitcast.4), calls=%async_computation.2 | async-start | bytes 262144 | tf_op jit(solution)/shard_map/all_to_all | solution.py:348
  53.8 1.1 %shard_map.143 = (bf16[512,128]{1,0:T(8,128)(2,1)}, f32[128,64]{1,0:T(8,128)S(1)}) custom-call(bf16[256,512]{1,0:T(8,128)(2,1)S(1)} %bitcast.9, f32[128,512]{1,0:T(8,128)S(1)} %get-tuple-element.37.gate_ref, bf16[128,512]{1,0:T(8,128)(2,1)S(1)} %get-tuple-element.43.returned_ref, bf16[128,128]{1,0:T(8,128)(2,1)S(1)} %get-tuple-element.36.own_ref), custom_call_target="tpu_custom_call" | custom-call | flops 67108864 | bytes 524288 | tf_op jit(solution)/shard_map/pallas_call | solution.py:401
  54.9 0.0 copy-start
  54.9 1.9 %shard_map.144.grads_ref = bf16[128,1024]{1,0:T(8,128)(2,1)S(1)} custom-call(bf16[256,512]{1,0:T(8,128)(2,1)S(1)} %bitcast.10, f32[2,512,256]{2,1,0:T(8,128)S(1)} %get-tuple-element.45.spectra_ref, bf16[128,128]{1,0:T(8,128)(2,1)S(1)} %copy-done.6, bf16[128,128]{1,0:T(8,128)(2,1)S(1)} %copy-done.5, f32[64,256]{1,0:T(8,128)S(1)} %copy-done.4, ...), custom_call_target="tpu_custom_call" | custom-call | flops 1073741824 | bytes 524288 | tf_op jit(solution)/shard_map/pallas_call | solution.py:395
  56.8 5.8 %all-to-all-done.2 = bf16[16,8,512]{2,1,0:T(8,128)(2,1)S(1)} async-done(((bf16[16,8,512]{2,1,0:T(8,128)(2,1)}), bf16[16,8,512]{2,1,0:T(8,128)(2,1)S(1)}, u32[]{:S(2)}, u32[]{:S(2)}) %all-to-all-start.2) | async-done | bytes 131104 | tf_op jit(solution)/shard_map/all_to_all | solution.py:348
  62.6 0.0 copy-done
  62.6 0.4 shard_map.145
  63.0 15.7 %all_to_all.21 = bf16[16,8,1152]{2,1,0:T(8,128)(2,1)S(1)} all-to-all(bf16[16,8,1152]{2,1,0:T(8,128)(2,1)S(1)} %bitcast.11), channel_id=1, replica_groups=mesh['seq'=16,'ch'=16] {'seq'}, dimensions={0} | all-to-all | bytes 589824 | tf_op jit(solution)/shard_map/all_to_all | solution.py:348
  78.7 1.0 %shard_map.146 = (bf16[512,128]{1,0:T(8,128)(2,1)}, bf16[512,128]{1,0:T(8,128)(2,1)}, f32[2,4,64]{2,1,0:T(4,128)}, f32[4,2,32]{2,1,0:T(2,128)}) custom-call(bf16[128,1152]{1,0:T(8,128)(2,1)S(1)} %bitcast.12), custom_call_target="tpu_custom_call" | custom-call | flops 67108864 | bytes 524288 | tf_op jit(solution)/shard_map/pallas_call | solution.py:406
  (1 shorter events, 0.0 us)
Async XLA Ops:
  2.6 14.7 %collective-permute-start = (bf16[32,512]{1,0:T(8,128)(2,1)S(1)}, bf16[32,512]{1,0:T(8,128)(2,1)S(1)}, u32[]{:S(2)}, u32[]{:S(2)}) collective-permute-start(bf16[32,512]{1,0:T(8,128)(2,1)S(1)} %get-tuple-element.29), channel_id=1, source_target_pairs={{0,1},{1,0},{2,3},{3,2},{4,5},{5,4},{6,7},{7,6},{8,9},{9,8},{10,11... | collective-permute-start | bytes 98312 | tf_op jit(solution)/shard_map/ppermute | solution.py:356
  2.7 14.7 %collective-permute-start.1 = (bf16[32,512]{1,0:T(8,128)(2,1)S(1)}, bf16[32,512]{1,0:T(8,128)(2,1)S(1)}, u32[]{:S(2)}, u32[]{:S(2)}) collective-permute-start(bf16[32,512]{1,0:T(8,128)(2,1)S(1)} %get-tuple-element.30), channel_id=1, source_target_pairs={{0,8},{1,9},{2,10},{3,11},{4,12},{5,13},{6,14},{7,15},{8,0},{9,1},... | collective-permute-start | bytes 98312 | tf_op jit(solution)/shard_map/ppermute | solution.py:356
  10.0 7.4 %collective-permute-start.2 = (bf16[32,512]{1,0:T(8,128)(2,1)S(1)}, bf16[32,512]{1,0:T(8,128)(2,1)S(1)}, u32[]{:S(2)}, u32[]{:S(2)}) collective-permute-start(bf16[32,512]{1,0:T(8,128)(2,1)S(1)} %get-tuple-element.31), channel_id=1, source_target_pairs={{0,9},{1,8},{2,11},{3,10},{4,13},{5,12},{6,15},{7,14},{8,1},{9,0},... | collective-permute-start | bytes 98312 | tf_op jit(solution)/shard_map/ppermute | solution.py:356
  10.0 7.1 %copy-start.1 = (bf16[512,128]{1,0:T(8,128)(2,1)S(1)}, bf16[512,128]{1,0:T(8,128)(2,1)}, u32[]{:S(2)}) copy-start(bf16[512,128]{1,0:T(8,128)(2,1)} %gate_ref.1) | copy-start | bytes 393220
  10.0 7.1 %copy-start.2 = (bf16[2,64,64]{2,1,0:T(8,128)(2,1)S(1)}, bf16[2,64,64]{2,1,0:T(8,128)(2,1)}, u32[]{:S(2)}) copy-start(bf16[2,64,64]{2,1,0:T(8,128)(2,1)} %w_first_ref.1) | copy-start | bytes 49156
  10.0 18.5 %all-to-all-start = ((bf16[16,16,512]{2,1,0:T(8,128)(2,1)}), bf16[16,16,512]{2,1,0:T(8,128)(2,1)S(1)}, u32[]{:S(2)}, u32[]{:S(2)}) async-start(bf16[16,16,512]{2,1,0:T(8,128)(2,1)} %bitcast), calls=%async_computation | async-start | bytes 524288 | tf_op jit(solution)/shard_map/all_to_all | solution.py:348
  17.4 11.1 %copy-start.3 = (bf16[2,256,256]{2,1,0:T(8,128)(2,1)S(1)}, bf16[2,256,256]{2,1,0:T(8,128)(2,1)}, u32[]{:S(2)}) copy-start(bf16[2,256,256]{2,1,0:T(8,128)(2,1)} %constant.11.clone.inner_ref) | copy-start | bytes 786436
  17.4 11.1 %copy-start.4 = (f32[64,256]{1,0:T(8,128)S(1)}, f32[64,256]{1,0:T(8,128)}, u32[]{:S(2)}) copy-start(f32[64,256]{1,0:T(8,128)} %constant.10.clone.twiddle_ref) | copy-start | bytes 196612
  17.4 11.1 %copy-start.5 = (bf16[128,128]{1,0:T(8,128)(2,1)S(1)}, bf16[128,128]{1,0:T(8,128)(2,1)}, u32[]{:S(2)}) copy-start(bf16[128,128]{1,0:T(8,128)(2,1)} %constant.9.clone.back_ref) | copy-start | bytes 98308
  17.4 11.1 %copy-start.6 = (bf16[128,128]{1,0:T(8,128)(2,1)S(1)}, bf16[128,128]{1,0:T(8,128)(2,1)}, u32[]{:S(2)}) copy-start(bf16[128,128]{1,0:T(8,128)(2,1)} %constant.8.clone.outer_ref) | copy-start | bytes 98308
  17.5 12.5 %collective-permute-start.3 = (bf16[32,512]{1,0:T(8,128)(2,1)S(1)}, bf16[32,512]{1,0:T(8,128)(2,1)S(1)}, u32[]{:S(2)}, u32[]{:S(2)}) collective-permute-start(bf16[32,512]{1,0:T(8,128)(2,1)S(1)} %get-tuple-element.33), channel_id=1, source_target_pairs={{0,2},{1,3},{2,4},{3,5},{4,6},{5,7},{6,0},{7,1},{8,10},{9,11},{10,... | collective-permute-start | bytes 98312 | tf_op jit(solution)/shard_map/ppermute | solution.py:356
  19.1 10.9 %collective-permute-start.4 = (bf16[32,512]{1,0:T(8,128)(2,1)S(1)}, bf16[32,512]{1,0:T(8,128)(2,1)S(1)}, u32[]{:S(2)}, u32[]{:S(2)}) collective-permute-start(bf16[32,512]{1,0:T(8,128)(2,1)S(1)} %get-tuple-element.34), channel_id=1, source_target_pairs={{0,4},{1,5},{2,6},{3,7},{4,0},{5,1},{6,2},{7,3},{8,12},{9,13},{10,... | collective-permute-start | bytes 98312 | tf_op jit(solution)/shard_map/ppermute | solution.py:356
  20.1 10.0 %collective-permute-start.5 = (bf16[32,512]{1,0:T(8,128)(2,1)S(1)}, bf16[32,512]{1,0:T(8,128)(2,1)S(1)}, u32[]{:S(2)}, u32[]{:S(2)}) collective-permute-start(bf16[32,512]{1,0:T(8,128)(2,1)S(1)} %get-tuple-element.35), channel_id=1, source_target_pairs={{0,6},{1,7},{2,0},{3,1},{4,2},{5,3},{6,4},{7,5},{8,14},{9,15},{10,... | collective-permute-start | bytes 98312 | tf_op jit(solution)/shard_map/ppermute | solution.py:356
  44.7 17.9 %all-to-all-start.2 = ((bf16[16,8,512]{2,1,0:T(8,128)(2,1)}), bf16[16,8,512]{2,1,0:T(8,128)(2,1)S(1)}, u32[]{:S(2)}, u32[]{:S(2)}) async-start(bf16[16,8,512]{2,1,0:T(8,128)(2,1)} %bitcast.4), calls=%async_computation.2 | async-start | bytes 262144 | tf_op jit(solution)/shard_map/all_to_all | solution.py:348
  54.9 7.7 %copy-start = (bf16[512,128]{1,0:T(8,128)(2,1)S(1)}, bf16[512,128]{1,0:T(8,128)(2,1)}, u32[]{:S(2)}) copy-start(bf16[512,128]{1,0:T(8,128)(2,1)} %d_out_ref.1) | copy-start | bytes 393220

commit v11 on v7

--- a/solution.py
+++ b/solution.py
@@ -48,7 +48,7 @@
     inner_high, inner_low = halves(inner.astype(np.float32))
     return (
         np.concatenate([outer_high, outer_low], 1),
-        np.stack([back_high, back_low]),
+        np.concatenate([back_high, back_low], 0),
         twiddle.astype(np.float32),
         np.stack([inner_high, inner_low]),
     )
@@ -94,29 +94,27 @@
     signal_hbm,
     filter_hbm,
     near_ref,
+    far_ref,
     core_ref,
-    far_ref,
-    pair_hbm,
+    signal_ref,
+    filter_ref,
     d_out_ref,
     w_second_ref,
-    both_ref,
-    pair_ref,
     sems,
 ):
     copies = [
         pltpu.make_async_copy(source, target, sems.at[index])
         for index, (source, target) in enumerate(
             (
-                (signal_hbm, both_ref.at[0]),
-                (filter_hbm, both_ref.at[1]),
                 (w_second_hbm, w_second_ref),
                 (d_out_hbm, d_out_ref),
+                (signal_hbm, signal_ref),
+                (filter_hbm, filter_ref),
             )
         )
     ]
     for copy in copies:
         copy.start()
-    pairs = pair_order()
     row, col = iotas(32, 128)
     copies_of = ones_where(row == col % 32)
     row, col = iotas(128, 128)
@@ -124,30 +122,32 @@
     block = 2 * partner(row // 8 % 4, row // 32, 1) + row // 4 % 2
     order = ones_where((block == col % 32) & (row % 4 == col // 32))
     copies[0].wait()
-    copies[1].wait()
-    both = jnp.concatenate([both_ref[0], both_ref[1]], axis=1)
-    pair_ref[...] = dot(pairs, both, NT).astype(BF16)
-    leave = pltpu.make_async_copy(pair_ref, pair_hbm, sems.at[4])
-    leave.start()
-    copies[2].wait()
     flat = w_second_ref[...].reshape(128, 32)
     spread = jnp.where(keep, dot(flat, copies_of), 0.0).astype(BF16)
     weights = dot(order, spread).astype(BF16)
+    copies[1].wait()
+    result = dot(weights, d_out_ref[...], NT).astype(BF16)
+    near_ref[...] = result[0:32, :]
+    far_ref[...] = result[64:96, :]
+    core_ref[0:32, :] = result[32:64, :]
+    core_ref[32:64, :] = result[96:128, :]
+    copies[2].wait()
     copies[3].wait()
-    result = dot(weights, d_out_ref[...], NT).astype(BF16)
-    for ref, start in zip((near_ref, core_ref, far_ref), (0, 32, 64)):
-        ref[...] = result[start : start + ref.shape[0], :]
-    leave.wait()
-
-
-def core_kernel(core_ref, far_ref, message_ref):
-    message_ref[0:32, :] = core_ref[...]
-    message_ref[32:64, :] = far_ref[32:64, :]
+
+
+def pair_kernel(signal_ref, filter_ref, pair_ref):
+    both = jnp.concatenate([signal_ref[...], filter_ref[...]], axis=1)
+    pair_ref[...] = dot(pair_order(), both, NT).astype(BF16)
+
+
+def far_kernel(far_ref, core_ref, message_ref):
+    message_ref[0:32, :] = far_ref[...]
+    message_ref[32:64, :] = core_ref[32:64, :]
 
 
 def repack_kernel(near_ref, core_ref, far_ref, *outs):
     near, core, far = (ref[...].astype(F32) for ref in (near_ref, core_ref, far_ref))
-    values = (near, core[0:32, :], far[0:32, :], core[32:64, :])
+    values = (near, core[0:32, :], far[0:32, :], far[32:64, :])
     for y, ref in enumerate(outs):
         ref[...] = jnp.concatenate([v[8 * y : 8 * y + 8, :] for v in values], axis=0).astype(BF16)
 
@@ -233,7 +233,8 @@
             jnp.concatenate([real * cosine + imag * sine, imag * cosine - real * sine], axis=0)
         )
     high, low = split(jnp.concatenate(columns, axis=1))
-    return dot(back_ref[0], high) + dot(back_ref[0], low) + dot(back_ref[1], high)
+    both = dot(back_ref[...], high)
+    return both[0:64, :] + both[64:128, :] + dot(back_ref[0:64, :], low)
 
 
 def conv_kernel(pair_ref, outer_ref, back_ref, twiddle_ref, inner_ref, conv_ref, spectra_ref, wide_ref):
@@ -367,22 +368,30 @@
     slab = ((rows, width), BF16)
     quarter, half = ((width // 4, rows), BF16), ((width // 2, rows), BF16)
     held = [pltpu.with_memory_space_constraint(v, pltpu.HBM) for v in (d_out, w_second, signal, filter_raw)]
-    near, core, far, pair = call(
+    near, far, core, signal, filter_raw = call(
         entry_kernel,
-        [quarter + (True,), quarter + (True,), half + (True,), double],
+        [
+            quarter + (True,),
+            quarter + (True,),
+            half + (True,),
+            slab + (True,),
+            slab + (True,),
+        ],
         [
             pltpu.VMEM(d_out.shape, BF16),
             pltpu.VMEM(w_second.shape, BF16),
-            pltpu.VMEM((2, rows, width), BF16),
-            pltpu.VMEM((2 * width, rows), BF16),
-            pltpu.SemaphoreType.DMA((5,)),
+            pltpu.SemaphoreType.DMA((4,)),
         ],
-        spaces=([pl.ANY] * 4, [pltpu.VMEM] * 3 + [pl.ANY]),
+        spaces=([pl.ANY] * 4, [pltpu.VMEM] * 5),
     )(*held)
+    core = shift(core, 0, 1)
+    pair = call(pair_kernel, [double])(signal, filter_raw)[0]
+    far = call(far_kernel, [half])(far, core)[0]
+    pair, far = lax.optimization_barrier((pair, far))
     far = shift(far, 0, 2)
+    gate, w_first, far = lax.optimization_barrier((gate, w_first, far))
     pair = exchange(pair, "seq")
-    core = shift(call(core_kernel, [half], flops=1 << 35)(core, far)[0], 0, 1)
-    near, *others = call(repack_kernel, [quarter] * 4)(near, core, far)
+    near, *others = call(repack_kernel, [quarter] * 4, flops=1 << 35)(near, core, far)
     pair = lax.optimization_barrier((pair, near))[0]
     others = [shift(value, y, 0) for y, value in zip((1, 2, 3), others)]
     square = ((128, 128), BF16)

time: 75.4 us -> 75.9 us (level)
  waiting for transfers between devices: 10.1 us -> 11.9 us
  local copies, waits for them, and re-layouts: 0.79 us -> 0.03 us
    all_to_all x2, waiting for transfers between devices: 9.87 us -> 11.6 us  [exchange(): lax.all_to_all(pieces, axis, split_axis=0, concat_axis=0, tiled=True)]
    pallas_call x2 -> x3, Pallas kernels: 0.02 us -> 0.99 us  [the longest x1 0.97 us: shards(): pair = call(pair_kernel, [double])(signal, filter_raw)[0]]
  transfers between devices with their start and end apart: 7 -> 7, of which waited for: 3 -> 3; matrix products, arithmetic and copies ran while one was open for 0% -> 0% of each run, Pallas kernels for 7% -> 8%
where the time goes in v11:
time: 75.9 us; the launch traced here: 75 us
  blocking collectives  29.1 us (38%)
  starting transfers between devices  23.9 us (31%)
  waiting for transfers between devices  11.9 us (16%)
  Pallas kernels  9.3 us (12%)
  between operations  0.77 us (1%)
    all_to_all x2, blocking collectives, exchange(): lax.all_to_all(pieces, axis, split_axis=0, concat_axis=0, tiled=True)  29.1 us
    ppermute x5, starting transfers between devices, shift(): return lax.ppermute(value, 'ch', pairs)  12.3 us
    all_to_all x2, starting transfers between devices, exchange(): lax.all_to_all(pieces, axis, split_axis=0, concat_axis=0, tiled=True)  11.6 us
    all_to_all x2, waiting for transfers between devices, exchange(): lax.all_to_all(pieces, axis, split_axis=0, concat_axis=0, tiled=True)  11.6 us
    pallas_call x1, Pallas kernels, shards(): call(adjoint_kernel, [((width, 2 * rows), BF16)], [pltpu.VMEM((2 * width...  1.92 us
  transfers between devices with their start and end apart: 7, of which 3 were waited for; matrix products, arithmetic and copies ran while one was open for 0% of the time, Pallas kernels for 8%

profile of v11, /device:TPU:8, one launch (start us, length us, event | category | flops | bytes accessed | tf_op | source)
XLA Modules:
  0.0 75.0 jit_solution(13082757184594709728)
XLA Ops:
  0.6 1.3 %shard_map.137 = (bf16[32,512]{1,0:T(8,128)(2,1)S(1)}, bf16[32,512]{1,0:T(8,128)(2,1)S(1)}, bf16[64,512]{1,0:T(8,128)(2,1)S(1)}, bf16[512,128]{1,0:T(8,128)(2,1)S(1)}, bf16[512,128]{1,0:T(8,128)(2,1)S(1)}) custom-call(bf16[512,128]{1,0:T(8,128)(2,1)} %d_out_ref.1, bf16[4,32,32]{2,1,0:T(8,128)(2,1)} %w_second_hbm.1, bf16[512,128]{1,0:T(8,128)(2,1)} %signal_hbm.1, ...), custom_call_target="tpu_custom_call" | custom-call | flops 67108864 | bytes 524288 | tf_op jit(solution)/shard_map/pallas_call | solution.py:371
  1.9 0.1 collective-permute-start
  2.0 1.0 %shard_map.138 = bf16[256,512]{1,0:T(8,128)(2,1)} custom-call(bf16[512,128]{1,0:T(8,128)(2,1)S(1)} %get-tuple-element.35.signal_ref, bf16[512,128]{1,0:T(8,128)(2,1)S(1)} %get-tuple-element.36.filter_ref), custom_call_target="tpu_custom_call" | custom-call | flops 67108864 | bytes 524288 | tf_op jit(solution)/shard_map/pallas_call | solution.py:388
  3.0 0.3 collective-permute-done.core_ref
  3.2 7.2 %collective-permute-start.1 = (bf16[64,512]{1,0:T(8,128)(2,1)S(1)}, bf16[64,512]{1,0:T(8,128)(2,1)S(1)}, u32[]{:S(2)}, u32[]{:S(2)}) collective-permute-start(bf16[64,512]{1,0:T(8,128)(2,1)S(1)} %shard_map.139), channel_id=1, source_target_pairs={{0,8},{1,9},{2,10},{3,11},{4,12},{5,13},{6,14},{7,15},{8,0},{9,1},... | collective-permute-start | bytes 196616 | tf_op jit(solution)/shard_map/ppermute | solution.py:361
  10.4 5.8 %all-to-all-start = ((bf16[16,16,512]{2,1,0:T(8,128)(2,1)}), bf16[16,16,512]{2,1,0:T(8,128)(2,1)S(1)}, u32[]{:S(2)}, u32[]{:S(2)}) async-start(bf16[16,16,512]{2,1,0:T(8,128)(2,1)} %bitcast), calls=%async_computation | async-start | bytes 524288 | tf_op jit(solution)/shard_map/all_to_all | solution.py:353
  16.2 0.0 collective-permute-done.1.far_ref
  16.2 0.0 copy-start.1
  16.2 0.0 copy-start.2
  16.2 0.0 copy-start.3
  16.3 1.7 %collective-permute-start.2 = (bf16[32,512]{1,0:T(8,128)(2,1)S(1)}, bf16[32,512]{1,0:T(8,128)(2,1)S(1)}, u32[]{:S(2)}, u32[]{:S(2)}) collective-permute-start(bf16[32,512]{1,0:T(8,128)(2,1)S(1)} %get-tuple-element.41), channel_id=1, source_target_pairs={{0,2},{1,3},{2,4},{3,5},{4,6},{5,7},{6,0},{7,1},{8,10},{9,11},{10,... | collective-permute-start | bytes 98312 | tf_op jit(solution)/shard_map/ppermute | solution.py:361
  17.9 0.9 %collective-permute-start.3 = (bf16[32,512]{1,0:T(8,128)(2,1)S(1)}, bf16[32,512]{1,0:T(8,128)(2,1)S(1)}, u32[]{:S(2)}, u32[]{:S(2)}) collective-permute-start(bf16[32,512]{1,0:T(8,128)(2,1)S(1)} %get-tuple-element.42), channel_id=1, source_target_pairs={{0,4},{1,5},{2,6},{3,7},{4,0},{5,1},{6,2},{7,3},{8,12},{9,13},{10,... | collective-permute-start | bytes 98312 | tf_op jit(solution)/shard_map/ppermute | solution.py:361
  18.9 0.0 copy-start.4
  18.9 0.0 copy-start.5
  18.9 0.0 copy-start.6
  18.9 2.4 %collective-permute-start.4 = (bf16[32,512]{1,0:T(8,128)(2,1)S(1)}, bf16[32,512]{1,0:T(8,128)(2,1)S(1)}, u32[]{:S(2)}, u32[]{:S(2)}) collective-permute-start(bf16[32,512]{1,0:T(8,128)(2,1)S(1)} %get-tuple-element.43), channel_id=1, source_target_pairs={{0,6},{1,7},{2,0},{3,1},{4,2},{5,3},{6,4},{7,5},{8,14},{9,15},{10,... | collective-permute-start | bytes 98312 | tf_op jit(solution)/shard_map/ppermute | solution.py:361
  21.3 0.0 copy-done.1
  21.3 0.0 copy-done.2
  21.3 0.2 shard_map.141
  21.5 5.8 %all-to-all-done = bf16[16,16,512]{2,1,0:T(8,128)(2,1)S(1)} async-done(((bf16[16,16,512]{2,1,0:T(8,128)(2,1)}), bf16[16,16,512]{2,1,0:T(8,128)(2,1)S(1)}, u32[]{:S(2)}, u32[]{:S(2)}) %all-to-all-start) | async-done | bytes 262176 | tf_op jit(solution)/shard_map/all_to_all | solution.py:353
  27.3 0.0 copy-done.3
  27.3 0.0 copy-done.4
  27.3 0.0 copy-done.5
  27.3 0.0 copy-done.6
  27.3 1.5 %shard_map.142 = (f32[512,128]{1,0:T(8,128)S(1)}, f32[2,512,256]{2,1,0:T(8,128)S(1)}) custom-call(bf16[256,512]{1,0:T(8,128)(2,1)S(1)} %bitcast.14, bf16[128,128]{1,0:T(8,128)(2,1)S(1)} %copy-done.6, bf16[128,128]{1,0:T(8,128)(2,1)S(1)} %copy-done.5, f32[64,256]{1,0:T(8,128)S(1)} %copy-done.4, bf16[2,256,256]{2,1,0:T(8,128)(2,1)S(1)} %copy-done.3), custom_call_target="tpu_custom_call" | custom-call | flops 1073741824 | bytes 524288 | tf_op jit(solution)/shard_map/pallas_call | solution.py:399
  28.8 0.0 collective-permute-done.2.first_ref
  28.8 0.0 collective-permute-done.3.second_ref
  28.8 0.0 collective-permute-done.4.third_ref
  28.8 0.2 shard_map.143
  29.0 13.4 %all_to_all.20 = bf16[16,16,512]{2,1,0:T(8,128)(2,1)S(1)} all-to-all(bf16[16,16,512]{2,1,0:T(8,128)(2,1)S(1)} %bitcast.15), channel_id=1, replica_groups=mesh['seq'=16,'ch'=16] {'seq'}, dimensions={0} | all-to-all | bytes 524288 | tf_op jit(solution)/shard_map/all_to_all | solution.py:353
  42.4 0.9 %shard_map.144 = bf16[128,512]{1,0:T(8,128)(2,1)} custom-call(bf16[256,512]{1,0:T(8,128)(2,1)S(1)} %bitcast.8, f32[128,512]{1,0:T(8,128)S(1)} %get-tuple-element.47.gate_ref, bf16[128,128]{1,0:T(8,128)(2,1)S(1)} %get-tuple-element.52.blocks_ref), custom_call_target="tpu_custom_call" | custom-call | flops 67108864 | bytes 524288 | tf_op jit(solution)/shard_map/pallas_call | solution.py:407
  43.3 5.8 %all-to-all-start.2 = ((bf16[16,8,512]{2,1,0:T(8,128)(2,1)}), bf16[16,8,512]{2,1,0:T(8,128)(2,1)S(1)}, u32[]{:S(2)}, u32[]{:S(2)}) async-start(bf16[16,8,512]{2,1,0:T(8,128)(2,1)} %bitcast.4), calls=%async_computation.2 | async-start | bytes 262144 | tf_op jit(solution)/shard_map/all_to_all | solution.py:353
  49.1 1.1 %shard_map.145 = (bf16[512,128]{1,0:T(8,128)(2,1)}, f32[128,64]{1,0:T(8,128)S(1)}) custom-call(bf16[256,512]{1,0:T(8,128)(2,1)S(1)} %bitcast.9, f32[128,512]{1,0:T(8,128)S(1)} %get-tuple-element.47.gate_ref, bf16[128,512]{1,0:T(8,128)(2,1)S(1)} %get-tuple-element.53.returned_ref, bf16[128,128]{1,0:T(8,128)(2,1)S(1)} %get-tuple-element.46.own_ref), custom_call_target="tpu_custom_call" | custom-call | flops 67108864 | bytes 524288 | tf_op jit(solution)/shard_map/pallas_call | solution.py:415
  50.2 0.0 copy-start
  50.2 1.9 %shard_map.146.grads_ref = bf16[128,1024]{1,0:T(8,128)(2,1)S(1)} custom-call(bf16[256,512]{1,0:T(8,128)(2,1)S(1)} %bitcast.10, f32[2,512,256]{2,1,0:T(8,128)S(1)} %get-tuple-element.55.spectra_ref, bf16[128,128]{1,0:T(8,128)(2,1)S(1)} %copy-done.6, bf16[128,128]{1,0:T(8,128)(2,1)S(1)} %copy-done.5, f32[64,256]{1,0:T(8,128)S(1)} %copy-done.4, ...), custom_call_target="tpu_custom_call" | custom-call | flops 1073741824 | bytes 524288 | tf_op jit(solution)/shard_map/pallas_call | solution.py:409
  52.1 5.8 %all-to-all-done.2 = bf16[16,8,512]{2,1,0:T(8,128)(2,1)S(1)} async-done(((bf16[16,8,512]{2,1,0:T(8,128)(2,1)}), bf16[16,8,512]{2,1,0:T(8,128)(2,1)S(1)}, u32[]{:S(2)}, u32[]{:S(2)}) %all-to-all-start.2) | async-done | bytes 131104 | tf_op jit(solution)/shard_map/all_to_all | solution.py:353
  57.9 0.0 copy-done
  57.9 0.4 shard_map.147
  58.3 15.7 %all_to_all.21 = bf16[16,8,1152]{2,1,0:T(8,128)(2,1)S(1)} all-to-all(bf16[16,8,1152]{2,1,0:T(8,128)(2,1)S(1)} %bitcast.11), channel_id=1, replica_groups=mesh['seq'=16,'ch'=16] {'seq'}, dimensions={0} | all-to-all | bytes 589824 | tf_op jit(solution)/shard_map/all_to_all | solution.py:353
  74.0 1.0 %shard_map.148 = (bf16[512,128]{1,0:T(8,128)(2,1)}, bf16[512,128]{1,0:T(8,128)(2,1)}, f32[2,4,64]{2,1,0:T(4,128)}, f32[4,2,32]{2,1,0:T(2,128)}) custom-call(bf16[128,1152]{1,0:T(8,128)(2,1)S(1)} %bitcast.12), custom_call_target="tpu_custom_call" | custom-call | flops 67108864 | bytes 524288 | tf_op jit(solution)/shard_map/pallas_call | solution.py:420
  (2 shorter events, 0.0 us)
Async XLA Ops:
  1.9 1.3 %collective-permute-start = (bf16[64,512]{1,0:T(8,128)(2,1)S(1)}, bf16[64,512]{1,0:T(8,128)(2,1)S(1)}, u32[]{:S(2)}, u32[]{:S(2)}) collective-permute-start(bf16[64,512]{1,0:T(8,128)(2,1)S(1)} %get-tuple-element.34), channel_id=1, source_target_pairs={{0,1},{1,0},{2,3},{3,2},{4,5},{5,4},{6,7},{7,6},{8,9},{9,8},{10,11... | collective-permute-start | bytes 196616 | tf_op jit(solution)/shard_map/ppermute | solution.py:361
  3.2 13.0 %collective-permute-start.1 = (bf16[64,512]{1,0:T(8,128)(2,1)S(1)}, bf16[64,512]{1,0:T(8,128)(2,1)S(1)}, u32[]{:S(2)}, u32[]{:S(2)}) collective-permute-start(bf16[64,512]{1,0:T(8,128)(2,1)S(1)} %shard_map.139), channel_id=1, source_target_pairs={{0,8},{1,9},{2,10},{3,11},{4,12},{5,13},{6,14},{7,15},{8,0},{9,1},... | collective-permute-start | bytes 196616 | tf_op jit(solution)/shard_map/ppermute | solution.py:361
  10.4 16.9 %all-to-all-start = ((bf16[16,16,512]{2,1,0:T(8,128)(2,1)}), bf16[16,16,512]{2,1,0:T(8,128)(2,1)S(1)}, u32[]{:S(2)}, u32[]{:S(2)}) async-start(bf16[16,16,512]{2,1,0:T(8,128)(2,1)} %bitcast), calls=%async_computation | async-start | bytes 524288 | tf_op jit(solution)/shard_map/all_to_all | solution.py:353
  16.2 5.1 %copy-start.1 = (bf16[512,128]{1,0:T(8,128)(2,1)S(1)}, bf16[512,128]{1,0:T(8,128)(2,1)}, u32[]{:S(2)}) copy-start(bf16[512,128]{1,0:T(8,128)(2,1)} %gate_ref) | copy-start | bytes 393220
  16.2 5.1 %copy-start.2 = (bf16[2,64,64]{2,1,0:T(8,128)(2,1)S(1)}, bf16[2,64,64]{2,1,0:T(8,128)(2,1)}, u32[]{:S(2)}) copy-start(bf16[2,64,64]{2,1,0:T(8,128)(2,1)} %w_first_ref) | copy-start | bytes 49156
  16.2 11.1 %copy-start.3 = (bf16[2,256,256]{2,1,0:T(8,128)(2,1)S(1)}, bf16[2,256,256]{2,1,0:T(8,128)(2,1)}, u32[]{:S(2)}) copy-start(bf16[2,256,256]{2,1,0:T(8,128)(2,1)} %constant.11.clone.inner_ref) | copy-start | bytes 786436
  16.3 12.5 %collective-permute-start.2 = (bf16[32,512]{1,0:T(8,128)(2,1)S(1)}, bf16[32,512]{1,0:T(8,128)(2,1)S(1)}, u32[]{:S(2)}, u32[]{:S(2)}) collective-permute-start(bf16[32,512]{1,0:T(8,128)(2,1)S(1)} %get-tuple-element.41), channel_id=1, source_target_pairs={{0,2},{1,3},{2,4},{3,5},{4,6},{5,7},{6,0},{7,1},{8,10},{9,11},{10,... | collective-permute-start | bytes 98312 | tf_op jit(solution)/shard_map/ppermute | solution.py:361
  17.9 10.9 %collective-permute-start.3 = (bf16[32,512]{1,0:T(8,128)(2,1)S(1)}, bf16[32,512]{1,0:T(8,128)(2,1)S(1)}, u32[]{:S(2)}, u32[]{:S(2)}) collective-permute-start(bf16[32,512]{1,0:T(8,128)(2,1)S(1)} %get-tuple-element.42), channel_id=1, source_target_pairs={{0,4},{1,5},{2,6},{3,7},{4,0},{5,1},{6,2},{7,3},{8,12},{9,13},{10,... | collective-permute-start | bytes 98312 | tf_op jit(solution)/shard_map/ppermute | solution.py:361
  18.9 8.4 %copy-start.4 = (f32[64,256]{1,0:T(8,128)S(1)}, f32[64,256]{1,0:T(8,128)}, u32[]{:S(2)}) copy-start(f32[64,256]{1,0:T(8,128)} %constant.10.clone.twiddle_ref) | copy-start | bytes 196612
  18.9 8.4 %copy-start.5 = (bf16[128,128]{1,0:T(8,128)(2,1)S(1)}, bf16[128,128]{1,0:T(8,128)(2,1)}, u32[]{:S(2)}) copy-start(bf16[128,128]{1,0:T(8,128)(2,1)} %constant.9.clone.back_ref) | copy-start | bytes 98308
  18.9 8.4 %copy-start.6 = (bf16[128,128]{1,0:T(8,128)(2,1)S(1)}, bf16[128,128]{1,0:T(8,128)(2,1)}, u32[]{:S(2)}) copy-start(bf16[128,128]{1,0:T(8,128)(2,1)} %constant.8.clone.outer_ref) | copy-start | bytes 98308
  18.9 9.9 %collective-permute-start.4 = (bf16[32,512]{1,0:T(8,128)(2,1)S(1)}, bf16[32,512]{1,0:T(8,128)(2,1)S(1)}, u32[]{:S(2)}, u32[]{:S(2)}) collective-permute-start(bf16[32,512]{1,0:T(8,128)(2,1)S(1)} %get-tuple-element.43), channel_id=1, source_target_pairs={{0,6},{1,7},{2,0},{3,1},{4,2},{5,3},{6,4},{7,5},{8,14},{9,15},{10,... | collective-permute-start | bytes 98312 | tf_op jit(solution)/shard_map/ppermute | solution.py:361
  43.3 14.6 %all-to-all-start.2 = ((bf16[16,8,512]{2,1,0:T(8,128)(2,1)}), bf16[16,8,512]{2,1,0:T(8,128)(2,1)S(1)}, u32[]{:S(2)}, u32[]{:S(2)}) async-start(bf16[16,8,512]{2,1,0:T(8,128)(2,1)} %bitcast.4), calls=%async_computation.2 | async-start | bytes 262144 | tf_op jit(solution)/shard_map/all_to_all | solution.py:353
  50.2 7.7 %copy-start = (bf16[512,128]{1,0:T(8,128)(2,1)S(1)}, bf16[512,128]{1,0:T(8,128)(2,1)}, u32[]{:S(2)}) copy-start(bf16[512,128]{1,0:T(8,128)(2,1)} %d_out_ref.1) | copy-start | bytes 393220

commit v12 on v10

--- a/solution.py
+++ b/solution.py
@@ -94,9 +94,7 @@
     signal_hbm,
     filter_hbm,
     near_ref,
-    core_ref,
     far_ref,
-    cross_ref,
     pair_hbm,
     d_out_ref,
     w_second_ref,
@@ -122,7 +120,7 @@
     copies_of = ones_where(row == col % 32)
     row, col = iotas(128, 128)
     keep = row // 32 == col // 32
-    block = 2 * partner(row // 8 % 4, row // 32, 1) + row // 4 % 2
+    block = 2 * partner(row // 16 % 4, row // 64 * 2 + row // 8 % 2, 1) + row // 4 % 2
     order = ones_where((block == col % 32) & (row % 4 == col // 32))
     copies[0].wait()
     copies[1].wait()
@@ -136,19 +134,26 @@
     weights = dot(order, spread).astype(BF16)
     copies[3].wait()
     result = dot(weights, d_out_ref[...], NT).astype(BF16)
-    for zc, ref in enumerate((near_ref, core_ref, far_ref, cross_ref)):
-        ref[...] = result[32 * zc : 32 * zc + 32, :]
+    near_ref[...] = result[0:64, :]
+    far_ref[...] = result[64:128, :]
     leave.wait()
 
 
-def repack_kernel(*refs):
+def y_kernel(near_ref, far_ref, *outs):
+    for y, ref in enumerate(outs):
+        ref[0:16, :] = near_ref[16 * y : 16 * y + 16, :]
+        ref[16:32, :] = far_ref[16 * y : 16 * y + 16, :]
+
+
+def core_kernel(*refs):
     values = [ref[...].astype(F32) for ref in refs[:4]]
-    for y, ref in enumerate(refs[4:]):
-        ref[...] = jnp.concatenate([v[8 * y : 8 * y + 8, :] for v in values], axis=0).astype(BF16)
+    for core, ref in enumerate(refs[4:]):
+        pieces = [v[16 * z + 8 * core : 16 * z + 8 * core + 8, :] for v in values for z in range(2)]
+        ref[...] = jnp.concatenate(pieces, axis=0).astype(BF16)
 
 
 def source(col):
-    return partner(col // 32, col // 8 % 4, -1)
+    return partner(col // 16 % 4, col // 8 % 2 * 2 + col // 64, -1)
 
 
 def prepare_kernel(gate_ref, w_first_ref, gate_out_ref, blocks_ref, own_ref):
@@ -162,9 +167,8 @@
     gate_out_ref[...] = dot(unit(), gate_ref[...], NT)
 
 
-def gate_kernel(near_ref, first_ref, second_ref, third_ref, own_ref, gate_ref, conv_ref, pair_ref, returned_ref):
-    pieces = [ref[...] for ref in (near_ref, first_ref, second_ref, third_ref)]
-    returned = jnp.concatenate(pieces, axis=0)
+def gate_kernel(near_ref, core_ref, own_ref, gate_ref, conv_ref, pair_ref, returned_ref):
+    returned = jnp.concatenate([near_ref[...], core_ref[...]], axis=0)
     returned_ref[...] = returned
     incoming = dot(own_ref[...], returned) * gate_ref[...]
     rows = []
@@ -361,11 +365,11 @@
     outer, back, twiddle, inner = (jnp.asarray(t) for t in tables(lax.axis_size("seq"), rows))
     single, double = ((width, rows), BF16), ((2 * width, rows), BF16)
     slab = ((rows, width), BF16)
-    quarter = ((width // 4, rows), BF16)
+    quarter, half = ((width // 4, rows), BF16), ((width // 2, rows), BF16)
     held = [pltpu.with_memory_space_constraint(v, pltpu.HBM) for v in (d_out, w_second, signal, filter_raw)]
-    near, *others, pair = call(
+    near, far, pair = call(
         entry_kernel,
-        [quarter + (True,)] * 4 + [double],
+        [half + (True,), half + (True,), double],
         [
             pltpu.VMEM(d_out.shape, BF16),
             pltpu.VMEM(w_second.shape, BF16),
@@ -373,13 +377,15 @@
             pltpu.VMEM((2 * width, rows), BF16),
             pltpu.SemaphoreType.DMA((5,)),
         ],
-        spaces=([pl.ANY] * 4, [pltpu.VMEM] * 4 + [pl.ANY]),
+        spaces=([pl.ANY] * 4, [pltpu.VMEM] * 2 + [pl.ANY]),
     )(*held)
-    others = [shift(value, 0, zc) for zc, value in zip((1, 2, 3), others)]
+    far = shift(far, 0, 2)
     pair = exchange(pair, "seq")
-    near, *others = call(repack_kernel, [quarter] * 4, flops=1 << 35)(near, *others)
+    own, *others = call(y_kernel, [quarter] * 4, flops=1 << 35)(near, far)
+    others = [shift(value, y, 0) for y, value in zip((1, 2, 3), others)]
+    near, core = call(core_kernel, [half] * 2)(own, *others)
     pair = lax.optimization_barrier((pair, near))[0]
-    others = [shift(value, y, 0) for y, value in zip((1, 2, 3), others)]
+    core = shift(core, 0, 1)
     square = ((128, 128), BF16)
     gate, blocks, own = call(prepare_kernel, [((width, rows), F32), square, square])(gate, w_first)
     conv, spectra = call(
@@ -388,7 +394,7 @@
         [pltpu.VMEM((2 * width * 4, 128), F32)],
         flops=1 << 30,
     )(pair, outer, back, twiddle, inner)
-    pair, returned = call(gate_kernel, [double, single])(near, *others, own, gate, conv)
+    pair, returned = call(gate_kernel, [double, single])(near, core, own, gate, conv)
     pair = exchange(pair, "seq")
     mix = call(mix_kernel, [single])(pair, gate, blocks)[0]
     received = exchange(mix, "ch")

time: 80.7 us -> 77.8 us (0.964)
  starting transfers between devices: 28.6 us -> 24.7 us
  blocking collectives: 29.3 us -> 31.2 us
  waiting for transfers between devices: 11.9 us -> 11 us
    all_to_all x2, starting transfers between devices: 16.2 us -> 12.3 us  [exchange(): lax.all_to_all(pieces, axis, split_axis=0, concat_axis=0, tiled=True)]
    all_to_all x2, waiting for transfers between devices: 11.8 us -> 9.13 us  [exchange(): lax.all_to_all(pieces, axis, split_axis=0, concat_axis=0, tiled=True)]
    all_to_all x2, blocking collectives: 29.3 us -> 31.2 us  [exchange(): lax.all_to_all(pieces, axis, split_axis=0, concat_axis=0, tiled=True)]
    ppermute x6 -> x5, waiting for transfers between devices: 0.02 us -> 1.83 us  [shift(): return lax.ppermute(value, 'ch', pairs)]
    ppermute x6 -> x5, starting transfers between devices: 12.4 us -> 12.4 us  [shift(): return lax.ppermute(value, 'ch', pairs)]
    pallas_call x3 -> x4, Pallas kernels: 2.16 us -> 2.17 us  [the longest x1 1.97 us: shards(): call(entry_kernel, [half + (True,), half + (True,), double], [pltpu.VMEM(...]
  transfers between devices with their start and end apart: 8 -> 7, of which waited for: 2 -> 3; matrix products, arithmetic and copies ran while one was open for 0% -> 0% of each run, Pallas kernels for 6% -> 6%
where the time goes in v12:
time: 77.8 us; the launch traced here: 76.8 us
  blocking collectives  31.2 us (40%)
  starting transfers between devices  24.7 us (32%)
  waiting for transfers between devices  11 us (14%)
  Pallas kernels  9.06 us (12%)
  between operations  0.78 us (1%)
    all_to_all x2, blocking collectives, exchange(): lax.all_to_all(pieces, axis, split_axis=0, concat_axis=0, tiled=True)  31.2 us
    ppermute x5, starting transfers between devices, shift(): return lax.ppermute(value, 'ch', pairs)  12.4 us
    all_to_all x2, starting transfers between devices, exchange(): lax.all_to_all(pieces, axis, split_axis=0, concat_axis=0, tiled=True)  12.3 us
    all_to_all x2, waiting for transfers between devices, exchange(): lax.all_to_all(pieces, axis, split_axis=0, concat_axis=0, tiled=True)  9.13 us
    pallas_call x1, Pallas kernels, shards(): call(entry_kernel, [half + (True,), half + (True,), double], [pltpu.VMEM(...  1.97 us
    pallas_call x1, Pallas kernels, shards(): call(adjoint_kernel, [((width, 2 * rows), BF16)], [pltpu.VMEM((2 * width...  1.92 us
    ppermute x5, waiting for transfers between devices, shift(): return lax.ppermute(value, 'ch', pairs)  1.83 us
  transfers between devices with their start and end apart: 7, of which 3 were waited for; matrix products, arithmetic and copies ran while one was open for 0% of the time, Pallas kernels for 6%

profile of v12, /device:TPU:8, one launch (start us, length us, event | category | flops | bytes accessed | tf_op | source)
XLA Modules:
  0.0 76.8 jit_solution(17890748452615369100)
XLA Ops:
  0.6 2.0 %shard_map.137 = (bf16[64,512]{1,0:T(8,128)(2,1)S(1)}, bf16[64,512]{1,0:T(8,128)(2,1)S(1)}, bf16[256,512]{1,0:T(8,128)(2,1)}) custom-call(bf16[512,128]{1,0:T(8,128)(2,1)} %d_out_ref.1, bf16[4,32,32]{2,1,0:T(8,128)(2,1)} %w_second_hbm.1, bf16[512,128]{1,0:T(8,128)(2,1)} %signal_hbm.1, bf16[512,128]{1,0:T(8,128)(2,1)} %filter_hbm.1), custom_call_target="tpu_custom_call" | custom-call | flops 67108864 | bytes 524288 | tf_op jit(solution)/shard_map/pallas_call | solution.py:370
  2.6 7.3 %collective-permute-start = (bf16[64,512]{1,0:T(8,128)(2,1)S(1)}, bf16[64,512]{1,0:T(8,128)(2,1)S(1)}, u32[]{:S(2)}, u32[]{:S(2)}) collective-permute-start(bf16[64,512]{1,0:T(8,128)(2,1)S(1)} %get-tuple-element.29), channel_id=1, source_target_pairs={{0,8},{1,9},{2,10},{3,11},{4,12},{5,13},{6,14},{7,15},{8,0},{9,1},... | collective-permute-start | bytes 196616 | tf_op jit(solution)/shard_map/ppermute | solution.py:360
  9.9 5.8 %all-to-all-start = ((bf16[16,16,512]{2,1,0:T(8,128)(2,1)}), bf16[16,16,512]{2,1,0:T(8,128)(2,1)S(1)}, u32[]{:S(2)}, u32[]{:S(2)}) async-start(bf16[16,16,512]{2,1,0:T(8,128)(2,1)} %bitcast), calls=%async_computation | async-start | bytes 524288 | tf_op jit(solution)/shard_map/all_to_all | solution.py:352
  15.7 0.0 collective-permute-done.far_ref
  15.7 0.0 copy-start.1
  15.7 0.0 copy-start.2
  15.7 0.0 copy-start.3
  15.7 1.7 %collective-permute-start.1 = (bf16[32,512]{1,0:T(8,128)(2,1)S(1)}, bf16[32,512]{1,0:T(8,128)(2,1)S(1)}, u32[]{:S(2)}, u32[]{:S(2)}) collective-permute-start(bf16[32,512]{1,0:T(8,128)(2,1)S(1)} %get-tuple-element.31), channel_id=1, source_target_pairs={{0,2},{1,3},{2,4},{3,5},{4,6},{5,7},{6,0},{7,1},{8,10},{9,11},{10,... | collective-permute-start | bytes 98312 | tf_op jit(solution)/shard_map/ppermute | solution.py:360
  17.4 0.9 %collective-permute-start.2 = (bf16[32,512]{1,0:T(8,128)(2,1)S(1)}, bf16[32,512]{1,0:T(8,128)(2,1)S(1)}, u32[]{:S(2)}, u32[]{:S(2)}) collective-permute-start(bf16[32,512]{1,0:T(8,128)(2,1)S(1)} %get-tuple-element.32), channel_id=1, source_target_pairs={{0,4},{1,5},{2,6},{3,7},{4,0},{5,1},{6,2},{7,3},{8,12},{9,13},{10,... | collective-permute-start | bytes 98312 | tf_op jit(solution)/shard_map/ppermute | solution.py:360
  18.3 2.4 %collective-permute-start.3 = (bf16[32,512]{1,0:T(8,128)(2,1)S(1)}, bf16[32,512]{1,0:T(8,128)(2,1)S(1)}, u32[]{:S(2)}, u32[]{:S(2)}) collective-permute-start(bf16[32,512]{1,0:T(8,128)(2,1)S(1)} %get-tuple-element.33), channel_id=1, source_target_pairs={{0,6},{1,7},{2,0},{3,1},{4,2},{5,3},{6,4},{7,5},{8,14},{9,15},{10,... | collective-permute-start | bytes 98312 | tf_op jit(solution)/shard_map/ppermute | solution.py:360
  20.7 0.0 copy-done.1
  20.7 0.0 copy-done.2
  20.7 0.2 shard_map.140
  21.0 0.0 collective-permute-done.1.refs_1_
  21.0 1.8 %collective-permute-done.2.refs_2_ = bf16[32,512]{1,0:T(8,128)(2,1)S(1)} collective-permute-done((bf16[32,512]{1,0:T(8,128)(2,1)S(1)}, bf16[32,512]{1,0:T(8,128)(2,1)S(1)}, u32[]{:S(2)}, u32[]{:S(2)}) %collective-permute-start.2) | collective-permute-done | bytes 32800 | tf_op jit(solution)/shard_map/ppermute | solution.py:360
  22.8 0.0 collective-permute-done.3.refs_3_
  22.8 0.0 copy-start.4
  22.8 0.0 copy-start.5
  22.8 0.0 copy-start.6
  22.8 0.1 collective-permute-start.4
  22.9 3.3 %all-to-all-done = bf16[16,16,512]{2,1,0:T(8,128)(2,1)S(1)} async-done(((bf16[16,16,512]{2,1,0:T(8,128)(2,1)}), bf16[16,16,512]{2,1,0:T(8,128)(2,1)S(1)}, u32[]{:S(2)}, u32[]{:S(2)}) %all-to-all-start) | async-done | bytes 262176 | tf_op jit(solution)/shard_map/all_to_all | solution.py:352
  26.3 0.0 copy-done.3
  26.3 0.0 copy-done.4
  26.3 0.0 copy-done.5
  26.3 0.0 copy-done.6
  26.3 1.5 %shard_map.141 = (f32[512,128]{1,0:T(8,128)S(1)}, f32[2,512,256]{2,1,0:T(8,128)S(1)}) custom-call(bf16[256,512]{1,0:T(8,128)(2,1)S(1)} %bitcast.14, bf16[128,128]{1,0:T(8,128)(2,1)S(1)} %copy-done.6, bf16[128,128]{1,0:T(8,128)(2,1)S(1)} %copy-done.5, f32[64,256]{1,0:T(8,128)S(1)} %copy-done.4, bf16[2,256,256]{2,1,0:T(8,128)(2,1)S(1)} %copy-done.3), custom_call_target="tpu_custom_call" | custom-call | flops 1073741824 | bytes 524288 | tf_op jit(solution)/shard_map/pallas_call | solution.py:391
  27.8 0.0 collective-permute-done.4.core_ref
  27.8 0.2 shard_map.142
  28.0 15.5 %all_to_all.20 = bf16[16,16,512]{2,1,0:T(8,128)(2,1)S(1)} all-to-all(bf16[16,16,512]{2,1,0:T(8,128)(2,1)S(1)} %bitcast.15), channel_id=1, replica_groups=mesh['seq'=16,'ch'=16] {'seq'}, dimensions={0} | all-to-all | bytes 524288 | tf_op jit(solution)/shard_map/all_to_all | solution.py:352
  43.5 0.9 %shard_map.143 = bf16[128,512]{1,0:T(8,128)(2,1)} custom-call(bf16[256,512]{1,0:T(8,128)(2,1)S(1)} %bitcast.8, f32[128,512]{1,0:T(8,128)S(1)} %get-tuple-element.37.gate_ref, bf16[128,128]{1,0:T(8,128)(2,1)S(1)} %get-tuple-element.42.blocks_ref), custom_call_target="tpu_custom_call" | custom-call | flops 67108864 | bytes 524288 | tf_op jit(solution)/shard_map/pallas_call | solution.py:399
  44.4 6.6 %all-to-all-start.2 = ((bf16[16,8,512]{2,1,0:T(8,128)(2,1)}), bf16[16,8,512]{2,1,0:T(8,128)(2,1)S(1)}, u32[]{:S(2)}, u32[]{:S(2)}) async-start(bf16[16,8,512]{2,1,0:T(8,128)(2,1)} %bitcast.4), calls=%async_computation.2 | async-start | bytes 262144 | tf_op jit(solution)/shard_map/all_to_all | solution.py:352
  50.9 1.1 %shard_map.144 = (bf16[512,128]{1,0:T(8,128)(2,1)}, f32[128,64]{1,0:T(8,128)S(1)}) custom-call(bf16[256,512]{1,0:T(8,128)(2,1)S(1)} %bitcast.9, f32[128,512]{1,0:T(8,128)S(1)} %get-tuple-element.37.gate_ref, bf16[128,512]{1,0:T(8,128)(2,1)S(1)} %get-tuple-element.43.returned_ref, bf16[128,128]{1,0:T(8,128)(2,1)S(1)} %get-tuple-element.36.own_ref), custom_call_target="tpu_custom_call" | custom-call | flops 67108864 | bytes 524288 | tf_op jit(solution)/shard_map/pallas_call | solution.py:407
  52.0 0.0 copy-start
  52.0 1.9 %shard_map.145.grads_ref = bf16[128,1024]{1,0:T(8,128)(2,1)S(1)} custom-call(bf16[256,512]{1,0:T(8,128)(2,1)S(1)} %bitcast.10, f32[2,512,256]{2,1,0:T(8,128)S(1)} %get-tuple-element.45.spectra_ref, bf16[128,128]{1,0:T(8,128)(2,1)S(1)} %copy-done.6, bf16[128,128]{1,0:T(8,128)(2,1)S(1)} %copy-done.5, f32[64,256]{1,0:T(8,128)S(1)} %copy-done.4, ...), custom_call_target="tpu_custom_call" | custom-call | flops 1073741824 | bytes 524288 | tf_op jit(solution)/shard_map/pallas_call | solution.py:401
  53.9 5.8 %all-to-all-done.2 = bf16[16,8,512]{2,1,0:T(8,128)(2,1)S(1)} async-done(((bf16[16,8,512]{2,1,0:T(8,128)(2,1)}), bf16[16,8,512]{2,1,0:T(8,128)(2,1)S(1)}, u32[]{:S(2)}, u32[]{:S(2)}) %all-to-all-start.2) | async-done | bytes 131104 | tf_op jit(solution)/shard_map/all_to_all | solution.py:352
  59.7 0.0 copy-done
  59.7 0.4 shard_map.146
  60.1 15.7 %all_to_all.21 = bf16[16,8,1152]{2,1,0:T(8,128)(2,1)S(1)} all-to-all(bf16[16,8,1152]{2,1,0:T(8,128)(2,1)S(1)} %bitcast.11), channel_id=1, replica_groups=mesh['seq'=16,'ch'=16] {'seq'}, dimensions={0} | all-to-all | bytes 589824 | tf_op jit(solution)/shard_map/all_to_all | solution.py:352
  75.8 1.0 %shard_map.147 = (bf16[512,128]{1,0:T(8,128)(2,1)}, bf16[512,128]{1,0:T(8,128)(2,1)}, f32[2,4,64]{2,1,0:T(4,128)}, f32[4,2,32]{2,1,0:T(2,128)}) custom-call(bf16[128,1152]{1,0:T(8,128)(2,1)S(1)} %bitcast.12), custom_call_target="tpu_custom_call" | custom-call | flops 67108864 | bytes 524288 | tf_op jit(solution)/shard_map/pallas_call | solution.py:412
  (2 shorter events, 0.0 us)
Async XLA Ops:
  2.6 13.1 %collective-permute-start = (bf16[64,512]{1,0:T(8,128)(2,1)S(1)}, bf16[64,512]{1,0:T(8,128)(2,1)S(1)}, u32[]{:S(2)}, u32[]{:S(2)}) collective-permute-start(bf16[64,512]{1,0:T(8,128)(2,1)S(1)} %get-tuple-element.29), channel_id=1, source_target_pairs={{0,8},{1,9},{2,10},{3,11},{4,12},{5,13},{6,14},{7,15},{8,0},{9,1},... | collective-permute-start | bytes 196616 | tf_op jit(solution)/shard_map/ppermute | solution.py:360
  9.9 16.4 %all-to-all-start = ((bf16[16,16,512]{2,1,0:T(8,128)(2,1)}), bf16[16,16,512]{2,1,0:T(8,128)(2,1)S(1)}, u32[]{:S(2)}, u32[]{:S(2)}) async-start(bf16[16,16,512]{2,1,0:T(8,128)(2,1)} %bitcast), calls=%async_computation | async-start | bytes 524288 | tf_op jit(solution)/shard_map/all_to_all | solution.py:352
  15.7 5.1 %copy-start.1 = (bf16[512,128]{1,0:T(8,128)(2,1)S(1)}, bf16[512,128]{1,0:T(8,128)(2,1)}, u32[]{:S(2)}) copy-start(bf16[512,128]{1,0:T(8,128)(2,1)} %gate_ref.1) | copy-start | bytes 393220
  15.7 5.1 %copy-start.2 = (bf16[2,64,64]{2,1,0:T(8,128)(2,1)S(1)}, bf16[2,64,64]{2,1,0:T(8,128)(2,1)}, u32[]{:S(2)}) copy-start(bf16[2,64,64]{2,1,0:T(8,128)(2,1)} %w_first_ref.1) | copy-start | bytes 49156
  15.7 10.6 %copy-start.3 = (bf16[2,256,256]{2,1,0:T(8,128)(2,1)S(1)}, bf16[2,256,256]{2,1,0:T(8,128)(2,1)}, u32[]{:S(2)}) copy-start(bf16[2,256,256]{2,1,0:T(8,128)(2,1)} %constant.11.clone.inner_ref) | copy-start | bytes 786436
  15.7 5.3 %collective-permute-start.1 = (bf16[32,512]{1,0:T(8,128)(2,1)S(1)}, bf16[32,512]{1,0:T(8,128)(2,1)S(1)}, u32[]{:S(2)}, u32[]{:S(2)}) collective-permute-start(bf16[32,512]{1,0:T(8,128)(2,1)S(1)} %get-tuple-element.31), channel_id=1, source_target_pairs={{0,2},{1,3},{2,4},{3,5},{4,6},{5,7},{6,0},{7,1},{8,10},{9,11},{10,... | collective-permute-start | bytes 98312 | tf_op jit(solution)/shard_map/ppermute | solution.py:360
  17.4 5.4 %collective-permute-start.2 = (bf16[32,512]{1,0:T(8,128)(2,1)S(1)}, bf16[32,512]{1,0:T(8,128)(2,1)S(1)}, u32[]{:S(2)}, u32[]{:S(2)}) collective-permute-start(bf16[32,512]{1,0:T(8,128)(2,1)S(1)} %get-tuple-element.32), channel_id=1, source_target_pairs={{0,4},{1,5},{2,6},{3,7},{4,0},{5,1},{6,2},{7,3},{8,12},{9,13},{10,... | collective-permute-start | bytes 98312 | tf_op jit(solution)/shard_map/ppermute | solution.py:360
  18.3 4.5 %collective-permute-start.3 = (bf16[32,512]{1,0:T(8,128)(2,1)S(1)}, bf16[32,512]{1,0:T(8,128)(2,1)S(1)}, u32[]{:S(2)}, u32[]{:S(2)}) collective-permute-start(bf16[32,512]{1,0:T(8,128)(2,1)S(1)} %get-tuple-element.33), channel_id=1, source_target_pairs={{0,6},{1,7},{2,0},{3,1},{4,2},{5,3},{6,4},{7,5},{8,14},{9,15},{10,... | collective-permute-start | bytes 98312 | tf_op jit(solution)/shard_map/ppermute | solution.py:360
  22.8 3.5 %copy-start.4 = (f32[64,256]{1,0:T(8,128)S(1)}, f32[64,256]{1,0:T(8,128)}, u32[]{:S(2)}) copy-start(f32[64,256]{1,0:T(8,128)} %constant.10.clone.twiddle_ref) | copy-start | bytes 196612
  22.8 3.5 %copy-start.5 = (bf16[128,128]{1,0:T(8,128)(2,1)S(1)}, bf16[128,128]{1,0:T(8,128)(2,1)}, u32[]{:S(2)}) copy-start(bf16[128,128]{1,0:T(8,128)(2,1)} %constant.9.clone.back_ref) | copy-start | bytes 98308
  22.8 3.5 %copy-start.6 = (bf16[128,128]{1,0:T(8,128)(2,1)S(1)}, bf16[128,128]{1,0:T(8,128)(2,1)}, u32[]{:S(2)}) copy-start(bf16[128,128]{1,0:T(8,128)(2,1)} %constant.8.clone.outer_ref) | copy-start | bytes 98308
  22.8 4.9 %collective-permute-start.4 = (bf16[64,512]{1,0:T(8,128)(2,1)S(1)}, bf16[64,512]{1,0:T(8,128)(2,1)S(1)}, u32[]{:S(2)}, u32[]{:S(2)}) collective-permute-start(bf16[64,512]{1,0:T(8,128)(2,1)S(1)} %get-tuple-element.35), channel_id=1, source_target_pairs={{0,1},{1,0},{2,3},{3,2},{4,5},{5,4},{6,7},{7,6},{8,9},{9,8},{10,11... | collective-permute-start | bytes 196616 | tf_op jit(solution)/shard_map/ppermute | solution.py:360
  44.4 15.3 %all-to-all-start.2 = ((bf16[16,8,512]{2,1,0:T(8,128)(2,1)}), bf16[16,8,512]{2,1,0:T(8,128)(2,1)S(1)}, u32[]{:S(2)}, u32[]{:S(2)}) async-start(bf16[16,8,512]{2,1,0:T(8,128)(2,1)} %bitcast.4), calls=%async_computation.2 | async-start | bytes 262144 | tf_op jit(solution)/shard_map/all_to_all | solution.py:352
  52.0 7.7 %copy-start = (bf16[512,128]{1,0:T(8,128)(2,1)S(1)}, bf16[512,128]{1,0:T(8,128)(2,1)}, u32[]{:S(2)}) copy-start(bf16[512,128]{1,0:T(8,128)(2,1)} %d_out_ref.1) | copy-start | bytes 393220

commit v13 on v7

--- a/solution.py
+++ b/solution.py
@@ -48,7 +48,7 @@
     inner_high, inner_low = halves(inner.astype(np.float32))
     return (
         np.concatenate([outer_high, outer_low], 1),
-        np.stack([back_high, back_low]),
+        np.concatenate([back_high, back_low], 0),
         twiddle.astype(np.float32),
         np.stack([inner_high, inner_low]),
     )
@@ -126,9 +126,14 @@
     copies[0].wait()
     copies[1].wait()
     both = jnp.concatenate([both_ref[0], both_ref[1]], axis=1)
-    pair_ref[...] = dot(pairs, both, NT).astype(BF16)
-    leave = pltpu.make_async_copy(pair_ref, pair_hbm, sems.at[4])
-    leave.start()
+    leaving = []
+    for part in range(2):
+        place_of = pl.ds(128 * part, 128)
+        pair_ref[place_of, :] = dot(pairs[128 * part : 128 * part + 128, :], both, NT).astype(BF16)
+        leaving.append(
+            pltpu.make_async_copy(pair_ref.at[place_of], pair_hbm.at[place_of], sems.at[4 + part])
+        )
+        leaving[-1].start()
     copies[2].wait()
     flat = w_second_ref[...].reshape(128, 32)
     spread = jnp.where(keep, dot(flat, copies_of), 0.0).astype(BF16)
@@ -137,7 +142,8 @@
     result = dot(weights, d_out_ref[...], NT).astype(BF16)
     for ref, start in zip((near_ref, core_ref, far_ref), (0, 32, 64)):
         ref[...] = result[start : start + ref.shape[0], :]
-    leave.wait()
+    for copy in leaving:
+        copy.wait()
 
 
 def core_kernel(core_ref, far_ref, message_ref):
@@ -233,7 +239,8 @@
             jnp.concatenate([real * cosine + imag * sine, imag * cosine - real * sine], axis=0)
         )
     high, low = split(jnp.concatenate(columns, axis=1))
-    return dot(back_ref[0], high) + dot(back_ref[0], low) + dot(back_ref[1], high)
+    both = dot(back_ref[...], high)
+    return both[0:64, :] + both[64:128, :] + dot(back_ref[0:64, :], low)
 
 
 def conv_kernel(pair_ref, outer_ref, back_ref, twiddle_ref, inner_ref, conv_ref, spectra_ref, wide_ref):
@@ -268,9 +275,19 @@
     return jnp.concatenate([wide[16 * p : 16 * p + 8, :] for p in range(16)], axis=0)
 
 
-def mix_kernel(pair_ref, gate_ref, blocks_ref, mix_ref):
+def mix_kernel(pair_ref, gate_ref, blocks_ref, mix_hbm, mix_ref, sems):
     product = (conv_rows(pair_ref) * gate_ref[...]).astype(BF16)
-    mix_ref[...] = dot(blocks_ref[...], product, TN).astype(BF16)
+    leaving = []
+    for part in range(2):
+        place_of = pl.ds(256 * part, 256)
+        values = product[:, 256 * part : 256 * part + 256]
+        mix_ref[:, place_of] = dot(blocks_ref[...], values, TN).astype(BF16)
+        leaving.append(
+            pltpu.make_async_copy(mix_ref.at[:, place_of], mix_hbm.at[:, place_of], sems.at[part])
+        )
+        leaving[-1].start()
+    for copy in leaving:
+        copy.wait()
 
 
 def first_kernel(pair_ref, gate_ref, returned_ref, own_ref, grad_gate_ref, partial_ref):
@@ -375,7 +392,7 @@
             pltpu.VMEM(w_second.shape, BF16),
             pltpu.VMEM((2, rows, width), BF16),
             pltpu.VMEM((2 * width, rows), BF16),
-            pltpu.SemaphoreType.DMA((5,)),
+            pltpu.SemaphoreType.DMA((6,)),
         ],
         spaces=([pl.ANY] * 4, [pltpu.VMEM] * 3 + [pl.ANY]),
     )(*held)
@@ -395,7 +412,12 @@
     )(pair, outer, back, twiddle, inner)
     pair, returned = call(gate_kernel, [double, single])(near, *others, own, gate, conv)
     pair = exchange(pair, "seq")
-    mix = call(mix_kernel, [single])(pair, gate, blocks)[0]
+    mix = call(
+        mix_kernel,
+        [single],
+        [pltpu.VMEM((width, rows), BF16), pltpu.SemaphoreType.DMA((2,))],
+        spaces=([pltpu.VMEM] * 3, [pl.ANY]),
+    )(pair, gate, blocks)[0]
     received = exchange(mix, "ch")
     grads = call(
         adjoint_kernel,

time: 75.4 us -> 75.4 us (level)
  transfers between devices with their start and end apart: 7 -> 7, of which waited for: 3 -> 3; matrix products, arithmetic and copies ran while one was open for 0% -> 0% of each run, Pallas kernels for 7% -> 6%
where the time goes in v13:
time: 75.4 us; the launch traced here: 74.4 us
  blocking collectives  29.2 us (39%)
  starting transfers between devices  24.4 us (32%)
  waiting for transfers between devices  10.2 us (14%)
  Pallas kernels  9.06 us (12%)
  local copies, waits for them, and re-layouts  0.79 us (1%)
  between operations  0.78 us (1%)
    all_to_all x2, blocking collectives, exchange(): lax.all_to_all(pieces, axis, split_axis=0, concat_axis=0, tiled=True)  29.2 us
    ppermute x5, starting transfers between devices, shift(): return lax.ppermute(value, 'ch', pairs)  12.4 us
    all_to_all x2, starting transfers between devices, exchange(): lax.all_to_all(pieces, axis, split_axis=0, concat_axis=0, tiled=True)  12 us
    all_to_all x2, waiting for transfers between devices, exchange(): lax.all_to_all(pieces, axis, split_axis=0, concat_axis=0, tiled=True)  9.98 us
    pallas_call x1, Pallas kernels, shards(): call(entry_kernel, [quarter + (True,), quarter + (True,), half + (True,),...  1.98 us
    pallas_call x1, Pallas kernels, shards(): call(adjoint_kernel, [((width, 2 * rows), BF16)], [pltpu.VMEM((2 * width...  1.92 us
  transfers between devices with their start and end apart: 7, of which 3 were waited for; matrix products, arithmetic and copies ran while one was open for 0% of the time, Pallas kernels for 6%

profile of v13, /device:TPU:8, one launch (start us, length us, event | category | flops | bytes accessed | tf_op | source)
XLA Modules:
  0.0 74.4 jit_solution(13329834802775200729)
XLA Ops:
  0.6 2.0 %shard_map.137 = (bf16[32,512]{1,0:T(8,128)(2,1)S(1)}, bf16[32,512]{1,0:T(8,128)(2,1)S(1)}, bf16[64,512]{1,0:T(8,128)(2,1)S(1)}, bf16[256,512]{1,0:T(8,128)(2,1)}) custom-call(bf16[512,128]{1,0:T(8,128)(2,1)} %d_out_ref.1, bf16[4,32,32]{2,1,0:T(8,128)(2,1)} %w_second_hbm.1, bf16[512,128]{1,0:T(8,128)(2,1)} %signal_hbm.1, bf16[512,128]{1,0:T(8,128)(2,1)} %filter_hbm.1), custom_call_target="tpu_custom_call" | custom-call | flops 67108864 | bytes 524288 | tf_op jit(solution)/shard_map/pallas_call | solution.py:387
  2.6 7.3 %collective-permute-start = (bf16[64,512]{1,0:T(8,128)(2,1)S(1)}, bf16[64,512]{1,0:T(8,128)(2,1)S(1)}, u32[]{:S(2)}, u32[]{:S(2)}) collective-permute-start(bf16[64,512]{1,0:T(8,128)(2,1)S(1)} %get-tuple-element.29), channel_id=1, source_target_pairs={{0,8},{1,9},{2,10},{3,11},{4,12},{5,13},{6,14},{7,15},{8,0},{9,1},... | collective-permute-start | bytes 196616 | tf_op jit(solution)/shard_map/ppermute | solution.py:377
  9.9 5.8 %all-to-all-start = ((bf16[16,16,512]{2,1,0:T(8,128)(2,1)}), bf16[16,16,512]{2,1,0:T(8,128)(2,1)S(1)}, u32[]{:S(2)}, u32[]{:S(2)}) async-start(bf16[16,16,512]{2,1,0:T(8,128)(2,1)} %bitcast), calls=%async_computation | async-start | bytes 524288 | tf_op jit(solution)/shard_map/all_to_all | solution.py:369
  15.7 0.0 collective-permute-done.far_ref
  15.7 0.0 copy-start.1
  15.7 0.0 copy-start.2
  15.7 0.0 copy-start.3
  15.7 0.1 collective-permute-start.1
  15.8 0.8 %copy-done.1 = bf16[512,128]{1,0:T(8,128)(2,1)S(1)} copy-done((bf16[512,128]{1,0:T(8,128)(2,1)S(1)}, bf16[512,128]{1,0:T(8,128)(2,1)}, u32[]{:S(2)}) %copy-start.1) | copy-done | bytes 131096
  16.6 0.0 copy-done.2
  16.6 0.2 shard_map.140
  16.8 0.3 collective-permute-done.1.core_ref
  17.1 0.0 copy-start.4
  17.1 0.0 copy-start.5
  17.1 0.0 copy-start.6
  17.1 1.7 %collective-permute-start.2 = (bf16[32,512]{1,0:T(8,128)(2,1)S(1)}, bf16[32,512]{1,0:T(8,128)(2,1)S(1)}, u32[]{:S(2)}, u32[]{:S(2)}) collective-permute-start(bf16[32,512]{1,0:T(8,128)(2,1)S(1)} %get-tuple-element.31), channel_id=1, source_target_pairs={{0,2},{1,3},{2,4},{3,5},{4,6},{5,7},{6,0},{7,1},{8,10},{9,11},{10,... | collective-permute-start | bytes 98312 | tf_op jit(solution)/shard_map/ppermute | solution.py:377
  18.7 0.9 %collective-permute-start.3 = (bf16[32,512]{1,0:T(8,128)(2,1)S(1)}, bf16[32,512]{1,0:T(8,128)(2,1)S(1)}, u32[]{:S(2)}, u32[]{:S(2)}) collective-permute-start(bf16[32,512]{1,0:T(8,128)(2,1)S(1)} %get-tuple-element.32), channel_id=1, source_target_pairs={{0,4},{1,5},{2,6},{3,7},{4,0},{5,1},{6,2},{7,3},{8,12},{9,13},{10,... | collective-permute-start | bytes 98312 | tf_op jit(solution)/shard_map/ppermute | solution.py:377
  19.7 2.4 %collective-permute-start.4 = (bf16[32,512]{1,0:T(8,128)(2,1)S(1)}, bf16[32,512]{1,0:T(8,128)(2,1)S(1)}, u32[]{:S(2)}, u32[]{:S(2)}) collective-permute-start(bf16[32,512]{1,0:T(8,128)(2,1)S(1)} %get-tuple-element.33), channel_id=1, source_target_pairs={{0,6},{1,7},{2,0},{3,1},{4,2},{5,3},{6,4},{7,5},{8,14},{9,15},{10,... | collective-permute-start | bytes 98312 | tf_op jit(solution)/shard_map/ppermute | solution.py:377
  22.1 4.2 %all-to-all-done = bf16[16,16,512]{2,1,0:T(8,128)(2,1)S(1)} async-done(((bf16[16,16,512]{2,1,0:T(8,128)(2,1)}), bf16[16,16,512]{2,1,0:T(8,128)(2,1)S(1)}, u32[]{:S(2)}, u32[]{:S(2)}) %all-to-all-start) | async-done | bytes 262176 | tf_op jit(solution)/shard_map/all_to_all | solution.py:369
  26.3 0.0 copy-done.3
  26.3 0.0 copy-done.4
  26.3 0.0 copy-done.5
  26.3 0.0 copy-done.6
  26.3 1.5 %shard_map.141 = (f32[512,128]{1,0:T(8,128)S(1)}, f32[2,512,256]{2,1,0:T(8,128)S(1)}) custom-call(bf16[256,512]{1,0:T(8,128)(2,1)S(1)} %bitcast.14, bf16[128,128]{1,0:T(8,128)(2,1)S(1)} %copy-done.6, bf16[128,128]{1,0:T(8,128)(2,1)S(1)} %copy-done.5, f32[64,256]{1,0:T(8,128)S(1)} %copy-done.4, bf16[2,256,256]{2,1,0:T(8,128)(2,1)S(1)} %copy-done.3), custom_call_target="tpu_custom_call" | custom-call | flops 1073741824 | bytes 524288 | tf_op jit(solution)/shard_map/pallas_call | solution.py:407
  27.8 0.0 collective-permute-done.2.first_ref
  27.8 0.0 collective-permute-done.3.second_ref
  27.8 0.0 collective-permute-done.4.third_ref
  27.8 0.2 shard_map.142
  28.0 13.5 %all_to_all.20 = bf16[16,16,512]{2,1,0:T(8,128)(2,1)S(1)} all-to-all(bf16[16,16,512]{2,1,0:T(8,128)(2,1)S(1)} %bitcast.15), channel_id=1, replica_groups=mesh['seq'=16,'ch'=16] {'seq'}, dimensions={0} | all-to-all | bytes 524288 | tf_op jit(solution)/shard_map/all_to_all | solution.py:369
  41.5 0.9 %shard_map.143 = bf16[128,512]{1,0:T(8,128)(2,1)} custom-call(bf16[256,512]{1,0:T(8,128)(2,1)S(1)} %bitcast.8, f32[128,512]{1,0:T(8,128)S(1)} %get-tuple-element.35.gate_ref, bf16[128,128]{1,0:T(8,128)(2,1)S(1)} %get-tuple-element.40.blocks_ref), custom_call_target="tpu_custom_call" | custom-call | flops 67108864 | bytes 524288 | tf_op jit(solution)/shard_map/pallas_call | solution.py:415
  42.4 6.2 %all-to-all-start.2 = ((bf16[16,8,512]{2,1,0:T(8,128)(2,1)}), bf16[16,8,512]{2,1,0:T(8,128)(2,1)S(1)}, u32[]{:S(2)}, u32[]{:S(2)}) async-start(bf16[16,8,512]{2,1,0:T(8,128)(2,1)} %bitcast.4), calls=%async_computation.2 | async-start | bytes 262144 | tf_op jit(solution)/shard_map/all_to_all | solution.py:369
  48.6 1.1 %shard_map.144 = (bf16[512,128]{1,0:T(8,128)(2,1)}, f32[128,64]{1,0:T(8,128)S(1)}) custom-call(bf16[256,512]{1,0:T(8,128)(2,1)S(1)} %bitcast.9, f32[128,512]{1,0:T(8,128)S(1)} %get-tuple-element.35.gate_ref, bf16[128,512]{1,0:T(8,128)(2,1)S(1)} %get-tuple-element.41.returned_ref, bf16[128,128]{1,0:T(8,128)(2,1)S(1)} %get-tuple-element.34.own_ref), custom_call_target="tpu_custom_call" | custom-call | flops 67108864 | bytes 524288 | tf_op jit(solution)/shard_map/pallas_call | solution.py:428
  49.7 0.0 copy-start
  49.7 1.9 %shard_map.145.grads_ref = bf16[128,1024]{1,0:T(8,128)(2,1)S(1)} custom-call(bf16[256,512]{1,0:T(8,128)(2,1)S(1)} %bitcast.10, f32[2,512,256]{2,1,0:T(8,128)S(1)} %get-tuple-element.43.spectra_ref, bf16[128,128]{1,0:T(8,128)(2,1)S(1)} %copy-done.6, bf16[128,128]{1,0:T(8,128)(2,1)S(1)} %copy-done.5, f32[64,256]{1,0:T(8,128)S(1)} %copy-done.4, ...), custom_call_target="tpu_custom_call" | custom-call | flops 1073741824 | bytes 524288 | tf_op jit(solution)/shard_map/pallas_call | solution.py:422
  51.6 5.8 %all-to-all-done.2 = bf16[16,8,512]{2,1,0:T(8,128)(2,1)S(1)} async-done(((bf16[16,8,512]{2,1,0:T(8,128)(2,1)}), bf16[16,8,512]{2,1,0:T(8,128)(2,1)S(1)}, u32[]{:S(2)}, u32[]{:S(2)}) %all-to-all-start.2) | async-done | bytes 131104 | tf_op jit(solution)/shard_map/all_to_all | solution.py:369
  57.4 0.0 copy-done
  57.4 0.4 shard_map.146
  57.8 15.6 %all_to_all.21 = bf16[16,8,1152]{2,1,0:T(8,128)(2,1)S(1)} all-to-all(bf16[16,8,1152]{2,1,0:T(8,128)(2,1)S(1)} %bitcast.11), channel_id=1, replica_groups=mesh['seq'=16,'ch'=16] {'seq'}, dimensions={0} | all-to-all | bytes 589824 | tf_op jit(solution)/shard_map/all_to_all | solution.py:369
  73.4 1.0 %shard_map.147 = (bf16[512,128]{1,0:T(8,128)(2,1)}, bf16[512,128]{1,0:T(8,128)(2,1)}, f32[2,4,64]{2,1,0:T(4,128)}, f32[4,2,32]{2,1,0:T(2,128)}) custom-call(bf16[128,1152]{1,0:T(8,128)(2,1)S(1)} %bitcast.12), custom_call_target="tpu_custom_call" | custom-call | flops 67108864 | bytes 524288 | tf_op jit(solution)/shard_map/pallas_call | solution.py:433
  (2 shorter events, 0.0 us)
Async XLA Ops:
  2.6 13.1 %collective-permute-start = (bf16[64,512]{1,0:T(8,128)(2,1)S(1)}, bf16[64,512]{1,0:T(8,128)(2,1)S(1)}, u32[]{:S(2)}, u32[]{:S(2)}) collective-permute-start(bf16[64,512]{1,0:T(8,128)(2,1)S(1)} %get-tuple-element.29), channel_id=1, source_target_pairs={{0,8},{1,9},{2,10},{3,11},{4,12},{5,13},{6,14},{7,15},{8,0},{9,1},... | collective-permute-start | bytes 196616 | tf_op jit(solution)/shard_map/ppermute | solution.py:377
  9.9 16.4 %all-to-all-start = ((bf16[16,16,512]{2,1,0:T(8,128)(2,1)}), bf16[16,16,512]{2,1,0:T(8,128)(2,1)S(1)}, u32[]{:S(2)}, u32[]{:S(2)}) async-start(bf16[16,16,512]{2,1,0:T(8,128)(2,1)} %bitcast), calls=%async_computation | async-start | bytes 524288 | tf_op jit(solution)/shard_map/all_to_all | solution.py:369
  15.7 0.9 %copy-start.1 = (bf16[512,128]{1,0:T(8,128)(2,1)S(1)}, bf16[512,128]{1,0:T(8,128)(2,1)}, u32[]{:S(2)}) copy-start(bf16[512,128]{1,0:T(8,128)(2,1)} %gate_ref.1) | copy-start | bytes 393220
  15.7 0.9 %copy-start.2 = (bf16[2,64,64]{2,1,0:T(8,128)(2,1)S(1)}, bf16[2,64,64]{2,1,0:T(8,128)(2,1)}, u32[]{:S(2)}) copy-start(bf16[2,64,64]{2,1,0:T(8,128)(2,1)} %w_first_ref.1) | copy-start | bytes 49156
  15.7 10.6 %copy-start.3 = (bf16[2,256,256]{2,1,0:T(8,128)(2,1)S(1)}, bf16[2,256,256]{2,1,0:T(8,128)(2,1)}, u32[]{:S(2)}) copy-start(bf16[2,256,256]{2,1,0:T(8,128)(2,1)} %constant.11.clone.inner_ref) | copy-start | bytes 786436
  15.7 1.3 %collective-permute-start.1 = (bf16[64,512]{1,0:T(8,128)(2,1)S(1)}, bf16[64,512]{1,0:T(8,128)(2,1)S(1)}, u32[]{:S(2)}, u32[]{:S(2)}) collective-permute-start(bf16[64,512]{1,0:T(8,128)(2,1)S(1)} %shard_map.138), channel_id=1, source_target_pairs={{0,1},{1,0},{2,3},{3,2},{4,5},{5,4},{6,7},{7,6},{8,9},{9,8},{10,11... | collective-permute-start | bytes 196616 | tf_op jit(solution)/shard_map/ppermute | solution.py:377
  17.1 9.2 %copy-start.4 = (f32[64,256]{1,0:T(8,128)S(1)}, f32[64,256]{1,0:T(8,128)}, u32[]{:S(2)}) copy-start(f32[64,256]{1,0:T(8,128)} %constant.10.clone.twiddle_ref) | copy-start | bytes 196612
  17.1 9.2 %copy-start.5 = (bf16[128,128]{1,0:T(8,128)(2,1)S(1)}, bf16[128,128]{1,0:T(8,128)(2,1)}, u32[]{:S(2)}) copy-start(bf16[128,128]{1,0:T(8,128)(2,1)} %constant.9.clone.back_ref) | copy-start | bytes 98308
  17.1 9.2 %copy-start.6 = (bf16[128,128]{1,0:T(8,128)(2,1)S(1)}, bf16[128,128]{1,0:T(8,128)(2,1)}, u32[]{:S(2)}) copy-start(bf16[128,128]{1,0:T(8,128)(2,1)} %constant.8.clone.outer_ref) | copy-start | bytes 98308
  17.1 10.7 %collective-permute-start.2 = (bf16[32,512]{1,0:T(8,128)(2,1)S(1)}, bf16[32,512]{1,0:T(8,128)(2,1)S(1)}, u32[]{:S(2)}, u32[]{:S(2)}) collective-permute-start(bf16[32,512]{1,0:T(8,128)(2,1)S(1)} %get-tuple-element.31), channel_id=1, source_target_pairs={{0,2},{1,3},{2,4},{3,5},{4,6},{5,7},{6,0},{7,1},{8,10},{9,11},{10,... | collective-permute-start | bytes 98312 | tf_op jit(solution)/shard_map/ppermute | solution.py:377
  18.7 9.0 %collective-permute-start.3 = (bf16[32,512]{1,0:T(8,128)(2,1)S(1)}, bf16[32,512]{1,0:T(8,128)(2,1)S(1)}, u32[]{:S(2)}, u32[]{:S(2)}) collective-permute-start(bf16[32,512]{1,0:T(8,128)(2,1)S(1)} %get-tuple-element.32), channel_id=1, source_target_pairs={{0,4},{1,5},{2,6},{3,7},{4,0},{5,1},{6,2},{7,3},{8,12},{9,13},{10,... | collective-permute-start | bytes 98312 | tf_op jit(solution)/shard_map/ppermute | solution.py:377
  19.7 8.1 %collective-permute-start.4 = (bf16[32,512]{1,0:T(8,128)(2,1)S(1)}, bf16[32,512]{1,0:T(8,128)(2,1)S(1)}, u32[]{:S(2)}, u32[]{:S(2)}) collective-permute-start(bf16[32,512]{1,0:T(8,128)(2,1)S(1)} %get-tuple-element.33), channel_id=1, source_target_pairs={{0,6},{1,7},{2,0},{3,1},{4,2},{5,3},{6,4},{7,5},{8,14},{9,15},{10,... | collective-permute-start | bytes 98312 | tf_op jit(solution)/shard_map/ppermute | solution.py:377
  42.4 15.0 %all-to-all-start.2 = ((bf16[16,8,512]{2,1,0:T(8,128)(2,1)}), bf16[16,8,512]{2,1,0:T(8,128)(2,1)S(1)}, u32[]{:S(2)}, u32[]{:S(2)}) async-start(bf16[16,8,512]{2,1,0:T(8,128)(2,1)} %bitcast.4), calls=%async_computation.2 | async-start | bytes 262144 | tf_op jit(solution)/shard_map/all_to_all | solution.py:369
  49.7 7.7 %copy-start = (bf16[512,128]{1,0:T(8,128)(2,1)S(1)}, bf16[512,128]{1,0:T(8,128)(2,1)}, u32[]{:S(2)}) copy-start(bf16[512,128]{1,0:T(8,128)(2,1)} %d_out_ref.1) | copy-start | bytes 393220

commit v14 on v7

--- a/solution.py
+++ b/solution.py
@@ -308,10 +308,9 @@
         copies.append(pltpu.make_async_copy(source, target, sems.at[len(copies)]))
         copies[-1].start()
 
-    square = unit()
     for field, target in enumerate((signal_hbm, filter_hbm)):
         values = sums_ref[:, 512 * field : 512 * field + 512]
-        both_ref[field] = dot(values, square, TN).astype(BF16)
+        both_ref[field] = values.T
         leave(both_ref.at[field], target)
     wide = sums_ref[:, 1024:1152].astype(F32)
     total = wide[0:8, :]

time: 75.4 us -> 75.2 us (level)
  no operation moved by 1% of the time
where the time goes in v14:
time: 75.2 us; the launch traced here: 74.3 us
  blocking collectives  29.2 us (39%)
  starting transfers between devices  24.3 us (32%)
  waiting for transfers between devices  10.1 us (13%)
  Pallas kernels  9.09 us (12%)
  local copies, waits for them, and re-layouts  0.79 us (1%)
  between operations  0.78 us (1%)
    all_to_all x2, blocking collectives, exchange(): lax.all_to_all(pieces, axis, split_axis=0, concat_axis=0, tiled=True)  29.2 us
    ppermute x5, starting transfers between devices, shift(): return lax.ppermute(value, 'ch', pairs)  12.4 us
    all_to_all x2, starting transfers between devices, exchange(): lax.all_to_all(pieces, axis, split_axis=0, concat_axis=0, tiled=True)  11.9 us
    all_to_all x2, waiting for transfers between devices, exchange(): lax.all_to_all(pieces, axis, split_axis=0, concat_axis=0, tiled=True)  9.87 us
    pallas_call x1, Pallas kernels, shards(): call(adjoint_kernel, [((width, 2 * rows), BF16)], [pltpu.VMEM((2 * width...  2.03 us
    pallas_call x1, Pallas kernels, shards(): call(entry_kernel, [quarter + (True,), quarter + (True,), half + (True,),...  1.98 us
    pallas_call x1, Pallas kernels, shards(): call(conv_kernel, [((4 * width, 128), F32), ((2, 512, 256), F32)], [pltpu...  1.52 us
  transfers between devices with their start and end apart: 7, of which 3 were waited for; matrix products, arithmetic and copies ran while one was open for 0% of the time, Pallas kernels for 7%

profile of v14, /device:TPU:8, one launch (start us, length us, event | category | flops | bytes accessed | tf_op | source)
XLA Modules:
  0.0 74.3 jit_solution(16088388265955771030)
XLA Ops:
  0.6 2.0 %shard_map.137 = (bf16[32,512]{1,0:T(8,128)(2,1)S(1)}, bf16[32,512]{1,0:T(8,128)(2,1)S(1)}, bf16[64,512]{1,0:T(8,128)(2,1)S(1)}, bf16[256,512]{1,0:T(8,128)(2,1)}) custom-call(bf16[512,128]{1,0:T(8,128)(2,1)} %d_out_ref.1, bf16[4,32,32]{2,1,0:T(8,128)(2,1)} %w_second_hbm.1, bf16[512,128]{1,0:T(8,128)(2,1)} %signal_hbm.1, bf16[512,128]{1,0:T(8,128)(2,1)} %filter_hbm.1), custom_call_target="tpu_custom_call" | custom-call | flops 67108864 | bytes 524288 | tf_op jit(solution)/shard_map/pallas_call | solution.py:369
  2.6 7.3 %collective-permute-start = (bf16[64,512]{1,0:T(8,128)(2,1)S(1)}, bf16[64,512]{1,0:T(8,128)(2,1)S(1)}, u32[]{:S(2)}, u32[]{:S(2)}) collective-permute-start(bf16[64,512]{1,0:T(8,128)(2,1)S(1)} %get-tuple-element.29), channel_id=1, source_target_pairs={{0,8},{1,9},{2,10},{3,11},{4,12},{5,13},{6,14},{7,15},{8,0},{9,1},... | collective-permute-start | bytes 196616 | tf_op jit(solution)/shard_map/ppermute | solution.py:359
  9.9 5.8 %all-to-all-start = ((bf16[16,16,512]{2,1,0:T(8,128)(2,1)}), bf16[16,16,512]{2,1,0:T(8,128)(2,1)S(1)}, u32[]{:S(2)}, u32[]{:S(2)}) async-start(bf16[16,16,512]{2,1,0:T(8,128)(2,1)} %bitcast), calls=%async_computation | async-start | bytes 524288 | tf_op jit(solution)/shard_map/all_to_all | solution.py:351
  15.7 0.0 collective-permute-done.far_ref
  15.7 0.0 copy-start.1
  15.7 0.0 copy-start.2
  15.7 0.0 copy-start.3
  15.7 0.1 collective-permute-start.1
  15.8 0.8 %copy-done.1 = bf16[512,128]{1,0:T(8,128)(2,1)S(1)} copy-done((bf16[512,128]{1,0:T(8,128)(2,1)S(1)}, bf16[512,128]{1,0:T(8,128)(2,1)}, u32[]{:S(2)}) %copy-start.1) | copy-done | bytes 131096
  16.6 0.0 copy-done.2
  16.6 0.2 shard_map.140
  16.8 0.3 collective-permute-done.1.core_ref
  17.1 0.0 copy-start.4
  17.1 0.0 copy-start.5
  17.1 0.0 copy-start.6
  17.1 1.7 %collective-permute-start.2 = (bf16[32,512]{1,0:T(8,128)(2,1)S(1)}, bf16[32,512]{1,0:T(8,128)(2,1)S(1)}, u32[]{:S(2)}, u32[]{:S(2)}) collective-permute-start(bf16[32,512]{1,0:T(8,128)(2,1)S(1)} %get-tuple-element.31), channel_id=1, source_target_pairs={{0,2},{1,3},{2,4},{3,5},{4,6},{5,7},{6,0},{7,1},{8,10},{9,11},{10,... | collective-permute-start | bytes 98312 | tf_op jit(solution)/shard_map/ppermute | solution.py:359
  18.7 0.9 %collective-permute-start.3 = (bf16[32,512]{1,0:T(8,128)(2,1)S(1)}, bf16[32,512]{1,0:T(8,128)(2,1)S(1)}, u32[]{:S(2)}, u32[]{:S(2)}) collective-permute-start(bf16[32,512]{1,0:T(8,128)(2,1)S(1)} %get-tuple-element.32), channel_id=1, source_target_pairs={{0,4},{1,5},{2,6},{3,7},{4,0},{5,1},{6,2},{7,3},{8,12},{9,13},{10,... | collective-permute-start | bytes 98312 | tf_op jit(solution)/shard_map/ppermute | solution.py:359
  19.7 2.4 %collective-permute-start.4 = (bf16[32,512]{1,0:T(8,128)(2,1)S(1)}, bf16[32,512]{1,0:T(8,128)(2,1)S(1)}, u32[]{:S(2)}, u32[]{:S(2)}) collective-permute-start(bf16[32,512]{1,0:T(8,128)(2,1)S(1)} %get-tuple-element.33), channel_id=1, source_target_pairs={{0,6},{1,7},{2,0},{3,1},{4,2},{5,3},{6,4},{7,5},{8,14},{9,15},{10,... | collective-permute-start | bytes 98312 | tf_op jit(solution)/shard_map/ppermute | solution.py:359
  22.1 4.2 %all-to-all-done = bf16[16,16,512]{2,1,0:T(8,128)(2,1)S(1)} async-done(((bf16[16,16,512]{2,1,0:T(8,128)(2,1)}), bf16[16,16,512]{2,1,0:T(8,128)(2,1)S(1)}, u32[]{:S(2)}, u32[]{:S(2)}) %all-to-all-start) | async-done | bytes 262176 | tf_op jit(solution)/shard_map/all_to_all | solution.py:351
  26.3 0.0 copy-done.3
  26.3 0.0 copy-done.4
  26.3 0.0 copy-done.5
  26.3 0.0 copy-done.6
  26.3 1.5 %shard_map.141 = (f32[512,128]{1,0:T(8,128)S(1)}, f32[2,512,256]{2,1,0:T(8,128)S(1)}) custom-call(bf16[256,512]{1,0:T(8,128)(2,1)S(1)} %bitcast.14, bf16[128,128]{1,0:T(8,128)(2,1)S(1)} %copy-done.6, bf16[2,64,128]{2,1,0:T(8,128)(2,1)S(1)} %copy-done.5, f32[64,256]{1,0:T(8,128)S(1)} %copy-done.4, bf16[2,256,256]{2,1,0:T(8,128)(2,1)S(1)} %copy-done.3), custom_call_target="tpu_custom_call" | custom-call | flops 1073741824 | bytes 524288 | tf_op jit(solution)/shard_map/pallas_call | solution.py:389
  27.8 0.0 collective-permute-done.2.first_ref
  27.8 0.0 collective-permute-done.3.second_ref
  27.8 0.0 collective-permute-done.4.third_ref
  27.9 0.2 shard_map.142
  28.0 13.5 %all_to_all.20 = bf16[16,16,512]{2,1,0:T(8,128)(2,1)S(1)} all-to-all(bf16[16,16,512]{2,1,0:T(8,128)(2,1)S(1)} %bitcast.15), channel_id=1, replica_groups=mesh['seq'=16,'ch'=16] {'seq'}, dimensions={0} | all-to-all | bytes 524288 | tf_op jit(solution)/shard_map/all_to_all | solution.py:351
  41.6 0.9 %shard_map.143 = bf16[128,512]{1,0:T(8,128)(2,1)} custom-call(bf16[256,512]{1,0:T(8,128)(2,1)S(1)} %bitcast.8, f32[128,512]{1,0:T(8,128)S(1)} %get-tuple-element.35.gate_ref, bf16[128,128]{1,0:T(8,128)(2,1)S(1)} %get-tuple-element.40.blocks_ref), custom_call_target="tpu_custom_call" | custom-call | flops 67108864 | bytes 524288 | tf_op jit(solution)/shard_map/pallas_call | solution.py:397
  42.4 6.2 %all-to-all-start.2 = ((bf16[16,8,512]{2,1,0:T(8,128)(2,1)}), bf16[16,8,512]{2,1,0:T(8,128)(2,1)S(1)}, u32[]{:S(2)}, u32[]{:S(2)}) async-start(bf16[16,8,512]{2,1,0:T(8,128)(2,1)} %bitcast.4), calls=%async_computation.2 | async-start | bytes 262144 | tf_op jit(solution)/shard_map/all_to_all | solution.py:351
  48.6 1.1 %shard_map.144 = (bf16[512,128]{1,0:T(8,128)(2,1)}, f32[128,64]{1,0:T(8,128)S(1)}) custom-call(bf16[256,512]{1,0:T(8,128)(2,1)S(1)} %bitcast.9, f32[128,512]{1,0:T(8,128)S(1)} %get-tuple-element.35.gate_ref, bf16[128,512]{1,0:T(8,128)(2,1)S(1)} %get-tuple-element.41.returned_ref, bf16[128,128]{1,0:T(8,128)(2,1)S(1)} %get-tuple-element.34.own_ref), custom_call_target="tpu_custom_call" | custom-call | flops 67108864 | bytes 524288 | tf_op jit(solution)/shard_map/pallas_call | solution.py:405
  49.6 0.0 copy-start
  49.6 2.0 %shard_map.145.grads_ref = bf16[128,1024]{1,0:T(8,128)(2,1)S(1)} custom-call(bf16[256,512]{1,0:T(8,128)(2,1)S(1)} %bitcast.10, f32[2,512,256]{2,1,0:T(8,128)S(1)} %get-tuple-element.43.spectra_ref, bf16[128,128]{1,0:T(8,128)(2,1)S(1)} %copy-done.6, bf16[2,64,128]{2,1,0:T(8,128)(2,1)S(1)} %copy-done.5, f32[64,256]{1,0:T(8,128)S(1)} %copy-done.4, ...), custom_call_target="tpu_custom_call" | custom-call | flops 1073741824 | bytes 524288 | tf_op jit(solution)/shard_map/pallas_call | solution.py:399
  51.7 5.7 %all-to-all-done.2 = bf16[16,8,512]{2,1,0:T(8,128)(2,1)S(1)} async-done(((bf16[16,8,512]{2,1,0:T(8,128)(2,1)}), bf16[16,8,512]{2,1,0:T(8,128)(2,1)S(1)}, u32[]{:S(2)}, u32[]{:S(2)}) %all-to-all-start.2) | async-done | bytes 131104 | tf_op jit(solution)/shard_map/all_to_all | solution.py:351
  57.4 0.0 copy-done
  57.4 0.4 shard_map.146
  57.7 15.6 %all_to_all.21 = bf16[16,8,1152]{2,1,0:T(8,128)(2,1)S(1)} all-to-all(bf16[16,8,1152]{2,1,0:T(8,128)(2,1)S(1)} %bitcast.11), channel_id=1, replica_groups=mesh['seq'=16,'ch'=16] {'seq'}, dimensions={0} | all-to-all | bytes 589824 | tf_op jit(solution)/shard_map/all_to_all | solution.py:351
  73.4 0.9 %shard_map.147 = (bf16[512,128]{1,0:T(8,128)(2,1)}, bf16[512,128]{1,0:T(8,128)(2,1)}, f32[2,4,64]{2,1,0:T(4,128)}, f32[4,2,32]{2,1,0:T(2,128)}) custom-call(bf16[128,1152]{1,0:T(8,128)(2,1)S(1)} %bitcast.12), custom_call_target="tpu_custom_call" | custom-call | flops 67108864 | bytes 524288 | tf_op jit(solution)/shard_map/pallas_call | solution.py:410
  (2 shorter events, 0.0 us)
Async XLA Ops:
  2.6 13.1 %collective-permute-start = (bf16[64,512]{1,0:T(8,128)(2,1)S(1)}, bf16[64,512]{1,0:T(8,128)(2,1)S(1)}, u32[]{:S(2)}, u32[]{:S(2)}) collective-permute-start(bf16[64,512]{1,0:T(8,128)(2,1)S(1)} %get-tuple-element.29), channel_id=1, source_target_pairs={{0,8},{1,9},{2,10},{3,11},{4,12},{5,13},{6,14},{7,15},{8,0},{9,1},... | collective-permute-start | bytes 196616 | tf_op jit(solution)/shard_map/ppermute | solution.py:359
  9.9 16.4 %all-to-all-start = ((bf16[16,16,512]{2,1,0:T(8,128)(2,1)}), bf16[16,16,512]{2,1,0:T(8,128)(2,1)S(1)}, u32[]{:S(2)}, u32[]{:S(2)}) async-start(bf16[16,16,512]{2,1,0:T(8,128)(2,1)} %bitcast), calls=%async_computation | async-start | bytes 524288 | tf_op jit(solution)/shard_map/all_to_all | solution.py:351
  15.7 0.9 %copy-start.1 = (bf16[512,128]{1,0:T(8,128)(2,1)S(1)}, bf16[512,128]{1,0:T(8,128)(2,1)}, u32[]{:S(2)}) copy-start(bf16[512,128]{1,0:T(8,128)(2,1)} %gate_ref.1) | copy-start | bytes 393220
  15.7 0.9 %copy-start.2 = (bf16[2,64,64]{2,1,0:T(8,128)(2,1)S(1)}, bf16[2,64,64]{2,1,0:T(8,128)(2,1)}, u32[]{:S(2)}) copy-start(bf16[2,64,64]{2,1,0:T(8,128)(2,1)} %w_first_ref.1) | copy-start | bytes 49156
  15.7 10.6 %copy-start.3 = (bf16[2,256,256]{2,1,0:T(8,128)(2,1)S(1)}, bf16[2,256,256]{2,1,0:T(8,128)(2,1)}, u32[]{:S(2)}) copy-start(bf16[2,256,256]{2,1,0:T(8,128)(2,1)} %constant.11.clone.inner_ref) | copy-start | bytes 786436
  15.7 1.3 %collective-permute-start.1 = (bf16[64,512]{1,0:T(8,128)(2,1)S(1)}, bf16[64,512]{1,0:T(8,128)(2,1)S(1)}, u32[]{:S(2)}, u32[]{:S(2)}) collective-permute-start(bf16[64,512]{1,0:T(8,128)(2,1)S(1)} %shard_map.138), channel_id=1, source_target_pairs={{0,1},{1,0},{2,3},{3,2},{4,5},{5,4},{6,7},{7,6},{8,9},{9,8},{10,11... | collective-permute-start | bytes 196616 | tf_op jit(solution)/shard_map/ppermute | solution.py:359
  17.1 9.2 %copy-start.4 = (f32[64,256]{1,0:T(8,128)S(1)}, f32[64,256]{1,0:T(8,128)}, u32[]{:S(2)}) copy-start(f32[64,256]{1,0:T(8,128)} %constant.10.clone.twiddle_ref) | copy-start | bytes 196612
  17.1 9.2 %copy-start.5 = (bf16[2,64,128]{2,1,0:T(8,128)(2,1)S(1)}, bf16[2,64,128]{2,1,0:T(8,128)(2,1)}, u32[]{:S(2)}) copy-start(bf16[2,64,128]{2,1,0:T(8,128)(2,1)} %constant.9.clone.back_ref) | copy-start | bytes 98308
  17.1 9.2 %copy-start.6 = (bf16[128,128]{1,0:T(8,128)(2,1)S(1)}, bf16[128,128]{1,0:T(8,128)(2,1)}, u32[]{:S(2)}) copy-start(bf16[128,128]{1,0:T(8,128)(2,1)} %constant.8.clone.outer_ref) | copy-start | bytes 98308
  17.1 10.7 %collective-permute-start.2 = (bf16[32,512]{1,0:T(8,128)(2,1)S(1)}, bf16[32,512]{1,0:T(8,128)(2,1)S(1)}, u32[]{:S(2)}, u32[]{:S(2)}) collective-permute-start(bf16[32,512]{1,0:T(8,128)(2,1)S(1)} %get-tuple-element.31), channel_id=1, source_target_pairs={{0,2},{1,3},{2,4},{3,5},{4,6},{5,7},{6,0},{7,1},{8,10},{9,11},{10,... | collective-permute-start | bytes 98312 | tf_op jit(solution)/shard_map/ppermute | solution.py:359
  18.7 9.1 %collective-permute-start.3 = (bf16[32,512]{1,0:T(8,128)(2,1)S(1)}, bf16[32,512]{1,0:T(8,128)(2,1)S(1)}, u32[]{:S(2)}, u32[]{:S(2)}) collective-permute-start(bf16[32,512]{1,0:T(8,128)(2,1)S(1)} %get-tuple-element.32), channel_id=1, source_target_pairs={{0,4},{1,5},{2,6},{3,7},{4,0},{5,1},{6,2},{7,3},{8,12},{9,13},{10,... | collective-permute-start | bytes 98312 | tf_op jit(solution)/shard_map/ppermute | solution.py:359
  19.7 8.2 %collective-permute-start.4 = (bf16[32,512]{1,0:T(8,128)(2,1)S(1)}, bf16[32,512]{1,0:T(8,128)(2,1)S(1)}, u32[]{:S(2)}, u32[]{:S(2)}) collective-permute-start(bf16[32,512]{1,0:T(8,128)(2,1)S(1)} %get-tuple-element.33), channel_id=1, source_target_pairs={{0,6},{1,7},{2,0},{3,1},{4,2},{5,3},{6,4},{7,5},{8,14},{9,15},{10,... | collective-permute-start | bytes 98312 | tf_op jit(solution)/shard_map/ppermute | solution.py:359
  42.4 15.0 %all-to-all-start.2 = ((bf16[16,8,512]{2,1,0:T(8,128)(2,1)}), bf16[16,8,512]{2,1,0:T(8,128)(2,1)S(1)}, u32[]{:S(2)}, u32[]{:S(2)}) async-start(bf16[16,8,512]{2,1,0:T(8,128)(2,1)} %bitcast.4), calls=%async_computation.2 | async-start | bytes 262144 | tf_op jit(solution)/shard_map/all_to_all | solution.py:351
  49.6 7.7 %copy-start = (bf16[512,128]{1,0:T(8,128)(2,1)S(1)}, bf16[512,128]{1,0:T(8,128)(2,1)}, u32[]{:S(2)}) copy-start(bf16[512,128]{1,0:T(8,128)(2,1)} %d_out_ref.1) | copy-start | bytes 393220

commit v15 on v7

--- a/solution.py
+++ b/solution.py
@@ -48,7 +48,7 @@
     inner_high, inner_low = halves(inner.astype(np.float32))
     return (
         np.concatenate([outer_high, outer_low], 1),
-        np.stack([back_high, back_low]),
+        np.concatenate([back_high, back_low], 0),
         twiddle.astype(np.float32),
         np.stack([inner_high, inner_low]),
     )
@@ -233,7 +233,8 @@
             jnp.concatenate([real * cosine + imag * sine, imag * cosine - real * sine], axis=0)
         )
     high, low = split(jnp.concatenate(columns, axis=1))
-    return dot(back_ref[0], high) + dot(back_ref[0], low) + dot(back_ref[1], high)
+    both = dot(back_ref[...], high)
+    return both[0:64, :] + both[64:128, :] + dot(back_ref[0:64, :], low)
 
 
 def conv_kernel(pair_ref, outer_ref, back_ref, twiddle_ref, inner_ref, conv_ref, spectra_ref, wide_ref):

time: 75.4 us -> 75.4 us (level)
  transfers between devices with their start and end apart: 7 -> 7, of which waited for: 3 -> 3; matrix products, arithmetic and copies ran while one was open for 0% -> 0% of each run, Pallas kernels for 7% -> 6%
where the time goes in v15:
time: 75.4 us; the launch traced here: 74.4 us
  blocking collectives  29.2 us (39%)
  starting transfers between devices  24.4 us (32%)
  waiting for transfers between devices  10.2 us (14%)
  Pallas kernels  9.05 us (12%)
  local copies, waits for them, and re-layouts  0.79 us (1%)
  between operations  0.78 us (1%)
    all_to_all x2, blocking collectives, exchange(): lax.all_to_all(pieces, axis, split_axis=0, concat_axis=0, tiled=True)  29.2 us
    ppermute x5, starting transfers between devices, shift(): return lax.ppermute(value, 'ch', pairs)  12.4 us
    all_to_all x2, starting transfers between devices, exchange(): lax.all_to_all(pieces, axis, split_axis=0, concat_axis=0, tiled=True)  12 us
    all_to_all x2, waiting for transfers between devices, exchange(): lax.all_to_all(pieces, axis, split_axis=0, concat_axis=0, tiled=True)  9.98 us
    pallas_call x1, Pallas kernels, shards(): call(entry_kernel, [quarter + (True,), quarter + (True,), half + (True,),...  1.98 us
    pallas_call x1, Pallas kernels, shards(): call(adjoint_kernel, [((width, 2 * rows), BF16)], [pltpu.VMEM((2 * width...  1.92 us
  transfers between devices with their start and end apart: 7, of which 3 were waited for; matrix products, arithmetic and copies ran while one was open for 0% of the time, Pallas kernels for 6%

profile of v15, /device:TPU:8, one launch (start us, length us, event | category | flops | bytes accessed | tf_op | source)
XLA Modules:
  0.0 74.4 jit_solution(11445496039099396056)
XLA Ops:
  0.6 2.0 %shard_map.137 = (bf16[32,512]{1,0:T(8,128)(2,1)S(1)}, bf16[32,512]{1,0:T(8,128)(2,1)S(1)}, bf16[64,512]{1,0:T(8,128)(2,1)S(1)}, bf16[256,512]{1,0:T(8,128)(2,1)}) custom-call(bf16[512,128]{1,0:T(8,128)(2,1)} %d_out_ref.1, bf16[4,32,32]{2,1,0:T(8,128)(2,1)} %w_second_hbm.1, bf16[512,128]{1,0:T(8,128)(2,1)} %signal_hbm.1, bf16[512,128]{1,0:T(8,128)(2,1)} %filter_hbm.1), custom_call_target="tpu_custom_call" | custom-call | flops 67108864 | bytes 524288 | tf_op jit(solution)/shard_map/pallas_call | solution.py:371
  2.6 7.3 %collective-permute-start = (bf16[64,512]{1,0:T(8,128)(2,1)S(1)}, bf16[64,512]{1,0:T(8,128)(2,1)S(1)}, u32[]{:S(2)}, u32[]{:S(2)}) collective-permute-start(bf16[64,512]{1,0:T(8,128)(2,1)S(1)} %get-tuple-element.29), channel_id=1, source_target_pairs={{0,8},{1,9},{2,10},{3,11},{4,12},{5,13},{6,14},{7,15},{8,0},{9,1},... | collective-permute-start | bytes 196616 | tf_op jit(solution)/shard_map/ppermute | solution.py:361
  9.9 5.8 %all-to-all-start = ((bf16[16,16,512]{2,1,0:T(8,128)(2,1)}), bf16[16,16,512]{2,1,0:T(8,128)(2,1)S(1)}, u32[]{:S(2)}, u32[]{:S(2)}) async-start(bf16[16,16,512]{2,1,0:T(8,128)(2,1)} %bitcast), calls=%async_computation | async-start | bytes 524288 | tf_op jit(solution)/shard_map/all_to_all | solution.py:353
  15.7 0.0 collective-permute-done.far_ref
  15.7 0.0 copy-start.1
  15.7 0.0 copy-start.2
  15.7 0.0 copy-start.3
  15.7 0.1 collective-permute-start.1
  15.8 0.8 %copy-done.1 = bf16[512,128]{1,0:T(8,128)(2,1)S(1)} copy-done((bf16[512,128]{1,0:T(8,128)(2,1)S(1)}, bf16[512,128]{1,0:T(8,128)(2,1)}, u32[]{:S(2)}) %copy-start.1) | copy-done | bytes 131096
  16.6 0.0 copy-done.2
  16.6 0.2 shard_map.140
  16.8 0.3 collective-permute-done.1.core_ref
  17.1 0.0 copy-start.4
  17.1 0.0 copy-start.5
  17.1 0.0 copy-start.6
  17.1 1.7 %collective-permute-start.2 = (bf16[32,512]{1,0:T(8,128)(2,1)S(1)}, bf16[32,512]{1,0:T(8,128)(2,1)S(1)}, u32[]{:S(2)}, u32[]{:S(2)}) collective-permute-start(bf16[32,512]{1,0:T(8,128)(2,1)S(1)} %get-tuple-element.31), channel_id=1, source_target_pairs={{0,2},{1,3},{2,4},{3,5},{4,6},{5,7},{6,0},{7,1},{8,10},{9,11},{10,... | collective-permute-start | bytes 98312 | tf_op jit(solution)/shard_map/ppermute | solution.py:361
  18.7 0.9 %collective-permute-start.3 = (bf16[32,512]{1,0:T(8,128)(2,1)S(1)}, bf16[32,512]{1,0:T(8,128)(2,1)S(1)}, u32[]{:S(2)}, u32[]{:S(2)}) collective-permute-start(bf16[32,512]{1,0:T(8,128)(2,1)S(1)} %get-tuple-element.32), channel_id=1, source_target_pairs={{0,4},{1,5},{2,6},{3,7},{4,0},{5,1},{6,2},{7,3},{8,12},{9,13},{10,... | collective-permute-start | bytes 98312 | tf_op jit(solution)/shard_map/ppermute | solution.py:361
  19.7 2.4 %collective-permute-start.4 = (bf16[32,512]{1,0:T(8,128)(2,1)S(1)}, bf16[32,512]{1,0:T(8,128)(2,1)S(1)}, u32[]{:S(2)}, u32[]{:S(2)}) collective-permute-start(bf16[32,512]{1,0:T(8,128)(2,1)S(1)} %get-tuple-element.33), channel_id=1, source_target_pairs={{0,6},{1,7},{2,0},{3,1},{4,2},{5,3},{6,4},{7,5},{8,14},{9,15},{10,... | collective-permute-start | bytes 98312 | tf_op jit(solution)/shard_map/ppermute | solution.py:361
  22.1 4.2 %all-to-all-done = bf16[16,16,512]{2,1,0:T(8,128)(2,1)S(1)} async-done(((bf16[16,16,512]{2,1,0:T(8,128)(2,1)}), bf16[16,16,512]{2,1,0:T(8,128)(2,1)S(1)}, u32[]{:S(2)}, u32[]{:S(2)}) %all-to-all-start) | async-done | bytes 262176 | tf_op jit(solution)/shard_map/all_to_all | solution.py:353
  26.3 0.0 copy-done.3
  26.3 0.0 copy-done.4
  26.3 0.0 copy-done.5
  26.3 0.0 copy-done.6
  26.3 1.5 %shard_map.141 = (f32[512,128]{1,0:T(8,128)S(1)}, f32[2,512,256]{2,1,0:T(8,128)S(1)}) custom-call(bf16[256,512]{1,0:T(8,128)(2,1)S(1)} %bitcast.14, bf16[128,128]{1,0:T(8,128)(2,1)S(1)} %copy-done.6, bf16[128,128]{1,0:T(8,128)(2,1)S(1)} %copy-done.5, f32[64,256]{1,0:T(8,128)S(1)} %copy-done.4, bf16[2,256,256]{2,1,0:T(8,128)(2,1)S(1)} %copy-done.3), custom_call_target="tpu_custom_call" | custom-call | flops 1073741824 | bytes 524288 | tf_op jit(solution)/shard_map/pallas_call | solution.py:391
  27.8 0.0 collective-permute-done.2.first_ref
  27.8 0.0 collective-permute-done.3.second_ref
  27.8 0.0 collective-permute-done.4.third_ref
  27.8 0.2 shard_map.142
  28.0 13.5 %all_to_all.20 = bf16[16,16,512]{2,1,0:T(8,128)(2,1)S(1)} all-to-all(bf16[16,16,512]{2,1,0:T(8,128)(2,1)S(1)} %bitcast.15), channel_id=1, replica_groups=mesh['seq'=16,'ch'=16] {'seq'}, dimensions={0} | all-to-all | bytes 524288 | tf_op jit(solution)/shard_map/all_to_all | solution.py:353
  41.5 0.9 %shard_map.143 = bf16[128,512]{1,0:T(8,128)(2,1)} custom-call(bf16[256,512]{1,0:T(8,128)(2,1)S(1)} %bitcast.8, f32[128,512]{1,0:T(8,128)S(1)} %get-tuple-element.35.gate_ref, bf16[128,128]{1,0:T(8,128)(2,1)S(1)} %get-tuple-element.40.blocks_ref), custom_call_target="tpu_custom_call" | custom-call | flops 67108864 | bytes 524288 | tf_op jit(solution)/shard_map/pallas_call | solution.py:399
  42.4 6.2 %all-to-all-start.2 = ((bf16[16,8,512]{2,1,0:T(8,128)(2,1)}), bf16[16,8,512]{2,1,0:T(8,128)(2,1)S(1)}, u32[]{:S(2)}, u32[]{:S(2)}) async-start(bf16[16,8,512]{2,1,0:T(8,128)(2,1)} %bitcast.4), calls=%async_computation.2 | async-start | bytes 262144 | tf_op jit(solution)/shard_map/all_to_all | solution.py:353
  48.6 1.1 %shard_map.144 = (bf16[512,128]{1,0:T(8,128)(2,1)}, f32[128,64]{1,0:T(8,128)S(1)}) custom-call(bf16[256,512]{1,0:T(8,128)(2,1)S(1)} %bitcast.9, f32[128,512]{1,0:T(8,128)S(1)} %get-tuple-element.35.gate_ref, bf16[128,512]{1,0:T(8,128)(2,1)S(1)} %get-tuple-element.41.returned_ref, bf16[128,128]{1,0:T(8,128)(2,1)S(1)} %get-tuple-element.34.own_ref), custom_call_target="tpu_custom_call" | custom-call | flops 67108864 | bytes 524288 | tf_op jit(solution)/shard_map/pallas_call | solution.py:407
  49.6 0.0 copy-start
  49.6 1.9 %shard_map.145.grads_ref = bf16[128,1024]{1,0:T(8,128)(2,1)S(1)} custom-call(bf16[256,512]{1,0:T(8,128)(2,1)S(1)} %bitcast.10, f32[2,512,256]{2,1,0:T(8,128)S(1)} %get-tuple-element.43.spectra_ref, bf16[128,128]{1,0:T(8,128)(2,1)S(1)} %copy-done.6, bf16[128,128]{1,0:T(8,128)(2,1)S(1)} %copy-done.5, f32[64,256]{1,0:T(8,128)S(1)} %copy-done.4, ...), custom_call_target="tpu_custom_call" | custom-call | flops 1073741824 | bytes 524288 | tf_op jit(solution)/shard_map/pallas_call | solution.py:401
  51.6 5.8 %all-to-all-done.2 = bf16[16,8,512]{2,1,0:T(8,128)(2,1)S(1)} async-done(((bf16[16,8,512]{2,1,0:T(8,128)(2,1)}), bf16[16,8,512]{2,1,0:T(8,128)(2,1)S(1)}, u32[]{:S(2)}, u32[]{:S(2)}) %all-to-all-start.2) | async-done | bytes 131104 | tf_op jit(solution)/shard_map/all_to_all | solution.py:353
  57.4 0.0 copy-done
  57.4 0.4 shard_map.146
  57.7 15.6 %all_to_all.21 = bf16[16,8,1152]{2,1,0:T(8,128)(2,1)S(1)} all-to-all(bf16[16,8,1152]{2,1,0:T(8,128)(2,1)S(1)} %bitcast.11), channel_id=1, replica_groups=mesh['seq'=16,'ch'=16] {'seq'}, dimensions={0} | all-to-all | bytes 589824 | tf_op jit(solution)/shard_map/all_to_all | solution.py:353
  73.4 1.0 %shard_map.147 = (bf16[512,128]{1,0:T(8,128)(2,1)}, bf16[512,128]{1,0:T(8,128)(2,1)}, f32[2,4,64]{2,1,0:T(4,128)}, f32[4,2,32]{2,1,0:T(2,128)}) custom-call(bf16[128,1152]{1,0:T(8,128)(2,1)S(1)} %bitcast.12), custom_call_target="tpu_custom_call" | custom-call | flops 67108864 | bytes 524288 | tf_op jit(solution)/shard_map/pallas_call | solution.py:412
  (2 shorter events, 0.0 us)
Async XLA Ops:
  2.6 13.1 %collective-permute-start = (bf16[64,512]{1,0:T(8,128)(2,1)S(1)}, bf16[64,512]{1,0:T(8,128)(2,1)S(1)}, u32[]{:S(2)}, u32[]{:S(2)}) collective-permute-start(bf16[64,512]{1,0:T(8,128)(2,1)S(1)} %get-tuple-element.29), channel_id=1, source_target_pairs={{0,8},{1,9},{2,10},{3,11},{4,12},{5,13},{6,14},{7,15},{8,0},{9,1},... | collective-permute-start | bytes 196616 | tf_op jit(solution)/shard_map/ppermute | solution.py:361
  9.9 16.4 %all-to-all-start = ((bf16[16,16,512]{2,1,0:T(8,128)(2,1)}), bf16[16,16,512]{2,1,0:T(8,128)(2,1)S(1)}, u32[]{:S(2)}, u32[]{:S(2)}) async-start(bf16[16,16,512]{2,1,0:T(8,128)(2,1)} %bitcast), calls=%async_computation | async-start | bytes 524288 | tf_op jit(solution)/shard_map/all_to_all | solution.py:353
  15.7 0.9 %copy-start.1 = (bf16[512,128]{1,0:T(8,128)(2,1)S(1)}, bf16[512,128]{1,0:T(8,128)(2,1)}, u32[]{:S(2)}) copy-start(bf16[512,128]{1,0:T(8,128)(2,1)} %gate_ref.1) | copy-start | bytes 393220
  15.7 0.9 %copy-start.2 = (bf16[2,64,64]{2,1,0:T(8,128)(2,1)S(1)}, bf16[2,64,64]{2,1,0:T(8,128)(2,1)}, u32[]{:S(2)}) copy-start(bf16[2,64,64]{2,1,0:T(8,128)(2,1)} %w_first_ref.1) | copy-start | bytes 49156
  15.7 10.6 %copy-start.3 = (bf16[2,256,256]{2,1,0:T(8,128)(2,1)S(1)}, bf16[2,256,256]{2,1,0:T(8,128)(2,1)}, u32[]{:S(2)}) copy-start(bf16[2,256,256]{2,1,0:T(8,128)(2,1)} %constant.11.clone.inner_ref) | copy-start | bytes 786436
  15.7 1.3 %collective-permute-start.1 = (bf16[64,512]{1,0:T(8,128)(2,1)S(1)}, bf16[64,512]{1,0:T(8,128)(2,1)S(1)}, u32[]{:S(2)}, u32[]{:S(2)}) collective-permute-start(bf16[64,512]{1,0:T(8,128)(2,1)S(1)} %shard_map.138), channel_id=1, source_target_pairs={{0,1},{1,0},{2,3},{3,2},{4,5},{5,4},{6,7},{7,6},{8,9},{9,8},{10,11... | collective-permute-start | bytes 196616 | tf_op jit(solution)/shard_map/ppermute | solution.py:361
  17.1 9.2 %copy-start.4 = (f32[64,256]{1,0:T(8,128)S(1)}, f32[64,256]{1,0:T(8,128)}, u32[]{:S(2)}) copy-start(f32[64,256]{1,0:T(8,128)} %constant.10.clone.twiddle_ref) | copy-start | bytes 196612
  17.1 9.2 %copy-start.5 = (bf16[128,128]{1,0:T(8,128)(2,1)S(1)}, bf16[128,128]{1,0:T(8,128)(2,1)}, u32[]{:S(2)}) copy-start(bf16[128,128]{1,0:T(8,128)(2,1)} %constant.9.clone.back_ref) | copy-start | bytes 98308
  17.1 9.2 %copy-start.6 = (bf16[128,128]{1,0:T(8,128)(2,1)S(1)}, bf16[128,128]{1,0:T(8,128)(2,1)}, u32[]{:S(2)}) copy-start(bf16[128,128]{1,0:T(8,128)(2,1)} %constant.8.clone.outer_ref) | copy-start | bytes 98308
  17.1 10.7 %collective-permute-start.2 = (bf16[32,512]{1,0:T(8,128)(2,1)S(1)}, bf16[32,512]{1,0:T(8,128)(2,1)S(1)}, u32[]{:S(2)}, u32[]{:S(2)}) collective-permute-start(bf16[32,512]{1,0:T(8,128)(2,1)S(1)} %get-tuple-element.31), channel_id=1, source_target_pairs={{0,2},{1,3},{2,4},{3,5},{4,6},{5,7},{6,0},{7,1},{8,10},{9,11},{10,... | collective-permute-start | bytes 98312 | tf_op jit(solution)/shard_map/ppermute | solution.py:361
  18.7 9.0 %collective-permute-start.3 = (bf16[32,512]{1,0:T(8,128)(2,1)S(1)}, bf16[32,512]{1,0:T(8,128)(2,1)S(1)}, u32[]{:S(2)}, u32[]{:S(2)}) collective-permute-start(bf16[32,512]{1,0:T(8,128)(2,1)S(1)} %get-tuple-element.32), channel_id=1, source_target_pairs={{0,4},{1,5},{2,6},{3,7},{4,0},{5,1},{6,2},{7,3},{8,12},{9,13},{10,... | collective-permute-start | bytes 98312 | tf_op jit(solution)/shard_map/ppermute | solution.py:361
  19.7 8.1 %collective-permute-start.4 = (bf16[32,512]{1,0:T(8,128)(2,1)S(1)}, bf16[32,512]{1,0:T(8,128)(2,1)S(1)}, u32[]{:S(2)}, u32[]{:S(2)}) collective-permute-start(bf16[32,512]{1,0:T(8,128)(2,1)S(1)} %get-tuple-element.33), channel_id=1, source_target_pairs={{0,6},{1,7},{2,0},{3,1},{4,2},{5,3},{6,4},{7,5},{8,14},{9,15},{10,... | collective-permute-start | bytes 98312 | tf_op jit(solution)/shard_map/ppermute | solution.py:361
  42.4 15.0 %all-to-all-start.2 = ((bf16[16,8,512]{2,1,0:T(8,128)(2,1)}), bf16[16,8,512]{2,1,0:T(8,128)(2,1)S(1)}, u32[]{:S(2)}, u32[]{:S(2)}) async-start(bf16[16,8,512]{2,1,0:T(8,128)(2,1)} %bitcast.4), calls=%async_computation.2 | async-start | bytes 262144 | tf_op jit(solution)/shard_map/all_to_all | solution.py:353
  49.6 7.7 %copy-start = (bf16[512,128]{1,0:T(8,128)(2,1)S(1)}, bf16[512,128]{1,0:T(8,128)(2,1)}, u32[]{:S(2)}) copy-start(bf16[512,128]{1,0:T(8,128)(2,1)} %d_out_ref.1) | copy-start | bytes 393220
